TPU v7x, 128 devices: a whole 4x4x4 slice. The times are simulated.
128 devices in a mesh: rows: 64 (over y, z, x), rhs: 2 (over core).
Axes of the slice: x: 4, y: 4, z: 4, core: 2. Of those that a mesh axis runs over, the one named last changes fastest.
Arguments:
- rhs: float32 [2, 32768, 4096], P(None, 'rows', 'rhs'), may hold values from -8 to 8
- factor: bfloat16 [2, 32768, 4, 512], P(None, 'rows', None, 'rhs'), may hold values from -0.125 to 0.125
- inverses: float32 [4, 512, 512], replicated, may hold values from -1 to 1, as said below
Outputs:
- state: float32 [2, 32768, 4096], P(None, 'rows', 'rhs')
Inputs may be any that keep to these rules, and one draw needn't show every extreme that they name: Each inverses[p] is unit lower triangular: ones on the diagonal, zeros above it.
All inputs are finite; a program needn't handle non-finite values.
Results may differ from a plain program's by a relative error of at most 0.003.
Values may be sent and summed in bfloat16 or wider, within the bound.
No kernel may reach another device: no remote copies, remote signals or barrier semaphores. Data moves between devices by JAX's collectives and lax.ppermute only.
A program may use at most 128 MiB of HBM per device.

v0:
```python
import jax
import jax.numpy as jnp
from jax import lax
from jax.sharding import PartitionSpec as P


def from_root(value, axis, root):
    mine = lax.axis_index(axis) == root
    return lax.psum(jnp.where(mine, value, jnp.zeros_like(value)), axis)


def local(rhs, factor, inverses):
    count = lax.axis_size("rows")
    place = lax.axis_index("rows")
    cycles = rhs.shape[0]
    panels = inverses.shape[0]
    tile_ids = jnp.arange(cycles, dtype=jnp.int32) * count + place
    whole = lax.all_gather(factor, "rhs", axis=3, tiled=True)
    state = rhs
    for panel in range(panels):
        panel_cols = whole[:, :, panel, :]
        solved = jnp.dot(inverses[panel], state[0], precision=lax.Precision.HIGHEST)
        solved, sent = (solved, from_root(solved.astype(jnp.bfloat16), "rows", panel))
        first = jnp.where(place == panel, solved, state[0])
        state = jnp.concatenate([first[None], state[1:]], axis=0)
        delta = jnp.einsum("crk,kn->crn", panel_cols, sent, preferred_element_type=jnp.float32)
        keep = (tile_ids > panel)[:, None, None]
        state = state - jnp.where(keep, delta, jnp.float32(0.0))
    return state


def solution(mesh):
    return jax.shard_map(
        local,
        mesh=mesh,
        in_specs=(P(None, "rows", "rhs"), P(None, "rows", None, "rhs"), P()),
        out_specs=P(None, "rows", "rhs"),
        check_vma=False,
    )
```

profile of v0, /device:TPU:6, one launch (start us, length us, event | category | flops | bytes accessed | tf_op | source)
XLA Modules:
  0.0 612.6 jit_solution(14402450064248325402)
XLA Ops:
  7.4 10.9 %convert_select_fusion = (bf16[512,2048]{1,0:T(8,128)(2,1)}, f32[512,2048]{1,0:T(8,128)}) fusion(pred[]{:T(512)S(6)} %eq.19, f32[2,512,2048]{2,1,0:T(8,128)} %param.3, f32[4,512,512]{2,1,0:T(8,128)} %param.5), kind=kOutput, calls=%fused_computation.31 | convolution fusion | flops 6444548096 | bytes 11534337 | tf_op jit(solution)/shard_map/dot_general | solution.py:22
  18.3 0.0 all-gather.2.cloned.1.call-start
  18.4 1.6 copy.4
  20.1 4.7 slice.54
  24.8 5.2 fusion.5
  30.0 121.7 %all-reduce.5.cloned.1.call-done = bf16[512,2048]{1,0:T(8,128)(2,1)} async-done(((bf16[512,2048]{1,0:T(8,128)(2,1)}), bf16[512,2048]{1,0:T(8,128)(2,1)}) %all-reduce.5.cloned.1.call-update) | async-done | bytes 2097168 | tf_op jit(solution)/shard_map/psum | solution.py:9
  151.7 7.0 %maximum_subtract_fusion = f32[2,512,2048]{2,1,0:T(8,128)S(1)} fusion(f32[1,512,2048]{2,1,0:T(8,128)} %slice.54, f32[1,512,2048]{2,1,0:T(8,128)} %fusion.5, pred[2]{0:T(512)(128)(4,1)S(1)} %broadcast_compare_fusion.3, bf16[512,2048]{1,0:T(8,128)(2,1)} %all-reduce.5.cloned.1.call-done, bf16[2,512,4,512]{3,1,0,2:T(8,128)(2,1)} %all-gather.2.cloned.1.call-done), kind=kOutput, calls=%fused_computation | convolution fusion | flops 2153775104 | bytes 19922946 | tf_op jit(solution)/shard_map/crk,kn->crn/dot_general | solution.py:26
  158.8 10.8 %fusion.10 = (bf16[512,2048]{1,0:T(8,128)(2,1)}, f32[2048,512]{0,1:T(8,128)}) fusion(pred[]{:T(512)S(6)} %eq.18, f32[4,512,512]{2,1,0:T(8,128)} %param.5, f32[2,512,2048]{2,1,0:T(8,128)S(1)} %maximum_subtract_fusion), kind=kOutput, calls=%fused_computation.24 | convolution fusion | flops 6444548096 | bytes 11534337 | tf_op jit(solution)/shard_map/dot_general | solution.py:22
  169.6 0.2 all-reduce.9.cloned.1.call-start
  169.9 4.8 slice.70
  174.7 4.9 fusion.2
  179.6 120.0 %all-reduce.7.cloned.1.call-done = bf16[512,2048]{1,0:T(8,128)(2,1)} async-done(((bf16[512,2048]{1,0:T(8,128)(2,1)}), bf16[512,2048]{1,0:T(8,128)(2,1)}) %all-reduce.7.cloned.1.call-update) | async-done | bytes 2097168 | tf_op jit(solution)/shard_map/psum | solution.py:9
  299.6 7.0 %maximum_subtract_fusion.1 = f32[2,512,2048]{2,1,0:T(8,128)S(1)} fusion(f32[1,512,2048]{2,1,0:T(8,128)} %slice.70, f32[1,512,2048]{2,1,0:T(8,128)} %fusion.2, pred[2]{0:T(512)(128)(4,1)S(1)} %broadcast_compare_fusion.2, bf16[512,2048]{1,0:T(8,128)(2,1)} %all-reduce.7.cloned.1.call-done, bf16[2,512,4,512]{3,1,0,2:T(8,128)(2,1)} %all-gather.2.cloned.1.call-done), kind=kOutput, calls=%fused_computation.1 | convolution fusion | flops 2153775104 | bytes 19922946 | tf_op jit(solution)/shard_map/crk,kn->crn/dot_general | solution.py:26
  306.6 10.8 %fusion.11 = (bf16[512,2048]{1,0:T(8,128)(2,1)}, f32[2048,512]{0,1:T(8,128)}) fusion(pred[]{:T(512)S(6)} %eq.17, f32[4,512,512]{2,1,0:T(8,128)} %param.5, f32[2,512,2048]{2,1,0:T(8,128)S(1)} %maximum_subtract_fusion.1), kind=kOutput, calls=%fused_computation.25 | convolution fusion | flops 6444548096 | bytes 11534337 | tf_op jit(solution)/shard_map/dot_general | solution.py:22
  317.5 0.3 all-reduce.11.cloned.1.call-start
  317.8 4.8 slice.73
  322.6 4.9 fusion.1
  327.5 119.9 %all-reduce.9.cloned.1.call-done = bf16[512,2048]{1,0:T(8,128)(2,1)} async-done(((bf16[512,2048]{1,0:T(8,128)(2,1)}), bf16[512,2048]{1,0:T(8,128)(2,1)}) %all-reduce.9.cloned.1.call-update) | async-done | bytes 2097168 | tf_op jit(solution)/shard_map/psum | solution.py:9
  447.5 7.0 %maximum_subtract_fusion.2 = f32[2,512,2048]{2,1,0:T(8,128)S(1)} fusion(f32[1,512,2048]{2,1,0:T(8,128)} %slice.73, f32[1,512,2048]{2,1,0:T(8,128)} %fusion.1, pred[2]{0:T(512)(128)(4,1)S(1)} %broadcast_compare_fusion.1, bf16[512,2048]{1,0:T(8,128)(2,1)} %all-reduce.9.cloned.1.call-done, bf16[2,512,4,512]{3,1,0,2:T(8,128)(2,1)} %all-gather.2.cloned.1.call-done), kind=kOutput, calls=%fused_computation.2 | convolution fusion | flops 2153775104 | bytes 19922946 | tf_op jit(solution)/shard_map/crk,kn->crn/dot_general | solution.py:26
  454.5 10.8 %fusion.12 = (bf16[512,2048]{1,0:T(8,128)(2,1)}, f32[2048,512]{0,1:T(8,128)}) fusion(pred[]{:T(512)S(6)} %eq.16, f32[4,512,512]{2,1,0:T(8,128)} %param.5, f32[2,512,2048]{2,1,0:T(8,128)S(1)} %maximum_subtract_fusion.2), kind=kOutput, calls=%fused_computation.26 | convolution fusion | flops 6444548096 | bytes 11534337 | tf_op jit(solution)/shard_map/dot_general | solution.py:22
  465.4 4.8 slice.76
  470.2 4.9 fusion
  475.1 120.3 %all-reduce.11.cloned.1.call-done = bf16[512,2048]{1,0:T(8,128)(2,1)} async-done(((bf16[512,2048]{1,0:T(8,128)(2,1)}), bf16[512,2048]{1,0:T(8,128)(2,1)}) %all-reduce.11.cloned.1.call-update) | async-done | bytes 2097168 | tf_op jit(solution)/shard_map/psum | solution.py:9
  595.3 10.1 %maximum_subtract_fusion.3 = f32[2,512,2048]{2,1,0:T(8,128)} fusion(f32[1,512,2048]{2,1,0:T(8,128)} %slice.76, f32[1,512,2048]{2,1,0:T(8,128)} %fusion, pred[2]{0:T(512)(128)(4,1)S(1)} %broadcast_compare_fusion, bf16[512,2048]{1,0:T(8,128)(2,1)} %all-reduce.11.cloned.1.call-done, bf16[2,512,4,512]{3,1,0,2:T(8,128)(2,1)} %all-gather.2.cloned.1.call-done), kind=kOutput, calls=%fused_computation.3 | convolution fusion | flops 2153775104 | bytes 19922946 | tf_op jit(solution)/shard_map/crk,kn->crn/dot_general | solution.py:26
  (26 shorter events, 0.2 us)
Async XLA Ops:
  7.4 144.4 %all-reduce.5.cloned.1.call-start = ((), (), s32[]{:S(2)}) async-start(), calls=%async_computation | async-start | bytes 4194304 | tf_op jit(solution)/shard_map/psum | solution.py:9
  7.4 11.0 %copy-start.6 = (bf16[2,512,4,256]{3,2,1,0:T(4,128)(2,1)S(1)}, bf16[2,512,4,256]{3,2,1,0:T(4,128)(2,1)}, u32[]{:S(2)}) copy-start(bf16[2,512,4,256]{3,2,1,0:T(4,128)(2,1)} %param.4) | copy-start | bytes 6291460
  18.3 133.4 %all-gather.2.cloned.1.call-start = ((), (), s32[]{:S(2)}) async-start(), calls=%async_computation.1 | async-start | bytes 6291456 | tf_op jit(solution)/shard_map/all_gather | solution.py:18
  20.0 279.6 %all-reduce.7.cloned.1.call-start = ((), (), s32[]{:S(2)}) async-start(), calls=%async_computation.2 | async-start | bytes 4194304 | tf_op jit(solution)/shard_map/psum | solution.py:9
  158.7 10.8 %copy-start.3 = (f32[2,512,2048]{2,1,0:T(8,128)}, f32[2,512,2048]{2,1,0:T(8,128)S(1)}, u32[]{:S(2)}) copy-start(f32[2,512,2048]{2,1,0:T(8,128)S(1)} %maximum_subtract_fusion) | copy-start | bytes 25165828
  169.6 277.9 %all-reduce.9.cloned.1.call-start = ((), (), s32[]{:S(2)}) async-start(), calls=%async_computation.3 | async-start | bytes 4194304 | tf_op jit(solution)/shard_map/psum | solution.py:9
  169.9 4.8 copy-start
  306.6 10.8 %copy-start.4 = (f32[2,512,2048]{2,1,0:T(8,128)}, f32[2,512,2048]{2,1,0:T(8,128)S(1)}, u32[]{:S(2)}) copy-start(f32[2,512,2048]{2,1,0:T(8,128)S(1)} %maximum_subtract_fusion.1) | copy-start | bytes 25165828
  317.5 277.9 %all-reduce.11.cloned.1.call-start = ((), (), s32[]{:S(2)}) async-start(), calls=%async_computation.4 | async-start | bytes 4194304 | tf_op jit(solution)/shard_map/psum | solution.py:9
  317.8 4.8 copy-start.1
  454.5 10.8 %copy-start.5 = (f32[2,512,2048]{2,1,0:T(8,128)}, f32[2,512,2048]{2,1,0:T(8,128)S(1)}, u32[]{:S(2)}) copy-start(f32[2,512,2048]{2,1,0:T(8,128)S(1)} %maximum_subtract_fusion.2) | copy-start | bytes 25165828
  465.3 4.8 copy-start.2
Sparse Core Ops, SparseCore 0:
  18.5 133.2 all-reduce.4
  169.7 129.8 all-reduce.6
  317.6 129.8 all-reduce.8
  465.5 129.8 all-reduce.10
Sparse Core Ops, SparseCore 1:
  20.5 18.0 all-gather.1
where the time goes:
time: 615 us; the launch traced here: 613 us
  waiting for transfers between devices  482 us (78%)
  matrix products  74.5 us (12%)
  local copies, waits for them, and re-layouts  20.8 us (3%)
  other arithmetic  20 us (3%)
  between operations  14.7 us (2%)
    psum x4, waiting for transfers between devices, from_root(): return lax.psum(jnp.where(mine, value, jnp.zeros_like(value)), axis)  482 us
    dot_general x4, matrix products, local(): solved = jnp.dot(inverses[panel], state[0], precision=lax.Precision.HIGHEST)  43.4 us
    dot_general x4, matrix products, local(): jnp.einsum('crk,kn->crn', panel_cols, sent, preferred_element_type=jnp.fl...  31.1 us
    broadcast_in_dim x4, other arithmetic, local(): state = jnp.concatenate([first[None], state[1:]], axis=0)  20 us
    slice x4, local copies, waits for them, and re-layouts, local(): state = jnp.concatenate([first[None], state[1:]], axis=0)  19.1 us
  transfers between devices with their start and end apart: 5, of which 4 were waited for; matrix products, arithmetic and copies ran while one was open for 7% of the time, Pallas kernels for 0%

commit v1 on v0

v1 whole, which is shorter than its diff:
```python
import jax
import jax.numpy as jnp
from jax import lax
from jax.experimental import pallas as pl
from jax.experimental.pallas import tpu as pltpu
from jax.sharding import Mesh, PartitionSpec as P

ROWS = ("y", "z", "x")
BF = jnp.bfloat16
F32 = jnp.float32


def flat(x, y, z):
    return ((y % 4) * 4 + (z % 4)) * 4 + (x % 4)


def permute(value, moves):
    return lax.ppermute(value, ROWS, [(flat(*a), flat(*b)) for a, b in moves])


def ring(value, axis, step):
    return lax.ppermute(value, axis, [(i, (i + step) % 4) for i in range(4)])


def ring_gather(value, axis):
    at = lax.axis_index(axis)
    parts = [value] + [ring(value, axis, 4 - d) for d in (1, 2, 3)]
    both = jnp.stack(parts + parts[:3])
    return lax.dynamic_slice_in_dim(both, (4 - at) % 4, 4, 0)


def update_kernel(place_ref, factor_ref, rhs_ref, sent_ref, out_ref):
    panels = sent_ref.shape[1]
    depth = panels * sent_ref.shape[2]
    both = jnp.concatenate([sent_ref[i].reshape(depth, 128) for i in range(2)], axis=1)
    for c in range(2):
        out_ref[c] = rhs_ref[c] - jnp.dot(factor_ref[c], both, preferred_element_type=F32)
    place = place_ref[0]

    @pl.when(place < panels)
    def _():
        for i in range(2):
            out_ref[0, :, i * 128:(i + 1) * 128] = sent_ref[i, place].astype(F32)


def update(place, factor, rhs, sent):
    cycles, tile, depth = factor.shape
    cols = rhs.shape[2]
    return pl.pallas_call(
        update_kernel,
        grid=(cols // 256,),
        in_specs=[
            pl.BlockSpec(memory_space=pltpu.SMEM),
            pl.BlockSpec((cycles, tile, depth), lambda j: (0, 0, 0)),
            pl.BlockSpec((cycles, tile, 256), lambda j: (0, 0, j)),
            pl.BlockSpec((2, 4, tile, 128), lambda j: (j, 0, 0, 0)),
        ],
        out_specs=pl.BlockSpec((cycles, tile, 256), lambda j: (0, 0, j)),
        out_shape=jax.ShapeDtypeStruct(rhs.shape, F32),
        compiler_params=pltpu.CompilerParams(vmem_limit_bytes=48 << 20),
    )(place[None], factor, rhs, sent)


def local(rhs, factor, inverses):
    x, y, z = (lax.axis_index(a) for a in ("x", "y", "z"))
    core = lax.axis_index("rhs")
    place = (y * 4 + z) * 4 + x
    owner = place < 4

    tile = rhs[0]
    high = lax.reduce_precision(tile, 8, 7)
    low = (tile - high).astype(BF)
    high = high.astype(BF)
    blocks = lambda v: v.reshape(512, 16, 128).transpose(1, 0, 2)
    shards = factor[0, :, :3].reshape(16, 192, 128)
    load_a = jnp.concatenate([blocks(high), shards[:, :96]], axis=1).reshape(4, 4, 608, 128)
    load_b = jnp.concatenate([blocks(low), shards[:, 96:]], axis=1).reshape(4, 4, 608, 128)

    zero = jnp.zeros((), BF)
    hold_a = jnp.where(owner, load_a[0], zero)
    hold_b = jnp.where(owner, load_b[:, 0], zero)
    for d in (1, 3, 2):
        hold_a = hold_a + permute(load_a[d], [((i, 0, 0), (i, d, 0)) for i in range(4)])
        hold_b = hold_b + permute(load_b[:, d], [((i, 0, 0), (i, 0, d)) for i in range(4)])
    mine_a = jnp.where(z == 0, hold_a[0], zero)
    mine_b = jnp.where(y == 0, hold_b[0], zero)
    for d in (1, 3, 2):
        mine_a = mine_a + permute(hold_a[d], [((i, j, 0), (i, j, d)) for i in range(4) for j in range(4)])
        mine_b = mine_b + permute(hold_b[d], [((i, 0, j), (i, d, j)) for i in range(4) for j in range(4)])

    shard = jnp.concatenate([mine_a[512:], mine_b[512:]], axis=0)
    half = ring_gather(ring_gather(shard, "z"), "y").reshape(512, 3, 256)
    other = lax.ppermute(half, "rhs", [(0, 1), (1, 0)])
    own = jnp.where(core == 0, jnp.concatenate([half, other], axis=2), jnp.concatenate([other, half], axis=2))

    inverse = lax.dynamic_index_in_dim(inverses, x, 0, keepdims=False)
    state = mine_a[:512].astype(F32) + mine_b[:512].astype(F32)
    sent = None
    for t in range(4):
        if t > 0:
            got = sum(permute(sent, [((t - 1, j, k), (i, j, k)) for j in range(4) for k in range(4)]) for i in range(t, 4))
            state = state - jnp.dot(own[:, t - 1], got, preferred_element_type=F32)
        sent = jnp.dot(inverse, state, precision=lax.Precision.HIGHEST).astype(BF)

    everything = lax.all_gather(sent, ROWS, axis=0).reshape(16, 4, 512, 128)

    whole = lax.all_gather(factor, "rhs", axis=3, tiled=True)
    tiles = jnp.arange(2, dtype=jnp.int32) * 64 + place
    keep = tiles[:, None] > jnp.arange(4, dtype=jnp.int32)[None]
    whole = jnp.where(keep[:, None, :, None], whole, zero).reshape(2, 512, 2048)
    return update(place, whole, rhs, everything)


def solution(mesh):
    grid = Mesh(mesh.devices.reshape(4, 4, 4, 2), ("y", "z", "x", "rhs"))
    return jax.shard_map(
        local,
        mesh=grid,
        in_specs=(P(None, ROWS, "rhs"), P(None, ROWS, None, "rhs"), P()),
        out_specs=P(None, ROWS, "rhs"),
        check_vma=False,
    )
```

time: 615 us -> 236 us (0.38)
  waiting for transfers between devices: 482 us -> 107 us
  matrix products: 74.5 us -> 6.91 us
  starting transfers between devices: 0.57 us -> 42 us
  Pallas kernels: 0 us -> 15.1 us
  local copies, waits for them, and re-layouts: 20.8 us -> 33.1 us
    psum x4 -> x0, waiting for transfers between devices: 482 us -> none  [from_root(): return lax.psum(jnp.where(mine, value, jnp.zeros_like(value)), axis)]
    dot_general x8 -> x7, matrix products: 74.5 us -> 6.91 us  [the longest x4 6.01 us: local(): sent = jnp.dot(inverse, state, precision=lax.Precision.HIGHEST).astype(BF)]
    all_gather x0 -> x1, waiting for transfers between devices: none -> 62.7 us  [local(): everything = lax.all_gather(sent, ROWS, axis=0).reshape(16, 4, 512, 128)]
    ppermute x0 -> x25, waiting for transfers between devices: none -> 44.5 us  [the longest x18 35.6 us: permute(): return lax.ppermute(value, ROWS, [(flat(*a), flat(*b)) for a, b in moves])]
    ppermute x0 -> x25, starting transfers between devices: none -> 41.9 us  [the longest x18 29.8 us: permute(): return lax.ppermute(value, ROWS, [(flat(*a), flat(*b)) for a, b in moves])]
    broadcast_in_dim x4 -> x0, other arithmetic: 20 us -> none  [local(): state = jnp.concatenate([first[None], state[1:]], axis=0)]
    pallas_call x0 -> x1, Pallas kernels: none -> 15.1 us  [update(): pl.pallas_call(update_kernel, grid=(cols // 256,), in_specs=[pl.BlockSpec...]
    slice x4 -> x6, local copies, waits for them, and re-layouts: 19.1 us -> 8.62 us  [the longest x1 4.7 us: local(): tile = rhs[0]]
  transfers between devices with their start and end apart: 5 -> 27, of which waited for: 4 -> 13; matrix products, arithmetic and copies ran while one was open for 7% -> 13% of each run, Pallas kernels for 0% -> 0%
where the time goes in v1:
time: 236 us; the launch traced here: 234 us
  waiting for transfers between devices  107 us (45%)
  starting transfers between devices  42 us (18%)
  local copies, waits for them, and re-layouts  33.1 us (14%)
  other arithmetic  15.5 us (7%)
  Pallas kernels  15.1 us (6%)
  between operations  13.9 us (6%)
  matrix products  6.91 us (3%)
    all_gather x1, waiting for transfers between devices, local(): everything = lax.all_gather(sent, ROWS, axis=0).reshape(16, 4, 512, 128)  62.7 us
    ppermute x18, waiting for transfers between devices, permute(): return lax.ppermute(value, ROWS, [(flat(*a), flat(*b)) for a, b in moves])  35.6 us
    ppermute x18, starting transfers between devices, permute(): return lax.ppermute(value, ROWS, [(flat(*a), flat(*b)) for a, b in moves])  29.8 us
    pallas_call x1, Pallas kernels, update(): pl.pallas_call(update_kernel, grid=(cols // 256,), in_specs=[pl.BlockSpec...  15.1 us
    ppermute x6, starting transfers between devices, ring(): return lax.ppermute(value, axis, [(i, (i + step) % 4) for i in range(4)])  12 us
    ppermute x6, waiting for transfers between devices, ring(): return lax.ppermute(value, axis, [(i, (i + step) % 4) for i in range(4)])  8.96 us
    reshape x1, local copies, waits for them, and re-layouts, local(): whole = jnp.where(keep[:, None, :, None], whole, zero).reshape(2, 512, 2048)  7.81 us
    unnamed x17, local copies, waits for them, and re-layouts  7.81 us
  transfers between devices with their start and end apart: 27, of which 13 were waited for; matrix products, arithmetic and copies ran while one was open for 13% of the time, Pallas kernels for 0%

profile of v1, /device:TPU:6, one launch (start us, length us, event | category | flops | bytes accessed | tf_op | source)
XLA Modules:
  0.0 233.8 jit_solution(1886766801182936920)
XLA Ops:
  8.9 4.7 %slice.85 = f32[1,512,2048]{2,1,0:T(8,128)} slice(f32[2,512,2048]{2,1,0:T(8,128)} %rhs_ref.1), slice={[0:1], [0:512], [0:2048]} | slice | bytes 8388608 | tf_op jit(solution)/shard_map/slice | solution.py:70
  13.6 5.4 %copy.24 = f32[1,512,2048]{1,2,0:T(8,128)} copy(f32[1,512,2048]{2,1,0:T(8,128)} %slice.85) | data formatting | bytes 8388608
  19.0 5.3 %copy.12 = f32[512,16,128]{2,0,1:T(8,128)} copy(f32[512,16,128]{0,2,1:T(8,128)} %bitcast.114) | data formatting | bytes 8388608 | tf_op jit(solution)/shard_map/squeeze | solution.py:70
  24.3 2.9 %fusion.2 = (bf16[16,512,128]{2,1,0:T(8,128)(2,1)S(1)}, bf16[16,512,128]{2,1,0:T(8,128)(2,1)S(1)}) fusion(f32[512,16,128]{2,0,1:T(8,128)} %copy.12), kind=kLoop, calls=%fused_computation.12 | loop fusion | flops 4194304 | bytes 8388608 | tf_op jit(solution)/shard_map/transpose | solution.py:74
  28.7 3.8 %collective-permute-start.6 = (bf16[4,608,128]{2,1,0:T(8,128)(2,1)S(1)}, bf16[4,608,128]{2,1,0:T(8,128)(2,1)S(1)}, u32[]{:S(2)}, u32[]{:S(2)}) collective-permute-start(bf16[4,608,128]{2,1,0:T(8,128)(2,1)S(1)} %get-tuple-element.12), channel_id=1, source_target_pairs={{0,8},{2,10},{4,12},{6,14},{1,9},{3,11},{5,13},{7,15}} | collective-permute-start | bytes 1867784 | tf_op jit(solution)/shard_map/ppermute | solution.py:18
  32.6 3.6 %collective-permute-start.7 = (bf16[4,608,128]{2,1,0:T(8,128)(2,1)}, bf16[4,608,128]{2,1,0:T(8,128)(2,1)}, u32[]{:S(2)}, u32[]{:S(2)}) collective-permute-start(bf16[4,608,128]{2,1,0:T(8,128)(2,1)} %get-tuple-element.13), channel_id=1, source_target_pairs={{0,24},{2,26},{4,28},{6,30},{1,25},{3,27},{5,29},{7,31}} | collective-permute-start | bytes 1867784 | tf_op jit(solution)/shard_map/ppermute | solution.py:18
  39.6 2.1 collective-permute-start
  41.7 2.1 collective-permute-start.2
  43.8 3.1 %collective-permute-done.6 = bf16[4,608,128]{2,1,0:T(8,128)(2,1)S(1)} collective-permute-done((bf16[4,608,128]{2,1,0:T(8,128)(2,1)S(1)}, bf16[4,608,128]{2,1,0:T(8,128)(2,1)S(1)}, u32[]{:S(2)}, u32[]{:S(2)}) %collective-permute-start.6) | collective-permute-done | bytes 622624 | tf_op jit(solution)/shard_map/ppermute | solution.py:18
  46.9 2.1 collective-permute-start.1
  49.1 10.2 %collective-permute-done.8 = bf16[4,608,128]{2,1,0:T(8,128)(2,1)} collective-permute-done((bf16[4,608,128]{2,1,0:T(8,128)(2,1)}, bf16[4,608,128]{2,1,0:T(8,128)(2,1)}, u32[]{:S(2)}, u32[]{:S(2)}) %collective-permute-start.8) | collective-permute-done | bytes 622624 | tf_op jit(solution)/shard_map/ppermute | solution.py:18
  64.8 4.2 %collective-permute-done.2 = bf16[4,608,128]{2,1,0:T(8,128)(2,1)} collective-permute-done((bf16[4,608,128]{2,1,0:T(8,128)(2,1)}, bf16[4,608,128]{2,1,0:T(8,128)(2,1)}, u32[]{:S(2)}, u32[]{:S(2)}) %collective-permute-start.2) | collective-permute-done | bytes 622624 | tf_op jit(solution)/shard_map/ppermute | solution.py:18
  77.5 3.9 %collective-permute-start.13 = (bf16[192,128]{1,0:T(8,128)(2,1)S(1)}, bf16[192,128]{1,0:T(8,128)(2,1)S(1)}, u32[]{:S(2)}, u32[]{:S(2)}) collective-permute-start(bf16[192,128]{1,0:T(8,128)(2,1)S(1)} %pad_maximum_fusion.2), channel_id=1, source_target_pairs={{0,16},{8,24},{16,0},{24,8},{1,17},{9,25},{17,1},{25,9},{2,18},{10... | collective-permute-start | bytes 147464 | tf_op jit(solution)/shard_map/ppermute | solution.py:22
  89.1 3.9 %collective-permute-start.16 = (bf16[4,192,128]{2,1,0:T(8,128)(2,1)S(1)}, bf16[4,192,128]{2,1,0:T(8,128)(2,1)S(1)}, u32[]{:S(2)}, u32[]{:S(2)}) collective-permute-start(bf16[4,192,128]{2,1,0:T(8,128)(2,1)S(1)} %get-tuple-element.6), channel_id=1, source_target_pairs={{0,64},{32,96},{64,0},{96,32},{1,65},{33,97},{65,1},{97,33},{2,66}... | collective-permute-start | bytes 589832 | tf_op jit(solution)/shard_map/ppermute | solution.py:22
  93.1 5.7 %collective-permute-done.16 = bf16[4,192,128]{2,1,0:T(8,128)(2,1)S(1)} collective-permute-done((bf16[4,192,128]{2,1,0:T(8,128)(2,1)S(1)}, bf16[4,192,128]{2,1,0:T(8,128)(2,1)S(1)}, u32[]{:S(2)}, u32[]{:S(2)}) %collective-permute-start.16) | collective-permute-done | bytes 196640 | tf_op jit(solution)/shard_map/ppermute | solution.py:22
  99.8 2.4 %convolution_convert_fusion.3 = bf16[512,128]{1,0:T(8,128)(2,1)S(1)} fusion(f32[4,512,512]{2,1,0:T(8,128)} %param.5, s32[]{:T(128)S(6)} %select_n.71, bf16[608,128]{1,0:T(8,128)(2,1)S(1)} %fusion.32, bf16[608,128]{1,0:T(8,128)(2,1)S(1)} %fusion.36), kind=kOutput, calls=%fused_computation.20 | convolution fusion | flops 402915328 | bytes 1441796 | tf_op jit(solution)/shard_map/dot_general | solution.py:103
  107.5 2.3 fusion.46
  114.6 8.3 %collective-permute-done.23 = bf16[512,128]{1,0:T(8,128)(2,1)S(1)} collective-permute-done((bf16[512,128]{1,0:T(8,128)(2,1)S(1)}, bf16[512,128]{1,0:T(8,128)(2,1)S(1)}, u32[]{:S(2)}, u32[]{:S(2)}) %collective-permute-start.23) | collective-permute-done | bytes 131104 | tf_op jit(solution)/shard_map/ppermute | solution.py:18
  125.6 5.6 %collective-permute-done.24 = bf16[512,128]{1,0:T(8,128)(2,1)S(1)} collective-permute-done((bf16[512,128]{1,0:T(8,128)(2,1)S(1)}, bf16[512,128]{1,0:T(8,128)(2,1)S(1)}, u32[]{:S(2)}, u32[]{:S(2)}) %collective-permute-start.24) | collective-permute-done | bytes 131104 | tf_op jit(solution)/shard_map/ppermute | solution.py:18
  133.2 5.9 %broadcast_select_fusion = bf16[2,512,4,512]{3,2,1,0:T(4,128)(2,1)} fusion(bf16[2,512,4,512]{3,2,1,0:T(4,128)(2,1)} %all-gather.4.cloned.1.call-done, pred[2,4]{1,0:T(4,128)(4,1)S(1)} %iota_compare_fusion), kind=kLoop, calls=%fused_computation.3 | loop fusion | flops 2097152 | bytes 8388616 | tf_op jit(solution)/shard_map/jit(_where)/select_n | solution.py:110
  139.1 7.8 %reshape.59.factor_ref = bf16[2,512,2048]{2,1,0:T(8,128)(2,1)} reshape(bf16[2,512,4,512]{3,2,1,0:T(4,128)(2,1)} %broadcast_select_fusion) | data formatting | bytes 8388608 | tf_op jit(solution)/shard_map/reshape | solution.py:110
  146.9 62.7 %all-gather.6.cloned.1.call-done = bf16[32768,128]{1,0:T(8,128)(2,1)} async-done(((bf16[512,128]{1,0:T(8,128)(2,1)}), bf16[32768,128]{1,0:T(8,128)(2,1)}) %all-gather.6.cloned.1.call-update) | async-done | bytes 8388624 | tf_op jit(solution)/shard_map/all_gather | solution.py:105
  209.6 2.2 copy-done
  211.8 15.1 %shard_map.37 = f32[2,512,2048]{2,1,0:T(8,128)} custom-call(s32[1]{0:T(128)} %bitcast.place_ref, bf16[2,512,2048]{2,1,0:T(8,128)(2,1)S(1)} %copy-done, f32[2,512,2048]{2,1,0:T(8,128)} %rhs_ref.1, bf16[16,4,512,128]{3,2,1,0:T(8,128)(2,1)} %bitcast.117), custom_call_target="tpu_custom_call" | custom-call | tf_op jit(solution)/shard_map/pallas_call | solution.py:49
  (89 shorter events, 44.5 us)
Async XLA Ops:
  6.5 126.7 %all-gather.4.cloned.1.call-start = ((), (), s32[]{:S(2)}) async-start(), calls=%async_computation | async-start | bytes 6291456 | tf_op jit(solution)/shard_map/all_gather | solution.py:107
  28.7 18.2 %collective-permute-start.6 = (bf16[4,608,128]{2,1,0:T(8,128)(2,1)S(1)}, bf16[4,608,128]{2,1,0:T(8,128)(2,1)S(1)}, u32[]{:S(2)}, u32[]{:S(2)}) collective-permute-start(bf16[4,608,128]{2,1,0:T(8,128)(2,1)S(1)} %get-tuple-element.12), channel_id=1, source_target_pairs={{0,8},{2,10},{4,12},{6,14},{1,9},{3,11},{5,13},{7,15}} | collective-permute-start | bytes 1867784 | tf_op jit(solution)/shard_map/ppermute | solution.py:18
  32.6 16.5 %collective-permute-start.7 = (bf16[4,608,128]{2,1,0:T(8,128)(2,1)}, bf16[4,608,128]{2,1,0:T(8,128)(2,1)}, u32[]{:S(2)}, u32[]{:S(2)}) collective-permute-start(bf16[4,608,128]{2,1,0:T(8,128)(2,1)} %get-tuple-element.13), channel_id=1, source_target_pairs={{0,24},{2,26},{4,28},{6,30},{1,25},{3,27},{5,29},{7,31}} | collective-permute-start | bytes 1867784 | tf_op jit(solution)/shard_map/ppermute | solution.py:18
  36.2 23.1 %collective-permute-start.8 = (bf16[4,608,128]{2,1,0:T(8,128)(2,1)}, bf16[4,608,128]{2,1,0:T(8,128)(2,1)}, u32[]{:S(2)}, u32[]{:S(2)}) collective-permute-start(bf16[4,608,128]{2,1,0:T(8,128)(2,1)} %get-tuple-element.14), channel_id=1, source_target_pairs={{0,16},{2,18},{4,20},{6,22},{1,17},{3,19},{5,21},{7,23}} | collective-permute-start | bytes 1867784 | tf_op jit(solution)/shard_map/ppermute | solution.py:18
  39.6 23.9 %collective-permute-start = (bf16[4,608,128]{2,1,0:T(8,128)(2,1)}, bf16[4,608,128]{2,1,0:T(8,128)(2,1)}, u32[]{:S(2)}, u32[]{:S(2)}) collective-permute-start(bf16[4,608,128]{2,1,0:T(8,128)(2,1)} %get-tuple-element.9), channel_id=1, source_target_pairs={{0,32},{2,34},{4,36},{6,38},{1,33},{3,35},{5,37},{7,39}} | collective-permute-start | bytes 1867784 | tf_op jit(solution)/shard_map/ppermute | solution.py:18
  41.7 27.2 %collective-permute-start.2 = (bf16[4,608,128]{2,1,0:T(8,128)(2,1)}, bf16[4,608,128]{2,1,0:T(8,128)(2,1)}, u32[]{:S(2)}, u32[]{:S(2)}) collective-permute-start(bf16[4,608,128]{2,1,0:T(8,128)(2,1)} %get-tuple-element.10), channel_id=1, source_target_pairs={{0,64},{2,66},{4,68},{6,70},{1,65},{3,67},{5,69},{7,71}} | collective-permute-start | bytes 1867784 | tf_op jit(solution)/shard_map/ppermute | solution.py:18
  46.9 22.0 %collective-permute-start.1 = (bf16[4,608,128]{2,1,0:T(8,128)(2,1)}, bf16[4,608,128]{2,1,0:T(8,128)(2,1)}, u32[]{:S(2)}, u32[]{:S(2)}) collective-permute-start(bf16[4,608,128]{2,1,0:T(8,128)(2,1)} %get-tuple-element.11), channel_id=1, source_target_pairs={{0,96},{2,98},{4,100},{6,102},{1,97},{3,99},{5,101},{7,103}} | collective-permute-start | bytes 1867784 | tf_op jit(solution)/shard_map/ppermute | solution.py:18
  60.8 12.6 %collective-permute-start.9 = (bf16[608,128]{1,0:T(8,128)(2,1)S(1)}, bf16[608,128]{1,0:T(8,128)(2,1)S(1)}, u32[]{:S(2)}, u32[]{:S(2)}) collective-permute-start(bf16[608,128]{1,0:T(8,128)(2,1)S(1)} %get-tuple-element.23), channel_id=1, source_target_pairs={{0,32},{8,40},{16,48},{24,56},{2,34},{10,42},{18,50},{26,58},{4,36... | collective-permute-start | bytes 466952 | tf_op jit(solution)/shard_map/ppermute | solution.py:18
  62.1 12.6 %collective-permute-start.11 = (bf16[608,128]{1,0:T(8,128)(2,1)S(1)}, bf16[608,128]{1,0:T(8,128)(2,1)S(1)}, u32[]{:S(2)}, u32[]{:S(2)}) collective-permute-start(bf16[608,128]{1,0:T(8,128)(2,1)S(1)} %get-tuple-element.24), channel_id=1, source_target_pairs={{0,64},{8,72},{16,80},{24,88},{2,66},{10,74},{18,82},{26,90},{4,68... | collective-permute-start | bytes 466952 | tf_op jit(solution)/shard_map/ppermute | solution.py:18
  63.5 11.3 %collective-permute-start.10 = (bf16[608,128]{1,0:T(8,128)(2,1)S(1)}, bf16[608,128]{1,0:T(8,128)(2,1)S(1)}, u32[]{:S(2)}, u32[]{:S(2)}) collective-permute-start(bf16[608,128]{1,0:T(8,128)(2,1)S(1)} %get-tuple-element.25), channel_id=1, source_target_pairs={{0,96},{8,104},{16,112},{24,120},{2,98},{10,106},{18,114},{26,122}... | collective-permute-start | bytes 466952 | tf_op jit(solution)/shard_map/ppermute | solution.py:18
  72.1 5.2 %collective-permute-start.5 = (bf16[608,128]{1,0:T(8,128)(2,1)S(1)}, bf16[608,128]{1,0:T(8,128)(2,1)S(1)}, u32[]{:S(2)}, u32[]{:S(2)}) collective-permute-start(bf16[608,128]{1,0:T(8,128)(2,1)S(1)} %get-tuple-element.21), channel_id=1, source_target_pairs={{0,16},{32,48},{64,80},{96,112},{2,18},{34,50},{66,82},{98,114},{4... | collective-permute-start | bytes 466952 | tf_op jit(solution)/shard_map/ppermute | solution.py:18
  77.5 8.0 %collective-permute-start.13 = (bf16[192,128]{1,0:T(8,128)(2,1)S(1)}, bf16[192,128]{1,0:T(8,128)(2,1)S(1)}, u32[]{:S(2)}, u32[]{:S(2)}) collective-permute-start(bf16[192,128]{1,0:T(8,128)(2,1)S(1)} %pad_maximum_fusion.2), channel_id=1, source_target_pairs={{0,16},{8,24},{16,0},{24,8},{1,17},{9,25},{17,1},{25,9},{2,18},{10... | collective-permute-start | bytes 147464 | tf_op jit(solution)/shard_map/ppermute | solution.py:22
  81.4 5.3 %collective-permute-start.14 = (bf16[192,128]{1,0:T(8,128)(2,1)S(1)}, bf16[192,128]{1,0:T(8,128)(2,1)S(1)}, u32[]{:S(2)}, u32[]{:S(2)}) collective-permute-start(bf16[192,128]{1,0:T(8,128)(2,1)S(1)} %pad_maximum_fusion.2), channel_id=1, source_target_pairs={{0,8},{8,16},{16,24},{24,0},{1,9},{9,17},{17,25},{25,1},{2,10},{10... | collective-permute-start | bytes 147464 | tf_op jit(solution)/shard_map/ppermute | solution.py:22
  86.9 6.2 %collective-permute-start.15 = (bf16[4,192,128]{2,1,0:T(8,128)(2,1)S(1)}, bf16[4,192,128]{2,1,0:T(8,128)(2,1)S(1)}, u32[]{:S(2)}, u32[]{:S(2)}) collective-permute-start(bf16[4,192,128]{2,1,0:T(8,128)(2,1)S(1)} %get-tuple-element.6), channel_id=1, source_target_pairs={{0,96},{32,0},{64,32},{96,64},{1,97},{33,1},{65,33},{97,65},{2,98}... | collective-permute-start | bytes 589832 | tf_op jit(solution)/shard_map/ppermute | solution.py:22
  87.0 122.7 %all-gather.6.cloned.1.call-start = ((), (), s32[]{:S(2)}) async-start(), calls=%async_computation.1 | async-start | bytes 8519680 | tf_op jit(solution)/shard_map/all_gather | solution.py:105
  87.0 11.8 %collective-permute-start.17 = (bf16[4,192,128]{2,1,0:T(8,128)(2,1)S(1)}, bf16[4,192,128]{2,1,0:T(8,128)(2,1)S(1)}, u32[]{:S(2)}, u32[]{:S(2)}) collective-permute-start(bf16[4,192,128]{2,1,0:T(8,128)(2,1)S(1)} %get-tuple-element.6), channel_id=1, source_target_pairs={{0,32},{32,64},{64,96},{96,0},{1,33},{33,65},{65,97},{97,1},{2,34}... | collective-permute-start | bytes 589832 | tf_op jit(solution)/shard_map/ppermute | solution.py:22
  89.1 9.7 %collective-permute-start.16 = (bf16[4,192,128]{2,1,0:T(8,128)(2,1)S(1)}, bf16[4,192,128]{2,1,0:T(8,128)(2,1)S(1)}, u32[]{:S(2)}, u32[]{:S(2)}) collective-permute-start(bf16[4,192,128]{2,1,0:T(8,128)(2,1)S(1)} %get-tuple-element.6), channel_id=1, source_target_pairs={{0,64},{32,96},{64,0},{96,32},{1,65},{33,97},{65,1},{97,33},{2,66}... | collective-permute-start | bytes 589832 | tf_op jit(solution)/shard_map/ppermute | solution.py:22
  99.8 5.3 %collective-permute-start.18 = (bf16[512,3,256]{2,0,1:T(8,128)(2,1)S(1)}, bf16[512,3,256]{2,0,1:T(8,128)(2,1)S(1)}, u32[]{:S(2)}, u32[]{:S(2)}) collective-permute-start(bf16[512,3,256]{2,0,1:T(8,128)(2,1)S(1)} %copy.18), channel_id=1, source_target_pairs={{0,1},{1,0},{2,3},{3,2},{4,5},{5,4},{6,7},{7,6},{8,9},{9,8},{10,11... | collective-permute-start | bytes 2359304 | tf_op jit(solution)/shard_map/ppermute | solution.py:93
  102.2 9.1 %collective-permute-start.21 = (bf16[512,128]{1,0:T(8,128)(2,1)S(1)}, bf16[512,128]{1,0:T(8,128)(2,1)S(1)}, u32[]{:S(2)}, u32[]{:S(2)}) collective-permute-start(bf16[512,128]{1,0:T(8,128)(2,1)S(1)} %convolution_convert_fusion.3), channel_id=1, source_target_pairs={{0,6},{8,14},{16,22},{24,30},{32,38},{40,46},{48,54},{56,62},{64,7... | collective-permute-start | bytes 393224 | tf_op jit(solution)/shard_map/ppermute | solution.py:18
  103.5 7.8 %collective-permute-start.20 = (bf16[512,128]{1,0:T(8,128)(2,1)S(1)}, bf16[512,128]{1,0:T(8,128)(2,1)S(1)}, u32[]{:S(2)}, u32[]{:S(2)}) collective-permute-start(bf16[512,128]{1,0:T(8,128)(2,1)S(1)} %convolution_convert_fusion.3), channel_id=1, source_target_pairs={{0,4},{8,12},{16,20},{24,28},{32,36},{40,44},{48,52},{56,60},{64,6... | collective-permute-start | bytes 393224 | tf_op jit(solution)/shard_map/ppermute | solution.py:18
  104.2 7.1 %collective-permute-start.19 = (bf16[512,128]{1,0:T(8,128)(2,1)S(1)}, bf16[512,128]{1,0:T(8,128)(2,1)S(1)}, u32[]{:S(2)}, u32[]{:S(2)}) collective-permute-start(bf16[512,128]{1,0:T(8,128)(2,1)S(1)} %convolution_convert_fusion.3), channel_id=1, source_target_pairs={{0,2},{8,10},{16,18},{24,26},{32,34},{40,42},{48,50},{56,58},{64,6... | collective-permute-start | bytes 393224 | tf_op jit(solution)/shard_map/ppermute | solution.py:18
  112.6 10.3 %collective-permute-start.23 = (bf16[512,128]{1,0:T(8,128)(2,1)S(1)}, bf16[512,128]{1,0:T(8,128)(2,1)S(1)}, u32[]{:S(2)}, u32[]{:S(2)}) collective-permute-start(bf16[512,128]{1,0:T(8,128)(2,1)S(1)} %convolution_convert_fusion.2), channel_id=1, source_target_pairs={{2,6},{10,14},{18,22},{26,30},{34,38},{42,46},{50,54},{58,62},{66,... | collective-permute-start | bytes 393224 | tf_op jit(solution)/shard_map/ppermute | solution.py:18
  113.9 9.0 %collective-permute-start.22 = (bf16[512,128]{1,0:T(8,128)(2,1)S(1)}, bf16[512,128]{1,0:T(8,128)(2,1)S(1)}, u32[]{:S(2)}, u32[]{:S(2)}) collective-permute-start(bf16[512,128]{1,0:T(8,128)(2,1)S(1)} %convolution_convert_fusion.2), channel_id=1, source_target_pairs={{2,4},{10,12},{18,20},{26,28},{34,36},{42,44},{50,52},{58,60},{66,... | collective-permute-start | bytes 393224 | tf_op jit(solution)/shard_map/ppermute | solution.py:18
  124.3 6.9 %collective-permute-start.24 = (bf16[512,128]{1,0:T(8,128)(2,1)S(1)}, bf16[512,128]{1,0:T(8,128)(2,1)S(1)}, u32[]{:S(2)}, u32[]{:S(2)}) collective-permute-start(bf16[512,128]{1,0:T(8,128)(2,1)S(1)} %convolution_convert_fusion.1), channel_id=1, source_target_pairs={{4,6},{12,14},{20,22},{28,30},{36,38},{44,46},{52,54},{60,62},{68,... | collective-permute-start | bytes 393224 | tf_op jit(solution)/shard_map/ppermute | solution.py:18
  (6 other events, 31.5 us)
Sparse Core Ops, SparseCore 0:
  87.1 18.0 all-gather.3
  133.2 76.3 all-gather.5

commit v2 on v1

v2 whole, which is shorter than its diff:
```python
import jax
import jax.numpy as jnp
from jax import lax
from jax.experimental import pallas as pl
from jax.experimental.pallas import tpu as pltpu
from jax.sharding import Mesh, PartitionSpec as P

ROWS = ("y", "z", "x")
BF = jnp.bfloat16
F32 = jnp.float32


def flat(x, y, z):
    return ((y % 4) * 4 + (z % 4)) * 4 + (x % 4)


def permute(value, moves):
    return lax.ppermute(value, ROWS, [(flat(*a), flat(*b)) for a, b in moves])


ODD = [(j, k) for j in range(4) for k in range(4) if (j + k) % 2 == 1]
ROUTES = [((1, 0), (2, 1)), ((0, 1), (3, 2)), ((3, 0), (2, 3)), ((0, 3), (1, 2))]


def update_kernel(place_ref, factor_ref, rhs_ref, sent_ref, out_ref):
    panels = sent_ref.shape[1]
    depth = panels * sent_ref.shape[2]
    both = jnp.concatenate([sent_ref[i].reshape(depth, 128) for i in range(2)], axis=1)
    for c in range(2):
        out_ref[c] = rhs_ref[c] - jnp.dot(factor_ref[c], both, preferred_element_type=F32)
    place = place_ref[0]

    @pl.when(place < panels)
    def _():
        for i in range(2):
            out_ref[0, :, i * 128:(i + 1) * 128] = sent_ref[i, place].astype(F32)


def update(place, factor, rhs, sent):
    cycles, tile, depth = factor.shape
    cols = rhs.shape[2]
    return pl.pallas_call(
        update_kernel,
        grid=(cols // 256,),
        in_specs=[
            pl.BlockSpec(memory_space=pltpu.SMEM),
            pl.BlockSpec((cycles, tile, depth), lambda j: (0, 0, 0)),
            pl.BlockSpec((cycles, tile, 256), lambda j: (0, 0, j)),
            pl.BlockSpec((2, 4, tile, 128), lambda j: (j, 0, 0, 0)),
        ],
        out_specs=pl.BlockSpec((cycles, tile, 256), lambda j: (0, 0, j)),
        out_shape=jax.ShapeDtypeStruct(rhs.shape, F32),
        compiler_params=pltpu.CompilerParams(vmem_limit_bytes=48 << 20),
    )(place[None], factor, rhs, sent)


def local(rhs, factor, inverses):
    x, y, z = (lax.axis_index(a) for a in ("x", "y", "z"))
    core = lax.axis_index("rhs")
    place = (y * 4 + z) * 4 + x
    owner = place < 4

    mask = jnp.where(owner, factor[0, :, :3], jnp.zeros((), BF)).transpose(1, 0, 2)
    half = lax.psum(mask, ("y", "z"))
    other = lax.ppermute(half, "rhs", [(0, 1), (1, 0)])
    own = jnp.where(core == 0, jnp.concatenate([half, other], axis=2), jnp.concatenate([other, half], axis=2))

    def piece(site):
        at = (site[0] * 2 + site[1] // 2) * 256
        return rhs[0, :, at:at + 256]

    def from_owner(value, site):
        return permute(value, [((i, 0, 0), (i,) + site) for i in range(4)])

    hold = sum(from_owner(piece(far), near) for near, far in ROUTES)
    state = sum(from_owner(piece(near), near) for near, far in ROUTES)
    state = state + permute(hold, [((i,) + near, (i,) + far) for near, far in ROUTES for i in range(4)])

    inverse = lax.dynamic_index_in_dim(inverses, x, 0, keepdims=False)
    sent = None
    for t in range(4):
        if t > 0:
            got = sum(permute(sent, [((t - 1, j, k), (i, j, k)) for j, k in ODD]) for i in range(t, 4))
            state = state - jnp.dot(own[t - 1], got, preferred_element_type=F32)
        sent = jnp.dot(inverse, state, precision=lax.Precision.HIGHEST).astype(BF)

    left, right = sent[:, :128], sent[:, 128:]
    even = z % 2 == 0
    give = permute(jnp.where(even, right, left), [((i, j, k), (i, j, k ^ 1)) for j, k in ODD for i in range(4)])
    share = jnp.where((y + z) % 2 == 1, jnp.where(even, left, right), give)
    everything = lax.all_gather(share, ROWS, axis=0).reshape(16, 4, 512, 128)

    zero = jnp.zeros((), BF)
    whole = lax.all_gather(factor, "rhs", axis=3, tiled=True)
    tiles = jnp.arange(2, dtype=jnp.int32) * 64 + place
    keep = tiles[:, None] > jnp.arange(4, dtype=jnp.int32)[None]
    whole = jnp.where(keep[:, None, :, None], whole, zero).reshape(2, 512, 2048)
    return update(place, whole, rhs, everything)


def solution(mesh):
    grid = Mesh(mesh.devices.reshape(4, 4, 4, 2), ("y", "z", "x", "rhs"))
    return jax.shard_map(
        local,
        mesh=grid,
        in_specs=(P(None, ROWS, "rhs"), P(None, ROWS, None, "rhs"), P()),
        out_specs=P(None, ROWS, "rhs"),
        check_vma=False,
    )
```

time: 236 us -> 259 us (1.097)
  waiting for transfers between devices: 107 us -> 160 us
  local copies, waits for them, and re-layouts: 33.1 us -> 15.2 us
  starting transfers between devices: 42 us -> 29.6 us
    psum x0 -> x1, waiting for transfers between devices: none -> 54.9 us  [local(): half = lax.psum(mask, ('y', 'z'))]
    ppermute x6 -> x0, starting transfers between devices: 12 us -> none  [ring(): return lax.ppermute(value, axis, [(i, (i + step) % 4) for i in range(4)])]
    ppermute x6 -> x0, waiting for transfers between devices: 8.96 us -> none  [ring(): return lax.ppermute(value, axis, [(i, (i + step) % 4) for i in range(4)])]
    slice x6 -> x1, local copies, waits for them, and re-layouts: 8.62 us -> 1.59 us  [local(): factor[0, :, :3]]
    unnamed x17 -> x6, local copies, waits for them, and re-layouts: 7.81 us -> 2.19 us
    ppermute x18 -> x16, waiting for transfers between devices: 35.6 us -> 40.8 us  [permute(): return lax.ppermute(value, ROWS, [(flat(*a), flat(*b)) for a, b in moves])]
    squeeze x4 -> x1, local copies, waits for them, and re-layouts: 6.7 us -> 3.56 us  [piece(): return rhs[0, :, at:at + 256]]
    ppermute x18 -> x16, starting transfers between devices: 29.8 us -> 29.5 us  [permute(): return lax.ppermute(value, ROWS, [(flat(*a), flat(*b)) for a, b in moves])]
  transfers between devices with their start and end apart: 27 -> 20, of which waited for: 13 -> 5; matrix products, arithmetic and copies ran while one was open for 13% -> 13% of each run, Pallas kernels for 0% -> 0%
where the time goes in v2:
time: 259 us; the launch traced here: 257 us
  waiting for transfers between devices  160 us (62%)
  starting transfers between devices  29.6 us (11%)
  local copies, waits for them, and re-layouts  15.2 us (6%)
  Pallas kernels  15.1 us (6%)
  between operations  15.1 us (6%)
  other arithmetic  13.6 us (5%)
  matrix products  8.98 us (3%)
    all_gather x1, waiting for transfers between devices, local(): everything = lax.all_gather(share, ROWS, axis=0).reshape(16, 4, 512, 128)  64 us
    psum x1, waiting for transfers between devices, local(): half = lax.psum(mask, ('y', 'z'))  54.9 us
    ppermute x16, waiting for transfers between devices, permute(): return lax.ppermute(value, ROWS, [(flat(*a), flat(*b)) for a, b in moves])  40.8 us
    ppermute x16, starting transfers between devices, permute(): return lax.ppermute(value, ROWS, [(flat(*a), flat(*b)) for a, b in moves])  29.5 us
    pallas_call x1, Pallas kernels, update(): pl.pallas_call(update_kernel, grid=(cols // 256,), in_specs=[pl.BlockSpec...  15.1 us
    reshape x1, local copies, waits for them, and re-layouts, local(): whole = jnp.where(keep[:, None, :, None], whole, zero).reshape(2, 512, 2048)  7.88 us
    dot_general x4, matrix products, local(): sent = jnp.dot(inverse, state, precision=lax.Precision.HIGHEST).astype(BF)  7.13 us
    select_n x1, other arithmetic, local(): whole = jnp.where(keep[:, None, :, None], whole, zero).reshape(2, 512, 2048)  5.92 us
  transfers between devices with their start and end apart: 20, of which 5 were waited for; matrix products, arithmetic and copies ran while one was open for 13% of the time, Pallas kernels for 0%

profile of v2, /device:TPU:6, one launch (start us, length us, event | category | flops | bytes accessed | tf_op | source)
XLA Modules:
  0.0 257.3 jit_solution(2797575490219752814)
XLA Ops:
  7.4 1.6 slice.50
  10.0 3.6 %slice_bitcast_fusion.12 = (f32[512,256]{1,0:T(8,128)S(1)}, f32[512,256]{1,0:T(8,128)}, f32[512,256]{1,0:T(8,128)}, f32[512,256]{1,0:T(8,128)}, f32[512,256]{1,0...) fusion(f32[2,512,2048]{2,1,0:T(8,128)} %rhs_ref.1), kind=kLoop, calls=%fused_computation.30 | loop fusion | bytes 8388608 | tf_op jit(solution)/shard_map/squeeze | solution.py:70
  13.6 4.9 %collective-permute-start.6 = (f32[512,256]{1,0:T(8,128)}, f32[512,256]{1,0:T(8,128)S(1)}, u32[]{:S(2)}, u32[]{:S(2)}) collective-permute-start(f32[512,256]{1,0:T(8,128)} %get-tuple-element.6), channel_id=1, source_target_pairs={{0,96},{2,98},{4,100},{6,102},{1,97},{3,99},{5,101},{7,103}} | collective-permute-start | bytes 1572872 | tf_op jit(solution)/shard_map/ppermute | solution.py:18
  18.5 2.1 collective-permute-start.5
  20.6 2.1 collective-permute-start.4
  22.7 2.1 collective-permute-start.7
  24.9 2.1 collective-permute-start.1
  27.0 6.2 %collective-permute-done.6 = f32[512,256]{1,0:T(8,128)S(1)} collective-permute-done((f32[512,256]{1,0:T(8,128)}, f32[512,256]{1,0:T(8,128)S(1)}, u32[]{:S(2)}, u32[]{:S(2)}) %collective-permute-start.6) | collective-permute-done | bytes 524320 | tf_op jit(solution)/shard_map/ppermute | solution.py:18
  33.1 2.1 collective-permute-start.3
  35.6 5.3 %collective-permute-start.2 = (f32[512,256]{1,0:T(8,128)S(1)}, f32[512,256]{1,0:T(8,128)}, u32[]{:S(2)}, u32[]{:S(2)}) collective-permute-start(f32[512,256]{1,0:T(8,128)S(1)} %get-tuple-element.10), channel_id=1, source_target_pairs={{0,96},{2,98},{4,100},{6,102},{1,97},{3,99},{5,101},{7,103}} | collective-permute-start | bytes 1572872 | tf_op jit(solution)/shard_map/ppermute | solution.py:18
  40.9 2.1 collective-permute-start
  43.0 2.3 add_add_fusion
  46.0 54.9 %all-reduce.2.cloned.1.call-done = bf16[3,512,256]{2,1,0:T(8,128)(2,1)} async-done(((bf16[3,512,256]{2,1,0:T(8,128)(2,1)}), bf16[3,512,256]{2,1,0:T(8,128)(2,1)}) %all-reduce.2.cloned.1.call-update) | async-done | bytes 786448 | tf_op jit(solution)/shard_map/psum | solution.py:64
  100.9 1.8 add_add_fusion.1
  102.7 2.9 %convolution_convert_fusion.3 = bf16[512,256]{1,0:T(8,128)(2,1)} fusion(f32[512,256]{1,0:T(8,128)S(1)} %add_add_fusion.1, f32[4,512,512]{2,1,0:T(8,128)} %param.5, s32[]{:T(128)S(6)} %select_n.61), kind=kOutput, calls=%fused_computation.8 | convolution fusion | flops 805437440 | bytes 1835012 | tf_op jit(solution)/shard_map/dot_general | solution.py:85
  106.9 1.4 collective-permute-start.10
  108.3 1.9 maximum_select_fusion
  116.2 2.2 convolution_convert_fusion
  119.8 34.2 %collective-permute-done.16 = bf16[512,128]{1,0:T(8,128)(2,1)S(1)} collective-permute-done((bf16[512,128]{1,0:T(8,128)(2,1)S(1)}, bf16[512,128]{1,0:T(8,128)(2,1)S(1)}, u32[]{:S(2)}, u32[]{:S(2)}) %collective-permute-start.16) | collective-permute-done | bytes 131104 | tf_op jit(solution)/shard_map/ppermute | solution.py:18
  154.8 5.9 %broadcast_select_fusion = bf16[2,512,4,512]{3,2,1,0:T(4,128)(2,1)} fusion(bf16[2,512,4,512]{3,2,1,0:T(4,128)(2,1)} %all-gather.4.cloned.1.call-done, pred[2,4]{1,0:T(4,128)(4,1)S(1)} %iota_compare_fusion), kind=kLoop, calls=%fused_computation | loop fusion | flops 2097152 | bytes 8388616 | tf_op jit(solution)/shard_map/jit(_where)/select_n | solution.py:97
  160.7 7.9 %reshape.34.factor_ref = bf16[2,512,2048]{2,1,0:T(8,128)(2,1)} reshape(bf16[2,512,4,512]{3,2,1,0:T(4,128)(2,1)} %broadcast_select_fusion) | data formatting | bytes 8388608 | tf_op jit(solution)/shard_map/reshape | solution.py:97
  168.6 64.0 %all-gather.6.cloned.1.call-done = bf16[32768,128]{1,0:T(8,128)(2,1)} async-done(((bf16[512,128]{1,0:T(8,128)(2,1)}), bf16[32768,128]{1,0:T(8,128)(2,1)}) %all-gather.6.cloned.1.call-update) | async-done | bytes 8388624 | tf_op jit(solution)/shard_map/all_gather | solution.py:91
  232.6 2.2 copy-done
  234.8 15.1 %shard_map.37 = f32[2,512,2048]{2,1,0:T(8,128)} custom-call(s32[1]{0:T(128)} %bitcast.place_ref, bf16[2,512,2048]{2,1,0:T(8,128)(2,1)S(1)} %copy-done, f32[2,512,2048]{2,1,0:T(8,128)} %rhs_ref.1, bf16[16,4,512,128]{3,2,1,0:T(8,128)(2,1)} %bitcast.45), custom_call_target="tpu_custom_call" | custom-call | tf_op jit(solution)/shard_map/pallas_call | solution.py:42
  (45 shorter events, 11.5 us)
Async XLA Ops:
  7.4 93.5 %all-reduce.2.cloned.1.call-start = ((), (), s32[]{:S(2)}) async-start(), calls=%async_computation.1 | async-start | bytes 1572864 | tf_op jit(solution)/shard_map/psum | solution.py:64
  10.0 144.8 %all-gather.4.cloned.1.call-start = ((), (), s32[]{:S(2)}) async-start(), calls=%async_computation | async-start | bytes 6291456 | tf_op jit(solution)/shard_map/all_gather | solution.py:94
  13.6 19.6 %collective-permute-start.6 = (f32[512,256]{1,0:T(8,128)}, f32[512,256]{1,0:T(8,128)S(1)}, u32[]{:S(2)}, u32[]{:S(2)}) collective-permute-start(f32[512,256]{1,0:T(8,128)} %get-tuple-element.6), channel_id=1, source_target_pairs={{0,96},{2,98},{4,100},{6,102},{1,97},{3,99},{5,101},{7,103}} | collective-permute-start | bytes 1572872 | tf_op jit(solution)/shard_map/ppermute | solution.py:18
  18.5 17.1 %collective-permute-start.5 = (f32[512,256]{1,0:T(8,128)}, f32[512,256]{1,0:T(8,128)}, u32[]{:S(2)}, u32[]{:S(2)}) collective-permute-start(f32[512,256]{1,0:T(8,128)} %get-tuple-element.7), channel_id=1, source_target_pairs={{0,8},{2,10},{4,12},{6,14},{1,9},{3,11},{5,13},{7,15}} | collective-permute-start | bytes 1572872 | tf_op jit(solution)/shard_map/ppermute | solution.py:18
  20.6 20.3 %collective-permute-start.4 = (f32[512,256]{1,0:T(8,128)}, f32[512,256]{1,0:T(8,128)}, u32[]{:S(2)}, u32[]{:S(2)}) collective-permute-start(f32[512,256]{1,0:T(8,128)} %get-tuple-element.8), channel_id=1, source_target_pairs={{0,32},{2,34},{4,36},{6,38},{1,33},{3,35},{5,37},{7,39}} | collective-permute-start | bytes 1572872 | tf_op jit(solution)/shard_map/ppermute | solution.py:18
  22.7 20.3 %collective-permute-start.7 = (f32[512,256]{1,0:T(8,128)S(1)}, f32[512,256]{1,0:T(8,128)}, u32[]{:S(2)}, u32[]{:S(2)}) collective-permute-start(f32[512,256]{1,0:T(8,128)S(1)} %get-tuple-element.12), channel_id=1, source_target_pairs={{0,24},{2,26},{4,28},{6,30},{1,25},{3,27},{5,29},{7,31}} | collective-permute-start | bytes 1572872 | tf_op jit(solution)/shard_map/ppermute | solution.py:18
  24.8 207.7 %all-gather.6.cloned.1.call-start = ((), (), s32[]{:S(2)}) async-start(), calls=%async_computation.2 | async-start | bytes 8519680 | tf_op jit(solution)/shard_map/all_gather | solution.py:91
  24.9 21.1 %collective-permute-start.1 = (f32[512,256]{1,0:T(8,128)S(1)}, f32[512,256]{1,0:T(8,128)}, u32[]{:S(2)}, u32[]{:S(2)}) collective-permute-start(f32[512,256]{1,0:T(8,128)S(1)} %get-tuple-element.5), channel_id=1, source_target_pairs={{0,8},{2,10},{4,12},{6,14},{1,9},{3,11},{5,13},{7,15}} | collective-permute-start | bytes 1572872 | tf_op jit(solution)/shard_map/ppermute | solution.py:18
  33.1 67.7 %collective-permute-start.3 = (f32[512,256]{1,0:T(8,128)S(1)}, f32[512,256]{1,0:T(8,128)}, u32[]{:S(2)}, u32[]{:S(2)}) collective-permute-start(f32[512,256]{1,0:T(8,128)S(1)} %get-tuple-element.9), channel_id=1, source_target_pairs={{0,24},{2,26},{4,28},{6,30},{1,25},{3,27},{5,29},{7,31}} | collective-permute-start | bytes 1572872 | tf_op jit(solution)/shard_map/ppermute | solution.py:18
  35.6 65.3 %collective-permute-start.2 = (f32[512,256]{1,0:T(8,128)S(1)}, f32[512,256]{1,0:T(8,128)}, u32[]{:S(2)}, u32[]{:S(2)}) collective-permute-start(f32[512,256]{1,0:T(8,128)S(1)} %get-tuple-element.10), channel_id=1, source_target_pairs={{0,96},{2,98},{4,100},{6,102},{1,97},{3,99},{5,101},{7,103}} | collective-permute-start | bytes 1572872 | tf_op jit(solution)/shard_map/ppermute | solution.py:18
  40.9 60.0 %collective-permute-start = (f32[512,256]{1,0:T(8,128)S(1)}, f32[512,256]{1,0:T(8,128)}, u32[]{:S(2)}, u32[]{:S(2)}) collective-permute-start(f32[512,256]{1,0:T(8,128)S(1)} %get-tuple-element.11), channel_id=1, source_target_pairs={{0,32},{2,34},{4,36},{6,38},{1,33},{3,35},{5,37},{7,39}} | collective-permute-start | bytes 1572872 | tf_op jit(solution)/shard_map/ppermute | solution.py:18
  45.3 55.6 %collective-permute-start.8 = (f32[512,256]{1,0:T(8,128)}, f32[512,256]{1,0:T(8,128)S(1)}, u32[]{:S(2)}, u32[]{:S(2)}) collective-permute-start(f32[512,256]{1,0:T(8,128)} %add_add_fusion), channel_id=1, source_target_pairs={{32,72},{34,74},{36,76},{38,78},{8,112},{10,114},{12,116},{14,118}... | collective-permute-start | bytes 1572872 | tf_op jit(solution)/shard_map/ppermute | solution.py:18
  100.9 7.5 %copy-start.2 = (bf16[3,512,256]{2,1,0:T(8,128)(2,1)S(1)}, bf16[3,512,256]{2,1,0:T(8,128)(2,1)}, u32[]{:S(2)}) copy-start(bf16[3,512,256]{2,1,0:T(8,128)(2,1)} %all-reduce.2.cloned.1.call-done) | copy-start | bytes 2359300
  100.9 7.5 %collective-permute-start.9 = (bf16[3,512,256]{2,1,0:T(8,128)(2,1)}, bf16[3,512,256]{2,1,0:T(8,128)(2,1)}, u32[]{:S(2)}, u32[]{:S(2)}) collective-permute-start(bf16[3,512,256]{2,1,0:T(8,128)(2,1)} %all-reduce.2.cloned.1.call-done), channel_id=1, source_target_pairs={{0,1},{1,0},{2,3},{3,2},{4,5},{5,4},{6,7},{7,6},{8,9},{9,8},{10,11... | collective-permute-start | bytes 2359304 | tf_op jit(solution)/shard_map/ppermute | solution.py:65
  105.6 4.6 %collective-permute-start.12 = (bf16[512,256]{1,0:T(8,128)(2,1)}, bf16[512,256]{1,0:T(8,128)(2,1)S(1)}, u32[]{:S(2)}, u32[]{:S(2)}) collective-permute-start(bf16[512,256]{1,0:T(8,128)(2,1)} %convolution_convert_fusion.3), channel_id=1, source_target_pairs={{8,14},{24,30},{32,38},{48,54},{72,78},{88,94},{96,102},{112,118},... | collective-permute-start | bytes 786440 | tf_op jit(solution)/shard_map/ppermute | solution.py:18
  106.3 4.0 %collective-permute-start.11 = (bf16[512,256]{1,0:T(8,128)(2,1)}, bf16[512,256]{1,0:T(8,128)(2,1)S(1)}, u32[]{:S(2)}, u32[]{:S(2)}) collective-permute-start(bf16[512,256]{1,0:T(8,128)(2,1)} %convolution_convert_fusion.3), channel_id=1, source_target_pairs={{8,12},{24,28},{32,36},{48,52},{72,76},{88,92},{96,100},{112,116},... | collective-permute-start | bytes 786440 | tf_op jit(solution)/shard_map/ppermute | solution.py:18
  106.9 3.3 %collective-permute-start.10 = (bf16[512,256]{1,0:T(8,128)(2,1)}, bf16[512,256]{1,0:T(8,128)(2,1)}, u32[]{:S(2)}, u32[]{:S(2)}) collective-permute-start(bf16[512,256]{1,0:T(8,128)(2,1)} %convolution_convert_fusion.3), channel_id=1, source_target_pairs={{8,10},{24,26},{32,34},{48,50},{72,74},{88,90},{96,98},{112,114},{... | collective-permute-start | bytes 786440 | tf_op jit(solution)/shard_map/ppermute | solution.py:18
  108.3 3.2 %copy-start.1 = (f32[4,512,512]{2,1,0:T(8,128)S(1)}, f32[4,512,512]{2,1,0:T(8,128)}, u32[]{:S(2)}) copy-start(f32[4,512,512]{2,1,0:T(8,128)} %param.5) | copy-start | bytes 12582916
  112.5 1.4 collective-permute-start.14
  113.2 0.7 collective-permute-start.13
  115.2 0.7 collective-permute-start.15
  118.5 35.5 %collective-permute-start.16 = (bf16[512,128]{1,0:T(8,128)(2,1)S(1)}, bf16[512,128]{1,0:T(8,128)(2,1)S(1)}, u32[]{:S(2)}, u32[]{:S(2)}) collective-permute-start(bf16[512,128]{1,0:T(8,128)(2,1)S(1)} %broadcast_select_fusion.1), channel_id=1, source_target_pairs={{8,0},{10,2},{12,4},{14,6},{24,16},{26,18},{28,20},{30,22},{32,40}... | collective-permute-start | bytes 393224 | tf_op jit(solution)/shard_map/ppermute | solution.py:18
  232.6 2.2 copy-start
Sparse Core Ops, SparseCore 0:
  11.4 89.3 all-reduce.1
Sparse Core Ops, SparseCore 1:
  24.9 11.9 all-gather.3
  154.8 77.8 all-gather.5

commit v3 on v2

--- a/solution.py
+++ b/solution.py
@@ -60,29 +60,56 @@
     place = (y * 4 + z) * 4 + x
     owner = place < 4
 
-    mask = jnp.where(owner, factor[0, :, :3], jnp.zeros((), BF)).transpose(1, 0, 2)
-    half = lax.psum(mask, ("y", "z"))
-    other = lax.ppermute(half, "rhs", [(0, 1), (1, 0)])
-    own = jnp.where(core == 0, jnp.concatenate([half, other], axis=2), jnp.concatenate([other, half], axis=2))
-
     def piece(site):
         at = (site[0] * 2 + site[1] // 2) * 256
         return rhs[0, :, at:at + 256]
 
-    def from_owner(value, site):
-        return permute(value, [((i, 0, 0), (i,) + site) for i in range(4)])
+    def from_owner(value, site, planes=(0, 1, 2, 3)):
+        return permute(value, [((i, 0, 0), (i,) + site) for i in planes])
+
+    def to_far(value, planes=(0, 1, 2, 3)):
+        return permute(value, [((i,) + near, (i,) + far) for near, far in ROUTES for i in planes])
+
+    def hop(value, start, end):
+        return permute(value, [((start, j, k), (end, j, k)) for j, k in ODD])
 
     hold = sum(from_owner(piece(far), near) for near, far in ROUTES)
     state = sum(from_owner(piece(near), near) for near, far in ROUTES)
-    state = state + permute(hold, [((i,) + near, (i,) + far) for near, far in ROUTES for i in range(4)])
+    first, state = lax.optimization_barrier((factor[0, :, 0], state))
+    state = state + to_far(hold)
+    rest = factor[0, :, 1:3].transpose(1, 0, 2)
+
+    def spread(value, planes):
+        near = sum(from_owner(value, site, planes) for site, _ in ROUTES)
+        mine = near + to_far(near, planes)
+        return mine, lax.ppermute(mine, "rhs", [(0, 1), (1, 0)])
+
+    first = spread(first, (1, 2, 3))
+    rest, _ = lax.optimization_barrier((rest, first[0]))
+    rest = spread(rest, (2, 3))
+    blocks = [first, [v[0] for v in rest], [v[1] for v in rest]]
+
+    def reduce(state, block, got):
+        mine = lax.dynamic_slice_in_dim(got, core * 256, 256, 0)
+        other = lax.dynamic_slice_in_dim(got, 256 - core * 256, 256, 0)
+        dot = lambda a, b: jnp.dot(a, b, preferred_element_type=F32)
+        return state - dot(block[0], mine) - dot(block[1], other)
 
     inverse = lax.dynamic_index_in_dim(inverses, x, 0, keepdims=False)
-    sent = None
-    for t in range(4):
-        if t > 0:
-            got = sum(permute(sent, [((t - 1, j, k), (i, j, k)) for j, k in ODD]) for i in range(t, 4))
-            state = state - jnp.dot(own[t - 1], got, preferred_element_type=F32)
-        sent = jnp.dot(inverse, state, precision=lax.Precision.HIGHEST).astype(BF)
+    solve = lambda s: jnp.dot(inverse, s, precision=lax.Precision.HIGHEST).astype(BF)
+    sent = solve(state)
+    at_1 = hop(sent, 0, 1)
+    at_3 = hop(sent, 0, 3)
+    at_2 = hop(at_3, 3, 2)
+    state = reduce(state, blocks[0], at_1 + at_3 + at_2)
+    sent = solve(state)
+    at_2 = hop(sent, 1, 2)
+    at_0 = hop(sent, 1, 0)
+    at_3 = hop(at_0, 0, 3)
+    state = reduce(state, blocks[1], at_2 + at_3)
+    sent = solve(state)
+    state = reduce(state, blocks[2], hop(sent, 2, 3))
+    sent = solve(state)
 
     left, right = sent[:, :128], sent[:, 128:]
     even = z % 2 == 0

time: 259 us -> 240 us (0.927)
  waiting for transfers between devices: 160 us -> 123 us
  starting transfers between devices: 29.6 us -> 52.6 us
  other arithmetic: 13.6 us -> 10.4 us
    psum x1 -> x0, waiting for transfers between devices: 54.9 us -> none  [local(): half = lax.psum(mask, ('y', 'z'))]
    ppermute x16 -> x27, starting transfers between devices: 29.5 us -> 52.3 us  [permute(): return lax.ppermute(value, ROWS, [(flat(*a), flat(*b)) for a, b in moves])]
    ppermute x16 -> x27, waiting for transfers between devices: 40.8 us -> 57 us  [permute(): return lax.ppermute(value, ROWS, [(flat(*a), flat(*b)) for a, b in moves])]
    dot_general x7 -> x10, matrix products: 8.98 us -> 7.91 us  [the longest x4 6.5 us: local(): jnp.dot(inverse, s, precision=lax.Precision.HIGHEST).astype(BF)]
  transfers between devices with their start and end apart: 20 -> 31, of which waited for: 5 -> 11; matrix products, arithmetic and copies ran while one was open for 13% -> 12% of each run, Pallas kernels for 0% -> 0%
where the time goes in v3:
time: 240 us; the launch traced here: 238 us
  waiting for transfers between devices  123 us (51%)
  starting transfers between devices  52.6 us (22%)
  Pallas kernels  15.1 us (6%)
  local copies, waits for them, and re-layouts  14.6 us (6%)
  between operations  14 us (6%)
  other arithmetic  10.4 us (4%)
  matrix products  7.91 us (3%)
    all_gather x1, waiting for transfers between devices, local(): everything = lax.all_gather(share, ROWS, axis=0).reshape(16, 4, 512, 128)  65.6 us
    ppermute x27, waiting for transfers between devices, permute(): return lax.ppermute(value, ROWS, [(flat(*a), flat(*b)) for a, b in moves])  57 us
    ppermute x27, starting transfers between devices, permute(): return lax.ppermute(value, ROWS, [(flat(*a), flat(*b)) for a, b in moves])  52.3 us
    pallas_call x1, Pallas kernels, update(): pl.pallas_call(update_kernel, grid=(cols // 256,), in_specs=[pl.BlockSpec...  15.1 us
    reshape x1, local copies, waits for them, and re-layouts, local(): whole = jnp.where(keep[:, None, :, None], whole, zero).reshape(2, 512, 2048)  7.84 us
    dot_general x4, matrix products, local(): jnp.dot(inverse, s, precision=lax.Precision.HIGHEST).astype(BF)  6.5 us
    select_n x1, other arithmetic, local(): whole = jnp.where(keep[:, None, :, None], whole, zero).reshape(2, 512, 2048)  5.92 us
  transfers between devices with their start and end apart: 31, of which 11 were waited for; matrix products, arithmetic and copies ran while one was open for 12% of the time, Pallas kernels for 0%

profile of v3, /device:TPU:6, one launch (start us, length us, event | category | flops | bytes accessed | tf_op | source)
XLA Modules:
  0.0 237.7 jit_solution(4728525511793645686)
XLA Ops:
  6.5 2.8 %slice_bitcast_fusion.2 = (f32[512,256]{1,0:T(8,128)S(1)}, f32[512,256]{1,0:T(8,128)S(1)}, f32[512,256]{1,0:T(8,128)S(1)}, f32[512,256]{1,0:T(8,128)S(1)}, f32[5...) fusion(f32[2,512,2048]{2,1,0:T(8,128)} %rhs_ref.1), kind=kLoop, calls=%fused_computation.24 | loop fusion | bytes 8388608 | tf_op jit(solution)/shard_map/squeeze | solution.py:65
  9.3 6.0 %collective-permute-start.3 = (f32[512,256]{1,0:T(8,128)S(1)}, f32[512,256]{1,0:T(8,128)S(1)}, u32[]{:S(2)}, u32[]{:S(2)}) collective-permute-start(f32[512,256]{1,0:T(8,128)S(1)} %get-tuple-element.14), channel_id=1, source_target_pairs={{0,24},{2,26},{4,28},{6,30},{1,25},{3,27},{5,29},{7,31}} | collective-permute-start | bytes 1572872 | tf_op jit(solution)/shard_map/ppermute | solution.py:18
  15.3 1.3 collective-permute-start.2
  16.6 1.3 collective-permute-start.1
  18.0 1.3 collective-permute-start
  19.3 1.3 collective-permute-start.5
  20.6 5.8 %collective-permute-done.3 = f32[512,256]{1,0:T(8,128)S(1)} collective-permute-done((f32[512,256]{1,0:T(8,128)S(1)}, f32[512,256]{1,0:T(8,128)S(1)}, u32[]{:S(2)}, u32[]{:S(2)}) %collective-permute-start.3) | collective-permute-done | bytes 524320 | tf_op jit(solution)/shard_map/ppermute | solution.py:18
  30.2 3.2 %collective-permute-start.7 = (f32[512,256]{1,0:T(8,128)S(1)}, f32[512,256]{1,0:T(8,128)S(1)}, u32[]{:S(2)}, u32[]{:S(2)}) collective-permute-start(f32[512,256]{1,0:T(8,128)S(1)} %get-tuple-element.18), channel_id=1, source_target_pairs={{0,24},{2,26},{4,28},{6,30},{1,25},{3,27},{5,29},{7,31}} | collective-permute-start | bytes 1572872 | tf_op jit(solution)/shard_map/ppermute | solution.py:18
  35.4 4.9 %collective-permute-done.5 = f32[512,256]{1,0:T(8,128)S(1)} collective-permute-done((f32[512,256]{1,0:T(8,128)S(1)}, f32[512,256]{1,0:T(8,128)S(1)}, u32[]{:S(2)}, u32[]{:S(2)}) %collective-permute-start.5) | collective-permute-done | bytes 524320 | tf_op jit(solution)/shard_map/ppermute | solution.py:18
  41.7 3.8 %collective-permute-start.10 = (bf16[512,256]{1,0:T(8,128)(2,1)S(1)}, bf16[512,256]{1,0:T(8,128)(2,1)S(1)}, u32[]{:S(2)}, u32[]{:S(2)}) collective-permute-start(bf16[512,256]{1,0:T(8,128)(2,1)S(1)} %bitcast.56), channel_id=1, source_target_pairs={{2,10},{4,12},{6,14},{3,11},{5,13},{7,15}} | collective-permute-start | bytes 786440 | tf_op jit(solution)/shard_map/ppermute | solution.py:18
  47.7 1.5 collective-permute-start.8
  50.1 1.3 collective-permute-done.9
  53.7 13.5 %collective-permute-start.21 = (bf16[2,512,256]{2,1,0:T(8,128)(2,1)}, bf16[2,512,256]{2,1,0:T(8,128)(2,1)S(1)}, u32[]{:S(2)}, u32[]{:S(2)}) collective-permute-start(bf16[2,512,256]{2,1,0:T(8,128)(2,1)} %bitcast.51), channel_id=1, source_target_pairs={{4,28},{6,30},{5,29},{7,31}} | collective-permute-start | bytes 1572872 | tf_op jit(solution)/shard_map/ppermute | solution.py:18
  67.2 1.3 collective-permute-start.20
  69.8 2.1 collective-permute-start.18
  73.0 2.2 convolution_convert_fusion.3
  87.7 2.3 convolution_convert_fusion
  90.1 1.5 collective-permute-start.28
  91.6 41.8 %collective-permute-done.28 = bf16[512,128]{1,0:T(8,128)(2,1)S(1)} collective-permute-done((bf16[512,128]{1,0:T(8,128)(2,1)S(1)}, bf16[512,128]{1,0:T(8,128)(2,1)S(1)}, u32[]{:S(2)}, u32[]{:S(2)}) %collective-permute-start.28) | collective-permute-done | bytes 131104 | tf_op jit(solution)/shard_map/ppermute | solution.py:18
  134.2 5.9 %broadcast_select_fusion = bf16[2,512,4,512]{3,2,1,0:T(4,128)(2,1)} fusion(bf16[2,512,4,512]{3,2,1,0:T(4,128)(2,1)} %all-gather.4.cloned.1.call-done, pred[2,4]{1,0:T(4,128)(4,1)S(1)} %iota_compare_fusion), kind=kLoop, calls=%fused_computation | loop fusion | flops 2097152 | bytes 8388616 | tf_op jit(solution)/shard_map/jit(_where)/select_n | solution.py:124
  140.1 7.8 %reshape.31.factor_ref = bf16[2,512,2048]{2,1,0:T(8,128)(2,1)} reshape(bf16[2,512,4,512]{3,2,1,0:T(4,128)(2,1)} %broadcast_select_fusion) | data formatting | bytes 8388608 | tf_op jit(solution)/shard_map/reshape | solution.py:124
  147.9 65.6 %all-gather.6.cloned.1.call-done = bf16[32768,128]{1,0:T(8,128)(2,1)} async-done(((bf16[512,128]{1,0:T(8,128)(2,1)}), bf16[32768,128]{1,0:T(8,128)(2,1)}) %all-gather.6.cloned.1.call-update) | async-done | bytes 8388624 | tf_op jit(solution)/shard_map/all_gather | solution.py:118
  213.5 2.2 copy-done
  215.7 15.1 %shard_map.37 = f32[2,512,2048]{2,1,0:T(8,128)} custom-call(s32[1]{0:T(128)} %bitcast.place_ref, bf16[2,512,2048]{2,1,0:T(8,128)(2,1)S(1)} %copy-done, f32[2,512,2048]{2,1,0:T(8,128)} %rhs_ref.1, bf16[16,4,512,128]{3,2,1,0:T(8,128)(2,1)} %bitcast.53), custom_call_target="tpu_custom_call" | custom-call | tf_op jit(solution)/shard_map/pallas_call | solution.py:42
  (77 shorter events, 27.7 us)
Async XLA Ops:
  6.5 127.6 %all-gather.4.cloned.1.call-start = ((), (), s32[]{:S(2)}) async-start(), calls=%async_computation | async-start | bytes 6291456 | tf_op jit(solution)/shard_map/all_gather | solution.py:121
  9.3 17.1 %collective-permute-start.3 = (f32[512,256]{1,0:T(8,128)S(1)}, f32[512,256]{1,0:T(8,128)S(1)}, u32[]{:S(2)}, u32[]{:S(2)}) collective-permute-start(f32[512,256]{1,0:T(8,128)S(1)} %get-tuple-element.14), channel_id=1, source_target_pairs={{0,24},{2,26},{4,28},{6,30},{1,25},{3,27},{5,29},{7,31}} | collective-permute-start | bytes 1572872 | tf_op jit(solution)/shard_map/ppermute | solution.py:18
  15.3 13.1 %collective-permute-start.2 = (f32[512,256]{1,0:T(8,128)S(1)}, f32[512,256]{1,0:T(8,128)S(1)}, u32[]{:S(2)}, u32[]{:S(2)}) collective-permute-start(f32[512,256]{1,0:T(8,128)S(1)} %get-tuple-element.15), channel_id=1, source_target_pairs={{0,96},{2,98},{4,100},{6,102},{1,97},{3,99},{5,101},{7,103}} | collective-permute-start | bytes 1572872 | tf_op jit(solution)/shard_map/ppermute | solution.py:18
  16.6 13.6 %collective-permute-start.1 = (f32[512,256]{1,0:T(8,128)S(1)}, f32[512,256]{1,0:T(8,128)S(1)}, u32[]{:S(2)}, u32[]{:S(2)}) collective-permute-start(f32[512,256]{1,0:T(8,128)S(1)} %get-tuple-element.16), channel_id=1, source_target_pairs={{0,8},{2,10},{4,12},{6,14},{1,9},{3,11},{5,13},{7,15}} | collective-permute-start | bytes 1572872 | tf_op jit(solution)/shard_map/ppermute | solution.py:18
  18.0 16.0 %collective-permute-start = (f32[512,256]{1,0:T(8,128)S(1)}, f32[512,256]{1,0:T(8,128)S(1)}, u32[]{:S(2)}, u32[]{:S(2)}) collective-permute-start(f32[512,256]{1,0:T(8,128)S(1)} %get-tuple-element.17), channel_id=1, source_target_pairs={{0,32},{2,34},{4,36},{6,38},{1,33},{3,35},{5,37},{7,39}} | collective-permute-start | bytes 1572872 | tf_op jit(solution)/shard_map/ppermute | solution.py:18
  19.3 21.0 %collective-permute-start.5 = (f32[512,256]{1,0:T(8,128)S(1)}, f32[512,256]{1,0:T(8,128)S(1)}, u32[]{:S(2)}, u32[]{:S(2)}) collective-permute-start(f32[512,256]{1,0:T(8,128)S(1)} %get-tuple-element.11), channel_id=1, source_target_pairs={{0,8},{2,10},{4,12},{6,14},{1,9},{3,11},{5,13},{7,15}} | collective-permute-start | bytes 1572872 | tf_op jit(solution)/shard_map/ppermute | solution.py:18
  26.4 15.2 %collective-permute-start.6 = (f32[512,256]{1,0:T(8,128)S(1)}, f32[512,256]{1,0:T(8,128)S(1)}, u32[]{:S(2)}, u32[]{:S(2)}) collective-permute-start(f32[512,256]{1,0:T(8,128)S(1)} %get-tuple-element.12), channel_id=1, source_target_pairs={{0,96},{2,98},{4,100},{6,102},{1,97},{3,99},{5,101},{7,103}} | collective-permute-start | bytes 1572872 | tf_op jit(solution)/shard_map/ppermute | solution.py:18
  28.4 17.0 %collective-permute-start.4 = (f32[512,256]{1,0:T(8,128)S(1)}, f32[512,256]{1,0:T(8,128)S(1)}, u32[]{:S(2)}, u32[]{:S(2)}) collective-permute-start(f32[512,256]{1,0:T(8,128)S(1)} %get-tuple-element.13), channel_id=1, source_target_pairs={{0,32},{2,34},{4,36},{6,38},{1,33},{3,35},{5,37},{7,39}} | collective-permute-start | bytes 1572872 | tf_op jit(solution)/shard_map/ppermute | solution.py:18
  30.2 16.5 %collective-permute-start.7 = (f32[512,256]{1,0:T(8,128)S(1)}, f32[512,256]{1,0:T(8,128)S(1)}, u32[]{:S(2)}, u32[]{:S(2)}) collective-permute-start(f32[512,256]{1,0:T(8,128)S(1)} %get-tuple-element.18), channel_id=1, source_target_pairs={{0,24},{2,26},{4,28},{6,30},{1,25},{3,27},{5,29},{7,31}} | collective-permute-start | bytes 1572872 | tf_op jit(solution)/shard_map/ppermute | solution.py:18
  34.1 15.3 %collective-permute-start.12 = (bf16[512,256]{1,0:T(8,128)(2,1)S(1)}, bf16[512,256]{1,0:T(8,128)(2,1)S(1)}, u32[]{:S(2)}, u32[]{:S(2)}) collective-permute-start(bf16[512,256]{1,0:T(8,128)(2,1)S(1)} %bitcast.54), channel_id=1, source_target_pairs={{2,26},{4,28},{6,30},{3,27},{5,29},{7,31}} | collective-permute-start | bytes 786440 | tf_op jit(solution)/shard_map/ppermute | solution.py:18
  40.3 9.0 %collective-permute-start.11 = (bf16[512,256]{1,0:T(8,128)(2,1)S(1)}, bf16[512,256]{1,0:T(8,128)(2,1)S(1)}, u32[]{:S(2)}, u32[]{:S(2)}) collective-permute-start(bf16[512,256]{1,0:T(8,128)(2,1)S(1)} %bitcast.55), channel_id=1, source_target_pairs={{2,98},{4,100},{6,102},{3,99},{5,101},{7,103}} | collective-permute-start | bytes 786440 | tf_op jit(solution)/shard_map/ppermute | solution.py:18
  41.7 8.4 %collective-permute-start.10 = (bf16[512,256]{1,0:T(8,128)(2,1)S(1)}, bf16[512,256]{1,0:T(8,128)(2,1)S(1)}, u32[]{:S(2)}, u32[]{:S(2)}) collective-permute-start(bf16[512,256]{1,0:T(8,128)(2,1)S(1)} %bitcast.56), channel_id=1, source_target_pairs={{2,10},{4,12},{6,14},{3,11},{5,13},{7,15}} | collective-permute-start | bytes 786440 | tf_op jit(solution)/shard_map/ppermute | solution.py:18
  45.4 6.0 %collective-permute-start.9 = (bf16[512,256]{1,0:T(8,128)(2,1)S(1)}, bf16[512,256]{1,0:T(8,128)(2,1)S(1)}, u32[]{:S(2)}, u32[]{:S(2)}) collective-permute-start(bf16[512,256]{1,0:T(8,128)(2,1)S(1)} %bitcast.57), channel_id=1, source_target_pairs={{2,34},{4,36},{6,38},{3,35},{5,37},{7,39}} | collective-permute-start | bytes 786440 | tf_op jit(solution)/shard_map/ppermute | solution.py:18
  47.7 24.2 %collective-permute-start.8 = (f32[512,256]{1,0:T(8,128)}, f32[512,256]{1,0:T(8,128)}, u32[]{:S(2)}, u32[]{:S(2)}) collective-permute-start(f32[512,256]{1,0:T(8,128)} %add_add_fusion.1), channel_id=1, source_target_pairs={{32,72},{34,74},{36,76},{38,78},{8,112},{10,114},{12,116},{14,118}... | collective-permute-start | bytes 1572872 | tf_op jit(solution)/shard_map/ppermute | solution.py:18
  53.7 22.5 %collective-permute-start.21 = (bf16[2,512,256]{2,1,0:T(8,128)(2,1)}, bf16[2,512,256]{2,1,0:T(8,128)(2,1)S(1)}, u32[]{:S(2)}, u32[]{:S(2)}) collective-permute-start(bf16[2,512,256]{2,1,0:T(8,128)(2,1)} %bitcast.51), channel_id=1, source_target_pairs={{4,28},{6,30},{5,29},{7,31}} | collective-permute-start | bytes 1572872 | tf_op jit(solution)/shard_map/ppermute | solution.py:18
  67.2 9.8 %collective-permute-start.20 = (bf16[2,512,256]{2,1,0:T(8,128)(2,1)}, bf16[2,512,256]{2,1,0:T(8,128)(2,1)S(1)}, u32[]{:S(2)}, u32[]{:S(2)}) collective-permute-start(bf16[2,512,256]{2,1,0:T(8,128)(2,1)} %bitcast.51), channel_id=1, source_target_pairs={{4,100},{6,102},{5,101},{7,103}} | collective-permute-start | bytes 1572872 | tf_op jit(solution)/shard_map/ppermute | solution.py:18
  68.5 9.3 %collective-permute-start.19 = (bf16[2,512,256]{2,1,0:T(8,128)(2,1)}, bf16[2,512,256]{2,1,0:T(8,128)(2,1)S(1)}, u32[]{:S(2)}, u32[]{:S(2)}) collective-permute-start(bf16[2,512,256]{2,1,0:T(8,128)(2,1)} %bitcast.51), channel_id=1, source_target_pairs={{4,12},{6,14},{5,13},{7,15}} | collective-permute-start | bytes 1572872 | tf_op jit(solution)/shard_map/ppermute | solution.py:18
  69.8 9.0 %collective-permute-start.18 = (bf16[2,512,256]{2,1,0:T(8,128)(2,1)}, bf16[2,512,256]{2,1,0:T(8,128)(2,1)}, u32[]{:S(2)}, u32[]{:S(2)}) collective-permute-start(bf16[2,512,256]{2,1,0:T(8,128)(2,1)} %bitcast.51), channel_id=1, source_target_pairs={{4,36},{6,38},{5,37},{7,39}} | collective-permute-start | bytes 1572872 | tf_op jit(solution)/shard_map/ppermute | solution.py:18
  76.0 137.6 %all-gather.6.cloned.1.call-start = ((), (), s32[]{:S(2)}) async-start(), calls=%async_computation.1 | async-start | bytes 8519680 | tf_op jit(solution)/shard_map/all_gather | solution.py:118
  76.0 4.7 %collective-permute-start.17 = (bf16[512,256]{1,0:T(8,128)(2,1)S(1)}, bf16[512,256]{1,0:T(8,128)(2,1)S(1)}, u32[]{:S(2)}, u32[]{:S(2)}) collective-permute-start(bf16[512,256]{1,0:T(8,128)(2,1)S(1)} %add.113), channel_id=1, source_target_pairs={{0,1},{1,0},{2,3},{3,2},{4,5},{5,4},{6,7},{7,6},{8,9},{9,8},{10,11... | collective-permute-start | bytes 786440 | tf_op jit(solution)/shard_map/ppermute | solution.py:85
  76.1 4.5 %collective-permute-start.14 = (bf16[512,256]{1,0:T(8,128)(2,1)S(1)}, bf16[512,256]{1,0:T(8,128)(2,1)S(1)}, u32[]{:S(2)}, u32[]{:S(2)}) collective-permute-start(bf16[512,256]{1,0:T(8,128)(2,1)S(1)} %convolution_convert_fusion.3), channel_id=1, source_target_pairs={{8,10},{24,26},{32,34},{48,50},{72,74},{88,90},{96,98},{112,114},{... | collective-permute-start | bytes 786440 | tf_op jit(solution)/shard_map/ppermute | solution.py:18
  77.0 3.7 %collective-permute-start.16 = (bf16[512,256]{1,0:T(8,128)(2,1)S(1)}, bf16[512,256]{1,0:T(8,128)(2,1)S(1)}, u32[]{:S(2)}, u32[]{:S(2)}) collective-permute-start(bf16[512,256]{1,0:T(8,128)(2,1)S(1)} %collective-permute-done.15), channel_id=1, source_target_pairs={{14,12},{30,28},{38,36},{54,52},{78,76},{94,92},{102,100},{118,116... | collective-permute-start | bytes 786440 | tf_op jit(solution)/shard_map/ppermute | solution.py:18
  80.0 3.0 %collective-permute-start.22 = (bf16[2,512,256]{2,1,0:T(8,128)(2,1)S(1)}, bf16[2,512,256]{2,1,0:T(8,128)(2,1)S(1)}, u32[]{:S(2)}, u32[]{:S(2)}) collective-permute-start(bf16[2,512,256]{2,1,0:T(8,128)(2,1)S(1)} %add_add_fusion), channel_id=1, source_target_pairs={{36,76},{38,78},{12,116},{14,118},{100,92},{102,94},{28,52},{30,54... | collective-permute-start | bytes 1572872 | tf_op jit(solution)/shard_map/ppermute | solution.py:18
  90.1 43.3 %collective-permute-start.28 = (bf16[512,128]{1,0:T(8,128)(2,1)S(1)}, bf16[512,128]{1,0:T(8,128)(2,1)S(1)}, u32[]{:S(2)}, u32[]{:S(2)}) collective-permute-start(bf16[512,128]{1,0:T(8,128)(2,1)S(1)} %broadcast_select_fusion.1), channel_id=1, source_target_pairs={{8,0},{10,2},{12,4},{14,6},{24,16},{26,18},{28,20},{30,22},{32,40}... | collective-permute-start | bytes 393224 | tf_op jit(solution)/shard_map/ppermute | solution.py:18
  (10 other events, 43.6 us)
Sparse Core Ops, SparseCore 0:
  76.1 13.4 all-gather.3
  134.2 79.2 all-gather.5

commit v4 on v1

v4 whole, which is shorter than its diff:
```python
import jax
import jax.numpy as jnp
from jax import lax
from jax.experimental import pallas as pl
from jax.experimental.pallas import tpu as pltpu
from jax.sharding import Mesh, PartitionSpec as P

ROWS = ("y", "z", "x")
BF = jnp.bfloat16
F32 = jnp.float32
ALL = [(j, k) for j in range(4) for k in range(4)]
ORDERS = (
    (("y", 1), ("y", 3), ("z", 1), ("z", 3)),
    (("y", 3), ("y", 1), ("z", 3), ("z", 1)),
    (("z", 1), ("z", 3), ("y", 1), ("y", 3)),
    (("z", 3), ("z", 1), ("y", 3), ("y", 1)),
)


def flat(x, y, z):
    return ((y % 4) * 4 + (z % 4)) * 4 + (x % 4)


def permute(value, moves):
    return lax.ppermute(value, ROWS, [(flat(*a), flat(*b)) for a, b in moves])


def hop(value, *planes):
    return permute(value, [((a, j, k), (b, j, k)) for a, b in planes for j, k in ALL])


def ring(value, axis, step):
    return lax.ppermute(value, axis, [(i, (i + step) % 4) for i in range(4)])


def ring_gather(value, axis):
    at = lax.axis_index(axis)
    parts = [value] + [ring(value, axis, 4 - d) for d in (1, 2, 3)]
    both = jnp.stack(parts + parts[:3])
    return lax.dynamic_slice_in_dim(both, (4 - at) % 4, 4, 0)


def swap(value, axis, flip):
    return lax.ppermute(value, axis, [(i, i ^ flip) for i in range(4)])


def spread(parts):
    parts = [p[None] for p in parts]
    for step in range(4):
        got = [swap(p, *order[step]) for p, order in zip(parts, ORDERS)]
        parts = [jnp.concatenate([p, g], axis=0) for p, g in zip(parts, got)]
    return parts


def places(y, z):
    sites = jnp.arange(16, dtype=jnp.int32)
    tables = []
    for order in ORDERS:
        off = {"y": (sites // 4) ^ y, "z": (sites % 4) ^ z}
        total = jnp.zeros_like(sites)
        for step, (axis, flip) in enumerate(order):
            o = off[axis]
            upper = o >> 1
            bit = upper if flip == 3 else (o & 1) ^ upper
            total = total + (bit << step)
        tables.append(total)
    return jnp.stack(tables).reshape(-1)


def update_kernel(scalars, factor_ref, rhs_ref, early_ref, *rest):
    late, out_ref, sent_ref = rest[:8], rest[8], rest[9]
    for h in range(2):
        lanes = slice(h * 128, (h + 1) * 128)
        sent_ref[:1024, lanes] = early_ref[h]
        for p in range(4):
            sent_ref[1024 + p * 256:1280 + p * 256, lanes] = late[p * 2 + h][0]
    for c in range(2):
        out_ref[c] = rhs_ref[c] - jnp.dot(factor_ref[c], sent_ref[...], preferred_element_type=F32)
    place = scalars[64]

    @pl.when(place < 4)
    def _():
        out_ref[0] = sent_ref[pl.ds(pl.multiple_of(place * 512, 512), 512), :].astype(F32)


def update(scalars, factor, rhs, early, late):
    cycles, tile, depth = factor.shape
    late_specs = [
        pl.BlockSpec((1, 256, 128), lambda j, s, p=p, h=h: (s[p * 16 + 2 * j + h], 0, 0))
        for p in range(4) for h in range(2)
    ]
    return pl.pallas_call(
        update_kernel,
        grid_spec=pltpu.PrefetchScalarGridSpec(
            num_scalar_prefetch=1,
            grid=(rhs.shape[2] // 256,),
            in_specs=[
                pl.BlockSpec((cycles, tile, depth), lambda j, s: (0, 0, 0)),
                pl.BlockSpec((cycles, tile, 256), lambda j, s: (0, 0, j)),
                pl.BlockSpec((2, 1024, 128), lambda j, s: (j, 0, 0)),
            ] + late_specs,
            out_specs=pl.BlockSpec((cycles, tile, 256), lambda j, s: (0, 0, j)),
            scratch_shapes=[pltpu.VMEM((depth, 256), BF)],
        ),
        out_shape=jax.ShapeDtypeStruct(rhs.shape, F32),
        compiler_params=pltpu.CompilerParams(vmem_limit_bytes=48 << 20),
    )(scalars, factor, rhs, early, *[late[p] for p in range(4) for _ in range(2)])


def local(rhs, factor, inverses):
    x, y, z = (lax.axis_index(a) for a in ("x", "y", "z"))
    core = lax.axis_index("rhs")
    place = (y * 4 + z) * 4 + x
    owner = place < 4
    zero = jnp.zeros((), BF)

    def high(slab):
        return lax.reduce_precision(slab, 8, 7).astype(BF)

    def low(slab):
        return (slab - lax.reduce_precision(slab, 8, 7)).astype(BF)

    shards = factor[0, :, :3].reshape(768, 512)

    def load_a(d):
        return jnp.concatenate([high(rhs[0, :, d * 512:(d + 1) * 512]), shards[d * 96:(d + 1) * 96]], axis=0)

    def load_b(d):
        slab = jnp.concatenate([rhs[0, :, j * 512 + d * 128:j * 512 + (d + 1) * 128] for j in range(4)], axis=1)
        return jnp.concatenate([low(slab), shards[384 + d * 96:384 + (d + 1) * 96]], axis=0)

    hold_a = jnp.where(owner, load_a(0), zero)
    hold_b = jnp.where(owner, load_b(0), zero)
    for d in (1, 3, 2):
        hold_a = hold_a + permute(load_a(d), [((i, 0, 0), (i, d, 0)) for i in range(4)])
        hold_b = hold_b + permute(load_b(d), [((i, 0, 0), (i, 0, d)) for i in range(4)])
    mine_a = jnp.where(z == 0, hold_a[:, :128], zero)
    mine_b = jnp.where(y == 0, hold_b[:, :128], zero)
    for d in (1, 3, 2):
        cut = slice(d * 128, (d + 1) * 128)
        mine_a = mine_a + permute(hold_a[:, cut], [((i, j, 0), (i, j, d)) for i in range(4) for j in range(4)])
        mine_b = mine_b + permute(hold_b[:, cut], [((i, 0, j), (i, d, j)) for i in range(4) for j in range(4)])

    shard = jnp.concatenate([mine_a[512:], mine_b[512:]], axis=0)
    every = ring_gather(ring_gather(shard, "z"), "y")
    top = every[:, :, :96].transpose(0, 2, 1, 3).reshape(384, 512)
    low_part = every[:, :, 96:].transpose(1, 2, 0, 3).reshape(384, 512)
    half = jnp.concatenate([top, low_part], axis=0).reshape(512, 3, 256).transpose(1, 0, 2)
    other = lax.ppermute(half, "rhs", [(0, 1), (1, 0)])

    def reduce(state, panel, got):
        mine = lax.dynamic_slice_in_dim(got, core * 256, 256, 0)
        rest = lax.dynamic_slice_in_dim(got, 256 - core * 256, 256, 0)
        dot = lambda a, b: jnp.dot(a, b, preferred_element_type=F32)
        return state - dot(half[panel], mine) - dot(other[panel], rest)

    inverse = lax.dynamic_index_in_dim(inverses, x, 0, keepdims=False)
    solve = lambda s: jnp.dot(inverse, s, precision=lax.Precision.HIGHEST).astype(BF)
    state = mine_a[:512].astype(F32) + mine_b[:512].astype(F32)

    sent = solve(state)
    got = hop(sent, (0, 1)) + hop(sent, (0, 3)) + hop(sent, (0, 2))
    panel_0 = jnp.where(x == 0, sent, got)
    state = reduce(state, 0, got)
    sent = solve(state)
    got = hop(sent, (1, 2)) + hop(sent, (1, 3))
    panel_1 = jnp.where(x == 1, sent, got + hop(sent, (1, 0)))
    early = lax.all_gather(jnp.concatenate([panel_0, panel_1], axis=0), ("y", "z"), axis=0)
    state = reduce(state, 1, got)
    sent = solve(state)
    got = hop(sent, (2, 3))
    state = reduce(state, 2, got)
    sent = solve(state)
    back = hop(sent, (2, 1), (3, 2))
    far = hop(sent, (2, 0), (3, 1))
    wrap = hop(sent, (3, 0))
    panel_2 = jnp.where(x == 2, sent, jnp.where(x == 3, got, jnp.where(x == 1, back, far)))
    panel_3 = jnp.where(x == 3, sent, jnp.where(x == 2, back, jnp.where(x == 1, far, wrap)))
    late = spread([panel_2[:256], panel_2[256:], panel_3[:256], panel_3[256:]])

    whole = lax.all_gather(factor, "rhs", axis=3, tiled=True)
    tiles = jnp.arange(2, dtype=jnp.int32) * 64 + place
    keep = tiles[:, None] > jnp.arange(4, dtype=jnp.int32)[None]
    whole = jnp.where(keep[:, None, :, None], whole, zero).reshape(2, 512, 2048)
    scalars = jnp.concatenate([places(y, z), place[None]]).astype(jnp.int32)
    return update(scalars, whole, rhs, early, late)


def solution(mesh):
    grid = Mesh(mesh.devices.reshape(4, 4, 4, 2), ("y", "z", "x", "rhs"))
    return jax.shard_map(
        local,
        mesh=grid,
        in_specs=(P(None, ROWS, "rhs"), P(None, ROWS, None, "rhs"), P()),
        out_specs=P(None, ROWS, "rhs"),
        check_vma=False,
    )
```

time: 236 us -> 232 us (0.983)
  waiting for transfers between devices: 107 us -> 75.2 us
  starting transfers between devices: 42 us -> 63.4 us
  local copies, waits for them, and re-layouts: 33.1 us -> 25.6 us
  matrix products: 6.91 us -> 13.1 us
  other arithmetic: 15.5 us -> 20.9 us
    all_gather x1, waiting for transfers between devices: 62.7 us -> 0.01 us  [local(): lax.all_gather(jnp.concatenate([panel_0, panel_1], axis=0), ('y', 'z'), a...]
    ppermute x0 -> x16, waiting for transfers between devices: none -> 25.7 us  [swap(): return lax.ppermute(value, axis, [(i, i ^ flip) for i in range(4)])]
    ppermute x0 -> x16, starting transfers between devices: none -> 19.3 us  [swap(): return lax.ppermute(value, axis, [(i, i ^ flip) for i in range(4)])]
    dot_general x7 -> x10, matrix products: 6.91 us -> 13.1 us  [the longest x4 8.91 us: local(): jnp.dot(inverse, s, precision=lax.Precision.HIGHEST).astype(BF)]
    convert_element_type x0 -> x5, other arithmetic: none -> 5.07 us  [the longest x4 2.61 us: low(): return (slab - lax.reduce_precision(slab, 8, 7)).astype(BF)]
    unnamed x17 -> x40, local copies, waits for them, and re-layouts: 7.81 us -> 2.75 us
    concatenate x2 -> x21, other arithmetic: 1.46 us -> 5.67 us  [the longest x3 2.61 us: load_a(): jnp.concatenate([high(rhs[0, :, d * 512:(d + 1) * 512]), shards[d * 96:(d...]
    squeeze x4 -> x1, local copies, waits for them, and re-layouts: 6.7 us -> 3.4 us  [load_b(): rhs[0, :, j * 512 + d * 128:j * 512 + (d + 1) * 128]]
  transfers between devices with their start and end apart: 27 -> 47, of which waited for: 13 -> 24; matrix products, arithmetic and copies ran while one was open for 13% -> 22% of each run, Pallas kernels for 0% -> 0%
where the time goes in v4:
time: 232 us; the launch traced here: 229 us
  waiting for transfers between devices  75.2 us (32%)
  starting transfers between devices  63.4 us (27%)
  local copies, waits for them, and re-layouts  25.6 us (11%)
  other arithmetic  20.9 us (9%)
  Pallas kernels  16.9 us (7%)
  between operations  14.3 us (6%)
  matrix products  13.1 us (6%)
    ppermute x22, waiting for transfers between devices, permute(): return lax.ppermute(value, ROWS, [(flat(*a), flat(*b)) for a, b in moves])  38.4 us
    ppermute x22, starting transfers between devices, permute(): return lax.ppermute(value, ROWS, [(flat(*a), flat(*b)) for a, b in moves])  32.6 us
    ppermute x16, waiting for transfers between devices, swap(): return lax.ppermute(value, axis, [(i, i ^ flip) for i in range(4)])  25.7 us
    ppermute x16, starting transfers between devices, swap(): return lax.ppermute(value, axis, [(i, i ^ flip) for i in range(4)])  19.3 us
    pallas_call x1, Pallas kernels, update(): pl.pallas_call(update_kernel, grid_spec=pltpu.PrefetchScalarGridSpec(num_...  16.9 us
    ppermute x6, starting transfers between devices, ring(): return lax.ppermute(value, axis, [(i, (i + step) % 4) for i in range(4)])  11.4 us
    ppermute x6, waiting for transfers between devices, ring(): return lax.ppermute(value, axis, [(i, (i + step) % 4) for i in range(4)])  11 us
    dot_general x4, matrix products, local(): jnp.dot(inverse, s, precision=lax.Precision.HIGHEST).astype(BF)  8.91 us
  transfers between devices with their start and end apart: 47, of which 24 were waited for; matrix products, arithmetic and copies ran while one was open for 22% of the time, Pallas kernels for 0%

profile of v4, /device:TPU:6, one launch (start us, length us, event | category | flops | bytes accessed | tf_op | source)
XLA Modules:
  0.0 229.5 jit_solution(2988843512834852533)
XLA Ops:
  6.5 2.4 %fusion.61 = (bf16[1,64,3,256]{3,2,1,0:T(4,128)(2,1)}, bf16[1,64,3,256]{3,2,1,0:T(4,128)(2,1)}, bf16[1,64,3,256]{3,2,1,0:T(4,128)(2,1)}, bf16[1,64,3,256]{3,2,1,...) fusion(bf16[2,512,4,256]{3,2,1,0:T(4,128)(2,1)} %param.4), kind=kLoop, calls=%fused_computation.186 | loop fusion | bytes 1572864 | tf_op jit(solution)/shard_map/slice | solution.py:126
  9.1 2.5 %fusion.21 = (bf16[512,512]{1,0:T(8,128)(2,1)S(1)}, bf16[512,512]{1,0:T(8,128)(2,1)S(1)}, bf16[512,512]{1,0:T(8,128)(2,1)S(1)}, bf16[512,512]{1,0:T(8,128)(2,1)S(1)}) fusion(f32[2,512,2048]{2,1,0:T(8,128)} %rhs_ref.1), kind=kLoop, calls=%fused_computation.46 | loop fusion | flops 2097152 | bytes 6291456 | tf_op jit(solution)/shard_map/convert_element_type | solution.py:118
  12.4 4.3 %collective-permute-start = (bf16[608,512]{1,0:T(8,128)(2,1)}, bf16[608,512]{1,0:T(8,128)(2,1)}, u32[]{:S(2)}, u32[]{:S(2)}) collective-permute-start(bf16[608,512]{1,0:T(8,128)(2,1)} %pad_maximum_fusion.1), channel_id=1, source_target_pairs={{0,32},{2,34},{4,36},{6,38},{1,33},{3,35},{5,37},{7,39}} | collective-permute-start | bytes 1867784 | tf_op jit(solution)/shard_map/ppermute | solution.py:25
  17.7 2.9 %collective-permute-start.1 = (bf16[608,512]{1,0:T(8,128)(2,1)}, bf16[608,512]{1,0:T(8,128)(2,1)}, u32[]{:S(2)}, u32[]{:S(2)}) collective-permute-start(bf16[608,512]{1,0:T(8,128)(2,1)} %pad_maximum_fusion.2), channel_id=1, source_target_pairs={{0,96},{2,98},{4,100},{6,102},{1,97},{3,99},{5,101},{7,103}} | collective-permute-start | bytes 1867784 | tf_op jit(solution)/shard_map/ppermute | solution.py:25
  23.8 3.4 %slice_bitcast_fusion.21 = (f32[512,128]{1,0:T(8,128)S(1)}, f32[512,128]{1,0:T(8,128)S(1)}, f32[512,128]{1,0:T(8,128)S(1)}, f32[512,128]{1,0:T(8,128)S(1)}, f32[...) fusion(f32[2,512,2048]{2,1,0:T(8,128)} %rhs_ref.1), kind=kLoop, calls=%fused_computation.91 | loop fusion | bytes 8388608 | tf_op jit(solution)/shard_map/squeeze | solution.py:129
  48.7 4.2 %collective-permute-done.7 = bf16[608,512]{1,0:T(8,128)(2,1)S(1)} collective-permute-done((bf16[608,512]{1,0:T(8,128)(2,1)}, bf16[608,512]{1,0:T(8,128)(2,1)S(1)}, u32[]{:S(2)}, u32[]{:S(2)}) %collective-permute-start.7) | collective-permute-done | bytes 622624 | tf_op jit(solution)/shard_map/ppermute | solution.py:25
  52.8 7.5 %collective-permute-done.8 = bf16[608,512]{1,0:T(8,128)(2,1)S(1)} collective-permute-done((bf16[608,512]{1,0:T(8,128)(2,1)S(1)}, bf16[608,512]{1,0:T(8,128)(2,1)S(1)}, u32[]{:S(2)}, u32[]{:S(2)}) %collective-permute-start.8) | collective-permute-done | bytes 622624 | tf_op jit(solution)/shard_map/ppermute | solution.py:25
  68.6 4.1 %collective-permute-start.16 = (bf16[192,128]{1,0:T(8,128)(2,1)S(1)}, bf16[192,128]{1,0:T(8,128)(2,1)S(1)}, u32[]{:S(2)}, u32[]{:S(2)}) collective-permute-start(bf16[192,128]{1,0:T(8,128)(2,1)S(1)} %pad_maximum_fusion.20), channel_id=1, source_target_pairs={{0,16},{8,24},{16,0},{24,8},{1,17},{9,25},{17,1},{25,9},{2,18},{10... | collective-permute-start | bytes 147464 | tf_op jit(solution)/shard_map/ppermute | solution.py:33
  78.4 3.8 %collective-permute-start.18 = (bf16[4,192,128]{2,1,0:T(8,128)(2,1)S(1)}, bf16[4,192,128]{2,1,0:T(8,128)(2,1)S(1)}, u32[]{:S(2)}, u32[]{:S(2)}) collective-permute-start(bf16[4,192,128]{2,1,0:T(8,128)(2,1)S(1)} %get-tuple-element.10), channel_id=1, source_target_pairs={{0,96},{32,0},{64,32},{96,64},{1,97},{33,1},{65,33},{97,65},{2,98}... | collective-permute-start | bytes 589832 | tf_op jit(solution)/shard_map/ppermute | solution.py:33
  86.0 3.7 %collective-permute-done.19 = bf16[4,192,128]{2,1,0:T(8,128)(2,1)S(1)} collective-permute-done((bf16[4,192,128]{2,1,0:T(8,128)(2,1)S(1)}, bf16[4,192,128]{2,1,0:T(8,128)(2,1)S(1)}, u32[]{:S(2)}, u32[]{:S(2)}) %collective-permute-start.19) | collective-permute-done | bytes 196640 | tf_op jit(solution)/shard_map/ppermute | solution.py:33
  98.0 7.7 %collective-permute-done.13 = bf16[512,128]{1,0:T(8,128)(2,1)S(1)} collective-permute-done((bf16[512,128]{1,0:T(8,128)(2,1)S(1)}, bf16[512,128]{1,0:T(8,128)(2,1)S(1)}, u32[]{:S(2)}, u32[]{:S(2)}) %collective-permute-start.13) | collective-permute-done | bytes 131104 | tf_op jit(solution)/shard_map/ppermute | solution.py:25
  109.0 2.3 convolution_convert_fusion.2
  113.9 7.9 %collective-permute-done.23 = bf16[512,128]{1,0:T(8,128)(2,1)S(1)} collective-permute-done((bf16[512,128]{1,0:T(8,128)(2,1)S(1)}, bf16[512,128]{1,0:T(8,128)(2,1)S(1)}, u32[]{:S(2)}, u32[]{:S(2)}) %collective-permute-start.23) | collective-permute-done | bytes 131104 | tf_op jit(solution)/shard_map/ppermute | solution.py:25
  127.7 5.5 %collective-permute-done.25 = bf16[512,128]{1,0:T(8,128)(2,1)S(1)} collective-permute-done((bf16[512,128]{1,0:T(8,128)(2,1)S(1)}, bf16[512,128]{1,0:T(8,128)(2,1)S(1)}, u32[]{:S(2)}, u32[]{:S(2)}) %collective-permute-start.25) | collective-permute-done | bytes 131104 | tf_op jit(solution)/shard_map/ppermute | solution.py:25
  146.0 3.1 %collective-permute-done.32 = bf16[1,256,128]{2,1,0:T(8,128)(2,1)S(1)} collective-permute-done((bf16[1,256,128]{2,1,0:T(8,128)(2,1)S(1)}, bf16[1,256,128]{2,1,0:T(8,128)(2,1)S(1)}, u32[]{:S(2)}, u32[]{:S(2)}) %collective-permute-start.32) | collective-permute-done | bytes 65568 | tf_op jit(solution)/shard_map/ppermute | solution.py:44
  154.1 2.7 %collective-permute-start.38 = (bf16[2,256,128]{2,1,0:T(8,128)(2,1)S(1)}, bf16[2,256,128]{2,1,0:T(8,128)(2,1)S(1)}, u32[]{:S(2)}, u32[]{:S(2)}) collective-permute-start(bf16[2,256,128]{2,1,0:T(8,128)(2,1)S(1)} %pad_maximum_fusion.18), channel_id=1, source_target_pairs={{0,24},{8,16},{16,8},{24,0},{1,25},{9,17},{17,9},{25,1},{2,26},{10... | collective-permute-start | bytes 393224 | tf_op jit(solution)/shard_map/ppermute | solution.py:44
  157.6 2.5 %collective-permute-done.29 = bf16[2,256,128]{2,1,0:T(8,128)(2,1)S(1)} collective-permute-done((bf16[2,256,128]{2,1,0:T(8,128)(2,1)S(1)}, bf16[2,256,128]{2,1,0:T(8,128)(2,1)S(1)}, u32[]{:S(2)}, u32[]{:S(2)}) %collective-permute-start.29) | collective-permute-done | bytes 131104 | tf_op jit(solution)/shard_map/ppermute | solution.py:44
  161.7 2.7 %collective-permute-start.43 = (bf16[4,256,128]{2,1,0:T(8,128)(2,1)S(1)}, bf16[4,256,128]{2,1,0:T(8,128)(2,1)S(1)}, u32[]{:S(2)}, u32[]{:S(2)}) collective-permute-start(bf16[4,256,128]{2,1,0:T(8,128)(2,1)S(1)} %pad_maximum_fusion.15), channel_id=1, source_target_pairs={{0,96},{32,64},{64,32},{96,0},{1,97},{33,65},{65,33},{97,1},{2,98}... | collective-permute-start | bytes 786440 | tf_op jit(solution)/shard_map/ppermute | solution.py:44
  164.7 9.0 %collective-permute-done.34 = bf16[4,256,128]{2,1,0:T(8,128)(2,1)S(1)} collective-permute-done((bf16[4,256,128]{2,1,0:T(8,128)(2,1)S(1)}, bf16[4,256,128]{2,1,0:T(8,128)(2,1)S(1)}, u32[]{:S(2)}, u32[]{:S(2)}) %collective-permute-start.34) | collective-permute-done | bytes 262176 | tf_op jit(solution)/shard_map/ppermute | solution.py:44
  173.9 3.3 %collective-permute-start.31 = (bf16[8,256,128]{2,1,0:T(8,128)(2,1)S(1)}, bf16[8,256,128]{2,1,0:T(8,128)(2,1)S(1)}, u32[]{:S(2)}, u32[]{:S(2)}) collective-permute-start(bf16[8,256,128]{2,1,0:T(8,128)(2,1)S(1)} %pad_maximum_fusion.7), channel_id=1, source_target_pairs={{0,24},{8,16},{16,8},{24,0},{1,25},{9,17},{17,9},{25,1},{2,26},{10... | collective-permute-start | bytes 1572872 | tf_op jit(solution)/shard_map/ppermute | solution.py:44
  179.4 8.5 %collective-permute-done.35 = bf16[8,256,128]{2,1,0:T(8,128)(2,1)S(1)} collective-permute-done((bf16[8,256,128]{2,1,0:T(8,128)(2,1)S(1)}, bf16[8,256,128]{2,1,0:T(8,128)(2,1)S(1)}, u32[]{:S(2)}, u32[]{:S(2)}) %collective-permute-start.35) | collective-permute-done | bytes 524320 | tf_op jit(solution)/shard_map/ppermute | solution.py:44
  190.7 5.9 %broadcast_select_fusion = bf16[2,512,4,512]{3,2,1,0:T(4,128)(2,1)} fusion(bf16[2,512,4,512]{3,2,1,0:T(4,128)(2,1)} %all-gather.4.cloned.1.call-done, pred[2,4]{1,0:T(4,128)(4,1)S(1)} %iota_compare_fusion), kind=kLoop, calls=%fused_computation | loop fusion | flops 2097152 | bytes 8388616 | tf_op jit(solution)/shard_map/jit(_where)/select_n | solution.py:184
  196.7 7.8 %reshape.217.factor_ref = bf16[2,512,2048]{2,1,0:T(8,128)(2,1)} reshape(bf16[2,512,4,512]{3,2,1,0:T(4,128)(2,1)} %broadcast_select_fusion) | data formatting | bytes 8388608 | tf_op jit(solution)/shard_map/reshape | solution.py:184
  205.7 16.9 %shard_map.37 = f32[2,512,2048]{2,1,0:T(8,128)} custom-call(s32[65]{0:T(128)S(1)} %pad_add_fusion.1.scalars, bf16[2,512,2048]{2,1,0:T(8,128)(2,1)} %reshape.217.factor_ref, f32[2,512,2048]{2,1,0:T(8,128)} %rhs_ref.1, bf16[16,1024,128]{2,1,0:T(8,128)(2,1)} %bitcast.125, bf16[16,256,128]{2,1,0:T(8,128)(2,1)S(1)} %constant_dynamic-update-slice_fusion.7.rest_0_.rest_1_, ...), custom_call_target="tpu_custom_call" | custom-call | tf_op jit(solution)/shard_map/pallas_call | solution.py:92
  (196 shorter events, 90.6 us)
Async XLA Ops:
  6.5 184.2 %all-gather.4.cloned.1.call-start = ((), (), s32[]{:S(2)}) async-start(), calls=%async_computation | async-start | bytes 6291456 | tf_op jit(solution)/shard_map/all_gather | solution.py:181
  12.4 28.5 %collective-permute-start = (bf16[608,512]{1,0:T(8,128)(2,1)}, bf16[608,512]{1,0:T(8,128)(2,1)}, u32[]{:S(2)}, u32[]{:S(2)}) collective-permute-start(bf16[608,512]{1,0:T(8,128)(2,1)} %pad_maximum_fusion.1), channel_id=1, source_target_pairs={{0,32},{2,34},{4,36},{6,38},{1,33},{3,35},{5,37},{7,39}} | collective-permute-start | bytes 1867784 | tf_op jit(solution)/shard_map/ppermute | solution.py:25
  17.7 24.6 %collective-permute-start.1 = (bf16[608,512]{1,0:T(8,128)(2,1)}, bf16[608,512]{1,0:T(8,128)(2,1)}, u32[]{:S(2)}, u32[]{:S(2)}) collective-permute-start(bf16[608,512]{1,0:T(8,128)(2,1)} %pad_maximum_fusion.2), channel_id=1, source_target_pairs={{0,96},{2,98},{4,100},{6,102},{1,97},{3,99},{5,101},{7,103}} | collective-permute-start | bytes 1867784 | tf_op jit(solution)/shard_map/ppermute | solution.py:25
  21.6 21.2 %collective-permute-start.2 = (bf16[608,512]{1,0:T(8,128)(2,1)}, bf16[608,512]{1,0:T(8,128)(2,1)}, u32[]{:S(2)}, u32[]{:S(2)}) collective-permute-start(bf16[608,512]{1,0:T(8,128)(2,1)} %pad_maximum_fusion.3), channel_id=1, source_target_pairs={{0,64},{2,66},{4,68},{6,70},{1,65},{3,67},{5,69},{7,71}} | collective-permute-start | bytes 1867784 | tf_op jit(solution)/shard_map/ppermute | solution.py:25
  31.1 16.3 %collective-permute-start.6 = (bf16[608,512]{1,0:T(8,128)(2,1)}, bf16[608,512]{1,0:T(8,128)(2,1)}, u32[]{:S(2)}, u32[]{:S(2)}) collective-permute-start(bf16[608,512]{1,0:T(8,128)(2,1)} %pad_maximum_fusion.4), channel_id=1, source_target_pairs={{0,8},{2,10},{4,12},{6,14},{1,9},{3,11},{5,13},{7,15}} | collective-permute-start | bytes 1867784 | tf_op jit(solution)/shard_map/ppermute | solution.py:25
  36.8 16.0 %collective-permute-start.7 = (bf16[608,512]{1,0:T(8,128)(2,1)}, bf16[608,512]{1,0:T(8,128)(2,1)S(1)}, u32[]{:S(2)}, u32[]{:S(2)}) collective-permute-start(bf16[608,512]{1,0:T(8,128)(2,1)} %pad_maximum_fusion.5), channel_id=1, source_target_pairs={{0,24},{2,26},{4,28},{6,30},{1,25},{3,27},{5,29},{7,31}} | collective-permute-start | bytes 1867784 | tf_op jit(solution)/shard_map/ppermute | solution.py:25
  40.9 19.4 %collective-permute-start.8 = (bf16[608,512]{1,0:T(8,128)(2,1)S(1)}, bf16[608,512]{1,0:T(8,128)(2,1)S(1)}, u32[]{:S(2)}, u32[]{:S(2)}) collective-permute-start(bf16[608,512]{1,0:T(8,128)(2,1)S(1)} %pad_maximum_fusion.6), channel_id=1, source_target_pairs={{0,16},{2,18},{4,20},{6,22},{1,17},{3,19},{5,21},{7,23}} | collective-permute-start | bytes 1867784 | tf_op jit(solution)/shard_map/ppermute | solution.py:25
  44.7 19.7 %collective-permute-start.3 = (bf16[608,128]{1,0:T(8,128)(2,1)S(1)}, bf16[608,128]{1,0:T(8,128)(2,1)S(1)}, u32[]{:S(2)}, u32[]{:S(2)}) collective-permute-start(bf16[608,128]{1,0:T(8,128)(2,1)S(1)} %get-tuple-element.44), channel_id=1, source_target_pairs={{0,8},{32,40},{64,72},{96,104},{2,10},{34,42},{66,74},{98,106},{4,... | collective-permute-start | bytes 466952 | tf_op jit(solution)/shard_map/ppermute | solution.py:25
  46.0 19.8 %collective-permute-start.5 = (bf16[608,128]{1,0:T(8,128)(2,1)S(1)}, bf16[608,128]{1,0:T(8,128)(2,1)S(1)}, u32[]{:S(2)}, u32[]{:S(2)}) collective-permute-start(bf16[608,128]{1,0:T(8,128)(2,1)S(1)} %get-tuple-element.45), channel_id=1, source_target_pairs={{0,16},{32,48},{64,80},{96,112},{2,18},{34,50},{66,82},{98,114},{4... | collective-permute-start | bytes 466952 | tf_op jit(solution)/shard_map/ppermute | solution.py:25
  47.3 18.5 %collective-permute-start.4 = (bf16[608,128]{1,0:T(8,128)(2,1)S(1)}, bf16[608,128]{1,0:T(8,128)(2,1)S(1)}, u32[]{:S(2)}, u32[]{:S(2)}) collective-permute-start(bf16[608,128]{1,0:T(8,128)(2,1)S(1)} %get-tuple-element.46), channel_id=1, source_target_pairs={{0,24},{32,56},{64,88},{96,120},{2,26},{34,58},{66,90},{98,122},{4... | collective-permute-start | bytes 466952 | tf_op jit(solution)/shard_map/ppermute | solution.py:25
  82.2 122.3 %all-gather.6.cloned.1.call-start = ((), (), s32[]{:S(2)}) async-start(), calls=%async_computation.1 | async-start | bytes 4456448 | tf_op jit(solution)/shard_map/all_gather | solution.py:168
  92.8 14.7 %collective-permute-start.21 = (bf16[3,512,256]{2,1,0:T(8,128)(2,1)S(1)}, bf16[3,512,256]{2,1,0:T(8,128)(2,1)}, u32[]{:S(2)}, u32[]{:S(2)}) collective-permute-start(bf16[3,512,256]{2,1,0:T(8,128)(2,1)S(1)} %copy.8), channel_id=1, source_target_pairs={{0,1},{1,0},{2,3},{3,2},{4,5},{5,4},{6,7},{7,6},{8,9},{9,8},{10,11... | collective-permute-start | bytes 2359304 | tf_op jit(solution)/shard_map/ppermute | solution.py:149
  95.8 9.9 %collective-permute-start.13 = (bf16[512,128]{1,0:T(8,128)(2,1)S(1)}, bf16[512,128]{1,0:T(8,128)(2,1)S(1)}, u32[]{:S(2)}, u32[]{:S(2)}) collective-permute-start(bf16[512,128]{1,0:T(8,128)(2,1)S(1)} %convolution_convert_fusion.3), channel_id=1, source_target_pairs={{0,6},{8,14},{16,22},{24,30},{32,38},{40,46},{48,54},{56,62},{64,7... | collective-permute-start | bytes 393224 | tf_op jit(solution)/shard_map/ppermute | solution.py:25
  111.9 9.9 %collective-permute-start.23 = (bf16[512,128]{1,0:T(8,128)(2,1)S(1)}, bf16[512,128]{1,0:T(8,128)(2,1)S(1)}, u32[]{:S(2)}, u32[]{:S(2)}) collective-permute-start(bf16[512,128]{1,0:T(8,128)(2,1)S(1)} %convolution_convert_fusion.2), channel_id=1, source_target_pairs={{2,6},{10,14},{18,22},{26,30},{34,38},{42,46},{50,54},{58,62},{66,... | collective-permute-start | bytes 393224 | tf_op jit(solution)/shard_map/ppermute | solution.py:25
  150.3 9.8 %collective-permute-start.29 = (bf16[2,256,128]{2,1,0:T(8,128)(2,1)S(1)}, bf16[2,256,128]{2,1,0:T(8,128)(2,1)S(1)}, u32[]{:S(2)}, u32[]{:S(2)}) collective-permute-start(bf16[2,256,128]{2,1,0:T(8,128)(2,1)S(1)} %pad_maximum_fusion.16), channel_id=1, source_target_pairs={{0,96},{32,64},{64,32},{96,0},{1,97},{33,65},{65,33},{97,1},{2,98}... | collective-permute-start | bytes 393224 | tf_op jit(solution)/shard_map/ppermute | solution.py:44
  154.1 10.4 %collective-permute-start.38 = (bf16[2,256,128]{2,1,0:T(8,128)(2,1)S(1)}, bf16[2,256,128]{2,1,0:T(8,128)(2,1)S(1)}, u32[]{:S(2)}, u32[]{:S(2)}) collective-permute-start(bf16[2,256,128]{2,1,0:T(8,128)(2,1)S(1)} %pad_maximum_fusion.18), channel_id=1, source_target_pairs={{0,24},{8,16},{16,8},{24,0},{1,25},{9,17},{17,9},{25,1},{2,26},{10... | collective-permute-start | bytes 393224 | tf_op jit(solution)/shard_map/ppermute | solution.py:44
  156.9 16.8 %collective-permute-start.34 = (bf16[4,256,128]{2,1,0:T(8,128)(2,1)S(1)}, bf16[4,256,128]{2,1,0:T(8,128)(2,1)S(1)}, u32[]{:S(2)}, u32[]{:S(2)}) collective-permute-start(bf16[4,256,128]{2,1,0:T(8,128)(2,1)S(1)} %pad_maximum_fusion.13), channel_id=1, source_target_pairs={{0,24},{8,16},{16,8},{24,0},{1,25},{9,17},{17,9},{25,1},{2,26},{10... | collective-permute-start | bytes 786440 | tf_op jit(solution)/shard_map/ppermute | solution.py:44
  160.1 13.7 %collective-permute-start.30 = (bf16[4,256,128]{2,1,0:T(8,128)(2,1)S(1)}, bf16[4,256,128]{2,1,0:T(8,128)(2,1)S(1)}, u32[]{:S(2)}, u32[]{:S(2)}) collective-permute-start(bf16[4,256,128]{2,1,0:T(8,128)(2,1)S(1)} %pad_maximum_fusion.12), channel_id=1, source_target_pairs={{0,8},{8,0},{16,24},{24,16},{1,9},{9,1},{17,25},{25,17},{2,10},{10... | collective-permute-start | bytes 786440 | tf_op jit(solution)/shard_map/ppermute | solution.py:44
  161.7 15.6 %collective-permute-start.43 = (bf16[4,256,128]{2,1,0:T(8,128)(2,1)S(1)}, bf16[4,256,128]{2,1,0:T(8,128)(2,1)S(1)}, u32[]{:S(2)}, u32[]{:S(2)}) collective-permute-start(bf16[4,256,128]{2,1,0:T(8,128)(2,1)S(1)} %pad_maximum_fusion.15), channel_id=1, source_target_pairs={{0,96},{32,64},{64,32},{96,0},{1,97},{33,65},{65,33},{97,1},{2,98}... | collective-permute-start | bytes 786440 | tf_op jit(solution)/shard_map/ppermute | solution.py:44
  164.5 12.9 %collective-permute-start.39 = (bf16[4,256,128]{2,1,0:T(8,128)(2,1)S(1)}, bf16[4,256,128]{2,1,0:T(8,128)(2,1)S(1)}, u32[]{:S(2)}, u32[]{:S(2)}) collective-permute-start(bf16[4,256,128]{2,1,0:T(8,128)(2,1)S(1)} %pad_maximum_fusion.14), channel_id=1, source_target_pairs={{0,32},{32,0},{64,96},{96,64},{1,33},{33,1},{65,97},{97,65},{2,34}... | collective-permute-start | bytes 786440 | tf_op jit(solution)/shard_map/ppermute | solution.py:44
  173.8 14.1 %collective-permute-start.35 = (bf16[8,256,128]{2,1,0:T(8,128)(2,1)S(1)}, bf16[8,256,128]{2,1,0:T(8,128)(2,1)S(1)}, u32[]{:S(2)}, u32[]{:S(2)}) collective-permute-start(bf16[8,256,128]{2,1,0:T(8,128)(2,1)S(1)} %pad_maximum_fusion.8), channel_id=1, source_target_pairs={{0,8},{8,0},{16,24},{24,16},{1,9},{9,1},{17,25},{25,17},{2,10},{10... | collective-permute-start | bytes 1572872 | tf_op jit(solution)/shard_map/ppermute | solution.py:44
  173.9 15.6 %collective-permute-start.31 = (bf16[8,256,128]{2,1,0:T(8,128)(2,1)S(1)}, bf16[8,256,128]{2,1,0:T(8,128)(2,1)S(1)}, u32[]{:S(2)}, u32[]{:S(2)}) collective-permute-start(bf16[8,256,128]{2,1,0:T(8,128)(2,1)S(1)} %pad_maximum_fusion.7), channel_id=1, source_target_pairs={{0,24},{8,16},{16,8},{24,0},{1,25},{9,17},{17,9},{25,1},{2,26},{10... | collective-permute-start | bytes 1572872 | tf_op jit(solution)/shard_map/ppermute | solution.py:44
  177.3 12.3 %collective-permute-start.44 = (bf16[8,256,128]{2,1,0:T(8,128)(2,1)S(1)}, bf16[8,256,128]{2,1,0:T(8,128)(2,1)S(1)}, u32[]{:S(2)}, u32[]{:S(2)}) collective-permute-start(bf16[8,256,128]{2,1,0:T(8,128)(2,1)S(1)} %pad_maximum_fusion.10), channel_id=1, source_target_pairs={{0,32},{32,0},{64,96},{96,64},{1,33},{33,1},{65,97},{97,65},{2,34}... | collective-permute-start | bytes 1572872 | tf_op jit(solution)/shard_map/ppermute | solution.py:44
  177.5 13.1 %collective-permute-start.40 = (bf16[8,256,128]{2,1,0:T(8,128)(2,1)S(1)}, bf16[8,256,128]{2,1,0:T(8,128)(2,1)S(1)}, u32[]{:S(2)}, u32[]{:S(2)}) collective-permute-start(bf16[8,256,128]{2,1,0:T(8,128)(2,1)S(1)} %pad_maximum_fusion.9), channel_id=1, source_target_pairs={{0,96},{32,64},{64,32},{96,0},{1,97},{33,65},{65,33},{97,1},{2,98}... | collective-permute-start | bytes 1572872 | tf_op jit(solution)/shard_map/ppermute | solution.py:44
  (31 other events, 181.2 us)
Sparse Core Ops, SparseCore 0:
  82.3 12.3 all-gather.3
  122.7 59.8 all-gather.5

commit v5 on v4

--- a/solution.py
+++ b/solution.py
@@ -44,12 +44,14 @@
     return lax.ppermute(value, axis, [(i, i ^ flip) for i in range(4)])
 
 
-def spread(parts):
+def spread(parts, whole):
     parts = [p[None] for p in parts]
     for step in range(4):
         got = [swap(p, *order[step]) for p, order in zip(parts, ORDERS)]
+        if step == 3:
+            whole, *got = lax.optimization_barrier((whole, *got))
         parts = [jnp.concatenate([p, g], axis=0) for p, g in zip(parts, got)]
-    return parts
+    return parts, whole
 
 
 def places(y, z):
@@ -65,6 +67,79 @@
             total = total + (bit << step)
         tables.append(total)
     return jnp.stack(tables).reshape(-1)
+
+
+def split(value):
+    high = value.astype(BF)
+    return high, (value - high.astype(F32)).astype(BF)
+
+
+def put_piece(factor_ref, base, out_ref):
+    for u in range(12):
+        rows = slice(base + u % 2 * 32, base + u % 2 * 32 + 32)
+        at = 512 + u % 3 * 32
+        out_ref[at:at + 32, u // 3 * 128:(u // 3 + 1) * 128] = factor_ref[rows, u // 2 * 128:(u // 2 + 1) * 128]
+
+
+def load_a_kernel(rhs_ref, factor_ref, *outs):
+    for d in range(4):
+        outs[d][:512] = rhs_ref[0, :, d * 512:(d + 1) * 512].astype(BF)
+        put_piece(factor_ref, d * 64, outs[d])
+
+
+def load_b_kernel(rhs_ref, factor_ref, *outs):
+    for d in range(4):
+        for j in range(4):
+            at = j * 512 + d * 128
+            outs[d][:512, j * 128:(j + 1) * 128] = split(rhs_ref[0, :, at:at + 128])[1]
+        put_piece(factor_ref, 256 + d * 64, outs[d])
+
+
+def loads(kernel, rhs, factor):
+    return pl.pallas_call(
+        kernel,
+        grid=(1,),
+        in_specs=[pl.BlockSpec((1, 512, 2048), lambda i: (0, 0, 0)), pl.BlockSpec((512, 1024), lambda i: (0, 0))],
+        out_specs=[pl.BlockSpec((608, 512), lambda i: (0, 0))] * 4,
+        out_shape=[jax.ShapeDtypeStruct((608, 512), BF)] * 4,
+        compiler_params=pltpu.CompilerParams(vmem_limit_bytes=40 << 20),
+    )(rhs, factor)
+
+
+def step_kernel(first, scalars, state_ref, high_ref, low_ref, *refs):
+    dot = lambda a, b: jnp.dot(a, b, preferred_element_type=F32)
+    state = state_ref[...]
+    if first:
+        sent_ref, = refs
+    else:
+        mine_ref, other_ref, got_ref, next_ref, sent_ref = refs
+        swap = scalars[0] == 1
+        left = jnp.where(swap, other_ref[0], mine_ref[0])
+        right = jnp.where(swap, mine_ref[0], other_ref[0])
+        state = state - dot(left, got_ref[:256]) - dot(right, got_ref[256:])
+        next_ref[...] = state
+    high, low = split(state)
+    sent_ref[...] = (dot(high_ref[...], high) + dot(high_ref[...], low) + dot(low_ref[...], high)).astype(BF)
+
+
+def step(core, state, inverse, mine=None, other=None, panel=0, got=None):
+    first = got is None
+    full = lambda shape: pl.BlockSpec(shape, lambda i, s: (0, 0))
+    part = pl.BlockSpec((1, 512, 256), lambda i, s: (panel, 0, 0))
+    tall, square = full((512, 128)), full((512, 512))
+    sent = jax.ShapeDtypeStruct((512, 128), BF)
+    new = jax.ShapeDtypeStruct((512, 128), F32)
+    return pl.pallas_call(
+        lambda *refs: step_kernel(first, *refs),
+        grid_spec=pltpu.PrefetchScalarGridSpec(
+            num_scalar_prefetch=1,
+            grid=(1,),
+            in_specs=[tall, square, square] + ([] if first else [part, part, tall]),
+            out_specs=tall if first else [tall, tall],
+        ),
+        out_shape=sent if first else [new, sent],
+        compiler_params=pltpu.CompilerParams(vmem_limit_bytes=32 << 20),
+    )(core[None], state, *inverse, *([] if first else [mine, other, got]))
 
 
 def update_kernel(scalars, factor_ref, rhs_ref, early_ref, *rest):
@@ -114,74 +189,69 @@
     owner = place < 4
     zero = jnp.zeros((), BF)
 
-    def high(slab):
-        return lax.reduce_precision(slab, 8, 7).astype(BF)
-
-    def low(slab):
-        return (slab - lax.reduce_precision(slab, 8, 7)).astype(BF)
-
-    shards = factor[0, :, :3].reshape(768, 512)
-
-    def load_a(d):
-        return jnp.concatenate([high(rhs[0, :, d * 512:(d + 1) * 512]), shards[d * 96:(d + 1) * 96]], axis=0)
-
-    def load_b(d):
-        slab = jnp.concatenate([rhs[0, :, j * 512 + d * 128:j * 512 + (d + 1) * 128] for j in range(4)], axis=1)
-        return jnp.concatenate([low(slab), shards[384 + d * 96:384 + (d + 1) * 96]], axis=0)
-
-    hold_a = jnp.where(owner, load_a(0), zero)
-    hold_b = jnp.where(owner, load_b(0), zero)
-    for d in (1, 3, 2):
-        hold_a = hold_a + permute(load_a(d), [((i, 0, 0), (i, d, 0)) for i in range(4)])
-        hold_b = hold_b + permute(load_b(d), [((i, 0, 0), (i, 0, d)) for i in range(4)])
-    mine_a = jnp.where(z == 0, hold_a[:, :128], zero)
-    mine_b = jnp.where(y == 0, hold_b[:, :128], zero)
-    for d in (1, 3, 2):
-        cut = slice(d * 128, (d + 1) * 128)
-        mine_a = mine_a + permute(hold_a[:, cut], [((i, j, 0), (i, j, d)) for i in range(4) for j in range(4)])
-        mine_b = mine_b + permute(hold_b[:, cut], [((i, 0, j), (i, d, j)) for i in range(4) for j in range(4)])
-
-    shard = jnp.concatenate([mine_a[512:], mine_b[512:]], axis=0)
-    every = ring_gather(ring_gather(shard, "z"), "y")
-    top = every[:, :, :96].transpose(0, 2, 1, 3).reshape(384, 512)
-    low_part = every[:, :, 96:].transpose(1, 2, 0, 3).reshape(384, 512)
-    half = jnp.concatenate([top, low_part], axis=0).reshape(512, 3, 256).transpose(1, 0, 2)
+    tile = factor[0].reshape(512, 1024)
+    load_a = loads(load_a_kernel, rhs, tile)
+    load_b = loads(load_b_kernel, rhs, tile)
+
+    def stage(bundles, axis):
+        hold = jnp.where(owner, bundles[0], zero)
+        for d in (1, 3, 2):
+            end = lambda i: (i, d, 0) if axis == "y" else (i, 0, d)
+            hold = hold + permute(bundles[d], [((i, 0, 0), end(i)) for i in range(4)])
+        return hold
+
+    def finish(hold, axis):
+        tail = [hold[512:, k * 128:(k + 1) * 128] for k in range(4)]
+        message = lambda d: jnp.concatenate([hold[:512, d * 128:(d + 1) * 128]] + tail, axis=0)
+        mine = jnp.where((z if axis == "y" else y) == 0, message(0), zero)
+        for d in (1, 3, 2):
+            if axis == "y":
+                moves = [((i, j, 0), (i, j, d)) for i in range(4) for j in range(4)]
+            else:
+                moves = [((i, 0, j), (i, d, j)) for i in range(4) for j in range(4)]
+            mine = mine + permute(message(d), moves)
+        return mine
+
+    whole = lax.all_gather(factor, "rhs", axis=3, tiled=True)
+    tiles = jnp.arange(2, dtype=jnp.int32) * 64 + place
+    keep = tiles[:, None] > jnp.arange(4, dtype=jnp.int32)[None]
+    whole = jnp.where(keep[:, None, :, None], whole, zero).reshape(2, 512, 2048)
+
+    hold_a = stage(load_a, "y")
+    hold_b = stage(load_b, "z")
+    mine_a = finish(hold_a, "y")
+    mine_b = finish(hold_b, "z")
+
+    top = ring_gather(mine_a[512:], "y")
+    bottom = ring_gather(mine_b[512:], "z")
+    half = jnp.concatenate([top, bottom], axis=0).reshape(8, 3, 2, 64, 128).transpose(1, 0, 3, 2, 4).reshape(3, 512, 256)
     other = lax.ppermute(half, "rhs", [(0, 1), (1, 0)])
 
-    def reduce(state, panel, got):
-        mine = lax.dynamic_slice_in_dim(got, core * 256, 256, 0)
-        rest = lax.dynamic_slice_in_dim(got, 256 - core * 256, 256, 0)
-        dot = lambda a, b: jnp.dot(a, b, preferred_element_type=F32)
-        return state - dot(half[panel], mine) - dot(other[panel], rest)
-
     inverse = lax.dynamic_index_in_dim(inverses, x, 0, keepdims=False)
-    solve = lambda s: jnp.dot(inverse, s, precision=lax.Precision.HIGHEST).astype(BF)
+    rounded = lax.reduce_precision(inverse, 8, 7)
+    inverse = (rounded.astype(BF), (inverse - rounded).astype(BF))
+    core = core.astype(jnp.int32)
     state = mine_a[:512].astype(F32) + mine_b[:512].astype(F32)
-
-    sent = solve(state)
+    state, *inverse = lax.optimization_barrier((state, *inverse))
+    advance = lambda state, panel, got: step(core, state, inverse, half, other, panel, got)
+
+    sent = step(core, state, inverse)
     got = hop(sent, (0, 1)) + hop(sent, (0, 3)) + hop(sent, (0, 2))
     panel_0 = jnp.where(x == 0, sent, got)
-    state = reduce(state, 0, got)
-    sent = solve(state)
+    state, sent = advance(state, 0, got)
     got = hop(sent, (1, 2)) + hop(sent, (1, 3))
     panel_1 = jnp.where(x == 1, sent, got + hop(sent, (1, 0)))
     early = lax.all_gather(jnp.concatenate([panel_0, panel_1], axis=0), ("y", "z"), axis=0)
-    state = reduce(state, 1, got)
-    sent = solve(state)
+    state, sent = advance(state, 1, got)
     got = hop(sent, (2, 3))
-    state = reduce(state, 2, got)
-    sent = solve(state)
+    state, sent = advance(state, 2, got)
     back = hop(sent, (2, 1), (3, 2))
     far = hop(sent, (2, 0), (3, 1))
     wrap = hop(sent, (3, 0))
     panel_2 = jnp.where(x == 2, sent, jnp.where(x == 3, got, jnp.where(x == 1, back, far)))
     panel_3 = jnp.where(x == 3, sent, jnp.where(x == 2, back, jnp.where(x == 1, far, wrap)))
-    late = spread([panel_2[:256], panel_2[256:], panel_3[:256], panel_3[256:]])
-
-    whole = lax.all_gather(factor, "rhs", axis=3, tiled=True)
-    tiles = jnp.arange(2, dtype=jnp.int32) * 64 + place
-    keep = tiles[:, None] > jnp.arange(4, dtype=jnp.int32)[None]
-    whole = jnp.where(keep[:, None, :, None], whole, zero).reshape(2, 512, 2048)
+    late, whole = spread([panel_2[:256], panel_2[256:], panel_3[:256], panel_3[256:]], whole)
+
     scalars = jnp.concatenate([places(y, z), place[None]]).astype(jnp.int32)
     return update(scalars, whole, rhs, early, late)
 

time: 232 us -> 216 us (0.931)
  the two profiles are of different devices: /device:TPU:6 before, /device:TPU:2 now
where the time goes in v5:
time: 216 us; the launch traced here: 215 us
  waiting for transfers between devices  73.3 us (34%)
  starting transfers between devices  62.4 us (29%)
  local copies, waits for them, and re-layouts  24.6 us (11%)
  Pallas kernels  23.2 us (11%)
  other arithmetic  17.1 us (8%)
  between operations  14.2 us (7%)
    ppermute x22, waiting for transfers between devices, permute(): return lax.ppermute(value, ROWS, [(flat(*a), flat(*b)) for a, b in moves])  52.8 us
    ppermute x22, starting transfers between devices, permute(): return lax.ppermute(value, ROWS, [(flat(*a), flat(*b)) for a, b in moves])  39.6 us
    ppermute x16, starting transfers between devices, swap(): return lax.ppermute(value, axis, [(i, i ^ flip) for i in range(4)])  18.2 us
    pallas_call x1, Pallas kernels, update(): pl.pallas_call(update_kernel, grid_spec=pltpu.PrefetchScalarGridSpec(num_...  17.3 us
    ppermute x16, waiting for transfers between devices, swap(): return lax.ppermute(value, axis, [(i, i ^ flip) for i in range(4)])  15.6 us
    unnamed x39, local copies, waits for them, and re-layouts  8.3 us
    reshape x1, local copies, waits for them, and re-layouts, local(): whole = jnp.where(keep[:, None, :, None], whole, zero).reshape(2, 512, 2048)  7.79 us
    select_n x1, other arithmetic, local(): whole = jnp.where(keep[:, None, :, None], whole, zero).reshape(2, 512, 2048)  5.92 us
  transfers between devices with their start and end apart: 47, of which 20 were waited for; matrix products, arithmetic and copies ran while one was open for 16% of the time, Pallas kernels for 2%

profile of v5, /device:TPU:2, one launch (start us, length us, event | category | flops | bytes accessed | tf_op | source)
XLA Modules:
  0.0 214.8 jit_solution(3675854370323802354)
XLA Ops:
  8.4 3.4 %copy-done = f32[2,512,2048]{2,1,0:T(8,128)S(1)} copy-done((f32[2,512,2048]{2,1,0:T(8,128)S(1)}, f32[2,512,2048]{2,1,0:T(8,128)}, u32[]{:S(2)}) %copy-start) | copy-done | bytes 8388632
  12.4 3.9 %collective-permute-start.6 = (bf16[608,512]{1,0:T(8,128)(2,1)S(1)}, bf16[608,512]{1,0:T(8,128)(2,1)S(1)}, u32[]{:S(2)}, u32[]{:S(2)}) collective-permute-start(bf16[608,512]{1,0:T(8,128)(2,1)S(1)} %get-tuple-element.31), channel_id=1, source_target_pairs={{0,8},{2,10},{4,12},{6,14},{1,9},{3,11},{5,13},{7,15}} | collective-permute-start | bytes 1867784 | tf_op jit(solution)/shard_map/ppermute | solution.py:25
  16.2 3.6 %collective-permute-start.7 = (bf16[608,512]{1,0:T(8,128)(2,1)S(1)}, bf16[608,512]{1,0:T(8,128)(2,1)}, u32[]{:S(2)}, u32[]{:S(2)}) collective-permute-start(bf16[608,512]{1,0:T(8,128)(2,1)S(1)} %get-tuple-element.32), channel_id=1, source_target_pairs={{0,24},{2,26},{4,28},{6,30},{1,25},{3,27},{5,29},{7,31}} | collective-permute-start | bytes 1867784 | tf_op jit(solution)/shard_map/ppermute | solution.py:25
  19.8 2.1 collective-permute-start.8
  23.4 2.2 %collective-permute-start = (bf16[608,512]{1,0:T(8,128)(2,1)}, bf16[608,512]{1,0:T(8,128)(2,1)}, u32[]{:S(2)}, u32[]{:S(2)}) collective-permute-start(bf16[608,512]{1,0:T(8,128)(2,1)} %get-tuple-element.27), channel_id=1, source_target_pairs={{0,32},{2,34},{4,36},{6,38},{1,33},{3,35},{5,37},{7,39}} | collective-permute-start | bytes 1867784 | tf_op jit(solution)/shard_map/ppermute | solution.py:25
  27.7 2.9 %collective-permute-done.6 = bf16[608,512]{1,0:T(8,128)(2,1)S(1)} collective-permute-done((bf16[608,512]{1,0:T(8,128)(2,1)S(1)}, bf16[608,512]{1,0:T(8,128)(2,1)S(1)}, u32[]{:S(2)}, u32[]{:S(2)}) %collective-permute-start.6) | collective-permute-done | bytes 622624 | tf_op jit(solution)/shard_map/ppermute | solution.py:25
  31.4 2.1 collective-permute-start.2
  33.7 9.1 %collective-permute-done.8 = bf16[608,512]{1,0:T(8,128)(2,1)} collective-permute-done((bf16[608,512]{1,0:T(8,128)(2,1)S(1)}, bf16[608,512]{1,0:T(8,128)(2,1)}, u32[]{:S(2)}, u32[]{:S(2)}) %collective-permute-start.8) | collective-permute-done | bytes 622624 | tf_op jit(solution)/shard_map/ppermute | solution.py:25
  42.8 8.7 %collective-permute-done.2 = bf16[608,512]{1,0:T(8,128)(2,1)} collective-permute-done((bf16[608,512]{1,0:T(8,128)(2,1)S(1)}, bf16[608,512]{1,0:T(8,128)(2,1)}, u32[]{:S(2)}, u32[]{:S(2)}) %collective-permute-start.2) | collective-permute-done | bytes 622624 | tf_op jit(solution)/shard_map/ppermute | solution.py:25
  51.5 2.2 %add_add_fusion = (bf16[608,512]{1,0:T(8,128)(2,1)S(1)}, bf16[608,512]{1,0:T(8,128)(2,1)S(1)}) fusion(bf16[608,512]{1,0:T(8,128)(2,1)} %collective-permute-done.8, bf16[608,512]{1,0:T(8,128)(2,1)} %collective-permute-done.7, bf16[608,512]{1,0:T(8,128)(2,1)} %copy-done.1, bf16[608,512]{1,0:T(8,128)(2,1)S(1)} %get-tuple-element.30, pred[]{:T(512)S(6)} %lt.36, ...), kind=kLoop, calls=%fused_computation.6 | loop fusion | flops 2490368 | bytes 6225921 | tf_op jit(solution)/shard_map/add | solution.py:200
  55.3 5.4 %collective-permute-start.11 = (bf16[896,128]{1,0:T(8,128)(2,1)S(1)}, bf16[896,128]{1,0:T(8,128)(2,1)S(1)}, u32[]{:S(2)}, u32[]{:S(2)}) collective-permute-start(bf16[896,128]{1,0:T(8,128)(2,1)S(1)} %get-tuple-element.86), channel_id=1, source_target_pairs={{0,64},{8,72},{16,80},{24,88},{2,66},{10,74},{18,82},{26,90},{4,68... | collective-permute-start | bytes 688136 | tf_op jit(solution)/shard_map/ppermute | solution.py:25
  66.7 2.8 %collective-permute-done.9 = bf16[896,128]{1,0:T(8,128)(2,1)S(1)} collective-permute-done((bf16[896,128]{1,0:T(8,128)(2,1)S(1)}, bf16[896,128]{1,0:T(8,128)(2,1)S(1)}, u32[]{:S(2)}, u32[]{:S(2)}) %collective-permute-start.9) | collective-permute-done | bytes 229408 | tf_op jit(solution)/shard_map/ppermute | solution.py:25
  72.0 3.8 %collective-permute-done.3 = bf16[896,128]{1,0:T(8,128)(2,1)S(1)} collective-permute-done((bf16[896,128]{1,0:T(8,128)(2,1)S(1)}, bf16[896,128]{1,0:T(8,128)(2,1)S(1)}, u32[]{:S(2)}, u32[]{:S(2)}) %collective-permute-start.3) | collective-permute-done | bytes 229408 | tf_op jit(solution)/shard_map/ppermute | solution.py:25
  78.4 2.4 %collective-permute-done.12 = bf16[384,128]{1,0:T(8,128)(2,1)S(1)} collective-permute-done((bf16[384,128]{1,0:T(8,128)(2,1)S(1)}, bf16[384,128]{1,0:T(8,128)(2,1)S(1)}, u32[]{:S(2)}, u32[]{:S(2)}) %collective-permute-start.12) | collective-permute-done | bytes 98336 | tf_op jit(solution)/shard_map/ppermute | solution.py:33
  89.6 9.4 %collective-permute-done.19 = bf16[512,128]{1,0:T(8,128)(2,1)S(1)} collective-permute-done((bf16[512,128]{1,0:T(8,128)(2,1)S(1)}, bf16[512,128]{1,0:T(8,128)(2,1)S(1)}, u32[]{:S(2)}, u32[]{:S(2)}) %collective-permute-start.19) | collective-permute-done | bytes 131104 | tf_op jit(solution)/shard_map/ppermute | solution.py:25
  117.7 12.4 %collective-permute-done.26 = bf16[512,128]{1,0:T(8,128)(2,1)S(1)} collective-permute-done((bf16[512,128]{1,0:T(8,128)(2,1)S(1)}, bf16[512,128]{1,0:T(8,128)(2,1)S(1)}, u32[]{:S(2)}, u32[]{:S(2)}) %collective-permute-start.26) | collective-permute-done | bytes 131104 | tf_op jit(solution)/shard_map/ppermute | solution.py:25
  138.2 2.1 collective-permute-done.27
  140.4 2.7 %collective-permute-start.28 = (bf16[2,256,128]{2,1,0:T(8,128)(2,1)S(1)}, bf16[2,256,128]{2,1,0:T(8,128)(2,1)S(1)}, u32[]{:S(2)}, u32[]{:S(2)}) collective-permute-start(bf16[2,256,128]{2,1,0:T(8,128)(2,1)S(1)} %pad_maximum_fusion.10), channel_id=1, source_target_pairs={{0,96},{32,64},{64,32},{96,0},{1,97},{33,65},{65,33},{97,1},{2,98}... | collective-permute-start | bytes 393224 | tf_op jit(solution)/shard_map/ppermute | solution.py:44
  149.7 2.2 %collective-permute-done.41 = bf16[2,256,128]{2,1,0:T(8,128)(2,1)S(1)} collective-permute-done((bf16[2,256,128]{2,1,0:T(8,128)(2,1)S(1)}, bf16[2,256,128]{2,1,0:T(8,128)(2,1)S(1)}, u32[]{:S(2)}, u32[]{:S(2)}) %collective-permute-start.41) | collective-permute-done | bytes 131104 | tf_op jit(solution)/shard_map/ppermute | solution.py:44
  154.4 7.7 %collective-permute-done.33 = bf16[4,256,128]{2,1,0:T(8,128)(2,1)S(1)} collective-permute-done((bf16[4,256,128]{2,1,0:T(8,128)(2,1)S(1)}, bf16[4,256,128]{2,1,0:T(8,128)(2,1)S(1)}, u32[]{:S(2)}, u32[]{:S(2)}) %collective-permute-start.33) | collective-permute-done | bytes 262176 | tf_op jit(solution)/shard_map/ppermute | solution.py:44
  168.2 2.5 %collective-permute-start.39 = (bf16[8,256,128]{2,1,0:T(8,128)(2,1)}, bf16[8,256,128]{2,1,0:T(8,128)(2,1)}, u32[]{:S(2)}, u32[]{:S(2)}) collective-permute-start(bf16[8,256,128]{2,1,0:T(8,128)(2,1)} %pad_maximum_fusion.3), channel_id=1, source_target_pairs={{0,96},{32,64},{64,32},{96,0},{1,97},{33,65},{65,33},{97,1},{2,98}... | collective-permute-start | bytes 1572872 | tf_op jit(solution)/shard_map/ppermute | solution.py:44
  171.6 5.9 %broadcast_select_fusion = bf16[2,512,4,512]{3,2,1,0:T(4,128)(2,1)} fusion(bf16[2,512,4,512]{3,2,1,0:T(4,128)(2,1)} %all-gather.4.cloned.1.call-done, pred[2,4]{1,0:T(4,128)(4,1)S(1)} %iota_compare_fusion), kind=kLoop, calls=%fused_computation | loop fusion | flops 2097152 | bytes 8388616 | tf_op jit(solution)/shard_map/jit(_where)/select_n | solution.py:218
  177.6 7.8 %reshape.198.factor_ref = bf16[2,512,2048]{2,1,0:T(8,128)(2,1)} reshape(bf16[2,512,4,512]{3,2,1,0:T(4,128)(2,1)} %broadcast_select_fusion) | data formatting | bytes 8388608 | tf_op jit(solution)/shard_map/reshape | solution.py:218
  190.6 17.3 %shard_map.43 = f32[2,512,2048]{2,1,0:T(8,128)} custom-call(s32[65]{0:T(128)S(1)} %pad_add_fusion.1.scalars, bf16[2,512,2048]{2,1,0:T(8,128)(2,1)} %reshape.198.factor_ref, f32[2,512,2048]{2,1,0:T(8,128)} %rhs_ref.5, bf16[16,1024,128]{2,1,0:T(8,128)(2,1)} %bitcast.53, bf16[16,256,128]{2,1,0:T(8,128)(2,1)S(1)} %constant_dynamic-update-slice_fusion.44.rest_0_.rest_1_, ...), custom_call_target="tpu_custom_call" | custom-call | tf_op jit(solution)/shard_map/pallas_call | solution.py:167
  (172 shorter events, 75.8 us)
Async XLA Ops:
  6.5 165.1 %all-gather.4.cloned.1.call-start = ((), (), s32[]{:S(2)}) async-start(), calls=%async_computation | async-start | bytes 6291456 | tf_op jit(solution)/shard_map/all_gather | solution.py:215
  12.4 18.2 %collective-permute-start.6 = (bf16[608,512]{1,0:T(8,128)(2,1)S(1)}, bf16[608,512]{1,0:T(8,128)(2,1)S(1)}, u32[]{:S(2)}, u32[]{:S(2)}) collective-permute-start(bf16[608,512]{1,0:T(8,128)(2,1)S(1)} %get-tuple-element.31), channel_id=1, source_target_pairs={{0,8},{2,10},{4,12},{6,14},{1,9},{3,11},{5,13},{7,15}} | collective-permute-start | bytes 1867784 | tf_op jit(solution)/shard_map/ppermute | solution.py:25
  16.2 17.5 %collective-permute-start.7 = (bf16[608,512]{1,0:T(8,128)(2,1)S(1)}, bf16[608,512]{1,0:T(8,128)(2,1)}, u32[]{:S(2)}, u32[]{:S(2)}) collective-permute-start(bf16[608,512]{1,0:T(8,128)(2,1)S(1)} %get-tuple-element.32), channel_id=1, source_target_pairs={{0,24},{2,26},{4,28},{6,30},{1,25},{3,27},{5,29},{7,31}} | collective-permute-start | bytes 1867784 | tf_op jit(solution)/shard_map/ppermute | solution.py:25
  19.8 23.0 %collective-permute-start.8 = (bf16[608,512]{1,0:T(8,128)(2,1)S(1)}, bf16[608,512]{1,0:T(8,128)(2,1)}, u32[]{:S(2)}, u32[]{:S(2)}) collective-permute-start(bf16[608,512]{1,0:T(8,128)(2,1)S(1)} %get-tuple-element.33), channel_id=1, source_target_pairs={{0,16},{2,18},{4,20},{6,22},{1,17},{3,19},{5,21},{7,23}} | collective-permute-start | bytes 1867784 | tf_op jit(solution)/shard_map/ppermute | solution.py:25
  23.4 19.4 %collective-permute-start = (bf16[608,512]{1,0:T(8,128)(2,1)}, bf16[608,512]{1,0:T(8,128)(2,1)}, u32[]{:S(2)}, u32[]{:S(2)}) collective-permute-start(bf16[608,512]{1,0:T(8,128)(2,1)} %get-tuple-element.27), channel_id=1, source_target_pairs={{0,32},{2,34},{4,36},{6,38},{1,33},{3,35},{5,37},{7,39}} | collective-permute-start | bytes 1867784 | tf_op jit(solution)/shard_map/ppermute | solution.py:25
  25.6 17.2 %collective-permute-start.1 = (bf16[608,512]{1,0:T(8,128)(2,1)}, bf16[608,512]{1,0:T(8,128)(2,1)}, u32[]{:S(2)}, u32[]{:S(2)}) collective-permute-start(bf16[608,512]{1,0:T(8,128)(2,1)} %get-tuple-element.28), channel_id=1, source_target_pairs={{0,96},{2,98},{4,100},{6,102},{1,97},{3,99},{5,101},{7,103}} | collective-permute-start | bytes 1867784 | tf_op jit(solution)/shard_map/ppermute | solution.py:25
  31.4 20.1 %collective-permute-start.2 = (bf16[608,512]{1,0:T(8,128)(2,1)S(1)}, bf16[608,512]{1,0:T(8,128)(2,1)}, u32[]{:S(2)}, u32[]{:S(2)}) collective-permute-start(bf16[608,512]{1,0:T(8,128)(2,1)S(1)} %get-tuple-element.29), channel_id=1, source_target_pairs={{0,64},{2,66},{4,68},{6,70},{1,65},{3,67},{5,69},{7,71}} | collective-permute-start | bytes 1867784 | tf_op jit(solution)/shard_map/ppermute | solution.py:25
  33.6 157.0 %all-gather.6.cloned.1.call-start = ((), (), s32[]{:S(2)}) async-start(), calls=%async_computation.1 | async-start | bytes 4456448 | tf_op jit(solution)/shard_map/all_gather | solution.py:244
  53.9 10.9 %collective-permute-start.10 = (bf16[896,128]{1,0:T(8,128)(2,1)S(1)}, bf16[896,128]{1,0:T(8,128)(2,1)S(1)}, u32[]{:S(2)}, u32[]{:S(2)}) collective-permute-start(bf16[896,128]{1,0:T(8,128)(2,1)S(1)} %get-tuple-element.85), channel_id=1, source_target_pairs={{0,96},{8,104},{16,112},{24,120},{2,98},{10,106},{18,114},{26,122}... | collective-permute-start | bytes 688136 | tf_op jit(solution)/shard_map/ppermute | solution.py:25
  55.3 11.4 %collective-permute-start.11 = (bf16[896,128]{1,0:T(8,128)(2,1)S(1)}, bf16[896,128]{1,0:T(8,128)(2,1)S(1)}, u32[]{:S(2)}, u32[]{:S(2)}) collective-permute-start(bf16[896,128]{1,0:T(8,128)(2,1)S(1)} %get-tuple-element.86), channel_id=1, source_target_pairs={{0,64},{8,72},{16,80},{24,88},{2,66},{10,74},{18,82},{26,90},{4,68... | collective-permute-start | bytes 688136 | tf_op jit(solution)/shard_map/ppermute | solution.py:25
  64.8 10.9 %collective-permute-start.3 = (bf16[896,128]{1,0:T(8,128)(2,1)S(1)}, bf16[896,128]{1,0:T(8,128)(2,1)S(1)}, u32[]{:S(2)}, u32[]{:S(2)}) collective-permute-start(bf16[896,128]{1,0:T(8,128)(2,1)S(1)} %get-tuple-element.59), channel_id=1, source_target_pairs={{0,8},{32,40},{64,72},{96,104},{2,10},{34,42},{66,74},{98,106},{4,... | collective-permute-start | bytes 688136 | tf_op jit(solution)/shard_map/ppermute | solution.py:25
  84.8 14.9 %collective-permute-start.18 = (bf16[3,512,256]{2,1,0:T(8,128)(2,1)S(1)}, bf16[3,512,256]{2,1,0:T(8,128)(2,1)S(1)}, u32[]{:S(2)}, u32[]{:S(2)}) collective-permute-start(bf16[3,512,256]{2,1,0:T(8,128)(2,1)S(1)} %reshape.200.refs_4_), channel_id=1, source_target_pairs={{0,1},{1,0},{2,3},{3,2},{4,5},{5,4},{6,7},{7,6},{8,9},{9,8},{10,11... | collective-permute-start | bytes 2359304 | tf_op jit(solution)/shard_map/ppermute | solution.py:228
  88.3 10.8 %collective-permute-start.19 = (bf16[512,128]{1,0:T(8,128)(2,1)S(1)}, bf16[512,128]{1,0:T(8,128)(2,1)S(1)}, u32[]{:S(2)}, u32[]{:S(2)}) collective-permute-start(bf16[512,128]{1,0:T(8,128)(2,1)S(1)} %shard_map.39), channel_id=1, source_target_pairs={{0,2},{8,10},{16,18},{24,26},{32,34},{40,42},{48,50},{56,58},{64,6... | collective-permute-start | bytes 393224 | tf_op jit(solution)/shard_map/ppermute | solution.py:25
  115.0 15.2 %collective-permute-start.26 = (bf16[512,128]{1,0:T(8,128)(2,1)S(1)}, bf16[512,128]{1,0:T(8,128)(2,1)S(1)}, u32[]{:S(2)}, u32[]{:S(2)}) collective-permute-start(bf16[512,128]{1,0:T(8,128)(2,1)S(1)} %get-tuple-element.41), channel_id=1, source_target_pairs={{4,0},{12,8},{20,16},{28,24},{36,32},{44,40},{52,48},{60,56},{68,6... | collective-permute-start | bytes 393224 | tf_op jit(solution)/shard_map/ppermute | solution.py:25
  116.3 14.8 %collective-permute-start.25 = (bf16[512,128]{1,0:T(8,128)(2,1)S(1)}, bf16[512,128]{1,0:T(8,128)(2,1)S(1)}, u32[]{:S(2)}, u32[]{:S(2)}) collective-permute-start(bf16[512,128]{1,0:T(8,128)(2,1)S(1)} %get-tuple-element.41), channel_id=1, source_target_pairs={{4,2},{12,10},{20,18},{28,26},{36,34},{44,42},{52,50},{60,58},{68,... | collective-permute-start | bytes 393224 | tf_op jit(solution)/shard_map/ppermute | solution.py:25
  134.1 9.7 %collective-permute-start.36 = (bf16[1,256,128]{2,1,0:T(8,128)(2,1)S(1)}, bf16[1,256,128]{2,1,0:T(8,128)(2,1)S(1)}, u32[]{:S(2)}, u32[]{:S(2)}) collective-permute-start(bf16[1,256,128]{2,1,0:T(8,128)(2,1)S(1)} %get-tuple-element.94), channel_id=1, source_target_pairs={{0,8},{8,0},{16,24},{24,16},{1,9},{9,1},{17,25},{25,17},{2,10},{10... | collective-permute-start | bytes 196616 | tf_op jit(solution)/shard_map/ppermute | solution.py:44
  145.9 16.2 %collective-permute-start.33 = (bf16[4,256,128]{2,1,0:T(8,128)(2,1)S(1)}, bf16[4,256,128]{2,1,0:T(8,128)(2,1)S(1)}, u32[]{:S(2)}, u32[]{:S(2)}) collective-permute-start(bf16[4,256,128]{2,1,0:T(8,128)(2,1)S(1)} %pad_maximum_fusion.6), channel_id=1, source_target_pairs={{0,24},{8,16},{16,8},{24,0},{1,25},{9,17},{17,9},{25,1},{2,26},{10... | collective-permute-start | bytes 786440 | tf_op jit(solution)/shard_map/ppermute | solution.py:44
  149.6 14.8 %collective-permute-start.29 = (bf16[4,256,128]{2,1,0:T(8,128)(2,1)S(1)}, bf16[4,256,128]{2,1,0:T(8,128)(2,1)S(1)}, u32[]{:S(2)}, u32[]{:S(2)}) collective-permute-start(bf16[4,256,128]{2,1,0:T(8,128)(2,1)S(1)} %pad_maximum_fusion.5), channel_id=1, source_target_pairs={{0,8},{8,0},{16,24},{24,16},{1,9},{9,1},{17,25},{25,17},{2,10},{10... | collective-permute-start | bytes 786440 | tf_op jit(solution)/shard_map/ppermute | solution.py:44
  151.9 14.6 %collective-permute-start.42 = (bf16[4,256,128]{2,1,0:T(8,128)(2,1)S(1)}, bf16[4,256,128]{2,1,0:T(8,128)(2,1)S(1)}, u32[]{:S(2)}, u32[]{:S(2)}) collective-permute-start(bf16[4,256,128]{2,1,0:T(8,128)(2,1)S(1)} %pad_maximum_fusion.8), channel_id=1, source_target_pairs={{0,96},{32,64},{64,32},{96,0},{1,97},{33,65},{65,33},{97,1},{2,98}... | collective-permute-start | bytes 786440 | tf_op jit(solution)/shard_map/ppermute | solution.py:44
  153.5 13.8 %collective-permute-start.38 = (bf16[4,256,128]{2,1,0:T(8,128)(2,1)S(1)}, bf16[4,256,128]{2,1,0:T(8,128)(2,1)S(1)}, u32[]{:S(2)}, u32[]{:S(2)}) collective-permute-start(bf16[4,256,128]{2,1,0:T(8,128)(2,1)S(1)} %pad_maximum_fusion.7), channel_id=1, source_target_pairs={{0,32},{32,0},{64,96},{96,64},{1,33},{33,1},{65,97},{97,65},{2,34}... | collective-permute-start | bytes 786440 | tf_op jit(solution)/shard_map/ppermute | solution.py:44
  163.0 22.4 %collective-permute-start.34 = (bf16[8,256,128]{2,1,0:T(8,128)(2,1)}, bf16[8,256,128]{2,1,0:T(8,128)(2,1)}, u32[]{:S(2)}, u32[]{:S(2)}) collective-permute-start(bf16[8,256,128]{2,1,0:T(8,128)(2,1)} %pad_maximum_fusion.2), channel_id=1, source_target_pairs={{0,8},{8,0},{16,24},{24,16},{1,9},{9,1},{17,25},{25,17},{2,10},{10... | collective-permute-start | bytes 1572872 | tf_op jit(solution)/shard_map/ppermute | solution.py:44
  165.2 20.1 %collective-permute-start.30 = (bf16[8,256,128]{2,1,0:T(8,128)(2,1)}, bf16[8,256,128]{2,1,0:T(8,128)(2,1)}, u32[]{:S(2)}, u32[]{:S(2)}) collective-permute-start(bf16[8,256,128]{2,1,0:T(8,128)(2,1)} %pad_maximum_fusion.1), channel_id=1, source_target_pairs={{0,24},{8,16},{16,8},{24,0},{1,25},{9,17},{17,9},{25,1},{2,26},{10... | collective-permute-start | bytes 1572872 | tf_op jit(solution)/shard_map/ppermute | solution.py:44
  167.4 18.0 %collective-permute-start.43 = (bf16[8,256,128]{2,1,0:T(8,128)(2,1)}, bf16[8,256,128]{2,1,0:T(8,128)(2,1)}, u32[]{:S(2)}, u32[]{:S(2)}) collective-permute-start(bf16[8,256,128]{2,1,0:T(8,128)(2,1)} %pad_maximum_fusion.4), channel_id=1, source_target_pairs={{0,32},{32,0},{64,96},{96,64},{1,33},{33,1},{65,97},{97,65},{2,34}... | collective-permute-start | bytes 1572872 | tf_op jit(solution)/shard_map/ppermute | solution.py:44
  168.2 17.1 %collective-permute-start.39 = (bf16[8,256,128]{2,1,0:T(8,128)(2,1)}, bf16[8,256,128]{2,1,0:T(8,128)(2,1)}, u32[]{:S(2)}, u32[]{:S(2)}) collective-permute-start(bf16[8,256,128]{2,1,0:T(8,128)(2,1)} %pad_maximum_fusion.3), channel_id=1, source_target_pairs={{0,96},{32,64},{64,32},{96,0},{1,97},{33,65},{65,33},{97,1},{2,98}... | collective-permute-start | bytes 1572872 | tf_op jit(solution)/shard_map/ppermute | solution.py:44
  (26 other events, 151.5 us)
Sparse Core Ops, SparseCore 0:
  33.7 13.3 all-gather.3
  111.3 66.6 all-gather.5

commit v6 on v5

v6 whole, which is shorter than its diff:
```python
import jax
import jax.numpy as jnp
from jax import lax
from jax.experimental import pallas as pl
from jax.experimental.pallas import tpu as pltpu
from jax.sharding import Mesh, PartitionSpec as P

ROWS = ("y", "z", "x")
BF = jnp.bfloat16
F32 = jnp.float32
ALL = [(j, k) for j in range(4) for k in range(4)]
ORDERS = (
    (("y", 1), ("y", 3), ("z", 1), ("z", 3)),
    (("y", 3), ("y", 1), ("z", 3), ("z", 1)),
    (("z", 1), ("z", 3), ("y", 1), ("y", 3)),
    (("z", 3), ("z", 1), ("y", 3), ("y", 1)),
)


def flat(x, y, z):
    return ((y % 4) * 4 + (z % 4)) * 4 + (x % 4)


def permute(value, moves):
    return lax.ppermute(value, ROWS, [(flat(*a), flat(*b)) for a, b in moves])


def hop(value, *planes):
    return permute(value, [((a, j, k), (b, j, k)) for a, b in planes for j, k in ALL])


def ring(value, axis, step):
    return lax.ppermute(value, axis, [(i, (i + step) % 4) for i in range(4)])


def ring_gather(value, axis):
    at = lax.axis_index(axis)
    parts = [value] + [ring(value, axis, 4 - d) for d in (1, 2, 3)]
    both = jnp.stack(parts + parts[:3])
    return lax.dynamic_slice_in_dim(both, (4 - at) % 4, 4, 0)


def swap(value, axis, flip):
    return lax.ppermute(value, axis, [(i, i ^ flip) for i in range(4)])


def spread(parts, whole):
    parts = [p[None] for p in parts]
    for step in range(3):
        got = [swap(p, *order[step]) for p, order in zip(parts, ORDERS)]
        parts = [jnp.concatenate([p, g], axis=0) for p, g in zip(parts, got)]
    got = [swap(p, *order[3]) for p, order in zip(parts, ORDERS)]
    whole, *got = lax.optimization_barrier((whole, *got))
    return parts, got, whole


def places(y, z):
    sites = jnp.arange(16, dtype=jnp.int32)
    tables = []
    for order in ORDERS:
        off = {"y": (sites // 4) ^ y, "z": (sites % 4) ^ z}
        total = jnp.zeros_like(sites)
        for step, (axis, flip) in enumerate(order):
            o = off[axis]
            upper = o >> 1
            bit = upper if flip == 3 else (o & 1) ^ upper
            total = total + (bit << step)
        tables.append(total)
    return jnp.stack(tables).reshape(-1)


def split(value):
    high = value.astype(BF)
    return high, (value - high.astype(F32)).astype(BF)


def put_piece(factor_ref, base, out_ref):
    for u in range(12):
        rows = slice(base + u % 2 * 32, base + u % 2 * 32 + 32)
        at = 512 + u % 3 * 32
        out_ref[at:at + 32, u // 3 * 128:(u // 3 + 1) * 128] = factor_ref[rows, u // 2 * 128:(u // 2 + 1) * 128]


def load_kernel(rhs_ref, factor_ref, *outs):
    for d in range(4):
        for j in range(4):
            lanes = slice(j * 128, (j + 1) * 128)
            at = d * 512 + j * 128
            outs[d][:512, lanes] = rhs_ref[0, :, at:at + 128].astype(BF)
            at = j * 512 + d * 128
            outs[4 + d][:512, lanes] = split(rhs_ref[0, :, at:at + 128])[1]
        put_piece(factor_ref, d * 64, outs[d])
        put_piece(factor_ref, 256 + d * 64, outs[4 + d])


def loads(rhs, factor):
    return pl.pallas_call(
        load_kernel,
        grid=(1,),
        in_specs=[pl.BlockSpec((1, 512, 2048), lambda i: (0, 0, 0)), pl.BlockSpec((512, 1024), lambda i: (0, 0))],
        out_specs=[pl.BlockSpec((608, 512), lambda i: (0, 0))] * 8,
        out_shape=[jax.ShapeDtypeStruct((608, 512), BF)] * 8,
        compiler_params=pltpu.CompilerParams(vmem_limit_bytes=48 << 20),
    )(rhs, factor)


def solve(high_ref, low_ref, state):
    high, low = split(state)
    dot = lambda a, b: jnp.dot(a, b, preferred_element_type=F32)
    return (dot(high_ref[...], high) + dot(high_ref[...], low) + dot(low_ref[...], high)).astype(BF)


def first_kernel(scalars, state_ref, high_ref, low_ref, sent_ref):
    sent_ref[...] = solve(high_ref, low_ref, state_ref[...])


def step_kernel(panel, scalars, state_ref, high_ref, low_ref, mine_ref, other_ref, *refs):
    dot = lambda a, b: jnp.dot(a, b, preferred_element_type=F32)
    swap = scalars[0] == 1
    left = jnp.where(swap, other_ref[0], mine_ref[0])
    right = jnp.where(swap, mine_ref[0], other_ref[0])
    gots = refs[:3 - panel]
    got = sum(g[...] for g in gots)
    state = state_ref[...] - dot(left, got[:256]) - dot(right, got[256:])
    here = scalars[1] == panel
    if panel == 0:
        sent_ref, next_ref, new_ref, done_ref = refs[3:]
        done_ref[...] = jnp.where(here, sent_ref[...], got)
    elif panel == 1:
        sent_ref, back_ref, last_ref, next_ref, new_ref, done_ref = refs[2:]
        done_ref[:512] = last_ref[...]
        done_ref[512:] = jnp.where(here, sent_ref[...], got + back_ref[...])
    else:
        next_ref, new_ref = refs[1:]
    next_ref[...] = state
    new_ref[...] = solve(high_ref, low_ref, state)


def step(scalars, state, inverse, factor=None, panel=None, more=()):
    full = lambda shape: pl.BlockSpec(shape, lambda i, s: (0, 0))
    part = pl.BlockSpec((1, 512, 256), lambda i, s: (panel, 0, 0))
    tall, square = full((512, 128)), full((512, 512))
    shapes = [jax.ShapeDtypeStruct((512, 128), BF)]
    if panel is None:
        kernel, ins, factor = first_kernel, [], ()
    else:
        kernel, ins = lambda *refs: step_kernel(panel, *refs), [part, part] + [tall] * len(more)
        shapes = [jax.ShapeDtypeStruct((512, 128), F32)] + shapes
        if panel < 2:
            shapes.append(jax.ShapeDtypeStruct((512 * (panel + 1), 128), BF))
    return pl.pallas_call(
        kernel,
        grid_spec=pltpu.PrefetchScalarGridSpec(
            num_scalar_prefetch=1,
            grid=(1,),
            in_specs=[tall, square, square] + ins,
            out_specs=[full(v.shape) for v in shapes],
        ),
        out_shape=shapes,
        compiler_params=pltpu.CompilerParams(vmem_limit_bytes=32 << 20),
    )(scalars, state, *inverse, *factor, *more)


def update_kernel(scalars, factor_ref, rhs_ref, early_ref, *rest):
    near, far, out_ref, sent_ref = rest[:8], rest[8:16], rest[16], rest[17]
    j = pl.program_id(0)
    for h in range(2):
        lanes = slice(h * 128, (h + 1) * 128)
        sent_ref[:1024, lanes] = early_ref[h]
        for p in range(4):
            rows = slice(1024 + p * 256, 1280 + p * 256)
            low = scalars[p * 16 + 2 * j + h] < 8

            @pl.when(low)
            def _():
                sent_ref[rows, lanes] = near[p * 2 + h][0]

            @pl.when(jnp.logical_not(low))
            def _():
                sent_ref[rows, lanes] = far[p * 2 + h][0]
    for c in range(2):
        out_ref[c] = rhs_ref[c] - jnp.dot(factor_ref[c], sent_ref[...], preferred_element_type=F32)
    place = scalars[64]

    @pl.when(place < 4)
    def _():
        out_ref[0] = sent_ref[pl.ds(pl.multiple_of(place * 512, 512), 512), :].astype(F32)


def update(scalars, factor, rhs, early, near, far):
    cycles, tile, depth = factor.shape
    pairs = [(p, h) for p in range(4) for h in range(2)]
    near_specs = [
        pl.BlockSpec((1, 256, 128), lambda j, s, p=p, h=h: (jnp.minimum(s[p * 16 + 2 * j + h], 7), 0, 0))
        for p, h in pairs
    ]
    far_specs = [
        pl.BlockSpec((1, 256, 128), lambda j, s, p=p, h=h: (jnp.maximum(s[p * 16 + 2 * j + h] - 8, 0), 0, 0))
        for p, h in pairs
    ]
    return pl.pallas_call(
        update_kernel,
        grid_spec=pltpu.PrefetchScalarGridSpec(
            num_scalar_prefetch=1,
            grid=(rhs.shape[2] // 256,),
            in_specs=[
                pl.BlockSpec((cycles, tile, depth), lambda j, s: (0, 0, 0)),
                pl.BlockSpec((cycles, tile, 256), lambda j, s: (0, 0, j)),
                pl.BlockSpec((2, 1024, 128), lambda j, s: (j, 0, 0)),
            ] + near_specs + far_specs,
            out_specs=pl.BlockSpec((cycles, tile, 256), lambda j, s: (0, 0, j)),
            scratch_shapes=[pltpu.VMEM((depth, 256), BF)],
        ),
        out_shape=jax.ShapeDtypeStruct(rhs.shape, F32),
        compiler_params=pltpu.CompilerParams(vmem_limit_bytes=48 << 20),
    )(scalars, factor, rhs, early, *[near[p] for p, _ in pairs], *[far[p] for p, _ in pairs])


def local(rhs, factor, inverses):
    x, y, z = (lax.axis_index(a) for a in ("x", "y", "z"))
    core = lax.axis_index("rhs")
    place = (y * 4 + z) * 4 + x
    owner = place < 4
    zero = jnp.zeros((), BF)

    tile = factor[0].reshape(512, 1024)
    slabs = loads(rhs, tile)
    outward = {
        (p, d): permute(slabs[4 * p + d], [((i, 0, 0), (i, 0, d) if p else (i, d, 0)) for i in range(4)])
        for p, d in ((0, 3), (0, 1), (1, 1), (0, 2), (1, 2), (1, 3))
    }
    hold_a = jnp.where(owner, slabs[0], zero) + outward[0, 1] + outward[0, 2] + outward[0, 3]
    own_b, hold_a = lax.optimization_barrier((slabs[4], hold_a))
    hold_b = jnp.where(owner, own_b, zero) + outward[1, 1] + outward[1, 2] + outward[1, 3]

    def finish(hold, axis):
        tail = [hold[512:, k * 128:(k + 1) * 128] for k in range(4)]
        message = lambda d: jnp.concatenate([hold[:512, d * 128:(d + 1) * 128]] + tail, axis=0)
        mine = jnp.where((z if axis == "y" else y) == 0, message(0), zero)
        for d in (1, 3, 2):
            if axis == "y":
                moves = [((i, j, 0), (i, j, d)) for i in range(4) for j in range(4)]
            else:
                moves = [((i, 0, j), (i, d, j)) for i in range(4) for j in range(4)]
            mine = mine + permute(message(d), moves)
        return mine

    whole = lax.all_gather(factor, "rhs", axis=3, tiled=True)
    tiles = jnp.arange(2, dtype=jnp.int32) * 64 + place
    keep = tiles[:, None] > jnp.arange(4, dtype=jnp.int32)[None]
    whole = jnp.where(keep[:, None, :, None], whole, zero).reshape(2, 512, 2048)

    mine_a = finish(hold_a, "y")
    mine_b = finish(hold_b, "z")

    inverse = lax.dynamic_index_in_dim(inverses, x, 0, keepdims=False)
    rounded = lax.reduce_precision(inverse, 8, 7)
    inverse = (rounded.astype(BF), (inverse - rounded).astype(BF))
    where = jnp.stack([core, x]).astype(jnp.int32)
    state = mine_a[:512].astype(F32) + mine_b[:512].astype(F32)
    state, *inverse = lax.optimization_barrier((state, *inverse))
    sent_0, = step(where, state, inverse)
    gots = [hop(sent_0, (0, 1)), hop(sent_0, (0, 3)), hop(sent_0, (0, 2))]

    piece_a, piece_b, _ = lax.optimization_barrier((mine_a[512:], mine_b[512:], sent_0))
    top = ring_gather(piece_a, "y")
    bottom = ring_gather(piece_b, "z")
    half = jnp.concatenate([top, bottom], axis=0).reshape(8, 3, 2, 64, 128).transpose(1, 0, 3, 2, 4).reshape(3, 512, 256)
    half, *gots = lax.optimization_barrier((half, *gots))
    block = (half, lax.ppermute(half, "rhs", [(0, 1), (1, 0)]))

    state, sent_1, panel_0 = step(where, state, inverse, block, 0, (*gots, sent_0))
    gots = [hop(sent_1, (1, 2)), hop(sent_1, (1, 3))]
    back_1 = hop(sent_1, (1, 0))
    state, sent_2, pair = step(where, state, inverse, block, 1, (*gots, sent_1, back_1, panel_0))
    early = lax.all_gather(pair, ("y", "z"), axis=0)
    got = hop(sent_2, (2, 3))
    state, sent = step(where, state, inverse, block, 2, (got,))
    sent_2 = jnp.where(x == 2, sent_2, zero)
    sent = jnp.where(x == 3, sent, sent_2)
    back = hop(sent, (2, 1), (3, 2))
    far = hop(sent, (2, 0), (3, 1))
    wrap = hop(sent, (3, 0))
    panel_2 = jnp.where(x == 2, sent, jnp.where(x == 3, got, jnp.where(x == 1, back, far)))
    panel_3 = jnp.where(x == 3, sent, jnp.where(x == 2, back, jnp.where(x == 1, far, wrap)))
    near, far_late, whole = spread([panel_2[:256], panel_2[256:], panel_3[:256], panel_3[256:]], whole)

    scalars = jnp.concatenate([places(y, z), place[None]]).astype(jnp.int32)
    return update(scalars, whole, rhs, early, near, far_late)


def solution(mesh):
    grid = Mesh(mesh.devices.reshape(4, 4, 4, 2), ("y", "z", "x", "rhs"))
    return jax.shard_map(
        local,
        mesh=grid,
        in_specs=(P(None, ROWS, "rhs"), P(None, ROWS, None, "rhs"), P()),
        out_specs=P(None, ROWS, "rhs"),
        check_vma=False,
    )
```

time: 216 us -> 210 us (0.972)
  the two profiles are of different devices: /device:TPU:2 before, /device:TPU:6 now
where the time goes in v6:
time: 210 us; the launch traced here: 207 us
  waiting for transfers between devices  77.3 us (37%)
  starting transfers between devices  63.4 us (30%)
  Pallas kernels  28.5 us (14%)
  between operations  14.1 us (7%)
  other arithmetic  11.8 us (6%)
  local copies, waits for them, and re-layouts  11.6 us (6%)
    ppermute x22, waiting for transfers between devices, permute(): return lax.ppermute(value, ROWS, [(flat(*a), flat(*b)) for a, b in moves])  48.1 us
    ppermute x22, starting transfers between devices, permute(): return lax.ppermute(value, ROWS, [(flat(*a), flat(*b)) for a, b in moves])  37.4 us
    ppermute x16, starting transfers between devices, swap(): return lax.ppermute(value, axis, [(i, i ^ flip) for i in range(4)])  19.4 us
    pallas_call x1, Pallas kernels, update(): pl.pallas_call(update_kernel, grid_spec=pltpu.PrefetchScalarGridSpec(num_...  17.8 us
    ppermute x16, waiting for transfers between devices, swap(): return lax.ppermute(value, axis, [(i, i ^ flip) for i in range(4)])  16.2 us
    ppermute x6, waiting for transfers between devices, ring(): return lax.ppermute(value, axis, [(i, (i + step) % 4) for i in range(4)])  10.6 us
    reshape x1, local copies, waits for them, and re-layouts, local(): whole = jnp.where(keep[:, None, :, None], whole, zero).reshape(2, 512, 2048)  7.77 us
    pallas_call x4, Pallas kernels, step(): pl.pallas_call(kernel, grid_spec=pltpu.PrefetchScalarGridSpec(num_scalar_...  6.73 us
  transfers between devices with their start and end apart: 47, of which 21 were waited for; matrix products, arithmetic and copies ran while one was open for 10% of the time, Pallas kernels for 3%

profile of v6, /device:TPU:6, one launch (start us, length us, event | category | flops | bytes accessed | tf_op | source)
XLA Modules:
  0.0 206.8 jit_solution(13119925572245267956)
XLA Ops:
  8.4 4.0 %shard_map.37 = (bf16[608,512]{1,0:T(8,128)(2,1)S(1)}, bf16[608,512]{1,0:T(8,128)(2,1)S(1)}, bf16[608,512]{1,0:T(8,128)(2,1)}, bf16[608,512]{1,0:T(8,128)(2,1)},...) custom-call(f32[2,512,2048]{2,1,0:T(8,128)} %rhs_ref.3, ...), custom_call_target="tpu_custom_call" | custom-call | tf_op jit(solution)/shard_map/pallas_call | solution.py:97
  12.3 4.3 %collective-permute-start = (bf16[608,512]{1,0:T(8,128)(2,1)S(1)}, bf16[608,512]{1,0:T(8,128)(2,1)}, u32[]{:S(2)}, u32[]{:S(2)}) collective-permute-start(bf16[608,512]{1,0:T(8,128)(2,1)S(1)} %get-tuple-element.38), channel_id=1, source_target_pairs={{0,32},{2,34},{4,36},{6,38},{1,33},{3,35},{5,37},{7,39}} | collective-permute-start | bytes 1867784 | tf_op jit(solution)/shard_map/ppermute | solution.py:25
  16.6 3.1 %collective-permute-start.1 = (bf16[608,512]{1,0:T(8,128)(2,1)}, bf16[608,512]{1,0:T(8,128)(2,1)}, u32[]{:S(2)}, u32[]{:S(2)}) collective-permute-start(bf16[608,512]{1,0:T(8,128)(2,1)} %get-tuple-element.39), channel_id=1, source_target_pairs={{0,64},{2,66},{4,68},{6,70},{1,65},{3,67},{5,69},{7,71}} | collective-permute-start | bytes 1867784 | tf_op jit(solution)/shard_map/ppermute | solution.py:25
  25.4 4.8 %collective-permute-done = bf16[608,512]{1,0:T(8,128)(2,1)} collective-permute-done((bf16[608,512]{1,0:T(8,128)(2,1)S(1)}, bf16[608,512]{1,0:T(8,128)(2,1)}, u32[]{:S(2)}, u32[]{:S(2)}) %collective-permute-start) | collective-permute-done | bytes 622624 | tf_op jit(solution)/shard_map/ppermute | solution.py:25
  33.9 8.6 %collective-permute-done.1 = bf16[608,512]{1,0:T(8,128)(2,1)} collective-permute-done((bf16[608,512]{1,0:T(8,128)(2,1)}, bf16[608,512]{1,0:T(8,128)(2,1)}, u32[]{:S(2)}, u32[]{:S(2)}) %collective-permute-start.1) | collective-permute-done | bytes 622624 | tf_op jit(solution)/shard_map/ppermute | solution.py:25
  44.5 5.7 %collective-permute-done.7 = bf16[608,512]{1,0:T(8,128)(2,1)} collective-permute-done((bf16[608,512]{1,0:T(8,128)(2,1)}, bf16[608,512]{1,0:T(8,128)(2,1)}, u32[]{:S(2)}, u32[]{:S(2)}) %collective-permute-start.7) | collective-permute-done | bytes 622624 | tf_op jit(solution)/shard_map/ppermute | solution.py:25
  57.2 5.3 %collective-permute-start.5 = (bf16[896,128]{1,0:T(8,128)(2,1)S(1)}, bf16[896,128]{1,0:T(8,128)(2,1)S(1)}, u32[]{:S(2)}, u32[]{:S(2)}) collective-permute-start(bf16[896,128]{1,0:T(8,128)(2,1)S(1)} %get-tuple-element.85), channel_id=1, source_target_pairs={{0,16},{32,48},{64,80},{96,112},{2,18},{34,50},{66,82},{98,114},{4... | collective-permute-start | bytes 688136 | tf_op jit(solution)/shard_map/ppermute | solution.py:25
  64.0 4.5 %collective-permute-done.5 = bf16[896,128]{1,0:T(8,128)(2,1)S(1)} collective-permute-done((bf16[896,128]{1,0:T(8,128)(2,1)S(1)}, bf16[896,128]{1,0:T(8,128)(2,1)S(1)}, u32[]{:S(2)}, u32[]{:S(2)}) %collective-permute-start.5) | collective-permute-done | bytes 229408 | tf_op jit(solution)/shard_map/ppermute | solution.py:25
  68.5 2.8 %collective-permute-done.3 = bf16[896,128]{1,0:T(8,128)(2,1)S(1)} collective-permute-done((bf16[896,128]{1,0:T(8,128)(2,1)S(1)}, bf16[896,128]{1,0:T(8,128)(2,1)S(1)}, u32[]{:S(2)}, u32[]{:S(2)}) %collective-permute-start.3) | collective-permute-done | bytes 229408 | tf_op jit(solution)/shard_map/ppermute | solution.py:25
  72.9 3.1 %collective-permute-start.12 = (bf16[384,128]{1,0:T(8,128)(2,1)S(1)}, bf16[384,128]{1,0:T(8,128)(2,1)S(1)}, u32[]{:S(2)}, u32[]{:S(2)}) collective-permute-start(bf16[384,128]{1,0:T(8,128)(2,1)S(1)} %slice.112), channel_id=1, source_target_pairs={{0,96},{32,0},{64,32},{96,64},{1,97},{33,1},{65,33},{97,65},{2,98}... | collective-permute-start | bytes 294920 | tf_op jit(solution)/shard_map/ppermute | solution.py:33
  76.0 2.5 %collective-permute-start.17 = (bf16[384,128]{1,0:T(8,128)(2,1)S(1)}, bf16[384,128]{1,0:T(8,128)(2,1)S(1)}, u32[]{:S(2)}, u32[]{:S(2)}) collective-permute-start(bf16[384,128]{1,0:T(8,128)(2,1)S(1)} %slice.113), channel_id=1, source_target_pairs={{0,8},{8,16},{16,24},{24,0},{1,9},{9,17},{17,25},{25,1},{2,10},{10... | collective-permute-start | bytes 294920 | tf_op jit(solution)/shard_map/ppermute | solution.py:33
  79.3 4.5 %collective-permute-done.15 = bf16[384,128]{1,0:T(8,128)(2,1)S(1)} collective-permute-done((bf16[384,128]{1,0:T(8,128)(2,1)S(1)}, bf16[384,128]{1,0:T(8,128)(2,1)S(1)}, u32[]{:S(2)}, u32[]{:S(2)}) %collective-permute-start.15) | collective-permute-done | bytes 98336 | tf_op jit(solution)/shard_map/ppermute | solution.py:33
  83.8 6.1 %collective-permute-done.16 = bf16[384,128]{1,0:T(8,128)(2,1)S(1)} collective-permute-done((bf16[384,128]{1,0:T(8,128)(2,1)S(1)}, bf16[384,128]{1,0:T(8,128)(2,1)S(1)}, u32[]{:S(2)}, u32[]{:S(2)}) %collective-permute-start.16) | collective-permute-done | bytes 98336 | tf_op jit(solution)/shard_map/ppermute | solution.py:33
  94.3 5.2 %collective-permute-done.19.refs_7_ = bf16[512,128]{1,0:T(8,128)(2,1)S(1)} collective-permute-done((bf16[512,128]{1,0:T(8,128)(2,1)S(1)}, bf16[512,128]{1,0:T(8,128)(2,1)S(1)}, u32[]{:S(2)}, u32[]{:S(2)}) %collective-permute-start.19) | collective-permute-done | bytes 131104 | tf_op jit(solution)/shard_map/ppermute | solution.py:25
  99.5 2.3 %collective-permute-done.21.refs_5_ = bf16[3,512,256]{2,1,0:T(8,128)(2,1)S(1)} collective-permute-done((bf16[3,512,256]{2,1,0:T(8,128)(2,1)S(1)}, bf16[3,512,256]{2,1,0:T(8,128)(2,1)S(1)}, u32[]{:S(2)}, u32[]{:S(2)}) %collective-permute-start.21) | collective-permute-done | bytes 786464 | tf_op jit(solution)/shard_map/ppermute | solution.py:270
  106.1 8.1 %collective-permute-done.23.refs_7_ = bf16[512,128]{1,0:T(8,128)(2,1)S(1)} collective-permute-done((bf16[512,128]{1,0:T(8,128)(2,1)S(1)}, bf16[512,128]{1,0:T(8,128)(2,1)S(1)}, u32[]{:S(2)}, u32[]{:S(2)}) %collective-permute-start.23) | collective-permute-done | bytes 131104 | tf_op jit(solution)/shard_map/ppermute | solution.py:25
  114.2 2.2 %shard_map.40 = (f32[512,128]{1,0:T(8,128)S(1)}, bf16[512,128]{1,0:T(8,128)(2,1)S(1)}, bf16[1024,128]{1,0:T(8,128)(2,1)}) custom-call(s32[2]{0:T(128)S(1)} %pad_add_fusion.2.scalars.refs_0_, f32[512,128]{1,0:T(8,128)S(1)} %get-tuple-element.55.refs_1_, bf16[512,512]{1,0:T(8,128)(2,1)S(1)} %get-tuple-element.47.high_ref.refs_2_, ...), custom_call_target="tpu_custom_call" | custom-call | tf_op jit(solution)/shard_map/pallas_call | solution.py:151
  117.8 5.5 %collective-permute-done.25.refs_6_ = bf16[512,128]{1,0:T(8,128)(2,1)S(1)} collective-permute-done((bf16[512,128]{1,0:T(8,128)(2,1)S(1)}, bf16[512,128]{1,0:T(8,128)(2,1)S(1)}, u32[]{:S(2)}, u32[]{:S(2)}) %collective-permute-start.25) | collective-permute-done | bytes 131104 | tf_op jit(solution)/shard_map/ppermute | solution.py:25
  141.4 2.3 %collective-permute-start.29 = (bf16[2,256,128]{2,1,0:T(8,128)(2,1)S(1)}, bf16[2,256,128]{2,1,0:T(8,128)(2,1)S(1)}, u32[]{:S(2)}, u32[]{:S(2)}) collective-permute-start(bf16[2,256,128]{2,1,0:T(8,128)(2,1)S(1)} %pad_maximum_fusion.9), channel_id=1, source_target_pairs={{0,96},{32,64},{64,32},{96,0},{1,97},{33,65},{65,33},{97,1},{2,98}... | collective-permute-start | bytes 393224 | tf_op jit(solution)/shard_map/ppermute | solution.py:44
  152.1 6.5 %collective-permute-done.39 = bf16[4,256,128]{2,1,0:T(8,128)(2,1)S(1)} collective-permute-done((bf16[4,256,128]{2,1,0:T(8,128)(2,1)S(1)}, bf16[4,256,128]{2,1,0:T(8,128)(2,1)S(1)}, u32[]{:S(2)}, u32[]{:S(2)}) %collective-permute-start.39) | collective-permute-done | bytes 262176 | tf_op jit(solution)/shard_map/ppermute | solution.py:44
  160.6 3.0 %collective-permute-done.43 = bf16[4,256,128]{2,1,0:T(8,128)(2,1)S(1)} collective-permute-done((bf16[4,256,128]{2,1,0:T(8,128)(2,1)S(1)}, bf16[4,256,128]{2,1,0:T(8,128)(2,1)S(1)}, u32[]{:S(2)}, u32[]{:S(2)}) %collective-permute-start.43) | collective-permute-done | bytes 262176 | tf_op jit(solution)/shard_map/ppermute | solution.py:44
  166.5 6.0 %broadcast_select_fusion = bf16[2,512,4,512]{3,2,1,0:T(4,128)(2,1)} fusion(bf16[2,512,4,512]{3,2,1,0:T(4,128)(2,1)} %all-gather.4.cloned.1.call-done, pred[2,4]{1,0:T(4,128)(4,1)S(1)} %iota_compare_fusion), kind=kLoop, calls=%fused_computation | loop fusion | flops 2097152 | bytes 8388616 | tf_op jit(solution)/shard_map/jit(_where)/select_n | solution.py:251
  172.5 7.8 %reshape.198.factor_ref = bf16[2,512,2048]{2,1,0:T(8,128)(2,1)} reshape(bf16[2,512,4,512]{3,2,1,0:T(4,128)(2,1)} %broadcast_select_fusion) | data formatting | bytes 8388608 | tf_op jit(solution)/shard_map/reshape | solution.py:251
  182.1 17.8 %shard_map.42 = f32[2,512,2048]{2,1,0:T(8,128)} custom-call(s32[65]{0:T(128)S(1)} %pad_add_fusion.1.scalars, bf16[2,512,2048]{2,1,0:T(8,128)(2,1)} %reshape.198.factor_ref, f32[2,512,2048]{2,1,0:T(8,128)} %rhs_ref.3, bf16[16,1024,128]{2,1,0:T(8,128)(2,1)} %bitcast.45, bf16[8,256,128]{2,1,0:T(8,128)(2,1)S(1)} %pad_maximum_fusion.1.rest_0_.rest_1_, ...), custom_call_target="tpu_custom_call" | custom-call | tf_op jit(solution)/shard_map/pallas_call | solution.py:201
  (146 shorter events, 66.6 us)
Async XLA Ops:
  6.5 160.0 %all-gather.4.cloned.1.call-start = ((), (), s32[]{:S(2)}) async-start(), calls=%async_computation | async-start | bytes 6291456 | tf_op jit(solution)/shard_map/all_gather | solution.py:248
  12.3 17.9 %collective-permute-start = (bf16[608,512]{1,0:T(8,128)(2,1)S(1)}, bf16[608,512]{1,0:T(8,128)(2,1)}, u32[]{:S(2)}, u32[]{:S(2)}) collective-permute-start(bf16[608,512]{1,0:T(8,128)(2,1)S(1)} %get-tuple-element.38), channel_id=1, source_target_pairs={{0,32},{2,34},{4,36},{6,38},{1,33},{3,35},{5,37},{7,39}} | collective-permute-start | bytes 1867784 | tf_op jit(solution)/shard_map/ppermute | solution.py:25
  16.6 25.9 %collective-permute-start.1 = (bf16[608,512]{1,0:T(8,128)(2,1)}, bf16[608,512]{1,0:T(8,128)(2,1)}, u32[]{:S(2)}, u32[]{:S(2)}) collective-permute-start(bf16[608,512]{1,0:T(8,128)(2,1)} %get-tuple-element.39), channel_id=1, source_target_pairs={{0,64},{2,66},{4,68},{6,70},{1,65},{3,67},{5,69},{7,71}} | collective-permute-start | bytes 1867784 | tf_op jit(solution)/shard_map/ppermute | solution.py:25
  19.8 22.8 %collective-permute-start.2 = (bf16[608,512]{1,0:T(8,128)(2,1)}, bf16[608,512]{1,0:T(8,128)(2,1)}, u32[]{:S(2)}, u32[]{:S(2)}) collective-permute-start(bf16[608,512]{1,0:T(8,128)(2,1)} %get-tuple-element.40), channel_id=1, source_target_pairs={{0,96},{2,98},{4,100},{6,102},{1,97},{3,99},{5,101},{7,103}} | collective-permute-start | bytes 1867784 | tf_op jit(solution)/shard_map/ppermute | solution.py:25
  21.9 22.5 %collective-permute-start.6 = (bf16[608,512]{1,0:T(8,128)(2,1)}, bf16[608,512]{1,0:T(8,128)(2,1)S(1)}, u32[]{:S(2)}, u32[]{:S(2)}) collective-permute-start(bf16[608,512]{1,0:T(8,128)(2,1)} %get-tuple-element.43), channel_id=1, source_target_pairs={{0,8},{2,10},{4,12},{6,14},{1,9},{3,11},{5,13},{7,15}} | collective-permute-start | bytes 1867784 | tf_op jit(solution)/shard_map/ppermute | solution.py:25
  23.3 26.9 %collective-permute-start.7 = (bf16[608,512]{1,0:T(8,128)(2,1)}, bf16[608,512]{1,0:T(8,128)(2,1)}, u32[]{:S(2)}, u32[]{:S(2)}) collective-permute-start(bf16[608,512]{1,0:T(8,128)(2,1)} %get-tuple-element.44), channel_id=1, source_target_pairs={{0,16},{2,18},{4,20},{6,22},{1,17},{3,19},{5,21},{7,23}} | collective-permute-start | bytes 1867784 | tf_op jit(solution)/shard_map/ppermute | solution.py:25
  30.2 19.9 %collective-permute-start.8 = (bf16[608,512]{1,0:T(8,128)(2,1)S(1)}, bf16[608,512]{1,0:T(8,128)(2,1)}, u32[]{:S(2)}, u32[]{:S(2)}) collective-permute-start(bf16[608,512]{1,0:T(8,128)(2,1)S(1)} %get-tuple-element.45), channel_id=1, source_target_pairs={{0,24},{2,26},{4,28},{6,30},{1,25},{3,27},{5,29},{7,31}} | collective-permute-start | bytes 1867784 | tf_op jit(solution)/shard_map/ppermute | solution.py:25
  32.4 149.8 %all-gather.6.cloned.1.call-start = ((), (), s32[]{:S(2)}) async-start(), calls=%async_computation.1 | async-start | bytes 4456448 | tf_op jit(solution)/shard_map/all_gather | solution.py:276
  51.7 10.8 %collective-permute-start.10 = (bf16[896,128]{1,0:T(8,128)(2,1)S(1)}, bf16[896,128]{1,0:T(8,128)(2,1)S(1)}, u32[]{:S(2)}, u32[]{:S(2)}) collective-permute-start(bf16[896,128]{1,0:T(8,128)(2,1)S(1)} %get-tuple-element.101), channel_id=1, source_target_pairs={{0,96},{8,104},{16,112},{24,120},{2,98},{10,106},{18,114},{26,122}... | collective-permute-start | bytes 688136 | tf_op jit(solution)/shard_map/ppermute | solution.py:25
  53.0 10.8 %collective-permute-start.11 = (bf16[896,128]{1,0:T(8,128)(2,1)S(1)}, bf16[896,128]{1,0:T(8,128)(2,1)S(1)}, u32[]{:S(2)}, u32[]{:S(2)}) collective-permute-start(bf16[896,128]{1,0:T(8,128)(2,1)S(1)} %get-tuple-element.102), channel_id=1, source_target_pairs={{0,64},{8,72},{16,80},{24,88},{2,66},{10,74},{18,82},{26,90},{4,68... | collective-permute-start | bytes 688136 | tf_op jit(solution)/shard_map/ppermute | solution.py:25
  57.2 11.3 %collective-permute-start.5 = (bf16[896,128]{1,0:T(8,128)(2,1)S(1)}, bf16[896,128]{1,0:T(8,128)(2,1)S(1)}, u32[]{:S(2)}, u32[]{:S(2)}) collective-permute-start(bf16[896,128]{1,0:T(8,128)(2,1)S(1)} %get-tuple-element.85), channel_id=1, source_target_pairs={{0,16},{32,48},{64,80},{96,112},{2,18},{34,50},{66,82},{98,114},{4... | collective-permute-start | bytes 688136 | tf_op jit(solution)/shard_map/ppermute | solution.py:25
  72.7 20.0 %collective-permute-start.14 = (bf16[384,128]{1,0:T(8,128)(2,1)S(1)}, bf16[384,128]{1,0:T(8,128)(2,1)S(1)}, u32[]{:S(2)}, u32[]{:S(2)}) collective-permute-start(bf16[384,128]{1,0:T(8,128)(2,1)S(1)} %slice.112), channel_id=1, source_target_pairs={{0,32},{32,64},{64,96},{96,0},{1,33},{33,65},{65,97},{97,1},{2,34}... | collective-permute-start | bytes 294920 | tf_op jit(solution)/shard_map/ppermute | solution.py:33
  72.8 19.9 %collective-permute-start.13 = (bf16[384,128]{1,0:T(8,128)(2,1)S(1)}, bf16[384,128]{1,0:T(8,128)(2,1)S(1)}, u32[]{:S(2)}, u32[]{:S(2)}) collective-permute-start(bf16[384,128]{1,0:T(8,128)(2,1)S(1)} %slice.112), channel_id=1, source_target_pairs={{0,64},{32,96},{64,0},{96,32},{1,65},{33,97},{65,1},{97,33},{2,66}... | collective-permute-start | bytes 294920 | tf_op jit(solution)/shard_map/ppermute | solution.py:33
  72.9 19.1 %collective-permute-start.12 = (bf16[384,128]{1,0:T(8,128)(2,1)S(1)}, bf16[384,128]{1,0:T(8,128)(2,1)S(1)}, u32[]{:S(2)}, u32[]{:S(2)}) collective-permute-start(bf16[384,128]{1,0:T(8,128)(2,1)S(1)} %slice.112), channel_id=1, source_target_pairs={{0,96},{32,0},{64,32},{96,64},{1,97},{33,1},{65,33},{97,65},{2,98}... | collective-permute-start | bytes 294920 | tf_op jit(solution)/shard_map/ppermute | solution.py:33
  76.0 14.5 %collective-permute-start.17 = (bf16[384,128]{1,0:T(8,128)(2,1)S(1)}, bf16[384,128]{1,0:T(8,128)(2,1)S(1)}, u32[]{:S(2)}, u32[]{:S(2)}) collective-permute-start(bf16[384,128]{1,0:T(8,128)(2,1)S(1)} %slice.113), channel_id=1, source_target_pairs={{0,8},{8,16},{16,24},{24,0},{1,9},{9,17},{17,25},{25,1},{2,10},{10... | collective-permute-start | bytes 294920 | tf_op jit(solution)/shard_map/ppermute | solution.py:33
  138.1 12.2 %collective-permute-start.33 = (bf16[2,256,128]{2,1,0:T(8,128)(2,1)S(1)}, bf16[2,256,128]{2,1,0:T(8,128)(2,1)S(1)}, u32[]{:S(2)}, u32[]{:S(2)}) collective-permute-start(bf16[2,256,128]{2,1,0:T(8,128)(2,1)S(1)} %pad_maximum_fusion.10), channel_id=1, source_target_pairs={{0,32},{32,0},{64,96},{96,64},{1,33},{33,1},{65,97},{97,65},{2,34}... | collective-permute-start | bytes 393224 | tf_op jit(solution)/shard_map/ppermute | solution.py:44
  145.5 13.1 %collective-permute-start.39 = (bf16[4,256,128]{2,1,0:T(8,128)(2,1)S(1)}, bf16[4,256,128]{2,1,0:T(8,128)(2,1)S(1)}, u32[]{:S(2)}, u32[]{:S(2)}) collective-permute-start(bf16[4,256,128]{2,1,0:T(8,128)(2,1)S(1)} %pad_maximum_fusion.7), channel_id=1, source_target_pairs={{0,32},{32,0},{64,96},{96,64},{1,33},{33,1},{65,97},{97,65},{2,34}... | collective-permute-start | bytes 786440 | tf_op jit(solution)/shard_map/ppermute | solution.py:44
  147.5 16.0 %collective-permute-start.43 = (bf16[4,256,128]{2,1,0:T(8,128)(2,1)S(1)}, bf16[4,256,128]{2,1,0:T(8,128)(2,1)S(1)}, u32[]{:S(2)}, u32[]{:S(2)}) collective-permute-start(bf16[4,256,128]{2,1,0:T(8,128)(2,1)S(1)} %pad_maximum_fusion.8), channel_id=1, source_target_pairs={{0,96},{32,64},{64,32},{96,0},{1,97},{33,65},{65,33},{97,1},{2,98}... | collective-permute-start | bytes 786440 | tf_op jit(solution)/shard_map/ppermute | solution.py:44
  148.9 15.7 %collective-permute-start.30 = (bf16[4,256,128]{2,1,0:T(8,128)(2,1)S(1)}, bf16[4,256,128]{2,1,0:T(8,128)(2,1)S(1)}, u32[]{:S(2)}, u32[]{:S(2)}) collective-permute-start(bf16[4,256,128]{2,1,0:T(8,128)(2,1)S(1)} %pad_maximum_fusion.5), channel_id=1, source_target_pairs={{0,8},{8,0},{16,24},{24,16},{1,9},{9,1},{17,25},{25,17},{2,10},{10... | collective-permute-start | bytes 786440 | tf_op jit(solution)/shard_map/ppermute | solution.py:44
  150.3 16.0 %collective-permute-start.34 = (bf16[4,256,128]{2,1,0:T(8,128)(2,1)S(1)}, bf16[4,256,128]{2,1,0:T(8,128)(2,1)S(1)}, u32[]{:S(2)}, u32[]{:S(2)}) collective-permute-start(bf16[4,256,128]{2,1,0:T(8,128)(2,1)S(1)} %pad_maximum_fusion.6), channel_id=1, source_target_pairs={{0,24},{8,16},{16,8},{24,0},{1,25},{9,17},{17,9},{25,1},{2,26},{10... | collective-permute-start | bytes 786440 | tf_op jit(solution)/shard_map/ppermute | solution.py:44
  158.7 22.7 %collective-permute-start.40 = (bf16[8,256,128]{2,1,0:T(8,128)(2,1)S(1)}, bf16[8,256,128]{2,1,0:T(8,128)(2,1)S(1)}, u32[]{:S(2)}, u32[]{:S(2)}) collective-permute-start(bf16[8,256,128]{2,1,0:T(8,128)(2,1)S(1)} %pad_maximum_fusion.3.rest_4_.rest_5_), channel_id=1, source_target_pairs={{0,96},{32,64},{64,32},{96,0},{1,97},{33,65},{65,33},{97,1},{2,98}... | collective-permute-start | bytes 1572872 | tf_op jit(solution)/shard_map/ppermute | solution.py:44
  163.6 17.7 %collective-permute-start.44 = (bf16[8,256,128]{2,1,0:T(8,128)(2,1)S(1)}, bf16[8,256,128]{2,1,0:T(8,128)(2,1)S(1)}, u32[]{:S(2)}, u32[]{:S(2)}) collective-permute-start(bf16[8,256,128]{2,1,0:T(8,128)(2,1)S(1)} %pad_maximum_fusion.4.rest_6_.rest_7_), channel_id=1, source_target_pairs={{0,32},{32,0},{64,96},{96,64},{1,33},{33,1},{65,97},{97,65},{2,34}... | collective-permute-start | bytes 1572872 | tf_op jit(solution)/shard_map/ppermute | solution.py:44
  164.7 17.4 %collective-permute-start.31 = (bf16[8,256,128]{2,1,0:T(8,128)(2,1)S(1)}, bf16[8,256,128]{2,1,0:T(8,128)(2,1)}, u32[]{:S(2)}, u32[]{:S(2)}) collective-permute-start(bf16[8,256,128]{2,1,0:T(8,128)(2,1)S(1)} %pad_maximum_fusion.1.rest_0_.rest_1_), channel_id=1, source_target_pairs={{0,24},{8,16},{16,8},{24,0},{1,25},{9,17},{17,9},{25,1},{2,26},{10... | collective-permute-start | bytes 1572872 | tf_op jit(solution)/shard_map/ppermute | solution.py:44
  166.4 15.7 %collective-permute-start.35 = (bf16[8,256,128]{2,1,0:T(8,128)(2,1)S(1)}, bf16[8,256,128]{2,1,0:T(8,128)(2,1)}, u32[]{:S(2)}, u32[]{:S(2)}) collective-permute-start(bf16[8,256,128]{2,1,0:T(8,128)(2,1)S(1)} %pad_maximum_fusion.2.rest_2_.rest_3_), channel_id=1, source_target_pairs={{0,8},{8,0},{16,24},{24,16},{1,9},{9,1},{17,25},{25,17},{2,10},{10... | collective-permute-start | bytes 1572872 | tf_op jit(solution)/shard_map/ppermute | solution.py:44
  (23 other events, 148.3 us)
Sparse Core Ops, SparseCore 0:
  32.5 13.3 all-gather.3
  116.5 64.6 all-gather.5

commit v7 on v6

--- a/solution.py
+++ b/solution.py
@@ -29,29 +29,16 @@
     return permute(value, [((a, j, k), (b, j, k)) for a, b in planes for j, k in ALL])
 
 
-def ring(value, axis, step):
-    return lax.ppermute(value, axis, [(i, (i + step) % 4) for i in range(4)])
-
-
-def ring_gather(value, axis):
-    at = lax.axis_index(axis)
-    parts = [value] + [ring(value, axis, 4 - d) for d in (1, 2, 3)]
-    both = jnp.stack(parts + parts[:3])
-    return lax.dynamic_slice_in_dim(both, (4 - at) % 4, 4, 0)
-
-
 def swap(value, axis, flip):
     return lax.ppermute(value, axis, [(i, i ^ flip) for i in range(4)])
 
 
-def spread(parts, whole):
+def spread(parts):
     parts = [p[None] for p in parts]
     for step in range(3):
         got = [swap(p, *order[step]) for p, order in zip(parts, ORDERS)]
         parts = [jnp.concatenate([p, g], axis=0) for p, g in zip(parts, got)]
-    got = [swap(p, *order[3]) for p, order in zip(parts, ORDERS)]
-    whole, *got = lax.optimization_barrier((whole, *got))
-    return parts, got, whole
+    return parts, [swap(p, *order[3]) for p, order in zip(parts, ORDERS)]
 
 
 def places(y, z):
@@ -78,7 +65,7 @@
     for u in range(12):
         rows = slice(base + u % 2 * 32, base + u % 2 * 32 + 32)
         at = 512 + u % 3 * 32
-        out_ref[at:at + 32, u // 3 * 128:(u // 3 + 1) * 128] = factor_ref[rows, u // 2 * 128:(u // 2 + 1) * 128]
+        out_ref[at:at + 32, u // 3 * 128:(u // 3 + 1) * 128] = factor_ref[0, rows, u // 2 * 128:(u // 2 + 1) * 128]
 
 
 def load_kernel(rhs_ref, factor_ref, *outs):
@@ -97,7 +84,7 @@
     return pl.pallas_call(
         load_kernel,
         grid=(1,),
-        in_specs=[pl.BlockSpec((1, 512, 2048), lambda i: (0, 0, 0)), pl.BlockSpec((512, 1024), lambda i: (0, 0))],
+        in_specs=[pl.BlockSpec((1, 512, 2048), lambda i: (0, 0, 0)), pl.BlockSpec((1, 512, 1024), lambda i: (0, 0, 0))],
         out_specs=[pl.BlockSpec((608, 512), lambda i: (0, 0))] * 8,
         out_shape=[jax.ShapeDtypeStruct((608, 512), BF)] * 8,
         compiler_params=pltpu.CompilerParams(vmem_limit_bytes=48 << 20),
@@ -114,14 +101,22 @@
     sent_ref[...] = solve(high_ref, low_ref, state_ref[...])
 
 
-def step_kernel(panel, scalars, state_ref, high_ref, low_ref, mine_ref, other_ref, *refs):
+def step_kernel(panel, scalars, state_ref, high_ref, low_ref, *refs):
     dot = lambda a, b: jnp.dot(a, b, preferred_element_type=F32)
-    swap = scalars[0] == 1
-    left = jnp.where(swap, other_ref[0], mine_ref[0])
-    right = jnp.where(swap, mine_ref[0], other_ref[0])
+    pieces, refs, block_ref = refs[:4], refs[4:-1], refs[-1]
+    core = scalars[0]
+    for source in range(2):
+        half = core if source == 0 else 1 - core
+        for side in range(2):
+            for i in range(4):
+                off = scalars[2 + side] ^ i
+                at = off ^ (off >> 1)
+                rows = slice(side * 256 + i * 64, side * 256 + i * 64 + 64)
+                for h in range(2):
+                    block_ref[half, rows, h * 128:(h + 1) * 128] = pieces[2 * source + side][at, 0, h * 64:(h + 1) * 64]
     gots = refs[:3 - panel]
     got = sum(g[...] for g in gots)
-    state = state_ref[...] - dot(left, got[:256]) - dot(right, got[256:])
+    state = state_ref[...] - dot(block_ref[0], got[:256]) - dot(block_ref[1], got[256:])
     here = scalars[1] == panel
     if panel == 0:
         sent_ref, next_ref, new_ref, done_ref = refs[3:]
@@ -138,13 +133,15 @@
 
 def step(scalars, state, inverse, factor=None, panel=None, more=()):
     full = lambda shape: pl.BlockSpec(shape, lambda i, s: (0, 0))
-    part = pl.BlockSpec((1, 512, 256), lambda i, s: (panel, 0, 0))
+    part = pl.BlockSpec((4, 1, 128, 128), lambda i, s: (0, panel, 0, 0))
     tall, square = full((512, 128)), full((512, 512))
     shapes = [jax.ShapeDtypeStruct((512, 128), BF)]
+    scratch = []
     if panel is None:
         kernel, ins, factor = first_kernel, [], ()
     else:
-        kernel, ins = lambda *refs: step_kernel(panel, *refs), [part, part] + [tall] * len(more)
+        kernel, ins = lambda *refs: step_kernel(panel, *refs), [part] * 4 + [tall] * len(more)
+        scratch = [pltpu.VMEM((2, 512, 256), BF)]
         shapes = [jax.ShapeDtypeStruct((512, 128), F32)] + shapes
         if panel < 2:
             shapes.append(jax.ShapeDtypeStruct((512 * (panel + 1), 128), BF))
@@ -155,40 +152,46 @@
             grid=(1,),
             in_specs=[tall, square, square] + ins,
             out_specs=[full(v.shape) for v in shapes],
+            scratch_shapes=scratch,
         ),
         out_shape=shapes,
         compiler_params=pltpu.CompilerParams(vmem_limit_bytes=32 << 20),
     )(scalars, state, *inverse, *factor, *more)
 
 
-def update_kernel(scalars, factor_ref, rhs_ref, early_ref, *rest):
+def update_kernel(scalars, mine_ref, other_ref, rhs_ref, early_ref, *rest):
     near, far, out_ref, sent_ref = rest[:8], rest[8:16], rest[16], rest[17]
     j = pl.program_id(0)
+    place, core = scalars[64], scalars[65]
+
+    def rows(panel, half):
+        return pl.ds(pl.multiple_of((core ^ half) * 1024 + panel * 256, 256), 256)
+
     for h in range(2):
         lanes = slice(h * 128, (h + 1) * 128)
-        sent_ref[:1024, lanes] = early_ref[h]
         for p in range(4):
-            rows = slice(1024 + p * 256, 1280 + p * 256)
+            sent_ref[rows(p // 2, p % 2), lanes] = early_ref[h, p * 256:(p + 1) * 256]
             low = scalars[p * 16 + 2 * j + h] < 8
 
             @pl.when(low)
             def _():
-                sent_ref[rows, lanes] = near[p * 2 + h][0]
+                sent_ref[rows(2 + p // 2, p % 2), lanes] = near[p * 2 + h][0]
 
             @pl.when(jnp.logical_not(low))
             def _():
-                sent_ref[rows, lanes] = far[p * 2 + h][0]
+                sent_ref[rows(2 + p // 2, p % 2), lanes] = far[p * 2 + h][0]
+    dot = lambda a, b: jnp.dot(a, b, preferred_element_type=F32)
     for c in range(2):
-        out_ref[c] = rhs_ref[c] - jnp.dot(factor_ref[c], sent_ref[...], preferred_element_type=F32)
-    place = scalars[64]
+        out_ref[c] = rhs_ref[c] - (dot(mine_ref[c], sent_ref[:1024]) + dot(other_ref[c], sent_ref[1024:]))
 
     @pl.when(place < 4)
     def _():
-        out_ref[0] = sent_ref[pl.ds(pl.multiple_of(place * 512, 512), 512), :].astype(F32)
-
-
-def update(scalars, factor, rhs, early, near, far):
-    cycles, tile, depth = factor.shape
+        for half in range(2):
+            out_ref[0, half * 256:(half + 1) * 256] = sent_ref[rows(place, half), :].astype(F32)
+
+
+def update(scalars, mine, other, rhs, early, near, far):
+    cycles, tile, depth = mine.shape
     pairs = [(p, h) for p in range(4) for h in range(2)]
     near_specs = [
         pl.BlockSpec((1, 256, 128), lambda j, s, p=p, h=h: (jnp.minimum(s[p * 16 + 2 * j + h], 7), 0, 0))
@@ -205,15 +208,16 @@
             grid=(rhs.shape[2] // 256,),
             in_specs=[
                 pl.BlockSpec((cycles, tile, depth), lambda j, s: (0, 0, 0)),
+                pl.BlockSpec((cycles, tile, depth), lambda j, s: (0, 0, 0)),
                 pl.BlockSpec((cycles, tile, 256), lambda j, s: (0, 0, j)),
                 pl.BlockSpec((2, 1024, 128), lambda j, s: (j, 0, 0)),
             ] + near_specs + far_specs,
             out_specs=pl.BlockSpec((cycles, tile, 256), lambda j, s: (0, 0, j)),
-            scratch_shapes=[pltpu.VMEM((depth, 256), BF)],
+            scratch_shapes=[pltpu.VMEM((2 * depth, 256), BF)],
         ),
         out_shape=jax.ShapeDtypeStruct(rhs.shape, F32),
         compiler_params=pltpu.CompilerParams(vmem_limit_bytes=48 << 20),
-    )(scalars, factor, rhs, early, *[near[p] for p, _ in pairs], *[far[p] for p, _ in pairs])
+    )(scalars, mine, other, rhs, early, *[near[p] for p, _ in pairs], *[far[p] for p, _ in pairs])
 
 
 def local(rhs, factor, inverses):
@@ -223,8 +227,9 @@
     owner = place < 4
     zero = jnp.zeros((), BF)
 
-    tile = factor[0].reshape(512, 1024)
-    slabs = loads(rhs, tile)
+    flat_factor = factor.reshape(2, 512, 1024)
+    other_factor = lax.ppermute(flat_factor, "rhs", [(0, 1), (1, 0)])
+    slabs = loads(rhs, flat_factor)
     outward = {
         (p, d): permute(slabs[4 * p + d], [((i, 0, 0), (i, 0, d) if p else (i, d, 0)) for i in range(4)])
         for p, d in ((0, 3), (0, 1), (1, 1), (0, 2), (1, 2), (1, 3))
@@ -245,29 +250,28 @@
             mine = mine + permute(message(d), moves)
         return mine
 
-    whole = lax.all_gather(factor, "rhs", axis=3, tiled=True)
-    tiles = jnp.arange(2, dtype=jnp.int32) * 64 + place
-    keep = tiles[:, None] > jnp.arange(4, dtype=jnp.int32)[None]
-    whole = jnp.where(keep[:, None, :, None], whole, zero).reshape(2, 512, 2048)
-
     mine_a = finish(hold_a, "y")
     mine_b = finish(hold_b, "z")
 
     inverse = lax.dynamic_index_in_dim(inverses, x, 0, keepdims=False)
     rounded = lax.reduce_precision(inverse, 8, 7)
     inverse = (rounded.astype(BF), (inverse - rounded).astype(BF))
-    where = jnp.stack([core, x]).astype(jnp.int32)
+    where = jnp.stack([core, x, y, z]).astype(jnp.int32)
     state = mine_a[:512].astype(F32) + mine_b[:512].astype(F32)
     state, *inverse = lax.optimization_barrier((state, *inverse))
     sent_0, = step(where, state, inverse)
     gots = [hop(sent_0, (0, 1)), hop(sent_0, (0, 3)), hop(sent_0, (0, 2))]
 
     piece_a, piece_b, _ = lax.optimization_barrier((mine_a[512:], mine_b[512:], sent_0))
-    top = ring_gather(piece_a, "y")
-    bottom = ring_gather(piece_b, "z")
-    half = jnp.concatenate([top, bottom], axis=0).reshape(8, 3, 2, 64, 128).transpose(1, 0, 3, 2, 4).reshape(3, 512, 256)
-    half, *gots = lax.optimization_barrier((half, *gots))
-    block = (half, lax.ppermute(half, "rhs", [(0, 1), (1, 0)]))
+    near_a, near_b = swap(piece_a, "y", 1), swap(piece_b, "z", 1)
+    near_a, near_b, *gots = lax.optimization_barrier((near_a, near_b, *gots))
+
+    def complete(piece, near, axis):
+        two = jnp.stack([piece, near])
+        return jnp.concatenate([two, swap(two, axis, 3)], axis=0).reshape(4, 3, 128, 128)
+
+    top, bottom = complete(piece_a, near_a, "y"), complete(piece_b, near_b, "z")
+    block = (top, bottom, lax.ppermute(top, "rhs", [(0, 1), (1, 0)]), lax.ppermute(bottom, "rhs", [(0, 1), (1, 0)]))
 
     state, sent_1, panel_0 = step(where, state, inverse, block, 0, (*gots, sent_0))
     gots = [hop(sent_1, (1, 2)), hop(sent_1, (1, 3))]
@@ -283,10 +287,10 @@
     wrap = hop(sent, (3, 0))
     panel_2 = jnp.where(x == 2, sent, jnp.where(x == 3, got, jnp.where(x == 1, back, far)))
     panel_3 = jnp.where(x == 3, sent, jnp.where(x == 2, back, jnp.where(x == 1, far, wrap)))
-    near, far_late, whole = spread([panel_2[:256], panel_2[256:], panel_3[:256], panel_3[256:]], whole)
-
-    scalars = jnp.concatenate([places(y, z), place[None]]).astype(jnp.int32)
-    return update(scalars, whole, rhs, early, near, far_late)
+    near, far_late = spread([panel_2[:256], panel_2[256:], panel_3[:256], panel_3[256:]])
+
+    scalars = jnp.concatenate([places(y, z), jnp.stack([place, core])]).astype(jnp.int32)
+    return update(scalars, flat_factor, other_factor, rhs, early, near, far_late)
 
 
 def solution(mesh):

time: 210 us -> 206 us (0.981)
  local copies, waits for them, and re-layouts: 11.6 us -> 4.95 us
  waiting for transfers between devices: 77.3 us -> 83.6 us
  other arithmetic: 11.8 us -> 5.54 us
  starting transfers between devices: 63.4 us -> 65.9 us
    ppermute x16 -> x20, waiting for transfers between devices: 16.2 us -> 34.2 us  [swap(): return lax.ppermute(value, axis, [(i, i ^ flip) for i in range(4)])]
    ppermute x7 -> x3, waiting for transfers between devices: 12.9 us -> 1.65 us  [the longest x1 1.09 us: local(): lax.ppermute(bottom, 'rhs', [(0, 1), (1, 0)])]
    ppermute x16 -> x20, starting transfers between devices: 19.4 us -> 27.8 us  [swap(): return lax.ppermute(value, axis, [(i, i ^ flip) for i in range(4)])]
    select_n x1 -> x0, other arithmetic: 6.01 us -> none  [local(): whole = jnp.where(keep[:, None, :, None], whole, zero).reshape(2, 512, 2048)]
    ppermute x7 -> x3, starting transfers between devices: 6.53 us -> 0.74 us  [the longest x1 0.56 us: local(): lax.ppermute(top, 'rhs', [(0, 1), (1, 0)])]
    reshape x3 -> x1, local copies, waits for them, and re-layouts: 9.08 us -> 4.47 us  [local(): flat_factor = factor.reshape(2, 512, 1024)]
  transfers between devices with their start and end apart: 47 -> 46, of which waited for: 21 -> 23; matrix products, arithmetic and copies ran while one was open for 10% -> 2% of each run, Pallas kernels for 3% -> 1%
where the time goes in v7:
time: 206 us; the launch traced here: 203 us
  waiting for transfers between devices  83.6 us (41%)
  starting transfers between devices  65.9 us (32%)
  Pallas kernels  29.3 us (14%)
  between operations  13.9 us (7%)
  other arithmetic  5.54 us (3%)
  local copies, waits for them, and re-layouts  4.95 us (2%)
    ppermute x22, waiting for transfers between devices, permute(): return lax.ppermute(value, ROWS, [(flat(*a), flat(*b)) for a, b in moves])  47.7 us
    ppermute x22, starting transfers between devices, permute(): return lax.ppermute(value, ROWS, [(flat(*a), flat(*b)) for a, b in moves])  37.4 us
    ppermute x20, waiting for transfers between devices, swap(): return lax.ppermute(value, axis, [(i, i ^ flip) for i in range(4)])  34.2 us
    ppermute x20, starting transfers between devices, swap(): return lax.ppermute(value, axis, [(i, i ^ flip) for i in range(4)])  27.8 us
    pallas_call x1, Pallas kernels, update(): pl.pallas_call(update_kernel, grid_spec=pltpu.PrefetchScalarGridSpec(num_...  17.9 us
    pallas_call x4, Pallas kernels, step(): pl.pallas_call(kernel, grid_spec=pltpu.PrefetchScalarGridSpec(num_scalar_...  7.04 us
    reshape x1, local copies, waits for them, and re-layouts, local(): flat_factor = factor.reshape(2, 512, 1024)  4.47 us
    pallas_call x1, Pallas kernels, loads(): pl.pallas_call(load_kernel, grid=(1,), in_specs=[pl.BlockSpec((1, 512, 20...  4.29 us
  transfers between devices with their start and end apart: 46, of which 23 were waited for; matrix products, arithmetic and copies ran while one was open for 2% of the time, Pallas kernels for 1%

profile of v7, /device:TPU:6, one launch (start us, length us, event | category | flops | bytes accessed | tf_op | source)
XLA Modules:
  0.0 203.1 jit_solution(11637200529541001103)
XLA Ops:
  6.5 4.5 %reshape.179.factor_ref.mine_ref = bf16[2,512,1024]{2,1,0:T(8,128)(2,1)} reshape(bf16[2,512,4,256]{3,2,1,0:T(4,128)(2,1)} %param.4) | data formatting | bytes 4194304 | tf_op jit(solution)/shard_map/reshape | solution.py:230
  11.0 4.3 %shard_map.37 = (bf16[608,512]{1,0:T(8,128)(2,1)S(1)}, bf16[608,512]{1,0:T(8,128)(2,1)S(1)}, bf16[608,512]{1,0:T(8,128)(2,1)}, bf16[608,512]{1,0:T(8,128)(2,1)},...) custom-call(f32[2,512,2048]{2,1,0:T(8,128)} %rhs_ref.3, ...), custom_call_target="tpu_custom_call" | custom-call | tf_op jit(solution)/shard_map/pallas_call | solution.py:84
  15.3 4.4 %collective-permute-start.1 = (bf16[608,512]{1,0:T(8,128)(2,1)S(1)}, bf16[608,512]{1,0:T(8,128)(2,1)}, u32[]{:S(2)}, u32[]{:S(2)}) collective-permute-start(bf16[608,512]{1,0:T(8,128)(2,1)S(1)} %get-tuple-element.34), channel_id=1, source_target_pairs={{0,32},{2,34},{4,36},{6,38},{1,33},{3,35},{5,37},{7,39}} | collective-permute-start | bytes 1867784 | tf_op jit(solution)/shard_map/ppermute | solution.py:25
  19.7 3.1 %collective-permute-start.2 = (bf16[608,512]{1,0:T(8,128)(2,1)}, bf16[608,512]{1,0:T(8,128)(2,1)}, u32[]{:S(2)}, u32[]{:S(2)}) collective-permute-start(bf16[608,512]{1,0:T(8,128)(2,1)} %get-tuple-element.35), channel_id=1, source_target_pairs={{0,64},{2,66},{4,68},{6,70},{1,65},{3,67},{5,69},{7,71}} | collective-permute-start | bytes 1867784 | tf_op jit(solution)/shard_map/ppermute | solution.py:25
  28.3 4.9 %collective-permute-done.1 = bf16[608,512]{1,0:T(8,128)(2,1)} collective-permute-done((bf16[608,512]{1,0:T(8,128)(2,1)S(1)}, bf16[608,512]{1,0:T(8,128)(2,1)}, u32[]{:S(2)}, u32[]{:S(2)}) %collective-permute-start.1) | collective-permute-done | bytes 622624 | tf_op jit(solution)/shard_map/ppermute | solution.py:25
  36.8 8.7 %collective-permute-done.2 = bf16[608,512]{1,0:T(8,128)(2,1)} collective-permute-done((bf16[608,512]{1,0:T(8,128)(2,1)}, bf16[608,512]{1,0:T(8,128)(2,1)}, u32[]{:S(2)}, u32[]{:S(2)}) %collective-permute-start.2) | collective-permute-done | bytes 622624 | tf_op jit(solution)/shard_map/ppermute | solution.py:25
  47.1 6.0 %collective-permute-done.8 = bf16[608,512]{1,0:T(8,128)(2,1)} collective-permute-done((bf16[608,512]{1,0:T(8,128)(2,1)}, bf16[608,512]{1,0:T(8,128)(2,1)}, u32[]{:S(2)}, u32[]{:S(2)}) %collective-permute-start.8) | collective-permute-done | bytes 622624 | tf_op jit(solution)/shard_map/ppermute | solution.py:25
  60.3 5.3 %collective-permute-start.6 = (bf16[896,128]{1,0:T(8,128)(2,1)S(1)}, bf16[896,128]{1,0:T(8,128)(2,1)S(1)}, u32[]{:S(2)}, u32[]{:S(2)}) collective-permute-start(bf16[896,128]{1,0:T(8,128)(2,1)S(1)} %get-tuple-element.77), channel_id=1, source_target_pairs={{0,16},{32,48},{64,80},{96,112},{2,18},{34,50},{66,82},{98,114},{4... | collective-permute-start | bytes 688136 | tf_op jit(solution)/shard_map/ppermute | solution.py:25
  67.0 4.5 %collective-permute-done.6 = bf16[896,128]{1,0:T(8,128)(2,1)S(1)} collective-permute-done((bf16[896,128]{1,0:T(8,128)(2,1)S(1)}, bf16[896,128]{1,0:T(8,128)(2,1)S(1)}, u32[]{:S(2)}, u32[]{:S(2)}) %collective-permute-start.6) | collective-permute-done | bytes 229408 | tf_op jit(solution)/shard_map/ppermute | solution.py:25
  71.6 2.8 %collective-permute-done.4 = bf16[896,128]{1,0:T(8,128)(2,1)S(1)} collective-permute-done((bf16[896,128]{1,0:T(8,128)(2,1)S(1)}, bf16[896,128]{1,0:T(8,128)(2,1)S(1)}, u32[]{:S(2)}, u32[]{:S(2)}) %collective-permute-start.4) | collective-permute-done | bytes 229408 | tf_op jit(solution)/shard_map/ppermute | solution.py:25
  78.5 2.6 %collective-permute-start.14 = (bf16[384,128]{1,0:T(8,128)(2,1)S(1)}, bf16[384,128]{1,0:T(8,128)(2,1)S(1)}, u32[]{:S(2)}, u32[]{:S(2)}) collective-permute-start(bf16[384,128]{1,0:T(8,128)(2,1)S(1)} %slice.109), channel_id=1, source_target_pairs={{0,8},{8,0},{16,24},{24,16},{1,9},{9,1},{17,25},{25,17},{2,10},{10... | collective-permute-start | bytes 294920 | tf_op jit(solution)/shard_map/ppermute | solution.py:33
  85.6 6.7 %collective-permute-done.19 = bf16[2,384,128]{2,1,0:T(8,128)(2,1)S(1)} collective-permute-done((bf16[2,384,128]{2,1,0:T(8,128)(2,1)S(1)}, bf16[2,384,128]{2,1,0:T(8,128)(2,1)S(1)}, u32[]{:S(2)}, u32[]{:S(2)}) %collective-permute-start.19) | collective-permute-done | bytes 196640 | tf_op jit(solution)/shard_map/ppermute | solution.py:33
  99.1 10.7 %collective-permute-done.23.refs_9_ = bf16[512,128]{1,0:T(8,128)(2,1)S(1)} collective-permute-done((bf16[512,128]{1,0:T(8,128)(2,1)S(1)}, bf16[512,128]{1,0:T(8,128)(2,1)S(1)}, u32[]{:S(2)}, u32[]{:S(2)}) %collective-permute-start.23) | collective-permute-done | bytes 131104 | tf_op jit(solution)/shard_map/ppermute | solution.py:25
  109.8 2.3 %shard_map.40 = (f32[512,128]{1,0:T(8,128)S(1)}, bf16[512,128]{1,0:T(8,128)(2,1)S(1)}, bf16[1024,128]{1,0:T(8,128)(2,1)}) custom-call(s32[4]{0:T(128)S(1)} %pad_add_fusion.2.scalars.refs_0_, f32[512,128]{1,0:T(8,128)S(1)} %get-tuple-element.52.refs_1_, bf16[512,512]{1,0:T(8,128)(2,1)S(1)} %get-tuple-element.43.high_ref.refs_2_, ...), custom_call_target="tpu_custom_call" | custom-call | tf_op jit(solution)/shard_map/pallas_call | solution.py:148
  113.5 5.6 %collective-permute-done.25.refs_8_ = bf16[512,128]{1,0:T(8,128)(2,1)S(1)} collective-permute-done((bf16[512,128]{1,0:T(8,128)(2,1)S(1)}, bf16[512,128]{1,0:T(8,128)(2,1)S(1)}, u32[]{:S(2)}, u32[]{:S(2)}) %collective-permute-start.25) | collective-permute-done | bytes 131104 | tf_op jit(solution)/shard_map/ppermute | solution.py:25
  128.0 2.9 %collective-permute-start.38 = (bf16[1,256,128]{2,1,0:T(8,128)(2,1)S(1)}, bf16[1,256,128]{2,1,0:T(8,128)(2,1)S(1)}, u32[]{:S(2)}, u32[]{:S(2)}) collective-permute-start(bf16[1,256,128]{2,1,0:T(8,128)(2,1)S(1)} %get-tuple-element.97), channel_id=1, source_target_pairs={{0,24},{8,16},{16,8},{24,0},{1,25},{9,17},{17,9},{25,1},{2,26},{10... | collective-permute-start | bytes 196616 | tf_op jit(solution)/shard_map/ppermute | solution.py:33
  137.9 2.3 %collective-permute-start.29 = (bf16[2,256,128]{2,1,0:T(8,128)(2,1)S(1)}, bf16[2,256,128]{2,1,0:T(8,128)(2,1)S(1)}, u32[]{:S(2)}, u32[]{:S(2)}) collective-permute-start(bf16[2,256,128]{2,1,0:T(8,128)(2,1)S(1)} %pad_maximum_fusion.12), channel_id=1, source_target_pairs={{0,96},{32,64},{64,32},{96,0},{1,97},{33,65},{65,33},{97,1},{2,98}... | collective-permute-start | bytes 393224 | tf_op jit(solution)/shard_map/ppermute | solution.py:33
  142.3 3.1 %collective-permute-start.40 = (bf16[4,256,128]{2,1,0:T(8,128)(2,1)S(1)}, bf16[4,256,128]{2,1,0:T(8,128)(2,1)S(1)}, u32[]{:S(2)}, u32[]{:S(2)}) collective-permute-start(bf16[4,256,128]{2,1,0:T(8,128)(2,1)S(1)} %pad_maximum_fusion.9), channel_id=1, source_target_pairs={{0,96},{32,64},{64,32},{96,0},{1,97},{33,65},{65,33},{97,1},{2,98}... | collective-permute-start | bytes 786440 | tf_op jit(solution)/shard_map/ppermute | solution.py:33
  146.3 2.3 %collective-permute-start.33 = (bf16[4,256,128]{2,1,0:T(8,128)(2,1)S(1)}, bf16[4,256,128]{2,1,0:T(8,128)(2,1)S(1)}, u32[]{:S(2)}, u32[]{:S(2)}) collective-permute-start(bf16[4,256,128]{2,1,0:T(8,128)(2,1)S(1)} %pad_maximum_fusion.7), channel_id=1, source_target_pairs={{0,24},{8,16},{16,8},{24,0},{1,25},{9,17},{17,9},{25,1},{2,26},{10... | collective-permute-start | bytes 786440 | tf_op jit(solution)/shard_map/ppermute | solution.py:33
  148.6 5.5 %collective-permute-done.37 = bf16[4,256,128]{2,1,0:T(8,128)(2,1)S(1)} collective-permute-done((bf16[4,256,128]{2,1,0:T(8,128)(2,1)S(1)}, bf16[4,256,128]{2,1,0:T(8,128)(2,1)S(1)}, u32[]{:S(2)}, u32[]{:S(2)}) %collective-permute-start.37) | collective-permute-done | bytes 262176 | tf_op jit(solution)/shard_map/ppermute | solution.py:33
  154.2 4.4 %collective-permute-start.43 = (bf16[8,256,128]{2,1,0:T(8,128)(2,1)S(1)}, bf16[8,256,128]{2,1,0:T(8,128)(2,1)S(1)}, u32[]{:S(2)}, u32[]{:S(2)}) collective-permute-start(bf16[8,256,128]{2,1,0:T(8,128)(2,1)S(1)} %pad_maximum_fusion.2.rest_4_.rest_5_), channel_id=1, source_target_pairs={{0,96},{32,64},{64,32},{96,0},{1,97},{33,65},{65,33},{97,1},{2,98}... | collective-permute-start | bytes 1572872 | tf_op jit(solution)/shard_map/ppermute | solution.py:33
  160.0 2.4 %collective-permute-start.41 = (bf16[8,256,128]{2,1,0:T(8,128)(2,1)S(1)}, bf16[8,256,128]{2,1,0:T(8,128)(2,1)}, u32[]{:S(2)}, u32[]{:S(2)}) collective-permute-start(bf16[8,256,128]{2,1,0:T(8,128)(2,1)S(1)} %pad_maximum_fusion.rest_0_.rest_1_), channel_id=1, source_target_pairs={{0,24},{8,16},{16,8},{24,0},{1,25},{9,17},{17,9},{25,1},{2,26},{10... | collective-permute-start | bytes 1572872 | tf_op jit(solution)/shard_map/ppermute | solution.py:33
  163.1 14.1 %collective-permute-done.43.rest_12_.rest_13_ = bf16[8,256,128]{2,1,0:T(8,128)(2,1)S(1)} collective-permute-done((bf16[8,256,128]{2,1,0:T(8,128)(2,1)S(1)}, bf16[8,256,128]{2,1,0:T(8,128)(2,1)S(1)}, u32[]{:S(2)}, u32[]{:S(2)}) %collective-permute-start.43) | collective-permute-done | bytes 524320 | tf_op jit(solution)/shard_map/ppermute | solution.py:33
  178.3 17.9 %shard_map.42 = f32[2,512,2048]{2,1,0:T(8,128)} custom-call(s32[66]{0:T(128)S(1)} %pad_add_fusion.1.scalars, bf16[2,512,1024]{2,1,0:T(8,128)(2,1)} %reshape.179.factor_ref.mine_ref, bf16[2,512,1024]{2,1,0:T(8,128)(2,1)} %collective-permute-done.other_ref, f32[2,512,2048]{2,1,0:T(8,128)} %rhs_ref.3, bf16[16,1024,128]{2,1,0:T(8,128)(2,1)} %bitcast.27, ...), custom_call_target="tpu_custom_call" | custom-call | tf_op jit(solution)/shard_map/pallas_call | solution.py:204
  (124 shorter events, 57.9 us)
Async XLA Ops:
  6.5 171.8 %all-gather.3.cloned.1.call-start = ((), (), s32[]{:S(2)}) async-start(), calls=%async_computation | async-start | bytes 4456448 | tf_op jit(solution)/shard_map/all_gather | solution.py:280
  15.3 17.9 %collective-permute-start.1 = (bf16[608,512]{1,0:T(8,128)(2,1)S(1)}, bf16[608,512]{1,0:T(8,128)(2,1)}, u32[]{:S(2)}, u32[]{:S(2)}) collective-permute-start(bf16[608,512]{1,0:T(8,128)(2,1)S(1)} %get-tuple-element.34), channel_id=1, source_target_pairs={{0,32},{2,34},{4,36},{6,38},{1,33},{3,35},{5,37},{7,39}} | collective-permute-start | bytes 1867784 | tf_op jit(solution)/shard_map/ppermute | solution.py:25
  19.7 25.8 %collective-permute-start.2 = (bf16[608,512]{1,0:T(8,128)(2,1)}, bf16[608,512]{1,0:T(8,128)(2,1)}, u32[]{:S(2)}, u32[]{:S(2)}) collective-permute-start(bf16[608,512]{1,0:T(8,128)(2,1)} %get-tuple-element.35), channel_id=1, source_target_pairs={{0,64},{2,66},{4,68},{6,70},{1,65},{3,67},{5,69},{7,71}} | collective-permute-start | bytes 1867784 | tf_op jit(solution)/shard_map/ppermute | solution.py:25
  22.7 22.7 %collective-permute-start.3 = (bf16[608,512]{1,0:T(8,128)(2,1)}, bf16[608,512]{1,0:T(8,128)(2,1)}, u32[]{:S(2)}, u32[]{:S(2)}) collective-permute-start(bf16[608,512]{1,0:T(8,128)(2,1)} %get-tuple-element.36), channel_id=1, source_target_pairs={{0,96},{2,98},{4,100},{6,102},{1,97},{3,99},{5,101},{7,103}} | collective-permute-start | bytes 1867784 | tf_op jit(solution)/shard_map/ppermute | solution.py:25
  24.9 22.2 %collective-permute-start.7 = (bf16[608,512]{1,0:T(8,128)(2,1)}, bf16[608,512]{1,0:T(8,128)(2,1)S(1)}, u32[]{:S(2)}, u32[]{:S(2)}) collective-permute-start(bf16[608,512]{1,0:T(8,128)(2,1)} %get-tuple-element.39), channel_id=1, source_target_pairs={{0,8},{2,10},{4,12},{6,14},{1,9},{3,11},{5,13},{7,15}} | collective-permute-start | bytes 1867784 | tf_op jit(solution)/shard_map/ppermute | solution.py:25
  26.2 26.9 %collective-permute-start.8 = (bf16[608,512]{1,0:T(8,128)(2,1)}, bf16[608,512]{1,0:T(8,128)(2,1)}, u32[]{:S(2)}, u32[]{:S(2)}) collective-permute-start(bf16[608,512]{1,0:T(8,128)(2,1)} %get-tuple-element.40), channel_id=1, source_target_pairs={{0,16},{2,18},{4,20},{6,22},{1,17},{3,19},{5,21},{7,23}} | collective-permute-start | bytes 1867784 | tf_op jit(solution)/shard_map/ppermute | solution.py:25
  33.2 19.9 %collective-permute-start.9 = (bf16[608,512]{1,0:T(8,128)(2,1)S(1)}, bf16[608,512]{1,0:T(8,128)(2,1)}, u32[]{:S(2)}, u32[]{:S(2)}) collective-permute-start(bf16[608,512]{1,0:T(8,128)(2,1)S(1)} %get-tuple-element.41), channel_id=1, source_target_pairs={{0,24},{2,26},{4,28},{6,30},{1,25},{3,27},{5,29},{7,31}} | collective-permute-start | bytes 1867784 | tf_op jit(solution)/shard_map/ppermute | solution.py:25
  54.8 10.8 %collective-permute-start.11 = (bf16[896,128]{1,0:T(8,128)(2,1)S(1)}, bf16[896,128]{1,0:T(8,128)(2,1)S(1)}, u32[]{:S(2)}, u32[]{:S(2)}) collective-permute-start(bf16[896,128]{1,0:T(8,128)(2,1)S(1)} %get-tuple-element.93), channel_id=1, source_target_pairs={{0,96},{8,104},{16,112},{24,120},{2,98},{10,106},{18,114},{26,122}... | collective-permute-start | bytes 688136 | tf_op jit(solution)/shard_map/ppermute | solution.py:25
  56.1 10.8 %collective-permute-start.12 = (bf16[896,128]{1,0:T(8,128)(2,1)S(1)}, bf16[896,128]{1,0:T(8,128)(2,1)S(1)}, u32[]{:S(2)}, u32[]{:S(2)}) collective-permute-start(bf16[896,128]{1,0:T(8,128)(2,1)S(1)} %get-tuple-element.94), channel_id=1, source_target_pairs={{0,64},{8,72},{16,80},{24,88},{2,66},{10,74},{18,82},{26,90},{4,68... | collective-permute-start | bytes 688136 | tf_op jit(solution)/shard_map/ppermute | solution.py:25
  57.4 9.5 %collective-permute-start.10 = (bf16[896,128]{1,0:T(8,128)(2,1)S(1)}, bf16[896,128]{1,0:T(8,128)(2,1)S(1)}, u32[]{:S(2)}, u32[]{:S(2)}) collective-permute-start(bf16[896,128]{1,0:T(8,128)(2,1)S(1)} %get-tuple-element.84), channel_id=1, source_target_pairs={{0,32},{8,40},{16,48},{24,56},{2,34},{10,42},{18,50},{26,58},{4,36... | collective-permute-start | bytes 688136 | tf_op jit(solution)/shard_map/ppermute | solution.py:25
  60.3 11.3 %collective-permute-start.6 = (bf16[896,128]{1,0:T(8,128)(2,1)S(1)}, bf16[896,128]{1,0:T(8,128)(2,1)S(1)}, u32[]{:S(2)}, u32[]{:S(2)}) collective-permute-start(bf16[896,128]{1,0:T(8,128)(2,1)S(1)} %get-tuple-element.77), channel_id=1, source_target_pairs={{0,16},{32,48},{64,80},{96,112},{2,18},{34,50},{66,82},{98,114},{4... | collective-permute-start | bytes 688136 | tf_op jit(solution)/shard_map/ppermute | solution.py:25
  76.4 9.0 %collective-permute-start.16 = (bf16[512,128]{1,0:T(8,128)(2,1)S(1)}, bf16[512,128]{1,0:T(8,128)(2,1)S(1)}, u32[]{:S(2)}, u32[]{:S(2)}) collective-permute-start(bf16[512,128]{1,0:T(8,128)(2,1)S(1)} %shard_map.38.refs_11_), channel_id=1, source_target_pairs={{0,6},{8,14},{16,22},{24,30},{32,38},{40,46},{48,54},{56,62},{64,7... | collective-permute-start | bytes 393224 | tf_op jit(solution)/shard_map/ppermute | solution.py:25
  97.1 12.7 %collective-permute-start.23 = (bf16[512,128]{1,0:T(8,128)(2,1)S(1)}, bf16[512,128]{1,0:T(8,128)(2,1)S(1)}, u32[]{:S(2)}, u32[]{:S(2)}) collective-permute-start(bf16[512,128]{1,0:T(8,128)(2,1)S(1)} %get-tuple-element.53.refs_10_), channel_id=1, source_target_pairs={{2,6},{10,14},{18,22},{26,30},{34,38},{42,46},{50,54},{58,62},{66,... | collective-permute-start | bytes 393224 | tf_op jit(solution)/shard_map/ppermute | solution.py:25
  98.4 11.4 %collective-permute-start.22 = (bf16[512,128]{1,0:T(8,128)(2,1)S(1)}, bf16[512,128]{1,0:T(8,128)(2,1)S(1)}, u32[]{:S(2)}, u32[]{:S(2)}) collective-permute-start(bf16[512,128]{1,0:T(8,128)(2,1)S(1)} %get-tuple-element.53.refs_10_), channel_id=1, source_target_pairs={{2,4},{10,12},{18,20},{26,28},{34,36},{42,44},{50,52},{58,60},{66,... | collective-permute-start | bytes 393224 | tf_op jit(solution)/shard_map/ppermute | solution.py:25
  124.9 38.2 %collective-permute-start = (bf16[2,512,1024]{2,1,0:T(8,128)(2,1)}, bf16[2,512,1024]{2,1,0:T(8,128)(2,1)}, u32[]{:S(2)}, u32[]{:S(2)}) collective-permute-start(bf16[2,512,1024]{2,1,0:T(8,128)(2,1)} %reshape.179.factor_ref.mine_ref), channel_id=1, source_target_pairs={{0,1},{1,0},{2,3},{3,2},{4,5},{5,4},{6,7},{7,6},{8,9},{9,8},{10,11... | collective-permute-start | bytes 6291464 | tf_op jit(solution)/shard_map/ppermute | solution.py:231
  133.6 12.7 %collective-permute-start.32 = (bf16[2,256,128]{2,1,0:T(8,128)(2,1)S(1)}, bf16[2,256,128]{2,1,0:T(8,128)(2,1)S(1)}, u32[]{:S(2)}, u32[]{:S(2)}) collective-permute-start(bf16[2,256,128]{2,1,0:T(8,128)(2,1)S(1)} %pad_maximum_fusion.13), channel_id=1, source_target_pairs={{0,32},{32,0},{64,96},{96,64},{1,33},{33,1},{65,97},{97,65},{2,34}... | collective-permute-start | bytes 393224 | tf_op jit(solution)/shard_map/ppermute | solution.py:33
  141.4 12.7 %collective-permute-start.37 = (bf16[4,256,128]{2,1,0:T(8,128)(2,1)S(1)}, bf16[4,256,128]{2,1,0:T(8,128)(2,1)S(1)}, u32[]{:S(2)}, u32[]{:S(2)}) collective-permute-start(bf16[4,256,128]{2,1,0:T(8,128)(2,1)S(1)} %pad_maximum_fusion.8), channel_id=1, source_target_pairs={{0,32},{32,0},{64,96},{96,64},{1,33},{33,1},{65,97},{97,65},{2,34}... | collective-permute-start | bytes 786440 | tf_op jit(solution)/shard_map/ppermute | solution.py:33
  142.3 16.3 %collective-permute-start.40 = (bf16[4,256,128]{2,1,0:T(8,128)(2,1)S(1)}, bf16[4,256,128]{2,1,0:T(8,128)(2,1)S(1)}, u32[]{:S(2)}, u32[]{:S(2)}) collective-permute-start(bf16[4,256,128]{2,1,0:T(8,128)(2,1)S(1)} %pad_maximum_fusion.9), channel_id=1, source_target_pairs={{0,96},{32,64},{64,32},{96,0},{1,97},{33,65},{65,33},{97,1},{2,98}... | collective-permute-start | bytes 786440 | tf_op jit(solution)/shard_map/ppermute | solution.py:33
  145.8 14.1 %collective-permute-start.30 = (bf16[4,256,128]{2,1,0:T(8,128)(2,1)S(1)}, bf16[4,256,128]{2,1,0:T(8,128)(2,1)S(1)}, u32[]{:S(2)}, u32[]{:S(2)}) collective-permute-start(bf16[4,256,128]{2,1,0:T(8,128)(2,1)S(1)} %pad_maximum_fusion.6), channel_id=1, source_target_pairs={{0,8},{8,0},{16,24},{24,16},{1,9},{9,1},{17,25},{25,17},{2,10},{10... | collective-permute-start | bytes 786440 | tf_op jit(solution)/shard_map/ppermute | solution.py:33
  146.3 16.1 %collective-permute-start.33 = (bf16[4,256,128]{2,1,0:T(8,128)(2,1)S(1)}, bf16[4,256,128]{2,1,0:T(8,128)(2,1)S(1)}, u32[]{:S(2)}, u32[]{:S(2)}) collective-permute-start(bf16[4,256,128]{2,1,0:T(8,128)(2,1)S(1)} %pad_maximum_fusion.7), channel_id=1, source_target_pairs={{0,24},{8,16},{16,8},{24,0},{1,25},{9,17},{17,9},{25,1},{2,26},{10... | collective-permute-start | bytes 786440 | tf_op jit(solution)/shard_map/ppermute | solution.py:33
  154.2 23.0 %collective-permute-start.43 = (bf16[8,256,128]{2,1,0:T(8,128)(2,1)S(1)}, bf16[8,256,128]{2,1,0:T(8,128)(2,1)S(1)}, u32[]{:S(2)}, u32[]{:S(2)}) collective-permute-start(bf16[8,256,128]{2,1,0:T(8,128)(2,1)S(1)} %pad_maximum_fusion.2.rest_4_.rest_5_), channel_id=1, source_target_pairs={{0,96},{32,64},{64,32},{96,0},{1,97},{33,65},{65,33},{97,1},{2,98}... | collective-permute-start | bytes 1572872 | tf_op jit(solution)/shard_map/ppermute | solution.py:33
  158.6 18.6 %collective-permute-start.44 = (bf16[8,256,128]{2,1,0:T(8,128)(2,1)S(1)}, bf16[8,256,128]{2,1,0:T(8,128)(2,1)S(1)}, u32[]{:S(2)}, u32[]{:S(2)}) collective-permute-start(bf16[8,256,128]{2,1,0:T(8,128)(2,1)S(1)} %pad_maximum_fusion.3.rest_6_.rest_7_), channel_id=1, source_target_pairs={{0,32},{32,0},{64,96},{96,64},{1,33},{33,1},{65,97},{97,65},{2,34}... | collective-permute-start | bytes 1572872 | tf_op jit(solution)/shard_map/ppermute | solution.py:33
  160.0 18.4 %collective-permute-start.41 = (bf16[8,256,128]{2,1,0:T(8,128)(2,1)S(1)}, bf16[8,256,128]{2,1,0:T(8,128)(2,1)}, u32[]{:S(2)}, u32[]{:S(2)}) collective-permute-start(bf16[8,256,128]{2,1,0:T(8,128)(2,1)S(1)} %pad_maximum_fusion.rest_0_.rest_1_), channel_id=1, source_target_pairs={{0,24},{8,16},{16,8},{24,0},{1,25},{9,17},{17,9},{25,1},{2,26},{10... | collective-permute-start | bytes 1572872 | tf_op jit(solution)/shard_map/ppermute | solution.py:33
  162.5 15.9 %collective-permute-start.42 = (bf16[8,256,128]{2,1,0:T(8,128)(2,1)S(1)}, bf16[8,256,128]{2,1,0:T(8,128)(2,1)}, u32[]{:S(2)}, u32[]{:S(2)}) collective-permute-start(bf16[8,256,128]{2,1,0:T(8,128)(2,1)S(1)} %pad_maximum_fusion.1.rest_2_.rest_3_), channel_id=1, source_target_pairs={{0,8},{8,0},{16,24},{24,16},{1,9},{9,1},{17,25},{25,17},{2,10},{10... | collective-permute-start | bytes 1572872 | tf_op jit(solution)/shard_map/ppermute | solution.py:33
  (22 other events, 128.2 us)
Sparse Core Ops, SparseCore 0:
  112.3 64.6 all-gather.2

commit v8 on v7

--- a/solution.py
+++ b/solution.py
@@ -33,12 +33,14 @@
     return lax.ppermute(value, axis, [(i, i ^ flip) for i in range(4)])
 
 
-def spread(parts):
+def spread(parts, factor):
     parts = [p[None] for p in parts]
     for step in range(3):
         got = [swap(p, *order[step]) for p, order in zip(parts, ORDERS)]
+        if step == 1:
+            factor, *got = lax.optimization_barrier((factor, *got))
         parts = [jnp.concatenate([p, g], axis=0) for p, g in zip(parts, got)]
-    return parts, [swap(p, *order[3]) for p, order in zip(parts, ORDERS)]
+    return parts, factor, [swap(p, *order[3]) for p, order in zip(parts, ORDERS)]
 
 
 def places(y, z):
@@ -117,16 +119,11 @@
     gots = refs[:3 - panel]
     got = sum(g[...] for g in gots)
     state = state_ref[...] - dot(block_ref[0], got[:256]) - dot(block_ref[1], got[256:])
-    here = scalars[1] == panel
-    if panel == 0:
-        sent_ref, next_ref, new_ref, done_ref = refs[3:]
-        done_ref[...] = jnp.where(here, sent_ref[...], got)
-    elif panel == 1:
-        sent_ref, back_ref, last_ref, next_ref, new_ref, done_ref = refs[2:]
-        done_ref[:512] = last_ref[...]
-        done_ref[512:] = jnp.where(here, sent_ref[...], got + back_ref[...])
+    if panel == 1:
+        sent_ref, back_ref, next_ref, new_ref, done_ref = refs[2:]
+        done_ref[...] = jnp.where(scalars[1] == 1, sent_ref[...], got + back_ref[...])
     else:
-        next_ref, new_ref = refs[1:]
+        next_ref, new_ref = refs[3 - panel:]
     next_ref[...] = state
     new_ref[...] = solve(high_ref, low_ref, state)
 
@@ -143,8 +140,8 @@
         kernel, ins = lambda *refs: step_kernel(panel, *refs), [part] * 4 + [tall] * len(more)
         scratch = [pltpu.VMEM((2, 512, 256), BF)]
         shapes = [jax.ShapeDtypeStruct((512, 128), F32)] + shapes
-        if panel < 2:
-            shapes.append(jax.ShapeDtypeStruct((512 * (panel + 1), 128), BF))
+        if panel == 1:
+            shapes.append(jax.ShapeDtypeStruct((512, 128), BF))
     return pl.pallas_call(
         kernel,
         grid_spec=pltpu.PrefetchScalarGridSpec(
@@ -159,18 +156,51 @@
     )(scalars, state, *inverse, *factor, *more)
 
 
+def begin_kernel(scalars, mine_ref, other_ref, rhs_ref, early_ref, out_ref, sent_ref):
+    place, core = scalars[64], scalars[65]
+    for h in range(2):
+        sent_ref[:, h * 128:(h + 1) * 128] = early_ref[h]
+    dot = lambda a, b: jnp.dot(a, b, preferred_element_type=F32)
+    near = sent_ref[pl.ds(pl.multiple_of(core * 256, 256), 256), :]
+    far = sent_ref[pl.ds(pl.multiple_of(256 - core * 256, 256), 256), :]
+    for c in range(2):
+        out_ref[c] = rhs_ref[c] - (dot(mine_ref[c], near) + dot(other_ref[c], far))
+
+    @pl.when(place == 0)
+    def _():
+        out_ref[0] = sent_ref[...].astype(F32)
+
+
+def begin(scalars, mine, other, rhs, early):
+    block = pl.BlockSpec((2, 512, 256), lambda j, s: (0, 0, j))
+    fixed = pl.BlockSpec((2, 512, 256), lambda j, s: (0, 0, 0))
+    return pl.pallas_call(
+        begin_kernel,
+        grid_spec=pltpu.PrefetchScalarGridSpec(
+            num_scalar_prefetch=1,
+            grid=(rhs.shape[2] // 256,),
+            in_specs=[fixed, fixed, block, pl.BlockSpec((2, 512, 128), lambda j, s: (j, 0, 0))],
+            out_specs=block,
+            scratch_shapes=[pltpu.VMEM((512, 256), BF)],
+        ),
+        out_shape=jax.ShapeDtypeStruct(rhs.shape, F32),
+        compiler_params=pltpu.CompilerParams(vmem_limit_bytes=48 << 20),
+    )(scalars, mine, other, rhs, early)
+
+
 def update_kernel(scalars, mine_ref, other_ref, rhs_ref, early_ref, *rest):
     near, far, out_ref, sent_ref = rest[:8], rest[8:16], rest[16], rest[17]
     j = pl.program_id(0)
     place, core = scalars[64], scalars[65]
 
     def rows(panel, half):
-        return pl.ds(pl.multiple_of((core ^ half) * 1024 + panel * 256, 256), 256)
+        return pl.ds(pl.multiple_of((core ^ half) * 768 + (panel - 1) * 256, 256), 256)
 
     for h in range(2):
         lanes = slice(h * 128, (h + 1) * 128)
+        for half in range(2):
+            sent_ref[rows(1, half), lanes] = early_ref[h, half * 256:(half + 1) * 256]
         for p in range(4):
-            sent_ref[rows(p // 2, p % 2), lanes] = early_ref[h, p * 256:(p + 1) * 256]
             low = scalars[p * 16 + 2 * j + h] < 8
 
             @pl.when(low)
@@ -182,9 +212,14 @@
                 sent_ref[rows(2 + p // 2, p % 2), lanes] = far[p * 2 + h][0]
     dot = lambda a, b: jnp.dot(a, b, preferred_element_type=F32)
     for c in range(2):
-        out_ref[c] = rhs_ref[c] - (dot(mine_ref[c], sent_ref[:1024]) + dot(other_ref[c], sent_ref[1024:]))
-
-    @pl.when(place < 4)
+        product = dot(mine_ref[c, :, 256:], sent_ref[:768]) + dot(other_ref[c, :, 256:], sent_ref[768:])
+        out_ref[c] = rhs_ref[c] - product
+
+    @pl.when(place == 0)
+    def _():
+        out_ref[0] = rhs_ref[0]
+
+    @pl.when(jnp.logical_and(place > 0, place < 4))
     def _():
         for half in range(2):
             out_ref[0, half * 256:(half + 1) * 256] = sent_ref[rows(place, half), :].astype(F32)
@@ -210,10 +245,10 @@
                 pl.BlockSpec((cycles, tile, depth), lambda j, s: (0, 0, 0)),
                 pl.BlockSpec((cycles, tile, depth), lambda j, s: (0, 0, 0)),
                 pl.BlockSpec((cycles, tile, 256), lambda j, s: (0, 0, j)),
-                pl.BlockSpec((2, 1024, 128), lambda j, s: (j, 0, 0)),
+                pl.BlockSpec((2, 512, 128), lambda j, s: (j, 0, 0)),
             ] + near_specs + far_specs,
             out_specs=pl.BlockSpec((cycles, tile, 256), lambda j, s: (0, 0, j)),
-            scratch_shapes=[pltpu.VMEM((2 * depth, 256), BF)],
+            scratch_shapes=[pltpu.VMEM((1536, 256), BF)],
         ),
         out_shape=jax.ShapeDtypeStruct(rhs.shape, F32),
         compiler_params=pltpu.CompilerParams(vmem_limit_bytes=48 << 20),
@@ -227,9 +262,7 @@
     owner = place < 4
     zero = jnp.zeros((), BF)
 
-    flat_factor = factor.reshape(2, 512, 1024)
-    other_factor = lax.ppermute(flat_factor, "rhs", [(0, 1), (1, 0)])
-    slabs = loads(rhs, flat_factor)
+    slabs = loads(rhs, factor[0].reshape(1, 512, 1024))
     outward = {
         (p, d): permute(slabs[4 * p + d], [((i, 0, 0), (i, 0, d) if p else (i, d, 0)) for i in range(4)])
         for p, d in ((0, 3), (0, 1), (1, 1), (0, 2), (1, 2), (1, 3))
@@ -273,11 +306,13 @@
     top, bottom = complete(piece_a, near_a, "y"), complete(piece_b, near_b, "z")
     block = (top, bottom, lax.ppermute(top, "rhs", [(0, 1), (1, 0)]), lax.ppermute(bottom, "rhs", [(0, 1), (1, 0)]))
 
-    state, sent_1, panel_0 = step(where, state, inverse, block, 0, (*gots, sent_0))
+    panel_0 = jnp.where(x == 0, sent_0, gots[0] + gots[1] + gots[2])
+    early_0 = lax.all_gather(panel_0, ("y", "z"), axis=0)
+    state, sent_1 = step(where, state, inverse, block, 0, gots)
     gots = [hop(sent_1, (1, 2)), hop(sent_1, (1, 3))]
     back_1 = hop(sent_1, (1, 0))
-    state, sent_2, pair = step(where, state, inverse, block, 1, (*gots, sent_1, back_1, panel_0))
-    early = lax.all_gather(pair, ("y", "z"), axis=0)
+    state, sent_2, panel_1 = step(where, state, inverse, block, 1, (*gots, sent_1, back_1))
+    early_1 = lax.all_gather(panel_1, ("y", "z"), axis=0)
     got = hop(sent_2, (2, 3))
     state, sent = step(where, state, inverse, block, 2, (got,))
     sent_2 = jnp.where(x == 2, sent_2, zero)
@@ -287,10 +322,14 @@
     wrap = hop(sent, (3, 0))
     panel_2 = jnp.where(x == 2, sent, jnp.where(x == 3, got, jnp.where(x == 1, back, far)))
     panel_3 = jnp.where(x == 3, sent, jnp.where(x == 2, back, jnp.where(x == 1, far, wrap)))
-    near, far_late = spread([panel_2[:256], panel_2[256:], panel_3[:256], panel_3[256:]])
+    parts = [panel_2[:256], panel_2[256:], panel_3[:256], panel_3[256:]]
+    near, flat_factor, far_late = spread(parts, factor.reshape(2, 512, 1024))
+    other_factor = lax.ppermute(flat_factor, "rhs", [(0, 1), (1, 0)])
 
     scalars = jnp.concatenate([places(y, z), jnp.stack([place, core])]).astype(jnp.int32)
-    return update(scalars, flat_factor, other_factor, rhs, early, near, far_late)
+    begun = begin(scalars, flat_factor, other_factor, rhs, early_0)
+    begun, *far_late = lax.optimization_barrier((begun, *far_late))
+    return update(scalars, flat_factor, other_factor, begun, early_1, near, far_late)
 
 
 def solution(mesh):

time: 206 us -> 209 us (1.015)
  starting transfers between devices: 65.9 us -> 55.2 us
  Pallas kernels: 29.3 us -> 38.8 us
  other arithmetic: 5.54 us -> 12.2 us
  waiting for transfers between devices: 83.6 us -> 80.9 us
    pallas_call x0 -> x1, Pallas kernels: none -> 11.8 us  [begin(): pl.pallas_call(begin_kernel, grid_spec=pltpu.PrefetchScalarGridSpec(num_s...]
    ppermute x20, starting transfers between devices: 27.8 us -> 16.3 us  [swap(): return lax.ppermute(value, axis, [(i, i ^ flip) for i in range(4)])]
    concatenate x12, other arithmetic: 0.38 us -> 6.3 us  [spread(): parts = [jnp.concatenate([p, g], axis=0) for p, g in zip(parts, got)]]
    ppermute x20, waiting for transfers between devices: 34.2 us -> 32.1 us  [swap(): return lax.ppermute(value, axis, [(i, i ^ flip) for i in range(4)])]
  transfers between devices with their start and end apart: 46 -> 47, of which waited for: 23 -> 21; matrix products, arithmetic and copies ran while one was open for 2% -> 6% of each run, Pallas kernels for 1% -> 8%
where the time goes in v8:
time: 209 us; the launch traced here: 207 us
  waiting for transfers between devices  80.9 us (39%)
  starting transfers between devices  55.2 us (26%)
  Pallas kernels  38.8 us (19%)
  between operations  14 us (7%)
  other arithmetic  12.2 us (6%)
  local copies, waits for them, and re-layouts  6.1 us (3%)
    ppermute x22, waiting for transfers between devices, permute(): return lax.ppermute(value, ROWS, [(flat(*a), flat(*b)) for a, b in moves])  47.1 us
    ppermute x22, starting transfers between devices, permute(): return lax.ppermute(value, ROWS, [(flat(*a), flat(*b)) for a, b in moves])  38.1 us
    ppermute x20, waiting for transfers between devices, swap(): return lax.ppermute(value, axis, [(i, i ^ flip) for i in range(4)])  32.1 us
    pallas_call x1, Pallas kernels, update(): pl.pallas_call(update_kernel, grid_spec=pltpu.PrefetchScalarGridSpec(num_...  16.7 us
    ppermute x20, starting transfers between devices, swap(): return lax.ppermute(value, axis, [(i, i ^ flip) for i in range(4)])  16.3 us
    pallas_call x1, Pallas kernels, begin(): pl.pallas_call(begin_kernel, grid_spec=pltpu.PrefetchScalarGridSpec(num_s...  11.8 us
    pallas_call x4, Pallas kernels, step(): pl.pallas_call(kernel, grid_spec=pltpu.PrefetchScalarGridSpec(num_scalar_...  6.39 us
    concatenate x12, other arithmetic, spread(): parts = [jnp.concatenate([p, g], axis=0) for p, g in zip(parts, got)]  6.3 us
  transfers between devices with their start and end apart: 47, of which 21 were waited for; matrix products, arithmetic and copies ran while one was open for 6% of the time, Pallas kernels for 8%

profile of v8, /device:TPU:6, one launch (start us, length us, event | category | flops | bytes accessed | tf_op | source)
XLA Modules:
  0.0 207.1 jit_solution(11904126671467377229)
XLA Ops:
  8.9 4.0 %shard_map.37 = (bf16[608,512]{1,0:T(8,128)(2,1)S(1)}, bf16[608,512]{1,0:T(8,128)(2,1)S(1)}, bf16[608,512]{1,0:T(8,128)(2,1)}, bf16[608,512]{1,0:T(8,128)(2,1)},...) custom-call(f32[2,512,2048]{2,1,0:T(8,128)} %rhs_ref.3, ...), custom_call_target="tpu_custom_call" | custom-call | tf_op jit(solution)/shard_map/pallas_call | solution.py:86
  12.9 4.3 %collective-permute-start = (bf16[608,512]{1,0:T(8,128)(2,1)S(1)}, bf16[608,512]{1,0:T(8,128)(2,1)}, u32[]{:S(2)}, u32[]{:S(2)}) collective-permute-start(bf16[608,512]{1,0:T(8,128)(2,1)S(1)} %get-tuple-element.43), channel_id=1, source_target_pairs={{0,32},{2,34},{4,36},{6,38},{1,33},{3,35},{5,37},{7,39}} | collective-permute-start | bytes 1867784 | tf_op jit(solution)/shard_map/ppermute | solution.py:25
  17.2 3.1 %collective-permute-start.1 = (bf16[608,512]{1,0:T(8,128)(2,1)}, bf16[608,512]{1,0:T(8,128)(2,1)}, u32[]{:S(2)}, u32[]{:S(2)}) collective-permute-start(bf16[608,512]{1,0:T(8,128)(2,1)} %get-tuple-element.44), channel_id=1, source_target_pairs={{0,64},{2,66},{4,68},{6,70},{1,65},{3,67},{5,69},{7,71}} | collective-permute-start | bytes 1867784 | tf_op jit(solution)/shard_map/ppermute | solution.py:25
  20.3 2.1 %collective-permute-start.2 = (bf16[608,512]{1,0:T(8,128)(2,1)}, bf16[608,512]{1,0:T(8,128)(2,1)}, u32[]{:S(2)}, u32[]{:S(2)}) collective-permute-start(bf16[608,512]{1,0:T(8,128)(2,1)} %get-tuple-element.45), channel_id=1, source_target_pairs={{0,96},{2,98},{4,100},{6,102},{1,97},{3,99},{5,101},{7,103}} | collective-permute-start | bytes 1867784 | tf_op jit(solution)/shard_map/ppermute | solution.py:25
  22.4 2.1 %collective-permute-start.6 = (bf16[608,512]{1,0:T(8,128)(2,1)}, bf16[608,512]{1,0:T(8,128)(2,1)}, u32[]{:S(2)}, u32[]{:S(2)}) collective-permute-start(bf16[608,512]{1,0:T(8,128)(2,1)} %get-tuple-element.48), channel_id=1, source_target_pairs={{0,8},{2,10},{4,12},{6,14},{1,9},{3,11},{5,13},{7,15}} | collective-permute-start | bytes 1867784 | tf_op jit(solution)/shard_map/ppermute | solution.py:25
  26.7 4.1 %collective-permute-done = bf16[608,512]{1,0:T(8,128)(2,1)} collective-permute-done((bf16[608,512]{1,0:T(8,128)(2,1)S(1)}, bf16[608,512]{1,0:T(8,128)(2,1)}, u32[]{:S(2)}, u32[]{:S(2)}) %collective-permute-start) | collective-permute-done | bytes 622624 | tf_op jit(solution)/shard_map/ppermute | solution.py:25
  34.4 8.7 %collective-permute-done.1 = bf16[608,512]{1,0:T(8,128)(2,1)} collective-permute-done((bf16[608,512]{1,0:T(8,128)(2,1)}, bf16[608,512]{1,0:T(8,128)(2,1)}, u32[]{:S(2)}, u32[]{:S(2)}) %collective-permute-start.1) | collective-permute-done | bytes 622624 | tf_op jit(solution)/shard_map/ppermute | solution.py:25
  44.7 6.0 %collective-permute-done.7 = bf16[608,512]{1,0:T(8,128)(2,1)} collective-permute-done((bf16[608,512]{1,0:T(8,128)(2,1)}, bf16[608,512]{1,0:T(8,128)(2,1)}, u32[]{:S(2)}, u32[]{:S(2)}) %collective-permute-start.7) | collective-permute-done | bytes 622624 | tf_op jit(solution)/shard_map/ppermute | solution.py:25
  57.9 5.3 %collective-permute-start.5 = (bf16[896,128]{1,0:T(8,128)(2,1)S(1)}, bf16[896,128]{1,0:T(8,128)(2,1)S(1)}, u32[]{:S(2)}, u32[]{:S(2)}) collective-permute-start(bf16[896,128]{1,0:T(8,128)(2,1)S(1)} %get-tuple-element.95), channel_id=1, source_target_pairs={{0,16},{32,48},{64,80},{96,112},{2,18},{34,50},{66,82},{98,114},{4... | collective-permute-start | bytes 688136 | tf_op jit(solution)/shard_map/ppermute | solution.py:25
  64.7 4.5 %collective-permute-done.5 = bf16[896,128]{1,0:T(8,128)(2,1)S(1)} collective-permute-done((bf16[896,128]{1,0:T(8,128)(2,1)S(1)}, bf16[896,128]{1,0:T(8,128)(2,1)S(1)}, u32[]{:S(2)}, u32[]{:S(2)}) %collective-permute-start.5) | collective-permute-done | bytes 229408 | tf_op jit(solution)/shard_map/ppermute | solution.py:25
  69.2 2.8 %collective-permute-done.3 = bf16[896,128]{1,0:T(8,128)(2,1)S(1)} collective-permute-done((bf16[896,128]{1,0:T(8,128)(2,1)S(1)}, bf16[896,128]{1,0:T(8,128)(2,1)S(1)}, u32[]{:S(2)}, u32[]{:S(2)}) %collective-permute-start.3) | collective-permute-done | bytes 229408 | tf_op jit(solution)/shard_map/ppermute | solution.py:25
  76.2 2.6 %collective-permute-start.13 = (bf16[384,128]{1,0:T(8,128)(2,1)S(1)}, bf16[384,128]{1,0:T(8,128)(2,1)S(1)}, u32[]{:S(2)}, u32[]{:S(2)}) collective-permute-start(bf16[384,128]{1,0:T(8,128)(2,1)S(1)} %slice.113), channel_id=1, source_target_pairs={{0,8},{8,0},{16,24},{24,16},{1,9},{9,1},{17,25},{25,17},{2,10},{10... | collective-permute-start | bytes 294920 | tf_op jit(solution)/shard_map/ppermute | solution.py:33
  84.0 6.7 %collective-permute-done.18 = bf16[2,384,128]{2,1,0:T(8,128)(2,1)S(1)} collective-permute-done((bf16[2,384,128]{2,1,0:T(8,128)(2,1)S(1)}, bf16[2,384,128]{2,1,0:T(8,128)(2,1)S(1)}, u32[]{:S(2)}, u32[]{:S(2)}) %collective-permute-start.18) | collective-permute-done | bytes 196640 | tf_op jit(solution)/shard_map/ppermute | solution.py:33
  97.5 10.7 %collective-permute-done.22.refs_9_ = bf16[512,128]{1,0:T(8,128)(2,1)S(1)} collective-permute-done((bf16[512,128]{1,0:T(8,128)(2,1)S(1)}, bf16[512,128]{1,0:T(8,128)(2,1)S(1)}, u32[]{:S(2)}, u32[]{:S(2)}) %collective-permute-start.22) | collective-permute-done | bytes 131104 | tf_op jit(solution)/shard_map/ppermute | solution.py:25
  111.2 5.6 %collective-permute-done.24.refs_8_ = bf16[512,128]{1,0:T(8,128)(2,1)S(1)} collective-permute-done((bf16[512,128]{1,0:T(8,128)(2,1)S(1)}, bf16[512,128]{1,0:T(8,128)(2,1)S(1)}, u32[]{:S(2)}, u32[]{:S(2)}) %collective-permute-start.24) | collective-permute-done | bytes 131104 | tf_op jit(solution)/shard_map/ppermute | solution.py:25
  125.7 3.2 %collective-permute-start.34 = (bf16[1,256,128]{2,1,0:T(8,128)(2,1)S(1)}, bf16[1,256,128]{2,1,0:T(8,128)(2,1)S(1)}, u32[]{:S(2)}, u32[]{:S(2)}) collective-permute-start(bf16[1,256,128]{2,1,0:T(8,128)(2,1)S(1)} %get-tuple-element.115), channel_id=1, source_target_pairs={{0,24},{8,16},{16,8},{24,0},{1,25},{9,17},{17,9},{25,1},{2,26},{10... | collective-permute-start | bytes 196616 | tf_op jit(solution)/shard_map/ppermute | solution.py:33
  134.0 3.3 %collective-permute-start.28 = (bf16[2,256,128]{2,1,0:T(8,128)(2,1)S(1)}, bf16[2,256,128]{2,1,0:T(8,128)(2,1)S(1)}, u32[]{:S(2)}, u32[]{:S(2)}) collective-permute-start(bf16[2,256,128]{2,1,0:T(8,128)(2,1)S(1)} %pad_maximum_fusion.12), channel_id=1, source_target_pairs={{0,96},{32,64},{64,32},{96,0},{1,97},{33,65},{65,33},{97,1},{2,98}... | collective-permute-start | bytes 393224 | tf_op jit(solution)/shard_map/ppermute | solution.py:33
  139.4 3.2 %reshape.179.mine_ref = bf16[2,512,1024]{2,1,0:T(8,128)(2,1)S(1)} reshape(bf16[2,512,4,256]{3,2,1,0:T(4,128)(2,1)} %param.4) | data formatting | bytes 4194304 | tf_op jit(solution)/shard_map/reshape | solution.py:326
  142.8 3.7 %collective-permute-done.33 = bf16[2,256,128]{2,1,0:T(8,128)(2,1)S(1)} collective-permute-done((bf16[2,256,128]{2,1,0:T(8,128)(2,1)}, bf16[2,256,128]{2,1,0:T(8,128)(2,1)S(1)}, u32[]{:S(2)}, u32[]{:S(2)}) %collective-permute-start.33) | collective-permute-done | bytes 131104 | tf_op jit(solution)/shard_map/ppermute | solution.py:33
  148.2 7.7 %collective-permute-done.37 = bf16[4,256,128]{2,1,0:T(8,128)(2,1)S(1)} collective-permute-done((bf16[4,256,128]{2,1,0:T(8,128)(2,1)S(1)}, bf16[4,256,128]{2,1,0:T(8,128)(2,1)S(1)}, u32[]{:S(2)}, u32[]{:S(2)}) %collective-permute-start.37) | collective-permute-done | bytes 262176 | tf_op jit(solution)/shard_map/ppermute | solution.py:33
  163.2 11.8 %shard_map.42.rhs_ref = f32[2,512,2048]{2,1,0:T(8,128)} custom-call(s32[66]{0:T(128)S(1)} %pad_add_fusion.1.scalars, bf16[2,512,1024]{2,1,0:T(8,128)(2,1)S(1)} %reshape.179.mine_ref, bf16[2,512,1024]{2,1,0:T(8,128)(2,1)} %collective-permute-done.36.other_ref, f32[2,512,2048]{2,1,0:T(8,128)} %rhs_ref.3, bf16[16,512,128]{2,1,0:T(8,128)(2,1)} %bitcast.28), custom_call_target="tpu_custom_call" | custom-call | tf_op jit(solution)/shard_map/pallas_call | solution.py:177
  175.0 5.4 %collective-permute-done.38.rest_8_.rest_9_ = bf16[8,256,128]{2,1,0:T(8,128)(2,1)} collective-permute-done((bf16[8,256,128]{2,1,0:T(8,128)(2,1)S(1)}, bf16[8,256,128]{2,1,0:T(8,128)(2,1)}, u32[]{:S(2)}, u32[]{:S(2)}) %collective-permute-start.38) | collective-permute-done | bytes 524320 | tf_op jit(solution)/shard_map/ppermute | solution.py:33
  180.4 3.2 %collective-permute-done.42.rest_12_.rest_13_ = bf16[8,256,128]{2,1,0:T(8,128)(2,1)} collective-permute-done((bf16[8,256,128]{2,1,0:T(8,128)(2,1)}, bf16[8,256,128]{2,1,0:T(8,128)(2,1)}, u32[]{:S(2)}, u32[]{:S(2)}) %collective-permute-start.42) | collective-permute-done | bytes 524320 | tf_op jit(solution)/shard_map/ppermute | solution.py:33
  183.6 16.7 %shard_map.43 = f32[2,512,2048]{2,1,0:T(8,128)} custom-call(s32[66]{0:T(128)S(1)} %pad_add_fusion.1.scalars, bf16[2,512,1024]{2,1,0:T(8,128)(2,1)} %copy-done, bf16[2,512,1024]{2,1,0:T(8,128)(2,1)} %collective-permute-done.36.other_ref, f32[2,512,2048]{2,1,0:T(8,128)} %shard_map.42.rhs_ref, bf16[16,512,128]{2,1,0:T(8,128)(2,1)} %bitcast.29, ...), custom_call_target="tpu_custom_call" | custom-call | tf_op jit(solution)/shard_map/pallas_call | solution.py:239
  (141 shorter events, 62.2 us)
Async XLA Ops:
  6.5 156.7 %all-gather.5.cloned.1.call-start = ((), (), s32[]{:S(2)}) async-start(), calls=%async_computation | async-start | bytes 2228224 | tf_op jit(solution)/shard_map/all_gather | solution.py:310
  12.9 17.9 %collective-permute-start = (bf16[608,512]{1,0:T(8,128)(2,1)S(1)}, bf16[608,512]{1,0:T(8,128)(2,1)}, u32[]{:S(2)}, u32[]{:S(2)}) collective-permute-start(bf16[608,512]{1,0:T(8,128)(2,1)S(1)} %get-tuple-element.43), channel_id=1, source_target_pairs={{0,32},{2,34},{4,36},{6,38},{1,33},{3,35},{5,37},{7,39}} | collective-permute-start | bytes 1867784 | tf_op jit(solution)/shard_map/ppermute | solution.py:25
  17.2 25.9 %collective-permute-start.1 = (bf16[608,512]{1,0:T(8,128)(2,1)}, bf16[608,512]{1,0:T(8,128)(2,1)}, u32[]{:S(2)}, u32[]{:S(2)}) collective-permute-start(bf16[608,512]{1,0:T(8,128)(2,1)} %get-tuple-element.44), channel_id=1, source_target_pairs={{0,64},{2,66},{4,68},{6,70},{1,65},{3,67},{5,69},{7,71}} | collective-permute-start | bytes 1867784 | tf_op jit(solution)/shard_map/ppermute | solution.py:25
  20.3 22.8 %collective-permute-start.2 = (bf16[608,512]{1,0:T(8,128)(2,1)}, bf16[608,512]{1,0:T(8,128)(2,1)}, u32[]{:S(2)}, u32[]{:S(2)}) collective-permute-start(bf16[608,512]{1,0:T(8,128)(2,1)} %get-tuple-element.45), channel_id=1, source_target_pairs={{0,96},{2,98},{4,100},{6,102},{1,97},{3,99},{5,101},{7,103}} | collective-permute-start | bytes 1867784 | tf_op jit(solution)/shard_map/ppermute | solution.py:25
  22.4 22.2 %collective-permute-start.6 = (bf16[608,512]{1,0:T(8,128)(2,1)}, bf16[608,512]{1,0:T(8,128)(2,1)}, u32[]{:S(2)}, u32[]{:S(2)}) collective-permute-start(bf16[608,512]{1,0:T(8,128)(2,1)} %get-tuple-element.48), channel_id=1, source_target_pairs={{0,8},{2,10},{4,12},{6,14},{1,9},{3,11},{5,13},{7,15}} | collective-permute-start | bytes 1867784 | tf_op jit(solution)/shard_map/ppermute | solution.py:25
  24.6 26.1 %collective-permute-start.7 = (bf16[608,512]{1,0:T(8,128)(2,1)}, bf16[608,512]{1,0:T(8,128)(2,1)}, u32[]{:S(2)}, u32[]{:S(2)}) collective-permute-start(bf16[608,512]{1,0:T(8,128)(2,1)} %get-tuple-element.49), channel_id=1, source_target_pairs={{0,16},{2,18},{4,20},{6,22},{1,17},{3,19},{5,21},{7,23}} | collective-permute-start | bytes 1867784 | tf_op jit(solution)/shard_map/ppermute | solution.py:25
  30.8 19.9 %collective-permute-start.8 = (bf16[608,512]{1,0:T(8,128)(2,1)S(1)}, bf16[608,512]{1,0:T(8,128)(2,1)}, u32[]{:S(2)}, u32[]{:S(2)}) collective-permute-start(bf16[608,512]{1,0:T(8,128)(2,1)S(1)} %get-tuple-element.50), channel_id=1, source_target_pairs={{0,24},{2,26},{4,28},{6,30},{1,25},{3,27},{5,29},{7,31}} | collective-permute-start | bytes 1867784 | tf_op jit(solution)/shard_map/ppermute | solution.py:25
  52.4 10.8 %collective-permute-start.10 = (bf16[896,128]{1,0:T(8,128)(2,1)S(1)}, bf16[896,128]{1,0:T(8,128)(2,1)S(1)}, u32[]{:S(2)}, u32[]{:S(2)}) collective-permute-start(bf16[896,128]{1,0:T(8,128)(2,1)S(1)} %get-tuple-element.111), channel_id=1, source_target_pairs={{0,96},{8,104},{16,112},{24,120},{2,98},{10,106},{18,114},{26,122}... | collective-permute-start | bytes 688136 | tf_op jit(solution)/shard_map/ppermute | solution.py:25
  53.7 10.8 %collective-permute-start.11 = (bf16[896,128]{1,0:T(8,128)(2,1)S(1)}, bf16[896,128]{1,0:T(8,128)(2,1)S(1)}, u32[]{:S(2)}, u32[]{:S(2)}) collective-permute-start(bf16[896,128]{1,0:T(8,128)(2,1)S(1)} %get-tuple-element.112), channel_id=1, source_target_pairs={{0,64},{8,72},{16,80},{24,88},{2,66},{10,74},{18,82},{26,90},{4,68... | collective-permute-start | bytes 688136 | tf_op jit(solution)/shard_map/ppermute | solution.py:25
  57.9 11.3 %collective-permute-start.5 = (bf16[896,128]{1,0:T(8,128)(2,1)S(1)}, bf16[896,128]{1,0:T(8,128)(2,1)S(1)}, u32[]{:S(2)}, u32[]{:S(2)}) collective-permute-start(bf16[896,128]{1,0:T(8,128)(2,1)S(1)} %get-tuple-element.95), channel_id=1, source_target_pairs={{0,16},{32,48},{64,80},{96,112},{2,18},{34,50},{66,82},{98,114},{4... | collective-permute-start | bytes 688136 | tf_op jit(solution)/shard_map/ppermute | solution.py:25
  83.7 99.9 %all-gather.7.cloned.1.call-start = ((), (), s32[]{:S(2)}) async-start(), calls=%async_computation.1 | async-start | bytes 2228224 | tf_op jit(solution)/shard_map/all_gather | solution.py:315
  95.5 12.7 %collective-permute-start.22 = (bf16[512,128]{1,0:T(8,128)(2,1)S(1)}, bf16[512,128]{1,0:T(8,128)(2,1)S(1)}, u32[]{:S(2)}, u32[]{:S(2)}) collective-permute-start(bf16[512,128]{1,0:T(8,128)(2,1)S(1)} %get-tuple-element.62.refs_10_), channel_id=1, source_target_pairs={{2,6},{10,14},{18,22},{26,30},{34,38},{42,46},{50,54},{58,62},{66,... | collective-permute-start | bytes 393224 | tf_op jit(solution)/shard_map/ppermute | solution.py:25
  96.8 11.4 %collective-permute-start.21 = (bf16[512,128]{1,0:T(8,128)(2,1)S(1)}, bf16[512,128]{1,0:T(8,128)(2,1)S(1)}, u32[]{:S(2)}, u32[]{:S(2)}) collective-permute-start(bf16[512,128]{1,0:T(8,128)(2,1)S(1)} %get-tuple-element.62.refs_10_), channel_id=1, source_target_pairs={{2,4},{10,12},{18,20},{26,28},{34,36},{42,44},{50,52},{58,60},{66,... | collective-permute-start | bytes 393224 | tf_op jit(solution)/shard_map/ppermute | solution.py:25
  125.7 11.6 %collective-permute-start.34 = (bf16[1,256,128]{2,1,0:T(8,128)(2,1)S(1)}, bf16[1,256,128]{2,1,0:T(8,128)(2,1)S(1)}, u32[]{:S(2)}, u32[]{:S(2)}) collective-permute-start(bf16[1,256,128]{2,1,0:T(8,128)(2,1)S(1)} %get-tuple-element.115), channel_id=1, source_target_pairs={{0,24},{8,16},{16,8},{24,0},{1,25},{9,17},{17,9},{25,1},{2,26},{10... | collective-permute-start | bytes 196616 | tf_op jit(solution)/shard_map/ppermute | solution.py:33
  128.9 9.7 %collective-permute-start.32 = (bf16[1,256,128]{2,1,0:T(8,128)(2,1)S(1)}, bf16[1,256,128]{2,1,0:T(8,128)(2,1)S(1)}, u32[]{:S(2)}, u32[]{:S(2)}) collective-permute-start(bf16[1,256,128]{2,1,0:T(8,128)(2,1)S(1)} %get-tuple-element.116), channel_id=1, source_target_pairs={{0,8},{8,0},{16,24},{24,16},{1,9},{9,1},{17,25},{25,17},{2,10},{10... | collective-permute-start | bytes 196616 | tf_op jit(solution)/shard_map/ppermute | solution.py:33
  131.2 11.5 %collective-permute-start.30 = (bf16[2,256,128]{2,1,0:T(8,128)(2,1)S(1)}, bf16[2,256,128]{2,1,0:T(8,128)(2,1)S(1)}, u32[]{:S(2)}, u32[]{:S(2)}) collective-permute-start(bf16[2,256,128]{2,1,0:T(8,128)(2,1)S(1)} %pad_maximum_fusion.13), channel_id=1, source_target_pairs={{0,32},{32,0},{64,96},{96,64},{1,33},{33,1},{65,97},{97,65},{2,34}... | collective-permute-start | bytes 393224 | tf_op jit(solution)/shard_map/ppermute | solution.py:33
  146.4 16.8 %collective-permute-start.36 = (bf16[2,512,1024]{2,1,0:T(8,128)(2,1)S(1)}, bf16[2,512,1024]{2,1,0:T(8,128)(2,1)}, u32[]{:S(2)}, u32[]{:S(2)}) collective-permute-start(bf16[2,512,1024]{2,1,0:T(8,128)(2,1)S(1)} %reshape.179.mine_ref), channel_id=1, source_target_pairs={{0,1},{1,0},{2,3},{3,2},{4,5},{5,4},{6,7},{7,6},{8,9},{9,8},{10,11... | collective-permute-start | bytes 6291464 | tf_op jit(solution)/shard_map/ppermute | solution.py:327
  146.6 10.9 %collective-permute-start.39 = (bf16[4,256,128]{2,1,0:T(8,128)(2,1)S(1)}, bf16[4,256,128]{2,1,0:T(8,128)(2,1)S(1)}, u32[]{:S(2)}, u32[]{:S(2)}) collective-permute-start(bf16[4,256,128]{2,1,0:T(8,128)(2,1)S(1)} %pad_maximum_fusion.7), channel_id=1, source_target_pairs={{0,24},{8,16},{16,8},{24,0},{1,25},{9,17},{17,9},{25,1},{2,26},{10... | collective-permute-start | bytes 786440 | tf_op jit(solution)/shard_map/ppermute | solution.py:33
  147.0 11.7 %collective-permute-start.41 = (bf16[4,256,128]{2,1,0:T(8,128)(2,1)S(1)}, bf16[4,256,128]{2,1,0:T(8,128)(2,1)S(1)}, u32[]{:S(2)}, u32[]{:S(2)}) collective-permute-start(bf16[4,256,128]{2,1,0:T(8,128)(2,1)S(1)} %pad_maximum_fusion.8), channel_id=1, source_target_pairs={{0,32},{32,0},{64,96},{96,64},{1,33},{33,1},{65,97},{97,65},{2,34}... | collective-permute-start | bytes 786440 | tf_op jit(solution)/shard_map/ppermute | solution.py:33
  148.0 12.6 %collective-permute-start.43 = (bf16[4,256,128]{2,1,0:T(8,128)(2,1)S(1)}, bf16[4,256,128]{2,1,0:T(8,128)(2,1)S(1)}, u32[]{:S(2)}, u32[]{:S(2)}) collective-permute-start(bf16[4,256,128]{2,1,0:T(8,128)(2,1)S(1)} %pad_maximum_fusion.9), channel_id=1, source_target_pairs={{0,96},{32,64},{64,32},{96,0},{1,97},{33,65},{65,33},{97,1},{2,98}... | collective-permute-start | bytes 786440 | tf_op jit(solution)/shard_map/ppermute | solution.py:33
  156.9 23.5 %collective-permute-start.38 = (bf16[8,256,128]{2,1,0:T(8,128)(2,1)S(1)}, bf16[8,256,128]{2,1,0:T(8,128)(2,1)}, u32[]{:S(2)}, u32[]{:S(2)}) collective-permute-start(bf16[8,256,128]{2,1,0:T(8,128)(2,1)S(1)} %pad_maximum_fusion.rest_0_.rest_1_), channel_id=1, source_target_pairs={{0,24},{8,16},{16,8},{24,0},{1,25},{9,17},{17,9},{25,1},{2,26},{10... | collective-permute-start | bytes 1572872 | tf_op jit(solution)/shard_map/ppermute | solution.py:33
  158.4 22.0 %collective-permute-start.40 = (bf16[8,256,128]{2,1,0:T(8,128)(2,1)S(1)}, bf16[8,256,128]{2,1,0:T(8,128)(2,1)}, u32[]{:S(2)}, u32[]{:S(2)}) collective-permute-start(bf16[8,256,128]{2,1,0:T(8,128)(2,1)S(1)} %pad_maximum_fusion.1.rest_2_.rest_3_), channel_id=1, source_target_pairs={{0,8},{8,0},{16,24},{24,16},{1,9},{9,1},{17,25},{25,17},{2,10},{10... | collective-permute-start | bytes 1572872 | tf_op jit(solution)/shard_map/ppermute | solution.py:33
  160.4 23.2 %collective-permute-start.42 = (bf16[8,256,128]{2,1,0:T(8,128)(2,1)}, bf16[8,256,128]{2,1,0:T(8,128)(2,1)}, u32[]{:S(2)}, u32[]{:S(2)}) collective-permute-start(bf16[8,256,128]{2,1,0:T(8,128)(2,1)} %pad_maximum_fusion.2.rest_4_.rest_5_), channel_id=1, source_target_pairs={{0,96},{32,64},{64,32},{96,0},{1,97},{33,65},{65,33},{97,1},{2,98}... | collective-permute-start | bytes 1572872 | tf_op jit(solution)/shard_map/ppermute | solution.py:33
  162.4 21.1 %collective-permute-start.44 = (bf16[8,256,128]{2,1,0:T(8,128)(2,1)}, bf16[8,256,128]{2,1,0:T(8,128)(2,1)}, u32[]{:S(2)}, u32[]{:S(2)}) collective-permute-start(bf16[8,256,128]{2,1,0:T(8,128)(2,1)} %pad_maximum_fusion.3.rest_6_.rest_7_), channel_id=1, source_target_pairs={{0,32},{32,0},{64,96},{96,64},{1,33},{33,1},{65,97},{97,65},{2,34}... | collective-permute-start | bytes 1572872 | tf_op jit(solution)/shard_map/ppermute | solution.py:33
  (28 other events, 220.9 us)
Sparse Core Ops, SparseCore 0:
  83.8 45.1 all-gather.4
  131.2 50.8 all-gather.6

commit v9 on v7

--- a/solution.py
+++ b/solution.py
@@ -33,12 +33,16 @@
     return lax.ppermute(value, axis, [(i, i ^ flip) for i in range(4)])
 
 
-def spread(parts):
+def spread(parts, factor, early):
     parts = [p[None] for p in parts]
     for step in range(3):
         got = [swap(p, *order[step]) for p, order in zip(parts, ORDERS)]
+        if step == 0:
+            early, *got = lax.optimization_barrier((early, *got))
+        if step == 1:
+            factor, *got = lax.optimization_barrier((factor, *got))
         parts = [jnp.concatenate([p, g], axis=0) for p, g in zip(parts, got)]
-    return parts, [swap(p, *order[3]) for p, order in zip(parts, ORDERS)]
+    return parts, factor, early, [swap(p, *order[3]) for p, order in zip(parts, ORDERS)]
 
 
 def places(y, z):
@@ -117,16 +121,7 @@
     gots = refs[:3 - panel]
     got = sum(g[...] for g in gots)
     state = state_ref[...] - dot(block_ref[0], got[:256]) - dot(block_ref[1], got[256:])
-    here = scalars[1] == panel
-    if panel == 0:
-        sent_ref, next_ref, new_ref, done_ref = refs[3:]
-        done_ref[...] = jnp.where(here, sent_ref[...], got)
-    elif panel == 1:
-        sent_ref, back_ref, last_ref, next_ref, new_ref, done_ref = refs[2:]
-        done_ref[:512] = last_ref[...]
-        done_ref[512:] = jnp.where(here, sent_ref[...], got + back_ref[...])
-    else:
-        next_ref, new_ref = refs[1:]
+    next_ref, new_ref = refs[3 - panel:]
     next_ref[...] = state
     new_ref[...] = solve(high_ref, low_ref, state)
 
@@ -143,8 +138,6 @@
         kernel, ins = lambda *refs: step_kernel(panel, *refs), [part] * 4 + [tall] * len(more)
         scratch = [pltpu.VMEM((2, 512, 256), BF)]
         shapes = [jax.ShapeDtypeStruct((512, 128), F32)] + shapes
-        if panel < 2:
-            shapes.append(jax.ShapeDtypeStruct((512 * (panel + 1), 128), BF))
     return pl.pallas_call(
         kernel,
         grid_spec=pltpu.PrefetchScalarGridSpec(
@@ -164,41 +157,47 @@
     j = pl.program_id(0)
     place, core = scalars[64], scalars[65]
 
-    def rows(panel, half):
-        return pl.ds(pl.multiple_of((core ^ half) * 1024 + panel * 256, 256), 256)
+    def rows(panel, half, size=256):
+        return pl.ds(pl.multiple_of((core ^ (half // 256)) * 1024 + panel * 256 + half % 256, 128), size)
+
+    def put(part_ref, p, lanes):
+        for u in range(3):
+            row = 512 + p * 384 + u * 128
+            sent_ref[rows(row // 512, row % 512, 128), lanes] = part_ref[0, u * 128:(u + 1) * 128]
 
     for h in range(2):
         lanes = slice(h * 128, (h + 1) * 128)
+        for half in (0, 256):
+            sent_ref[rows(0, half), lanes] = early_ref[h, half:half + 256]
         for p in range(4):
-            sent_ref[rows(p // 2, p % 2), lanes] = early_ref[h, p * 256:(p + 1) * 256]
             low = scalars[p * 16 + 2 * j + h] < 8
 
             @pl.when(low)
             def _():
-                sent_ref[rows(2 + p // 2, p % 2), lanes] = near[p * 2 + h][0]
+                put(near[p * 2 + h], p, lanes)
 
             @pl.when(jnp.logical_not(low))
             def _():
-                sent_ref[rows(2 + p // 2, p % 2), lanes] = far[p * 2 + h][0]
+                put(far[p * 2 + h], p, lanes)
     dot = lambda a, b: jnp.dot(a, b, preferred_element_type=F32)
     for c in range(2):
         out_ref[c] = rhs_ref[c] - (dot(mine_ref[c], sent_ref[:1024]) + dot(other_ref[c], sent_ref[1024:]))
 
     @pl.when(place < 4)
     def _():
-        for half in range(2):
-            out_ref[0, half * 256:(half + 1) * 256] = sent_ref[rows(place, half), :].astype(F32)
+        for half in (0, 256):
+            out_ref[0, half:half + 256] = sent_ref[rows(place, half), :].astype(F32)
 
 
 def update(scalars, mine, other, rhs, early, near, far):
     cycles, tile, depth = mine.shape
     pairs = [(p, h) for p in range(4) for h in range(2)]
     near_specs = [
-        pl.BlockSpec((1, 256, 128), lambda j, s, p=p, h=h: (jnp.minimum(s[p * 16 + 2 * j + h], 7), 0, 0))
+        pl.BlockSpec((1, 384, 128), lambda j, s, p=p, h=h: (jnp.minimum(s[p * 16 + 2 * j + h], 7), 0, 0))
         for p, h in pairs
     ]
     far_specs = [
-        pl.BlockSpec((1, 256, 128), lambda j, s, p=p, h=h: (jnp.maximum(s[p * 16 + 2 * j + h] - 8, 0), 0, 0))
+        pl.BlockSpec((1, 384, 128), lambda j, s, p=p, h=h: (jnp.maximum(s[p * 16 + 2 * j + h] - 8, 0), 0, 0))
         for p, h in pairs
     ]
     return pl.pallas_call(
@@ -210,10 +209,10 @@
                 pl.BlockSpec((cycles, tile, depth), lambda j, s: (0, 0, 0)),
                 pl.BlockSpec((cycles, tile, depth), lambda j, s: (0, 0, 0)),
                 pl.BlockSpec((cycles, tile, 256), lambda j, s: (0, 0, j)),
-                pl.BlockSpec((2, 1024, 128), lambda j, s: (j, 0, 0)),
+                pl.BlockSpec((2, 512, 128), lambda j, s: (j, 0, 0)),
             ] + near_specs + far_specs,
             out_specs=pl.BlockSpec((cycles, tile, 256), lambda j, s: (0, 0, j)),
-            scratch_shapes=[pltpu.VMEM((2 * depth, 256), BF)],
+            scratch_shapes=[pltpu.VMEM((2048, 256), BF)],
         ),
         out_shape=jax.ShapeDtypeStruct(rhs.shape, F32),
         compiler_params=pltpu.CompilerParams(vmem_limit_bytes=48 << 20),
@@ -227,9 +226,7 @@
     owner = place < 4
     zero = jnp.zeros((), BF)
 
-    flat_factor = factor.reshape(2, 512, 1024)
-    other_factor = lax.ppermute(flat_factor, "rhs", [(0, 1), (1, 0)])
-    slabs = loads(rhs, flat_factor)
+    slabs = loads(rhs, factor[0].reshape(1, 512, 1024))
     outward = {
         (p, d): permute(slabs[4 * p + d], [((i, 0, 0), (i, 0, d) if p else (i, d, 0)) for i in range(4)])
         for p, d in ((0, 3), (0, 1), (1, 1), (0, 2), (1, 2), (1, 3))
@@ -273,24 +270,28 @@
     top, bottom = complete(piece_a, near_a, "y"), complete(piece_b, near_b, "z")
     block = (top, bottom, lax.ppermute(top, "rhs", [(0, 1), (1, 0)]), lax.ppermute(bottom, "rhs", [(0, 1), (1, 0)]))
 
-    state, sent_1, panel_0 = step(where, state, inverse, block, 0, (*gots, sent_0))
-    gots = [hop(sent_1, (1, 2)), hop(sent_1, (1, 3))]
-    back_1 = hop(sent_1, (1, 0))
-    state, sent_2, pair = step(where, state, inverse, block, 1, (*gots, sent_1, back_1, panel_0))
-    early = lax.all_gather(pair, ("y", "z"), axis=0)
+    panel_0 = jnp.where(x == 0, sent_0, gots[0] + gots[1] + gots[2])
+    early_0 = lax.all_gather(panel_0, ("y", "z"), axis=0)
+    state, sent_1 = step(where, state, inverse, block, 0, gots)
+    gots_1 = [hop(sent_1, (1, 2)), hop(sent_1, (1, 3))]
+    state, sent_2 = step(where, state, inverse, block, 1, gots_1)
     got = hop(sent_2, (2, 3))
     state, sent = step(where, state, inverse, block, 2, (got,))
-    sent_2 = jnp.where(x == 2, sent_2, zero)
+    sent_2 = jnp.where(x == 2, sent_2, sent_1)
     sent = jnp.where(x == 3, sent, sent_2)
-    back = hop(sent, (2, 1), (3, 2))
+    back = hop(sent, (1, 0), (2, 1), (3, 2))
     far = hop(sent, (2, 0), (3, 1))
     wrap = hop(sent, (3, 0))
+    panel_1 = jnp.where(x == 1, sent, jnp.where(x == 0, back, gots_1[0] + gots_1[1]))
     panel_2 = jnp.where(x == 2, sent, jnp.where(x == 3, got, jnp.where(x == 1, back, far)))
     panel_3 = jnp.where(x == 3, sent, jnp.where(x == 2, back, jnp.where(x == 1, far, wrap)))
-    near, far_late = spread([panel_2[:256], panel_2[256:], panel_3[:256], panel_3[256:]])
+    cat = lambda *v: jnp.concatenate(v, axis=0)
+    parts = [panel_1[:384], cat(panel_1[384:], panel_2[:256]), cat(panel_2[256:], panel_3[:128]), panel_3[128:]]
+    near, flat_factor, early_0, far_late = spread(parts, factor.reshape(2, 512, 1024), early_0)
+    other_factor = lax.ppermute(flat_factor, "rhs", [(0, 1), (1, 0)])
 
     scalars = jnp.concatenate([places(y, z), jnp.stack([place, core])]).astype(jnp.int32)
-    return update(scalars, flat_factor, other_factor, rhs, early, near, far_late)
+    return update(scalars, flat_factor, other_factor, rhs, early_0, near, far_late)
 
 
 def solution(mesh):

time: 206 us -> 209 us (1.015)
  other arithmetic: 5.54 us -> 11 us
  starting transfers between devices: 65.9 us -> 62.8 us
    ppermute x22 -> x21, waiting for transfers between devices: 47.7 us -> 43 us  [permute(): return lax.ppermute(value, ROWS, [(flat(*a), flat(*b)) for a, b in moves])]
    concatenate x12, other arithmetic: 0.38 us -> 5.14 us  [spread(): parts = [jnp.concatenate([p, g], axis=0) for p, g in zip(parts, got)]]
    ppermute x20, waiting for transfers between devices: 34.2 us -> 38.9 us  [swap(): return lax.ppermute(value, axis, [(i, i ^ flip) for i in range(4)])]
    ppermute x20, starting transfers between devices: 27.8 us -> 24.4 us  [swap(): return lax.ppermute(value, axis, [(i, i ^ flip) for i in range(4)])]
    ppermute x22 -> x21, starting transfers between devices: 37.4 us -> 37.7 us  [permute(): return lax.ppermute(value, ROWS, [(flat(*a), flat(*b)) for a, b in moves])]
  transfers between devices with their start and end apart: 46 -> 45, of which waited for: 23 -> 24; matrix products, arithmetic and copies ran while one was open for 2% -> 4% of each run, Pallas kernels for 1% -> 3%
where the time goes in v9:
time: 209 us; the launch traced here: 206 us
  waiting for transfers between devices  84.6 us (40%)
  starting transfers between devices  62.8 us (30%)
  Pallas kernels  28.5 us (14%)
  between operations  13.9 us (7%)
  other arithmetic  11 us (5%)
  local copies, waits for them, and re-layouts  5.57 us (3%)
    ppermute x21, waiting for transfers between devices, permute(): return lax.ppermute(value, ROWS, [(flat(*a), flat(*b)) for a, b in moves])  43 us
    ppermute x20, waiting for transfers between devices, swap(): return lax.ppermute(value, axis, [(i, i ^ flip) for i in range(4)])  38.9 us
    ppermute x21, starting transfers between devices, permute(): return lax.ppermute(value, ROWS, [(flat(*a), flat(*b)) for a, b in moves])  37.7 us
    ppermute x20, starting transfers between devices, swap(): return lax.ppermute(value, axis, [(i, i ^ flip) for i in range(4)])  24.4 us
    pallas_call x1, Pallas kernels, update(): pl.pallas_call(update_kernel, grid_spec=pltpu.PrefetchScalarGridSpec(num_...  18.5 us
    pallas_call x4, Pallas kernels, step(): pl.pallas_call(kernel, grid_spec=pltpu.PrefetchScalarGridSpec(num_scalar_...  6.37 us
    concatenate x12, other arithmetic, spread(): parts = [jnp.concatenate([p, g], axis=0) for p, g in zip(parts, got)]  5.14 us
  transfers between devices with their start and end apart: 45, of which 24 were waited for; matrix products, arithmetic and copies ran while one was open for 4% of the time, Pallas kernels for 3%

profile of v9, /device:TPU:6, one launch (start us, length us, event | category | flops | bytes accessed | tf_op | source)
XLA Modules:
  0.0 206.4 jit_solution(966567630891410754)
XLA Ops:
  8.9 3.7 %shard_map.37 = (bf16[608,512]{1,0:T(8,128)(2,1)S(1)}, bf16[608,512]{1,0:T(8,128)(2,1)S(1)}, bf16[608,512]{1,0:T(8,128)(2,1)}, bf16[608,512]{1,0:T(8,128)(2,1)},...) custom-call(f32[2,512,2048]{2,1,0:T(8,128)} %rhs_ref.3, ...), custom_call_target="tpu_custom_call" | custom-call | tf_op jit(solution)/shard_map/pallas_call | solution.py:88
  12.6 4.3 %collective-permute-start = (bf16[608,512]{1,0:T(8,128)(2,1)S(1)}, bf16[608,512]{1,0:T(8,128)(2,1)}, u32[]{:S(2)}, u32[]{:S(2)}) collective-permute-start(bf16[608,512]{1,0:T(8,128)(2,1)S(1)} %get-tuple-element.42), channel_id=1, source_target_pairs={{0,32},{2,34},{4,36},{6,38},{1,33},{3,35},{5,37},{7,39}} | collective-permute-start | bytes 1867784 | tf_op jit(solution)/shard_map/ppermute | solution.py:25
  16.9 3.1 %collective-permute-start.1 = (bf16[608,512]{1,0:T(8,128)(2,1)}, bf16[608,512]{1,0:T(8,128)(2,1)}, u32[]{:S(2)}, u32[]{:S(2)}) collective-permute-start(bf16[608,512]{1,0:T(8,128)(2,1)} %get-tuple-element.43), channel_id=1, source_target_pairs={{0,64},{2,66},{4,68},{6,70},{1,65},{3,67},{5,69},{7,71}} | collective-permute-start | bytes 1867784 | tf_op jit(solution)/shard_map/ppermute | solution.py:25
  20.0 2.1 %collective-permute-start.2 = (bf16[608,512]{1,0:T(8,128)(2,1)}, bf16[608,512]{1,0:T(8,128)(2,1)}, u32[]{:S(2)}, u32[]{:S(2)}) collective-permute-start(bf16[608,512]{1,0:T(8,128)(2,1)} %get-tuple-element.44), channel_id=1, source_target_pairs={{0,96},{2,98},{4,100},{6,102},{1,97},{3,99},{5,101},{7,103}} | collective-permute-start | bytes 1867784 | tf_op jit(solution)/shard_map/ppermute | solution.py:25
  22.1 2.1 %collective-permute-start.6 = (bf16[608,512]{1,0:T(8,128)(2,1)}, bf16[608,512]{1,0:T(8,128)(2,1)}, u32[]{:S(2)}, u32[]{:S(2)}) collective-permute-start(bf16[608,512]{1,0:T(8,128)(2,1)} %get-tuple-element.47), channel_id=1, source_target_pairs={{0,8},{2,10},{4,12},{6,14},{1,9},{3,11},{5,13},{7,15}} | collective-permute-start | bytes 1867784 | tf_op jit(solution)/shard_map/ppermute | solution.py:25
  26.4 4.1 %collective-permute-done = bf16[608,512]{1,0:T(8,128)(2,1)} collective-permute-done((bf16[608,512]{1,0:T(8,128)(2,1)S(1)}, bf16[608,512]{1,0:T(8,128)(2,1)}, u32[]{:S(2)}, u32[]{:S(2)}) %collective-permute-start) | collective-permute-done | bytes 622624 | tf_op jit(solution)/shard_map/ppermute | solution.py:25
  34.0 8.7 %collective-permute-done.1 = bf16[608,512]{1,0:T(8,128)(2,1)} collective-permute-done((bf16[608,512]{1,0:T(8,128)(2,1)}, bf16[608,512]{1,0:T(8,128)(2,1)}, u32[]{:S(2)}, u32[]{:S(2)}) %collective-permute-start.1) | collective-permute-done | bytes 622624 | tf_op jit(solution)/shard_map/ppermute | solution.py:25
  44.3 5.9 %collective-permute-done.7 = bf16[608,512]{1,0:T(8,128)(2,1)} collective-permute-done((bf16[608,512]{1,0:T(8,128)(2,1)S(1)}, bf16[608,512]{1,0:T(8,128)(2,1)}, u32[]{:S(2)}, u32[]{:S(2)}) %collective-permute-start.7) | collective-permute-done | bytes 622624 | tf_op jit(solution)/shard_map/ppermute | solution.py:25
  57.5 5.4 %collective-permute-start.5 = (bf16[896,128]{1,0:T(8,128)(2,1)S(1)}, bf16[896,128]{1,0:T(8,128)(2,1)S(1)}, u32[]{:S(2)}, u32[]{:S(2)}) collective-permute-start(bf16[896,128]{1,0:T(8,128)(2,1)S(1)} %get-tuple-element.93), channel_id=1, source_target_pairs={{0,16},{32,48},{64,80},{96,112},{2,18},{34,50},{66,82},{98,114},{4... | collective-permute-start | bytes 688136 | tf_op jit(solution)/shard_map/ppermute | solution.py:25
  64.4 4.5 %collective-permute-done.5 = bf16[896,128]{1,0:T(8,128)(2,1)S(1)} collective-permute-done((bf16[896,128]{1,0:T(8,128)(2,1)S(1)}, bf16[896,128]{1,0:T(8,128)(2,1)S(1)}, u32[]{:S(2)}, u32[]{:S(2)}) %collective-permute-start.5) | collective-permute-done | bytes 229408 | tf_op jit(solution)/shard_map/ppermute | solution.py:25
  68.9 2.8 %collective-permute-done.3 = bf16[896,128]{1,0:T(8,128)(2,1)S(1)} collective-permute-done((bf16[896,128]{1,0:T(8,128)(2,1)S(1)}, bf16[896,128]{1,0:T(8,128)(2,1)S(1)}, u32[]{:S(2)}, u32[]{:S(2)}) %collective-permute-start.3) | collective-permute-done | bytes 229408 | tf_op jit(solution)/shard_map/ppermute | solution.py:25
  75.8 2.6 %collective-permute-start.13 = (bf16[384,128]{1,0:T(8,128)(2,1)S(1)}, bf16[384,128]{1,0:T(8,128)(2,1)S(1)}, u32[]{:S(2)}, u32[]{:S(2)}) collective-permute-start(bf16[384,128]{1,0:T(8,128)(2,1)S(1)} %slice.121), channel_id=1, source_target_pairs={{0,8},{8,0},{16,24},{24,16},{1,9},{9,1},{17,25},{25,17},{2,10},{10... | collective-permute-start | bytes 294920 | tf_op jit(solution)/shard_map/ppermute | solution.py:33
  83.7 6.7 %collective-permute-done.18 = bf16[2,384,128]{2,1,0:T(8,128)(2,1)S(1)} collective-permute-done((bf16[2,384,128]{2,1,0:T(8,128)(2,1)S(1)}, bf16[2,384,128]{2,1,0:T(8,128)(2,1)S(1)}, u32[]{:S(2)}, u32[]{:S(2)}) %collective-permute-start.18) | collective-permute-done | bytes 196640 | tf_op jit(solution)/shard_map/ppermute | solution.py:33
  96.5 7.0 %collective-permute-done.22.refs_9_ = bf16[512,128]{1,0:T(8,128)(2,1)S(1)} collective-permute-done((bf16[512,128]{1,0:T(8,128)(2,1)S(1)}, bf16[512,128]{1,0:T(8,128)(2,1)S(1)}, u32[]{:S(2)}, u32[]{:S(2)}) %collective-permute-start.22) | collective-permute-done | bytes 131104 | tf_op jit(solution)/shard_map/ppermute | solution.py:25
  106.4 5.6 %collective-permute-done.23.refs_8_ = bf16[512,128]{1,0:T(8,128)(2,1)S(1)} collective-permute-done((bf16[512,128]{1,0:T(8,128)(2,1)S(1)}, bf16[512,128]{1,0:T(8,128)(2,1)S(1)}, u32[]{:S(2)}, u32[]{:S(2)}) %collective-permute-start.23) | collective-permute-done | bytes 131104 | tf_op jit(solution)/shard_map/ppermute | solution.py:25
  123.1 2.6 %collective-permute-start.30 = (bf16[1,384,128]{2,1,0:T(8,128)(2,1)S(1)}, bf16[1,384,128]{2,1,0:T(8,128)(2,1)S(1)}, u32[]{:S(2)}, u32[]{:S(2)}) collective-permute-start(bf16[1,384,128]{2,1,0:T(8,128)(2,1)S(1)} %slice_bitcast_fusion), channel_id=1, source_target_pairs={{0,24},{8,16},{16,8},{24,0},{1,25},{9,17},{17,9},{25,1},{2,26},{10... | collective-permute-start | bytes 294920 | tf_op jit(solution)/shard_map/ppermute | solution.py:33
  125.7 3.2 %collective-permute-done.27 = bf16[1,384,128]{2,1,0:T(8,128)(2,1)S(1)} collective-permute-done((bf16[1,384,128]{2,1,0:T(8,128)(2,1)S(1)}, bf16[1,384,128]{2,1,0:T(8,128)(2,1)S(1)}, u32[]{:S(2)}, u32[]{:S(2)}) %collective-permute-start.27) | collective-permute-done | bytes 98336 | tf_op jit(solution)/shard_map/ppermute | solution.py:33
  136.3 3.2 %collective-permute-start.31 = (bf16[2,384,128]{2,1,0:T(8,128)(2,1)}, bf16[2,384,128]{2,1,0:T(8,128)(2,1)}, u32[]{:S(2)}, u32[]{:S(2)}) collective-permute-start(bf16[2,384,128]{2,1,0:T(8,128)(2,1)} %pad_maximum_fusion.12), channel_id=1, source_target_pairs={{0,96},{32,64},{64,32},{96,0},{1,97},{33,65},{65,33},{97,1},{2,98}... | collective-permute-start | bytes 589832 | tf_op jit(solution)/shard_map/ppermute | solution.py:33
  139.6 2.7 %reshape.179.mine_ref = bf16[2,512,1024]{2,1,0:T(8,128)(2,1)} reshape(bf16[2,512,4,256]{3,2,1,0:T(4,128)(2,1)S(1)} %copy-done) | data formatting | bytes 4194304 | tf_op jit(solution)/shard_map/reshape | solution.py:290
  147.0 3.3 %collective-permute-start.39 = (bf16[4,384,128]{2,1,0:T(8,128)(2,1)S(1)}, bf16[4,384,128]{2,1,0:T(8,128)(2,1)S(1)}, u32[]{:S(2)}, u32[]{:S(2)}) collective-permute-start(bf16[4,384,128]{2,1,0:T(8,128)(2,1)S(1)} %pad_maximum_fusion.9), channel_id=1, source_target_pairs={{0,96},{32,64},{64,32},{96,0},{1,97},{33,65},{65,33},{97,1},{2,98}... | collective-permute-start | bytes 1179656 | tf_op jit(solution)/shard_map/ppermute | solution.py:33
  150.2 5.9 %collective-permute-done.36 = bf16[4,384,128]{2,1,0:T(8,128)(2,1)S(1)} collective-permute-done((bf16[4,384,128]{2,1,0:T(8,128)(2,1)S(1)}, bf16[4,384,128]{2,1,0:T(8,128)(2,1)S(1)}, u32[]{:S(2)}, u32[]{:S(2)}) %collective-permute-start.36) | collective-permute-done | bytes 393248 | tf_op jit(solution)/shard_map/ppermute | solution.py:33
  158.9 3.3 %collective-permute-start.42 = (bf16[8,384,128]{2,1,0:T(8,128)(2,1)S(1)}, bf16[8,384,128]{2,1,0:T(8,128)(2,1)}, u32[]{:S(2)}, u32[]{:S(2)}) collective-permute-start(bf16[8,384,128]{2,1,0:T(8,128)(2,1)S(1)} %pad_maximum_fusion.2.rest_4_.rest_5_), channel_id=1, source_target_pairs={{0,96},{32,64},{64,32},{96,0},{1,97},{33,65},{65,33},{97,1},{2,98}... | collective-permute-start | bytes 2359304 | tf_op jit(solution)/shard_map/ppermute | solution.py:33
  162.6 15.1 %collective-permute-done.40.rest_8_.rest_9_ = bf16[8,384,128]{2,1,0:T(8,128)(2,1)} collective-permute-done((bf16[8,384,128]{2,1,0:T(8,128)(2,1)S(1)}, bf16[8,384,128]{2,1,0:T(8,128)(2,1)}, u32[]{:S(2)}, u32[]{:S(2)}) %collective-permute-start.40) | collective-permute-done | bytes 786464 | tf_op jit(solution)/shard_map/ppermute | solution.py:33
  181.1 18.5 %shard_map.42 = f32[2,512,2048]{2,1,0:T(8,128)} custom-call(s32[66]{0:T(128)S(1)} %pad_add_fusion.1.scalars, bf16[2,512,1024]{2,1,0:T(8,128)(2,1)} %reshape.179.mine_ref, bf16[2,512,1024]{2,1,0:T(8,128)(2,1)} %collective-permute-done.35.other_ref, f32[2,512,2048]{2,1,0:T(8,128)} %rhs_ref.3, bf16[16,512,128]{2,1,0:T(8,128)(2,1)} %bitcast.27, ...), custom_call_target="tpu_custom_call" | custom-call | tf_op jit(solution)/shard_map/pallas_call | solution.py:203
  (132 shorter events, 66.1 us)
Async XLA Ops:
  6.5 123.4 %all-gather.3.cloned.1.call-start = ((), (), s32[]{:S(2)}) async-start(), calls=%async_computation | async-start | bytes 2228224 | tf_op jit(solution)/shard_map/all_gather | solution.py:274
  12.6 17.9 %collective-permute-start = (bf16[608,512]{1,0:T(8,128)(2,1)S(1)}, bf16[608,512]{1,0:T(8,128)(2,1)}, u32[]{:S(2)}, u32[]{:S(2)}) collective-permute-start(bf16[608,512]{1,0:T(8,128)(2,1)S(1)} %get-tuple-element.42), channel_id=1, source_target_pairs={{0,32},{2,34},{4,36},{6,38},{1,33},{3,35},{5,37},{7,39}} | collective-permute-start | bytes 1867784 | tf_op jit(solution)/shard_map/ppermute | solution.py:25
  16.9 25.9 %collective-permute-start.1 = (bf16[608,512]{1,0:T(8,128)(2,1)}, bf16[608,512]{1,0:T(8,128)(2,1)}, u32[]{:S(2)}, u32[]{:S(2)}) collective-permute-start(bf16[608,512]{1,0:T(8,128)(2,1)} %get-tuple-element.43), channel_id=1, source_target_pairs={{0,64},{2,66},{4,68},{6,70},{1,65},{3,67},{5,69},{7,71}} | collective-permute-start | bytes 1867784 | tf_op jit(solution)/shard_map/ppermute | solution.py:25
  20.0 22.7 %collective-permute-start.2 = (bf16[608,512]{1,0:T(8,128)(2,1)}, bf16[608,512]{1,0:T(8,128)(2,1)}, u32[]{:S(2)}, u32[]{:S(2)}) collective-permute-start(bf16[608,512]{1,0:T(8,128)(2,1)} %get-tuple-element.44), channel_id=1, source_target_pairs={{0,96},{2,98},{4,100},{6,102},{1,97},{3,99},{5,101},{7,103}} | collective-permute-start | bytes 1867784 | tf_op jit(solution)/shard_map/ppermute | solution.py:25
  22.1 22.2 %collective-permute-start.6 = (bf16[608,512]{1,0:T(8,128)(2,1)}, bf16[608,512]{1,0:T(8,128)(2,1)}, u32[]{:S(2)}, u32[]{:S(2)}) collective-permute-start(bf16[608,512]{1,0:T(8,128)(2,1)} %get-tuple-element.47), channel_id=1, source_target_pairs={{0,8},{2,10},{4,12},{6,14},{1,9},{3,11},{5,13},{7,15}} | collective-permute-start | bytes 1867784 | tf_op jit(solution)/shard_map/ppermute | solution.py:25
  24.3 26.0 %collective-permute-start.7 = (bf16[608,512]{1,0:T(8,128)(2,1)S(1)}, bf16[608,512]{1,0:T(8,128)(2,1)}, u32[]{:S(2)}, u32[]{:S(2)}) collective-permute-start(bf16[608,512]{1,0:T(8,128)(2,1)S(1)} %get-tuple-element.48), channel_id=1, source_target_pairs={{0,16},{2,18},{4,20},{6,22},{1,17},{3,19},{5,21},{7,23}} | collective-permute-start | bytes 1867784 | tf_op jit(solution)/shard_map/ppermute | solution.py:25
  30.4 19.8 %collective-permute-start.8 = (bf16[608,512]{1,0:T(8,128)(2,1)S(1)}, bf16[608,512]{1,0:T(8,128)(2,1)}, u32[]{:S(2)}, u32[]{:S(2)}) collective-permute-start(bf16[608,512]{1,0:T(8,128)(2,1)S(1)} %get-tuple-element.49), channel_id=1, source_target_pairs={{0,24},{2,26},{4,28},{6,30},{1,25},{3,27},{5,29},{7,31}} | collective-permute-start | bytes 1867784 | tf_op jit(solution)/shard_map/ppermute | solution.py:25
  52.0 10.9 %collective-permute-start.10 = (bf16[896,128]{1,0:T(8,128)(2,1)S(1)}, bf16[896,128]{1,0:T(8,128)(2,1)S(1)}, u32[]{:S(2)}, u32[]{:S(2)}) collective-permute-start(bf16[896,128]{1,0:T(8,128)(2,1)S(1)} %get-tuple-element.109), channel_id=1, source_target_pairs={{0,96},{8,104},{16,112},{24,120},{2,98},{10,106},{18,114},{26,122}... | collective-permute-start | bytes 688136 | tf_op jit(solution)/shard_map/ppermute | solution.py:25
  53.3 10.9 %collective-permute-start.11 = (bf16[896,128]{1,0:T(8,128)(2,1)S(1)}, bf16[896,128]{1,0:T(8,128)(2,1)S(1)}, u32[]{:S(2)}, u32[]{:S(2)}) collective-permute-start(bf16[896,128]{1,0:T(8,128)(2,1)S(1)} %get-tuple-element.110), channel_id=1, source_target_pairs={{0,64},{8,72},{16,80},{24,88},{2,66},{10,74},{18,82},{26,90},{4,68... | collective-permute-start | bytes 688136 | tf_op jit(solution)/shard_map/ppermute | solution.py:25
  54.6 9.6 %collective-permute-start.9 = (bf16[896,128]{1,0:T(8,128)(2,1)S(1)}, bf16[896,128]{1,0:T(8,128)(2,1)S(1)}, u32[]{:S(2)}, u32[]{:S(2)}) collective-permute-start(bf16[896,128]{1,0:T(8,128)(2,1)S(1)} %get-tuple-element.100), channel_id=1, source_target_pairs={{0,32},{8,40},{16,48},{24,56},{2,34},{10,42},{18,50},{26,58},{4,36... | collective-permute-start | bytes 688136 | tf_op jit(solution)/shard_map/ppermute | solution.py:25
  57.5 11.4 %collective-permute-start.5 = (bf16[896,128]{1,0:T(8,128)(2,1)S(1)}, bf16[896,128]{1,0:T(8,128)(2,1)S(1)}, u32[]{:S(2)}, u32[]{:S(2)}) collective-permute-start(bf16[896,128]{1,0:T(8,128)(2,1)S(1)} %get-tuple-element.93), channel_id=1, source_target_pairs={{0,16},{32,48},{64,80},{96,112},{2,18},{34,50},{66,82},{98,114},{4... | collective-permute-start | bytes 688136 | tf_op jit(solution)/shard_map/ppermute | solution.py:25
  73.7 9.0 %collective-permute-start.15 = (bf16[512,128]{1,0:T(8,128)(2,1)S(1)}, bf16[512,128]{1,0:T(8,128)(2,1)S(1)}, u32[]{:S(2)}, u32[]{:S(2)}) collective-permute-start(bf16[512,128]{1,0:T(8,128)(2,1)S(1)} %shard_map.38), channel_id=1, source_target_pairs={{0,6},{8,14},{16,22},{24,30},{32,38},{40,46},{48,54},{56,62},{64,7... | collective-permute-start | bytes 393224 | tf_op jit(solution)/shard_map/ppermute | solution.py:25
  94.5 8.9 %collective-permute-start.22 = (bf16[512,128]{1,0:T(8,128)(2,1)S(1)}, bf16[512,128]{1,0:T(8,128)(2,1)S(1)}, u32[]{:S(2)}, u32[]{:S(2)}) collective-permute-start(bf16[512,128]{1,0:T(8,128)(2,1)S(1)} %get-tuple-element.61), channel_id=1, source_target_pairs={{2,6},{10,14},{18,22},{26,30},{34,38},{42,46},{50,54},{58,62},{66,... | collective-permute-start | bytes 393224 | tf_op jit(solution)/shard_map/ppermute | solution.py:25
  132.7 9.5 %collective-permute-start.34 = (bf16[2,384,128]{2,1,0:T(8,128)(2,1)}, bf16[2,384,128]{2,1,0:T(8,128)(2,1)S(1)}, u32[]{:S(2)}, u32[]{:S(2)}) collective-permute-start(bf16[2,384,128]{2,1,0:T(8,128)(2,1)} %pad_maximum_fusion.15), channel_id=1, source_target_pairs={{0,8},{8,0},{16,24},{24,16},{1,9},{9,1},{17,25},{25,17},{2,10},{10... | collective-permute-start | bytes 589832 | tf_op jit(solution)/shard_map/ppermute | solution.py:33
  133.3 9.0 %collective-permute-start.33 = (bf16[2,384,128]{2,1,0:T(8,128)(2,1)}, bf16[2,384,128]{2,1,0:T(8,128)(2,1)S(1)}, u32[]{:S(2)}, u32[]{:S(2)}) collective-permute-start(bf16[2,384,128]{2,1,0:T(8,128)(2,1)} %pad_maximum_fusion.14), channel_id=1, source_target_pairs={{0,24},{8,16},{16,8},{24,0},{1,25},{9,17},{17,9},{25,1},{2,26},{10... | collective-permute-start | bytes 589832 | tf_op jit(solution)/shard_map/ppermute | solution.py:33
  143.5 37.5 %collective-permute-start.35 = (bf16[2,512,1024]{2,1,0:T(8,128)(2,1)}, bf16[2,512,1024]{2,1,0:T(8,128)(2,1)}, u32[]{:S(2)}, u32[]{:S(2)}) collective-permute-start(bf16[2,512,1024]{2,1,0:T(8,128)(2,1)} %reshape.179.mine_ref), channel_id=1, source_target_pairs={{0,1},{1,0},{2,3},{3,2},{4,5},{5,4},{6,7},{7,6},{8,9},{9,8},{10,11... | collective-permute-start | bytes 6291464 | tf_op jit(solution)/shard_map/ppermute | solution.py:291
  144.5 11.6 %collective-permute-start.36 = (bf16[4,384,128]{2,1,0:T(8,128)(2,1)S(1)}, bf16[4,384,128]{2,1,0:T(8,128)(2,1)S(1)}, u32[]{:S(2)}, u32[]{:S(2)}) collective-permute-start(bf16[4,384,128]{2,1,0:T(8,128)(2,1)S(1)} %pad_maximum_fusion.6), channel_id=1, source_target_pairs={{0,8},{8,0},{16,24},{24,16},{1,9},{9,1},{17,25},{25,17},{2,10},{10... | collective-permute-start | bytes 1179656 | tf_op jit(solution)/shard_map/ppermute | solution.py:33
  146.1 12.5 %collective-permute-start.37 = (bf16[4,384,128]{2,1,0:T(8,128)(2,1)S(1)}, bf16[4,384,128]{2,1,0:T(8,128)(2,1)S(1)}, u32[]{:S(2)}, u32[]{:S(2)}) collective-permute-start(bf16[4,384,128]{2,1,0:T(8,128)(2,1)S(1)} %pad_maximum_fusion.7), channel_id=1, source_target_pairs={{0,24},{8,16},{16,8},{24,0},{1,25},{9,17},{17,9},{25,1},{2,26},{10... | collective-permute-start | bytes 1179656 | tf_op jit(solution)/shard_map/ppermute | solution.py:33
  146.8 12.0 %collective-permute-start.38 = (bf16[4,384,128]{2,1,0:T(8,128)(2,1)S(1)}, bf16[4,384,128]{2,1,0:T(8,128)(2,1)S(1)}, u32[]{:S(2)}, u32[]{:S(2)}) collective-permute-start(bf16[4,384,128]{2,1,0:T(8,128)(2,1)S(1)} %pad_maximum_fusion.8), channel_id=1, source_target_pairs={{0,32},{32,0},{64,96},{96,64},{1,33},{33,1},{65,97},{97,65},{2,34}... | collective-permute-start | bytes 1179656 | tf_op jit(solution)/shard_map/ppermute | solution.py:33
  147.0 15.2 %collective-permute-start.39 = (bf16[4,384,128]{2,1,0:T(8,128)(2,1)S(1)}, bf16[4,384,128]{2,1,0:T(8,128)(2,1)S(1)}, u32[]{:S(2)}, u32[]{:S(2)}) collective-permute-start(bf16[4,384,128]{2,1,0:T(8,128)(2,1)S(1)} %pad_maximum_fusion.9), channel_id=1, source_target_pairs={{0,96},{32,64},{64,32},{96,0},{1,97},{33,65},{65,33},{97,1},{2,98}... | collective-permute-start | bytes 1179656 | tf_op jit(solution)/shard_map/ppermute | solution.py:33
  157.1 20.6 %collective-permute-start.40 = (bf16[8,384,128]{2,1,0:T(8,128)(2,1)S(1)}, bf16[8,384,128]{2,1,0:T(8,128)(2,1)}, u32[]{:S(2)}, u32[]{:S(2)}) collective-permute-start(bf16[8,384,128]{2,1,0:T(8,128)(2,1)S(1)} %pad_maximum_fusion.rest_0_.rest_1_), channel_id=1, source_target_pairs={{0,24},{8,16},{16,8},{24,0},{1,25},{9,17},{17,9},{25,1},{2,26},{10... | collective-permute-start | bytes 2359304 | tf_op jit(solution)/shard_map/ppermute | solution.py:33
  158.7 19.0 %collective-permute-start.41 = (bf16[8,384,128]{2,1,0:T(8,128)(2,1)S(1)}, bf16[8,384,128]{2,1,0:T(8,128)(2,1)}, u32[]{:S(2)}, u32[]{:S(2)}) collective-permute-start(bf16[8,384,128]{2,1,0:T(8,128)(2,1)S(1)} %pad_maximum_fusion.1.rest_2_.rest_3_), channel_id=1, source_target_pairs={{0,8},{8,0},{16,24},{24,16},{1,9},{9,1},{17,25},{25,17},{2,10},{10... | collective-permute-start | bytes 2359304 | tf_op jit(solution)/shard_map/ppermute | solution.py:33
  158.9 20.5 %collective-permute-start.42 = (bf16[8,384,128]{2,1,0:T(8,128)(2,1)S(1)}, bf16[8,384,128]{2,1,0:T(8,128)(2,1)}, u32[]{:S(2)}, u32[]{:S(2)}) collective-permute-start(bf16[8,384,128]{2,1,0:T(8,128)(2,1)S(1)} %pad_maximum_fusion.2.rest_4_.rest_5_), channel_id=1, source_target_pairs={{0,96},{32,64},{64,32},{96,0},{1,97},{33,65},{65,33},{97,1},{2,98}... | collective-permute-start | bytes 2359304 | tf_op jit(solution)/shard_map/ppermute | solution.py:33
  162.3 18.8 %collective-permute-start.43 = (bf16[8,384,128]{2,1,0:T(8,128)(2,1)S(1)}, bf16[8,384,128]{2,1,0:T(8,128)(2,1)}, u32[]{:S(2)}, u32[]{:S(2)}) collective-permute-start(bf16[8,384,128]{2,1,0:T(8,128)(2,1)S(1)} %pad_maximum_fusion.3.rest_6_.rest_7_), channel_id=1, source_target_pairs={{0,32},{32,0},{64,96},{96,64},{1,33},{33,1},{65,97},{97,65},{2,34}... | collective-permute-start | bytes 2359304 | tf_op jit(solution)/shard_map/ppermute | solution.py:33
  (22 other events, 158.4 us)
Sparse Core Ops, SparseCore 0:
  83.5 46.3 all-gather.2

commit v10 on v9

--- a/solution.py
+++ b/solution.py
@@ -33,16 +33,16 @@
     return lax.ppermute(value, axis, [(i, i ^ flip) for i in range(4)])
 
 
-def spread(parts, factor, early):
+def spread(parts, early, other):
     parts = [p[None] for p in parts]
     for step in range(3):
         got = [swap(p, *order[step]) for p, order in zip(parts, ORDERS)]
         if step == 0:
-            early, *got = lax.optimization_barrier((early, *got))
-        if step == 1:
-            factor, *got = lax.optimization_barrier((factor, *got))
+            early, got[3] = lax.optimization_barrier((early, got[3]))
         parts = [jnp.concatenate([p, g], axis=0) for p, g in zip(parts, got)]
-    return parts, factor, early, [swap(p, *order[3]) for p, order in zip(parts, ORDERS)]
+    got = [swap(p, *order[3]) for p, order in zip(parts, ORDERS)]
+    other, *got = lax.optimization_barrier((other, *got))
+    return parts, early, other, got
 
 
 def places(y, z):
@@ -287,9 +287,9 @@
     panel_3 = jnp.where(x == 3, sent, jnp.where(x == 2, back, jnp.where(x == 1, far, wrap)))
     cat = lambda *v: jnp.concatenate(v, axis=0)
     parts = [panel_1[:384], cat(panel_1[384:], panel_2[:256]), cat(panel_2[256:], panel_3[:128]), panel_3[128:]]
-    near, flat_factor, early_0, far_late = spread(parts, factor.reshape(2, 512, 1024), early_0)
+    flat_factor = factor.reshape(2, 512, 1024)
     other_factor = lax.ppermute(flat_factor, "rhs", [(0, 1), (1, 0)])
-
+    near, early_0, other_factor, far_late = spread(parts, early_0, other_factor)
     scalars = jnp.concatenate([places(y, z), jnp.stack([place, core])]).astype(jnp.int32)
     return update(scalars, flat_factor, other_factor, rhs, early_0, near, far_late)
 

time: 209 us -> 199 us (0.952)
  waiting for transfers between devices: 84.6 us -> 79 us
  other arithmetic: 11 us -> 7.46 us
    concatenate x12, other arithmetic: 5.14 us -> 1.55 us  [spread(): parts = [jnp.concatenate([p, g], axis=0) for p, g in zip(parts, got)]]
    ppermute x21, waiting for transfers between devices: 43 us -> 40.3 us  [permute(): return lax.ppermute(value, ROWS, [(flat(*a), flat(*b)) for a, b in moves])]
  transfers between devices with their start and end apart: 45 -> 45, of which waited for: 24 -> 22; matrix products, arithmetic and copies ran while one was open for 4% -> 5% of each run, Pallas kernels for 3% -> 3%
where the time goes in v10:
time: 199 us; the launch traced here: 198 us
  waiting for transfers between devices  79 us (40%)
  starting transfers between devices  61.5 us (31%)
  Pallas kernels  28.5 us (14%)
  between operations  14 us (7%)
  other arithmetic  7.46 us (4%)
  local copies, waits for them, and re-layouts  7.29 us (4%)
    ppermute x21, waiting for transfers between devices, permute(): return lax.ppermute(value, ROWS, [(flat(*a), flat(*b)) for a, b in moves])  40.3 us
    ppermute x21, starting transfers between devices, permute(): return lax.ppermute(value, ROWS, [(flat(*a), flat(*b)) for a, b in moves])  37.6 us
    ppermute x20, waiting for transfers between devices, swap(): return lax.ppermute(value, axis, [(i, i ^ flip) for i in range(4)])  37.1 us
    ppermute x20, starting transfers between devices, swap(): return lax.ppermute(value, axis, [(i, i ^ flip) for i in range(4)])  23.2 us
    pallas_call x1, Pallas kernels, update(): pl.pallas_call(update_kernel, grid_spec=pltpu.PrefetchScalarGridSpec(num_...  18.5 us
    pallas_call x4, Pallas kernels, step(): pl.pallas_call(kernel, grid_spec=pltpu.PrefetchScalarGridSpec(num_scalar_...  6.37 us
    reshape x1, local copies, waits for them, and re-layouts, local(): flat_factor = factor.reshape(2, 512, 1024)  4.44 us
  transfers between devices with their start and end apart: 45, of which 22 were waited for; matrix products, arithmetic and copies ran while one was open for 5% of the time, Pallas kernels for 3%

profile of v10, /device:TPU:6, one launch (start us, length us, event | category | flops | bytes accessed | tf_op | source)
XLA Modules:
  0.0 197.8 jit_solution(14111244341736397469)
XLA Ops:
  8.9 3.7 %shard_map.37 = (bf16[608,512]{1,0:T(8,128)(2,1)S(1)}, bf16[608,512]{1,0:T(8,128)(2,1)S(1)}, bf16[608,512]{1,0:T(8,128)(2,1)}, bf16[608,512]{1,0:T(8,128)(2,1)},...) custom-call(f32[2,512,2048]{2,1,0:T(8,128)} %rhs_ref.3, ...), custom_call_target="tpu_custom_call" | custom-call | tf_op jit(solution)/shard_map/pallas_call | solution.py:88
  12.6 4.3 %collective-permute-start.1 = (bf16[608,512]{1,0:T(8,128)(2,1)S(1)}, bf16[608,512]{1,0:T(8,128)(2,1)}, u32[]{:S(2)}, u32[]{:S(2)}) collective-permute-start(bf16[608,512]{1,0:T(8,128)(2,1)S(1)} %get-tuple-element.39), channel_id=1, source_target_pairs={{0,32},{2,34},{4,36},{6,38},{1,33},{3,35},{5,37},{7,39}} | collective-permute-start | bytes 1867784 | tf_op jit(solution)/shard_map/ppermute | solution.py:25
  16.9 3.1 %collective-permute-start.2 = (bf16[608,512]{1,0:T(8,128)(2,1)}, bf16[608,512]{1,0:T(8,128)(2,1)}, u32[]{:S(2)}, u32[]{:S(2)}) collective-permute-start(bf16[608,512]{1,0:T(8,128)(2,1)} %get-tuple-element.40), channel_id=1, source_target_pairs={{0,64},{2,66},{4,68},{6,70},{1,65},{3,67},{5,69},{7,71}} | collective-permute-start | bytes 1867784 | tf_op jit(solution)/shard_map/ppermute | solution.py:25
  26.4 4.1 %collective-permute-done.1 = bf16[608,512]{1,0:T(8,128)(2,1)} collective-permute-done((bf16[608,512]{1,0:T(8,128)(2,1)S(1)}, bf16[608,512]{1,0:T(8,128)(2,1)}, u32[]{:S(2)}, u32[]{:S(2)}) %collective-permute-start.1) | collective-permute-done | bytes 622624 | tf_op jit(solution)/shard_map/ppermute | solution.py:25
  34.0 8.7 %collective-permute-done.2 = bf16[608,512]{1,0:T(8,128)(2,1)} collective-permute-done((bf16[608,512]{1,0:T(8,128)(2,1)}, bf16[608,512]{1,0:T(8,128)(2,1)}, u32[]{:S(2)}, u32[]{:S(2)}) %collective-permute-start.2) | collective-permute-done | bytes 622624 | tf_op jit(solution)/shard_map/ppermute | solution.py:25
  44.3 5.9 %collective-permute-done.8 = bf16[608,512]{1,0:T(8,128)(2,1)} collective-permute-done((bf16[608,512]{1,0:T(8,128)(2,1)S(1)}, bf16[608,512]{1,0:T(8,128)(2,1)}, u32[]{:S(2)}, u32[]{:S(2)}) %collective-permute-start.8) | collective-permute-done | bytes 622624 | tf_op jit(solution)/shard_map/ppermute | solution.py:25
  57.5 5.4 %collective-permute-start.6 = (bf16[896,128]{1,0:T(8,128)(2,1)S(1)}, bf16[896,128]{1,0:T(8,128)(2,1)S(1)}, u32[]{:S(2)}, u32[]{:S(2)}) collective-permute-start(bf16[896,128]{1,0:T(8,128)(2,1)S(1)} %get-tuple-element.87), channel_id=1, source_target_pairs={{0,16},{32,48},{64,80},{96,112},{2,18},{34,50},{66,82},{98,114},{4... | collective-permute-start | bytes 688136 | tf_op jit(solution)/shard_map/ppermute | solution.py:25
  64.4 4.5 %collective-permute-done.6 = bf16[896,128]{1,0:T(8,128)(2,1)S(1)} collective-permute-done((bf16[896,128]{1,0:T(8,128)(2,1)S(1)}, bf16[896,128]{1,0:T(8,128)(2,1)S(1)}, u32[]{:S(2)}, u32[]{:S(2)}) %collective-permute-start.6) | collective-permute-done | bytes 229408 | tf_op jit(solution)/shard_map/ppermute | solution.py:25
  68.9 2.8 %collective-permute-done.4 = bf16[896,128]{1,0:T(8,128)(2,1)S(1)} collective-permute-done((bf16[896,128]{1,0:T(8,128)(2,1)S(1)}, bf16[896,128]{1,0:T(8,128)(2,1)S(1)}, u32[]{:S(2)}, u32[]{:S(2)}) %collective-permute-start.4) | collective-permute-done | bytes 229408 | tf_op jit(solution)/shard_map/ppermute | solution.py:25
  75.9 2.6 %collective-permute-start.14 = (bf16[384,128]{1,0:T(8,128)(2,1)S(1)}, bf16[384,128]{1,0:T(8,128)(2,1)S(1)}, u32[]{:S(2)}, u32[]{:S(2)}) collective-permute-start(bf16[384,128]{1,0:T(8,128)(2,1)S(1)} %slice.121), channel_id=1, source_target_pairs={{0,8},{8,0},{16,24},{24,16},{1,9},{9,1},{17,25},{25,17},{2,10},{10... | collective-permute-start | bytes 294920 | tf_op jit(solution)/shard_map/ppermute | solution.py:33
  83.7 6.7 %collective-permute-done.19 = bf16[2,384,128]{2,1,0:T(8,128)(2,1)S(1)} collective-permute-done((bf16[2,384,128]{2,1,0:T(8,128)(2,1)S(1)}, bf16[2,384,128]{2,1,0:T(8,128)(2,1)S(1)}, u32[]{:S(2)}, u32[]{:S(2)}) %collective-permute-start.19) | collective-permute-done | bytes 196640 | tf_op jit(solution)/shard_map/ppermute | solution.py:33
  96.5 7.0 %collective-permute-done.23.refs_9_ = bf16[512,128]{1,0:T(8,128)(2,1)S(1)} collective-permute-done((bf16[512,128]{1,0:T(8,128)(2,1)S(1)}, bf16[512,128]{1,0:T(8,128)(2,1)S(1)}, u32[]{:S(2)}, u32[]{:S(2)}) %collective-permute-start.23) | collective-permute-done | bytes 131104 | tf_op jit(solution)/shard_map/ppermute | solution.py:25
  106.4 5.6 %collective-permute-done.24.refs_8_ = bf16[512,128]{1,0:T(8,128)(2,1)S(1)} collective-permute-done((bf16[512,128]{1,0:T(8,128)(2,1)S(1)}, bf16[512,128]{1,0:T(8,128)(2,1)S(1)}, u32[]{:S(2)}, u32[]{:S(2)}) %collective-permute-start.24) | collective-permute-done | bytes 131104 | tf_op jit(solution)/shard_map/ppermute | solution.py:25
  117.8 4.4 %reshape.179.mine_ref = bf16[2,512,1024]{2,1,0:T(8,128)(2,1)} reshape(bf16[2,512,4,256]{3,2,1,0:T(4,128)(2,1)} %param.4) | data formatting | bytes 4194304 | tf_op jit(solution)/shard_map/reshape | solution.py:290
  124.8 2.7 %collective-permute-start.40 = (bf16[1,384,128]{2,1,0:T(8,128)(2,1)S(1)}, bf16[1,384,128]{2,1,0:T(8,128)(2,1)S(1)}, u32[]{:S(2)}, u32[]{:S(2)}) collective-permute-start(bf16[1,384,128]{2,1,0:T(8,128)(2,1)S(1)} %slice_bitcast_fusion), channel_id=1, source_target_pairs={{0,24},{8,16},{16,8},{24,0},{1,25},{9,17},{17,9},{25,1},{2,26},{10... | collective-permute-start | bytes 294920 | tf_op jit(solution)/shard_map/ppermute | solution.py:33
  128.4 2.3 %collective-permute-start.37 = (bf16[2,384,128]{2,1,0:T(8,128)(2,1)S(1)}, bf16[2,384,128]{2,1,0:T(8,128)(2,1)S(1)}, u32[]{:S(2)}, u32[]{:S(2)}) collective-permute-start(bf16[2,384,128]{2,1,0:T(8,128)(2,1)S(1)} %pad_maximum_fusion.14), channel_id=1, source_target_pairs={{0,24},{8,16},{16,8},{24,0},{1,25},{9,17},{17,9},{25,1},{2,26},{10... | collective-permute-start | bytes 589832 | tf_op jit(solution)/shard_map/ppermute | solution.py:33
  131.4 2.3 %collective-permute-start.27 = (bf16[2,384,128]{2,1,0:T(8,128)(2,1)S(1)}, bf16[2,384,128]{2,1,0:T(8,128)(2,1)S(1)}, u32[]{:S(2)}, u32[]{:S(2)}) collective-permute-start(bf16[2,384,128]{2,1,0:T(8,128)(2,1)S(1)} %pad_maximum_fusion.12), channel_id=1, source_target_pairs={{0,96},{32,64},{64,32},{96,0},{1,97},{33,65},{65,33},{97,1},{2,98}... | collective-permute-start | bytes 589832 | tf_op jit(solution)/shard_map/ppermute | solution.py:33
  133.7 2.9 %collective-permute-done.37 = bf16[2,384,128]{2,1,0:T(8,128)(2,1)S(1)} collective-permute-done((bf16[2,384,128]{2,1,0:T(8,128)(2,1)S(1)}, bf16[2,384,128]{2,1,0:T(8,128)(2,1)S(1)}, u32[]{:S(2)}, u32[]{:S(2)}) %collective-permute-start.37) | collective-permute-done | bytes 196640 | tf_op jit(solution)/shard_map/ppermute | solution.py:33
  142.1 3.4 %collective-permute-done.41 = bf16[2,384,128]{2,1,0:T(8,128)(2,1)S(1)} collective-permute-done((bf16[2,384,128]{2,1,0:T(8,128)(2,1)S(1)}, bf16[2,384,128]{2,1,0:T(8,128)(2,1)S(1)}, u32[]{:S(2)}, u32[]{:S(2)}) %collective-permute-start.41) | collective-permute-done | bytes 196640 | tf_op jit(solution)/shard_map/ppermute | solution.py:33
  145.6 2.7 %collective-permute-start.42 = (bf16[4,384,128]{2,1,0:T(8,128)(2,1)S(1)}, bf16[4,384,128]{2,1,0:T(8,128)(2,1)S(1)}, u32[]{:S(2)}, u32[]{:S(2)}) collective-permute-start(bf16[4,384,128]{2,1,0:T(8,128)(2,1)S(1)} %pad_maximum_fusion.9), channel_id=1, source_target_pairs={{0,96},{32,64},{64,32},{96,0},{1,97},{33,65},{65,33},{97,1},{2,98}... | collective-permute-start | bytes 1179656 | tf_op jit(solution)/shard_map/ppermute | solution.py:33
  151.8 2.7 %collective-permute-start.29 = (bf16[8,384,128]{2,1,0:T(8,128)(2,1)S(1)}, bf16[8,384,128]{2,1,0:T(8,128)(2,1)}, u32[]{:S(2)}, u32[]{:S(2)}) collective-permute-start(bf16[8,384,128]{2,1,0:T(8,128)(2,1)S(1)} %pad_maximum_fusion.rest_0_.rest_1_), channel_id=1, source_target_pairs={{0,24},{8,16},{16,8},{24,0},{1,25},{9,17},{17,9},{25,1},{2,26},{10... | collective-permute-start | bytes 2359304 | tf_op jit(solution)/shard_map/ppermute | solution.py:33
  154.6 4.2 %collective-permute-done.42 = bf16[4,384,128]{2,1,0:T(8,128)(2,1)S(1)} collective-permute-done((bf16[4,384,128]{2,1,0:T(8,128)(2,1)S(1)}, bf16[4,384,128]{2,1,0:T(8,128)(2,1)S(1)}, u32[]{:S(2)}, u32[]{:S(2)}) %collective-permute-start.42) | collective-permute-done | bytes 393248 | tf_op jit(solution)/shard_map/ppermute | solution.py:33
  159.3 12.3 %collective-permute-done.39.rest_12_.rest_13_ = bf16[8,384,128]{2,1,0:T(8,128)(2,1)} collective-permute-done((bf16[8,384,128]{2,1,0:T(8,128)(2,1)S(1)}, bf16[8,384,128]{2,1,0:T(8,128)(2,1)}, u32[]{:S(2)}, u32[]{:S(2)}) %collective-permute-start.39) | collective-permute-done | bytes 786464 | tf_op jit(solution)/shard_map/ppermute | solution.py:33
  172.5 18.5 %shard_map.42 = f32[2,512,2048]{2,1,0:T(8,128)} custom-call(s32[66]{0:T(128)S(1)} %pad_add_fusion.1.scalars, bf16[2,512,1024]{2,1,0:T(8,128)(2,1)} %reshape.179.mine_ref, bf16[2,512,1024]{2,1,0:T(8,128)(2,1)} %collective-permute-done.other_ref, f32[2,512,2048]{2,1,0:T(8,128)} %rhs_ref.3, bf16[16,512,128]{2,1,0:T(8,128)(2,1)} %bitcast.27, ...), custom_call_target="tpu_custom_call" | custom-call | tf_op jit(solution)/shard_map/pallas_call | solution.py:203
  (130 shorter events, 60.8 us)
Async XLA Ops:
  6.5 131.0 %all-gather.3.cloned.1.call-start = ((), (), s32[]{:S(2)}) async-start(), calls=%async_computation | async-start | bytes 2228224 | tf_op jit(solution)/shard_map/all_gather | solution.py:274
  12.6 17.9 %collective-permute-start.1 = (bf16[608,512]{1,0:T(8,128)(2,1)S(1)}, bf16[608,512]{1,0:T(8,128)(2,1)}, u32[]{:S(2)}, u32[]{:S(2)}) collective-permute-start(bf16[608,512]{1,0:T(8,128)(2,1)S(1)} %get-tuple-element.39), channel_id=1, source_target_pairs={{0,32},{2,34},{4,36},{6,38},{1,33},{3,35},{5,37},{7,39}} | collective-permute-start | bytes 1867784 | tf_op jit(solution)/shard_map/ppermute | solution.py:25
  16.9 25.9 %collective-permute-start.2 = (bf16[608,512]{1,0:T(8,128)(2,1)}, bf16[608,512]{1,0:T(8,128)(2,1)}, u32[]{:S(2)}, u32[]{:S(2)}) collective-permute-start(bf16[608,512]{1,0:T(8,128)(2,1)} %get-tuple-element.40), channel_id=1, source_target_pairs={{0,64},{2,66},{4,68},{6,70},{1,65},{3,67},{5,69},{7,71}} | collective-permute-start | bytes 1867784 | tf_op jit(solution)/shard_map/ppermute | solution.py:25
  20.0 22.7 %collective-permute-start.3 = (bf16[608,512]{1,0:T(8,128)(2,1)}, bf16[608,512]{1,0:T(8,128)(2,1)}, u32[]{:S(2)}, u32[]{:S(2)}) collective-permute-start(bf16[608,512]{1,0:T(8,128)(2,1)} %get-tuple-element.41), channel_id=1, source_target_pairs={{0,96},{2,98},{4,100},{6,102},{1,97},{3,99},{5,101},{7,103}} | collective-permute-start | bytes 1867784 | tf_op jit(solution)/shard_map/ppermute | solution.py:25
  22.1 22.2 %collective-permute-start.7 = (bf16[608,512]{1,0:T(8,128)(2,1)}, bf16[608,512]{1,0:T(8,128)(2,1)}, u32[]{:S(2)}, u32[]{:S(2)}) collective-permute-start(bf16[608,512]{1,0:T(8,128)(2,1)} %get-tuple-element.44), channel_id=1, source_target_pairs={{0,8},{2,10},{4,12},{6,14},{1,9},{3,11},{5,13},{7,15}} | collective-permute-start | bytes 1867784 | tf_op jit(solution)/shard_map/ppermute | solution.py:25
  24.3 26.0 %collective-permute-start.8 = (bf16[608,512]{1,0:T(8,128)(2,1)S(1)}, bf16[608,512]{1,0:T(8,128)(2,1)}, u32[]{:S(2)}, u32[]{:S(2)}) collective-permute-start(bf16[608,512]{1,0:T(8,128)(2,1)S(1)} %get-tuple-element.45), channel_id=1, source_target_pairs={{0,16},{2,18},{4,20},{6,22},{1,17},{3,19},{5,21},{7,23}} | collective-permute-start | bytes 1867784 | tf_op jit(solution)/shard_map/ppermute | solution.py:25
  30.4 19.8 %collective-permute-start.9 = (bf16[608,512]{1,0:T(8,128)(2,1)S(1)}, bf16[608,512]{1,0:T(8,128)(2,1)}, u32[]{:S(2)}, u32[]{:S(2)}) collective-permute-start(bf16[608,512]{1,0:T(8,128)(2,1)S(1)} %get-tuple-element.46), channel_id=1, source_target_pairs={{0,24},{2,26},{4,28},{6,30},{1,25},{3,27},{5,29},{7,31}} | collective-permute-start | bytes 1867784 | tf_op jit(solution)/shard_map/ppermute | solution.py:25
  52.0 10.9 %collective-permute-start.11 = (bf16[896,128]{1,0:T(8,128)(2,1)S(1)}, bf16[896,128]{1,0:T(8,128)(2,1)S(1)}, u32[]{:S(2)}, u32[]{:S(2)}) collective-permute-start(bf16[896,128]{1,0:T(8,128)(2,1)S(1)} %get-tuple-element.103), channel_id=1, source_target_pairs={{0,96},{8,104},{16,112},{24,120},{2,98},{10,106},{18,114},{26,122}... | collective-permute-start | bytes 688136 | tf_op jit(solution)/shard_map/ppermute | solution.py:25
  53.3 10.9 %collective-permute-start.12 = (bf16[896,128]{1,0:T(8,128)(2,1)S(1)}, bf16[896,128]{1,0:T(8,128)(2,1)S(1)}, u32[]{:S(2)}, u32[]{:S(2)}) collective-permute-start(bf16[896,128]{1,0:T(8,128)(2,1)S(1)} %get-tuple-element.104), channel_id=1, source_target_pairs={{0,64},{8,72},{16,80},{24,88},{2,66},{10,74},{18,82},{26,90},{4,68... | collective-permute-start | bytes 688136 | tf_op jit(solution)/shard_map/ppermute | solution.py:25
  54.6 9.6 %collective-permute-start.10 = (bf16[896,128]{1,0:T(8,128)(2,1)S(1)}, bf16[896,128]{1,0:T(8,128)(2,1)S(1)}, u32[]{:S(2)}, u32[]{:S(2)}) collective-permute-start(bf16[896,128]{1,0:T(8,128)(2,1)S(1)} %get-tuple-element.94), channel_id=1, source_target_pairs={{0,32},{8,40},{16,48},{24,56},{2,34},{10,42},{18,50},{26,58},{4,36... | collective-permute-start | bytes 688136 | tf_op jit(solution)/shard_map/ppermute | solution.py:25
  57.5 11.4 %collective-permute-start.6 = (bf16[896,128]{1,0:T(8,128)(2,1)S(1)}, bf16[896,128]{1,0:T(8,128)(2,1)S(1)}, u32[]{:S(2)}, u32[]{:S(2)}) collective-permute-start(bf16[896,128]{1,0:T(8,128)(2,1)S(1)} %get-tuple-element.87), channel_id=1, source_target_pairs={{0,16},{32,48},{64,80},{96,112},{2,18},{34,50},{66,82},{98,114},{4... | collective-permute-start | bytes 688136 | tf_op jit(solution)/shard_map/ppermute | solution.py:25
  73.8 9.0 %collective-permute-start.16 = (bf16[512,128]{1,0:T(8,128)(2,1)S(1)}, bf16[512,128]{1,0:T(8,128)(2,1)S(1)}, u32[]{:S(2)}, u32[]{:S(2)}) collective-permute-start(bf16[512,128]{1,0:T(8,128)(2,1)S(1)} %shard_map.38), channel_id=1, source_target_pairs={{0,6},{8,14},{16,22},{24,30},{32,38},{40,46},{48,54},{56,62},{64,7... | collective-permute-start | bytes 393224 | tf_op jit(solution)/shard_map/ppermute | solution.py:25
  94.5 8.9 %collective-permute-start.23 = (bf16[512,128]{1,0:T(8,128)(2,1)S(1)}, bf16[512,128]{1,0:T(8,128)(2,1)S(1)}, u32[]{:S(2)}, u32[]{:S(2)}) collective-permute-start(bf16[512,128]{1,0:T(8,128)(2,1)S(1)} %get-tuple-element.58), channel_id=1, source_target_pairs={{2,6},{10,14},{18,22},{26,30},{34,38},{42,46},{50,54},{58,62},{66,... | collective-permute-start | bytes 393224 | tf_op jit(solution)/shard_map/ppermute | solution.py:25
  122.3 37.0 %collective-permute-start = (bf16[2,512,1024]{2,1,0:T(8,128)(2,1)}, bf16[2,512,1024]{2,1,0:T(8,128)(2,1)}, u32[]{:S(2)}, u32[]{:S(2)}) collective-permute-start(bf16[2,512,1024]{2,1,0:T(8,128)(2,1)} %reshape.179.mine_ref), channel_id=1, source_target_pairs={{0,1},{1,0},{2,3},{3,2},{4,5},{5,4},{6,7},{7,6},{8,9},{9,8},{10,11... | collective-permute-start | bytes 6291464 | tf_op jit(solution)/shard_map/ppermute | solution.py:291
  124.8 12.8 %collective-permute-start.40 = (bf16[1,384,128]{2,1,0:T(8,128)(2,1)S(1)}, bf16[1,384,128]{2,1,0:T(8,128)(2,1)S(1)}, u32[]{:S(2)}, u32[]{:S(2)}) collective-permute-start(bf16[1,384,128]{2,1,0:T(8,128)(2,1)S(1)} %slice_bitcast_fusion), channel_id=1, source_target_pairs={{0,24},{8,16},{16,8},{24,0},{1,25},{9,17},{17,9},{25,1},{2,26},{10... | collective-permute-start | bytes 294920 | tf_op jit(solution)/shard_map/ppermute | solution.py:33
  130.8 9.3 %collective-permute-start.32 = (bf16[2,384,128]{2,1,0:T(8,128)(2,1)S(1)}, bf16[2,384,128]{2,1,0:T(8,128)(2,1)S(1)}, u32[]{:S(2)}, u32[]{:S(2)}) collective-permute-start(bf16[2,384,128]{2,1,0:T(8,128)(2,1)S(1)} %pad_maximum_fusion.13), channel_id=1, source_target_pairs={{0,32},{32,0},{64,96},{96,64},{1,33},{33,1},{65,97},{97,65},{2,34}... | collective-permute-start | bytes 589832 | tf_op jit(solution)/shard_map/ppermute | solution.py:33
  136.6 11.6 %collective-permute-start.38 = (bf16[4,384,128]{2,1,0:T(8,128)(2,1)S(1)}, bf16[4,384,128]{2,1,0:T(8,128)(2,1)}, u32[]{:S(2)}, u32[]{:S(2)}) collective-permute-start(bf16[4,384,128]{2,1,0:T(8,128)(2,1)S(1)} %pad_maximum_fusion.8), channel_id=1, source_target_pairs={{0,32},{32,0},{64,96},{96,64},{1,33},{33,1},{65,97},{97,65},{2,34}... | collective-permute-start | bytes 1179656 | tf_op jit(solution)/shard_map/ppermute | solution.py:33
  139.1 12.6 %collective-permute-start.28 = (bf16[4,384,128]{2,1,0:T(8,128)(2,1)S(1)}, bf16[4,384,128]{2,1,0:T(8,128)(2,1)S(1)}, u32[]{:S(2)}, u32[]{:S(2)}) collective-permute-start(bf16[4,384,128]{2,1,0:T(8,128)(2,1)S(1)} %pad_maximum_fusion.6), channel_id=1, source_target_pairs={{0,8},{8,0},{16,24},{24,16},{1,9},{9,1},{17,25},{25,17},{2,10},{10... | collective-permute-start | bytes 1179656 | tf_op jit(solution)/shard_map/ppermute | solution.py:33
  140.2 14.2 %collective-permute-start.33 = (bf16[4,384,128]{2,1,0:T(8,128)(2,1)S(1)}, bf16[4,384,128]{2,1,0:T(8,128)(2,1)S(1)}, u32[]{:S(2)}, u32[]{:S(2)}) collective-permute-start(bf16[4,384,128]{2,1,0:T(8,128)(2,1)S(1)} %pad_maximum_fusion.7), channel_id=1, source_target_pairs={{0,24},{8,16},{16,8},{24,0},{1,25},{9,17},{17,9},{25,1},{2,26},{10... | collective-permute-start | bytes 1179656 | tf_op jit(solution)/shard_map/ppermute | solution.py:33
  145.6 13.3 %collective-permute-start.42 = (bf16[4,384,128]{2,1,0:T(8,128)(2,1)S(1)}, bf16[4,384,128]{2,1,0:T(8,128)(2,1)S(1)}, u32[]{:S(2)}, u32[]{:S(2)}) collective-permute-start(bf16[4,384,128]{2,1,0:T(8,128)(2,1)S(1)} %pad_maximum_fusion.9), channel_id=1, source_target_pairs={{0,96},{32,64},{64,32},{96,0},{1,97},{33,65},{65,33},{97,1},{2,98}... | collective-permute-start | bytes 1179656 | tf_op jit(solution)/shard_map/ppermute | solution.py:33
  149.3 22.2 %collective-permute-start.39 = (bf16[8,384,128]{2,1,0:T(8,128)(2,1)S(1)}, bf16[8,384,128]{2,1,0:T(8,128)(2,1)}, u32[]{:S(2)}, u32[]{:S(2)}) collective-permute-start(bf16[8,384,128]{2,1,0:T(8,128)(2,1)S(1)} %pad_maximum_fusion.2.rest_4_.rest_5_), channel_id=1, source_target_pairs={{0,96},{32,64},{64,32},{96,0},{1,97},{33,65},{65,33},{97,1},{2,98}... | collective-permute-start | bytes 2359304 | tf_op jit(solution)/shard_map/ppermute | solution.py:33
  151.8 19.8 %collective-permute-start.29 = (bf16[8,384,128]{2,1,0:T(8,128)(2,1)S(1)}, bf16[8,384,128]{2,1,0:T(8,128)(2,1)}, u32[]{:S(2)}, u32[]{:S(2)}) collective-permute-start(bf16[8,384,128]{2,1,0:T(8,128)(2,1)S(1)} %pad_maximum_fusion.rest_0_.rest_1_), channel_id=1, source_target_pairs={{0,24},{8,16},{16,8},{24,0},{1,25},{9,17},{17,9},{25,1},{2,26},{10... | collective-permute-start | bytes 2359304 | tf_op jit(solution)/shard_map/ppermute | solution.py:33
  154.5 17.7 %collective-permute-start.34 = (bf16[8,384,128]{2,1,0:T(8,128)(2,1)S(1)}, bf16[8,384,128]{2,1,0:T(8,128)(2,1)}, u32[]{:S(2)}, u32[]{:S(2)}) collective-permute-start(bf16[8,384,128]{2,1,0:T(8,128)(2,1)S(1)} %pad_maximum_fusion.1.rest_2_.rest_3_), channel_id=1, source_target_pairs={{0,8},{8,0},{16,24},{24,16},{1,9},{9,1},{17,25},{25,17},{2,10},{10... | collective-permute-start | bytes 2359304 | tf_op jit(solution)/shard_map/ppermute | solution.py:33
  158.9 13.5 %collective-permute-start.43 = (bf16[8,384,128]{2,1,0:T(8,128)(2,1)S(1)}, bf16[8,384,128]{2,1,0:T(8,128)(2,1)}, u32[]{:S(2)}, u32[]{:S(2)}) collective-permute-start(bf16[8,384,128]{2,1,0:T(8,128)(2,1)S(1)} %pad_maximum_fusion.3.rest_6_.rest_7_), channel_id=1, source_target_pairs={{0,32},{32,0},{64,96},{96,64},{1,33},{33,1},{65,97},{97,65},{2,34}... | collective-permute-start | bytes 2359304 | tf_op jit(solution)/shard_map/ppermute | solution.py:33
  (21 other events, 138.8 us)
Sparse Core Ops, SparseCore 0:
  83.5 45.0 all-gather.2

commit v11 on v10

--- a/solution.py
+++ b/solution.py
@@ -30,14 +30,14 @@
 
 
 def swap(value, axis, flip):
-    return lax.ppermute(value, axis, [(i, i ^ flip) for i in range(4)])
+    return lax.ppermute(value, axis, [(i, i ^ flip) for i in range(lax.axis_size(axis))])
 
 
 def spread(parts, early, other):
     parts = [p[None] for p in parts]
     for step in range(3):
         got = [swap(p, *order[step]) for p, order in zip(parts, ORDERS)]
-        if step == 0:
+        if step == 1:
             early, got[3] = lax.optimization_barrier((early, got[3]))
         parts = [jnp.concatenate([p, g], axis=0) for p, g in zip(parts, got)]
     got = [swap(p, *order[3]) for p, order in zip(parts, ORDERS)]
@@ -255,20 +255,18 @@
     inverse = (rounded.astype(BF), (inverse - rounded).astype(BF))
     where = jnp.stack([core, x, y, z]).astype(jnp.int32)
     state = mine_a[:512].astype(F32) + mine_b[:512].astype(F32)
+    piece_a, piece_b = mine_a[512:], mine_b[512:]
     state, *inverse = lax.optimization_barrier((state, *inverse))
     sent_0, = step(where, state, inverse)
     gots = [hop(sent_0, (0, 1)), hop(sent_0, (0, 3)), hop(sent_0, (0, 2))]
 
-    piece_a, piece_b, _ = lax.optimization_barrier((mine_a[512:], mine_b[512:], sent_0))
-    near_a, near_b = swap(piece_a, "y", 1), swap(piece_b, "z", 1)
-    near_a, near_b, *gots = lax.optimization_barrier((near_a, near_b, *gots))
-
-    def complete(piece, near, axis):
-        two = jnp.stack([piece, near])
-        return jnp.concatenate([two, swap(two, axis, 3)], axis=0).reshape(4, 3, 128, 128)
-
-    top, bottom = complete(piece_a, near_a, "y"), complete(piece_b, near_b, "z")
-    block = (top, bottom, lax.ppermute(top, "rhs", [(0, 1), (1, 0)]), lax.ppermute(bottom, "rhs", [(0, 1), (1, 0)]))
+    two_a = jnp.stack([piece_a, swap(piece_a, "y", 1)])
+    two_b = jnp.stack([piece_b, swap(piece_b, "z", 1)])
+    two_a, two_b, _ = lax.optimization_barrier((two_a, two_b, sent_0))
+    four_a, four_b, *gots = lax.optimization_barrier((swap(two_a, "y", 3), swap(two_b, "z", 3), *gots))
+    top = jnp.concatenate([two_a, four_a], axis=0).reshape(4, 3, 128, 128)
+    bottom = jnp.concatenate([two_b, four_b], axis=0).reshape(4, 3, 128, 128)
+    block = (top, bottom, swap(top, "rhs", 1), swap(bottom, "rhs", 1))
 
     panel_0 = jnp.where(x == 0, sent_0, gots[0] + gots[1] + gots[2])
     early_0 = lax.all_gather(panel_0, ("y", "z"), axis=0)

time: 199 us -> 205 us (1.030)
  waiting for transfers between devices: 79 us -> 82.1 us
  other arithmetic: 7.46 us -> 10.2 us
    ppermute x21, waiting for transfers between devices: 40.3 us -> 46.6 us  [permute(): return lax.ppermute(value, ROWS, [(flat(*a), flat(*b)) for a, b in moves])]
    ppermute x22, waiting for transfers between devices: 38.7 us -> 35.5 us  [swap(): lax.ppermute(value, axis, [(i, i ^ flip) for i in range(lax.axis_size(axi...]
    concatenate x12, other arithmetic: 1.55 us -> 4.29 us  [spread(): parts = [jnp.concatenate([p, g], axis=0) for p, g in zip(parts, got)]]
  transfers between devices with their start and end apart: 45 -> 45, of which waited for: 22 -> 20; matrix products, arithmetic and copies ran while one was open for 5% -> 6% of each run, Pallas kernels for 3% -> 3%
where the time goes in v11:
time: 205 us; the launch traced here: 204 us
  waiting for transfers between devices  82.1 us (40%)
  starting transfers between devices  62 us (30%)
  Pallas kernels  28.5 us (14%)
  between operations  14 us (7%)
  other arithmetic  10.2 us (5%)
  local copies, waits for them, and re-layouts  7.31 us (4%)
    ppermute x21, waiting for transfers between devices, permute(): return lax.ppermute(value, ROWS, [(flat(*a), flat(*b)) for a, b in moves])  46.6 us
    ppermute x21, starting transfers between devices, permute(): return lax.ppermute(value, ROWS, [(flat(*a), flat(*b)) for a, b in moves])  37.6 us
    ppermute x22, waiting for transfers between devices, swap(): lax.ppermute(value, axis, [(i, i ^ flip) for i in range(lax.axis_size(axi...  35.5 us
    ppermute x22, starting transfers between devices, swap(): lax.ppermute(value, axis, [(i, i ^ flip) for i in range(lax.axis_size(axi...  24.4 us
    pallas_call x1, Pallas kernels, update(): pl.pallas_call(update_kernel, grid_spec=pltpu.PrefetchScalarGridSpec(num_...  18.5 us
    pallas_call x4, Pallas kernels, step(): pl.pallas_call(kernel, grid_spec=pltpu.PrefetchScalarGridSpec(num_scalar_...  6.36 us
    reshape x1, local copies, waits for them, and re-layouts, local(): flat_factor = factor.reshape(2, 512, 1024)  4.45 us
    concatenate x12, other arithmetic, spread(): parts = [jnp.concatenate([p, g], axis=0) for p, g in zip(parts, got)]  4.29 us
  transfers between devices with their start and end apart: 45, of which 20 were waited for; matrix products, arithmetic and copies ran while one was open for 6% of the time, Pallas kernels for 3%

profile of v11, /device:TPU:6, one launch (start us, length us, event | category | flops | bytes accessed | tf_op | source)
XLA Modules:
  0.0 204.1 jit_solution(16249250677840508309)
XLA Ops:
  8.9 3.7 %shard_map.37 = (bf16[608,512]{1,0:T(8,128)(2,1)S(1)}, bf16[608,512]{1,0:T(8,128)(2,1)S(1)}, bf16[608,512]{1,0:T(8,128)(2,1)}, bf16[608,512]{1,0:T(8,128)(2,1)},...) custom-call(f32[2,512,2048]{2,1,0:T(8,128)} %rhs_ref.3, ...), custom_call_target="tpu_custom_call" | custom-call | tf_op jit(solution)/shard_map/pallas_call | solution.py:88
  12.6 4.4 %collective-permute-start.1 = (bf16[608,512]{1,0:T(8,128)(2,1)S(1)}, bf16[608,512]{1,0:T(8,128)(2,1)}, u32[]{:S(2)}, u32[]{:S(2)}) collective-permute-start(bf16[608,512]{1,0:T(8,128)(2,1)S(1)} %get-tuple-element.39), channel_id=1, source_target_pairs={{0,32},{2,34},{4,36},{6,38},{1,33},{3,35},{5,37},{7,39}} | collective-permute-start | bytes 1867784 | tf_op jit(solution)/shard_map/ppermute | solution.py:25
  16.9 3.1 %collective-permute-start.2 = (bf16[608,512]{1,0:T(8,128)(2,1)}, bf16[608,512]{1,0:T(8,128)(2,1)}, u32[]{:S(2)}, u32[]{:S(2)}) collective-permute-start(bf16[608,512]{1,0:T(8,128)(2,1)} %get-tuple-element.40), channel_id=1, source_target_pairs={{0,64},{2,66},{4,68},{6,70},{1,65},{3,67},{5,69},{7,71}} | collective-permute-start | bytes 1867784 | tf_op jit(solution)/shard_map/ppermute | solution.py:25
  26.4 4.1 %collective-permute-done.1 = bf16[608,512]{1,0:T(8,128)(2,1)} collective-permute-done((bf16[608,512]{1,0:T(8,128)(2,1)S(1)}, bf16[608,512]{1,0:T(8,128)(2,1)}, u32[]{:S(2)}, u32[]{:S(2)}) %collective-permute-start.1) | collective-permute-done | bytes 622624 | tf_op jit(solution)/shard_map/ppermute | solution.py:25
  34.0 8.7 %collective-permute-done.2 = bf16[608,512]{1,0:T(8,128)(2,1)} collective-permute-done((bf16[608,512]{1,0:T(8,128)(2,1)}, bf16[608,512]{1,0:T(8,128)(2,1)}, u32[]{:S(2)}, u32[]{:S(2)}) %collective-permute-start.2) | collective-permute-done | bytes 622624 | tf_op jit(solution)/shard_map/ppermute | solution.py:25
  44.3 5.9 %collective-permute-done.8 = bf16[608,512]{1,0:T(8,128)(2,1)} collective-permute-done((bf16[608,512]{1,0:T(8,128)(2,1)S(1)}, bf16[608,512]{1,0:T(8,128)(2,1)}, u32[]{:S(2)}, u32[]{:S(2)}) %collective-permute-start.8) | collective-permute-done | bytes 622624 | tf_op jit(solution)/shard_map/ppermute | solution.py:25
  57.5 5.4 %collective-permute-start.6 = (bf16[896,128]{1,0:T(8,128)(2,1)S(1)}, bf16[896,128]{1,0:T(8,128)(2,1)S(1)}, u32[]{:S(2)}, u32[]{:S(2)}) collective-permute-start(bf16[896,128]{1,0:T(8,128)(2,1)S(1)} %get-tuple-element.87), channel_id=1, source_target_pairs={{0,16},{32,48},{64,80},{96,112},{2,18},{34,50},{66,82},{98,114},{4... | collective-permute-start | bytes 688136 | tf_op jit(solution)/shard_map/ppermute | solution.py:25
  64.5 4.4 %collective-permute-done.6 = bf16[896,128]{1,0:T(8,128)(2,1)S(1)} collective-permute-done((bf16[896,128]{1,0:T(8,128)(2,1)S(1)}, bf16[896,128]{1,0:T(8,128)(2,1)S(1)}, u32[]{:S(2)}, u32[]{:S(2)}) %collective-permute-start.6) | collective-permute-done | bytes 229408 | tf_op jit(solution)/shard_map/ppermute | solution.py:25
  68.9 3.9 %collective-permute-done.4 = bf16[896,128]{1,0:T(8,128)(2,1)S(1)} collective-permute-done((bf16[896,128]{1,0:T(8,128)(2,1)S(1)}, bf16[896,128]{1,0:T(8,128)(2,1)S(1)}, u32[]{:S(2)}, u32[]{:S(2)}) %collective-permute-start.4) | collective-permute-done | bytes 229408 | tf_op jit(solution)/shard_map/ppermute | solution.py:25
  74.3 3.4 %collective-permute-done.13 = bf16[384,128]{1,0:T(8,128)(2,1)S(1)} collective-permute-done((bf16[384,128]{1,0:T(8,128)(2,1)S(1)}, bf16[384,128]{1,0:T(8,128)(2,1)S(1)}, u32[]{:S(2)}, u32[]{:S(2)}) %collective-permute-start.13) | collective-permute-done | bytes 98336 | tf_op jit(solution)/shard_map/ppermute | solution.py:33
  80.6 7.0 %collective-permute-done.18.refs_9_ = bf16[512,128]{1,0:T(8,128)(2,1)S(1)} collective-permute-done((bf16[512,128]{1,0:T(8,128)(2,1)S(1)}, bf16[512,128]{1,0:T(8,128)(2,1)S(1)}, u32[]{:S(2)}, u32[]{:S(2)}) %collective-permute-start.18) | collective-permute-done | bytes 131104 | tf_op jit(solution)/shard_map/ppermute | solution.py:25
  94.4 7.0 %collective-permute-done.23.refs_9_ = bf16[512,128]{1,0:T(8,128)(2,1)S(1)} collective-permute-done((bf16[512,128]{1,0:T(8,128)(2,1)S(1)}, bf16[512,128]{1,0:T(8,128)(2,1)S(1)}, u32[]{:S(2)}, u32[]{:S(2)}) %collective-permute-start.23) | collective-permute-done | bytes 131104 | tf_op jit(solution)/shard_map/ppermute | solution.py:25
  104.3 5.6 %collective-permute-done.24.refs_8_ = bf16[512,128]{1,0:T(8,128)(2,1)S(1)} collective-permute-done((bf16[512,128]{1,0:T(8,128)(2,1)S(1)}, bf16[512,128]{1,0:T(8,128)(2,1)S(1)}, u32[]{:S(2)}, u32[]{:S(2)}) %collective-permute-start.24) | collective-permute-done | bytes 131104 | tf_op jit(solution)/shard_map/ppermute | solution.py:25
  115.7 4.4 %reshape.173.mine_ref = bf16[2,512,1024]{2,1,0:T(8,128)(2,1)} reshape(bf16[2,512,4,256]{3,2,1,0:T(4,128)(2,1)} %param.4) | data formatting | bytes 4194304 | tf_op jit(solution)/shard_map/reshape | solution.py:288
  120.3 2.6 %collective-permute-start.36 = (bf16[1,384,128]{2,1,0:T(8,128)(2,1)S(1)}, bf16[1,384,128]{2,1,0:T(8,128)(2,1)S(1)}, u32[]{:S(2)}, u32[]{:S(2)}) collective-permute-start(bf16[1,384,128]{2,1,0:T(8,128)(2,1)S(1)} %maximum_bitcast_fusion.1), channel_id=1, source_target_pairs={{0,8},{8,0},{16,24},{24,16},{1,9},{9,1},{17,25},{25,17},{2,10},{10... | collective-permute-start | bytes 294920 | tf_op jit(solution)/shard_map/ppermute | solution.py:33
  122.9 3.2 %collective-permute-start.31 = (bf16[1,384,128]{2,1,0:T(8,128)(2,1)S(1)}, bf16[1,384,128]{2,1,0:T(8,128)(2,1)S(1)}, u32[]{:S(2)}, u32[]{:S(2)}) collective-permute-start(bf16[1,384,128]{2,1,0:T(8,128)(2,1)S(1)} %maximum_bitcast_fusion), channel_id=1, source_target_pairs={{0,96},{32,64},{64,32},{96,0},{1,97},{33,65},{65,33},{97,1},{2,98}... | collective-permute-start | bytes 294920 | tf_op jit(solution)/shard_map/ppermute | solution.py:33
  126.1 2.6 %collective-permute-start.40 = (bf16[1,384,128]{2,1,0:T(8,128)(2,1)S(1)}, bf16[1,384,128]{2,1,0:T(8,128)(2,1)S(1)}, u32[]{:S(2)}, u32[]{:S(2)}) collective-permute-start(bf16[1,384,128]{2,1,0:T(8,128)(2,1)S(1)} %slice_bitcast_fusion), channel_id=1, source_target_pairs={{0,24},{8,16},{16,8},{24,0},{1,25},{9,17},{17,9},{25,1},{2,26},{10... | collective-permute-start | bytes 294920 | tf_op jit(solution)/shard_map/ppermute | solution.py:33
  128.8 2.5 %collective-permute-start.37 = (bf16[2,384,128]{2,1,0:T(8,128)(2,1)S(1)}, bf16[2,384,128]{2,1,0:T(8,128)(2,1)S(1)}, u32[]{:S(2)}, u32[]{:S(2)}) collective-permute-start(bf16[2,384,128]{2,1,0:T(8,128)(2,1)S(1)} %pad_maximum_fusion.14), channel_id=1, source_target_pairs={{0,24},{8,16},{16,8},{24,0},{1,25},{9,17},{17,9},{25,1},{2,26},{10... | collective-permute-start | bytes 589832 | tf_op jit(solution)/shard_map/ppermute | solution.py:33
  134.9 5.7 %collective-permute-done.37 = bf16[2,384,128]{2,1,0:T(8,128)(2,1)S(1)} collective-permute-done((bf16[2,384,128]{2,1,0:T(8,128)(2,1)S(1)}, bf16[2,384,128]{2,1,0:T(8,128)(2,1)S(1)}, u32[]{:S(2)}, u32[]{:S(2)}) %collective-permute-start.37) | collective-permute-done | bytes 196640 | tf_op jit(solution)/shard_map/ppermute | solution.py:33
  146.9 3.4 %collective-permute-done.41 = bf16[2,384,128]{2,1,0:T(8,128)(2,1)S(1)} collective-permute-done((bf16[2,384,128]{2,1,0:T(8,128)(2,1)S(1)}, bf16[2,384,128]{2,1,0:T(8,128)(2,1)S(1)}, u32[]{:S(2)}, u32[]{:S(2)}) %collective-permute-start.41) | collective-permute-done | bytes 196640 | tf_op jit(solution)/shard_map/ppermute | solution.py:33
  154.9 2.3 %collective-permute-done.28 = bf16[4,384,128]{2,1,0:T(8,128)(2,1)} collective-permute-done((bf16[4,384,128]{2,1,0:T(8,128)(2,1)}, bf16[4,384,128]{2,1,0:T(8,128)(2,1)}, u32[]{:S(2)}, u32[]{:S(2)}) %collective-permute-start.28) | collective-permute-done | bytes 393248 | tf_op jit(solution)/shard_map/ppermute | solution.py:33
  160.9 2.4 %collective-permute-done.42 = bf16[4,384,128]{2,1,0:T(8,128)(2,1)S(1)} collective-permute-done((bf16[4,384,128]{2,1,0:T(8,128)(2,1)S(1)}, bf16[4,384,128]{2,1,0:T(8,128)(2,1)S(1)}, u32[]{:S(2)}, u32[]{:S(2)}) %collective-permute-start.42) | collective-permute-done | bytes 393248 | tf_op jit(solution)/shard_map/ppermute | solution.py:33
  163.7 12.7 %collective-permute-done.39.rest_12_.rest_13_ = bf16[8,384,128]{2,1,0:T(8,128)(2,1)} collective-permute-done((bf16[8,384,128]{2,1,0:T(8,128)(2,1)S(1)}, bf16[8,384,128]{2,1,0:T(8,128)(2,1)}, u32[]{:S(2)}, u32[]{:S(2)}) %collective-permute-start.39) | collective-permute-done | bytes 786464 | tf_op jit(solution)/shard_map/ppermute | solution.py:33
  178.8 18.5 %shard_map.42 = f32[2,512,2048]{2,1,0:T(8,128)} custom-call(s32[66]{0:T(128)S(1)} %pad_add_fusion.1.scalars, bf16[2,512,1024]{2,1,0:T(8,128)(2,1)} %reshape.173.mine_ref, bf16[2,512,1024]{2,1,0:T(8,128)(2,1)} %collective-permute-done.other_ref, f32[2,512,2048]{2,1,0:T(8,128)} %rhs_ref.3, bf16[16,512,128]{2,1,0:T(8,128)(2,1)} %bitcast.33, ...), custom_call_target="tpu_custom_call" | custom-call | tf_op jit(solution)/shard_map/pallas_call | solution.py:203
  (130 shorter events, 63.3 us)
Async XLA Ops:
  6.5 143.8 %all-gather.3.cloned.1.call-start = ((), (), s32[]{:S(2)}) async-start(), calls=%async_computation | async-start | bytes 2228224 | tf_op jit(solution)/shard_map/all_gather | solution.py:272
  12.6 17.9 %collective-permute-start.1 = (bf16[608,512]{1,0:T(8,128)(2,1)S(1)}, bf16[608,512]{1,0:T(8,128)(2,1)}, u32[]{:S(2)}, u32[]{:S(2)}) collective-permute-start(bf16[608,512]{1,0:T(8,128)(2,1)S(1)} %get-tuple-element.39), channel_id=1, source_target_pairs={{0,32},{2,34},{4,36},{6,38},{1,33},{3,35},{5,37},{7,39}} | collective-permute-start | bytes 1867784 | tf_op jit(solution)/shard_map/ppermute | solution.py:25
  16.9 25.8 %collective-permute-start.2 = (bf16[608,512]{1,0:T(8,128)(2,1)}, bf16[608,512]{1,0:T(8,128)(2,1)}, u32[]{:S(2)}, u32[]{:S(2)}) collective-permute-start(bf16[608,512]{1,0:T(8,128)(2,1)} %get-tuple-element.40), channel_id=1, source_target_pairs={{0,64},{2,66},{4,68},{6,70},{1,65},{3,67},{5,69},{7,71}} | collective-permute-start | bytes 1867784 | tf_op jit(solution)/shard_map/ppermute | solution.py:25
  20.0 22.7 %collective-permute-start.3 = (bf16[608,512]{1,0:T(8,128)(2,1)}, bf16[608,512]{1,0:T(8,128)(2,1)}, u32[]{:S(2)}, u32[]{:S(2)}) collective-permute-start(bf16[608,512]{1,0:T(8,128)(2,1)} %get-tuple-element.41), channel_id=1, source_target_pairs={{0,96},{2,98},{4,100},{6,102},{1,97},{3,99},{5,101},{7,103}} | collective-permute-start | bytes 1867784 | tf_op jit(solution)/shard_map/ppermute | solution.py:25
  22.1 22.2 %collective-permute-start.7 = (bf16[608,512]{1,0:T(8,128)(2,1)}, bf16[608,512]{1,0:T(8,128)(2,1)}, u32[]{:S(2)}, u32[]{:S(2)}) collective-permute-start(bf16[608,512]{1,0:T(8,128)(2,1)} %get-tuple-element.44), channel_id=1, source_target_pairs={{0,8},{2,10},{4,12},{6,14},{1,9},{3,11},{5,13},{7,15}} | collective-permute-start | bytes 1867784 | tf_op jit(solution)/shard_map/ppermute | solution.py:25
  24.3 26.0 %collective-permute-start.8 = (bf16[608,512]{1,0:T(8,128)(2,1)S(1)}, bf16[608,512]{1,0:T(8,128)(2,1)}, u32[]{:S(2)}, u32[]{:S(2)}) collective-permute-start(bf16[608,512]{1,0:T(8,128)(2,1)S(1)} %get-tuple-element.45), channel_id=1, source_target_pairs={{0,16},{2,18},{4,20},{6,22},{1,17},{3,19},{5,21},{7,23}} | collective-permute-start | bytes 1867784 | tf_op jit(solution)/shard_map/ppermute | solution.py:25
  30.4 19.8 %collective-permute-start.9 = (bf16[608,512]{1,0:T(8,128)(2,1)S(1)}, bf16[608,512]{1,0:T(8,128)(2,1)}, u32[]{:S(2)}, u32[]{:S(2)}) collective-permute-start(bf16[608,512]{1,0:T(8,128)(2,1)S(1)} %get-tuple-element.46), channel_id=1, source_target_pairs={{0,24},{2,26},{4,28},{6,30},{1,25},{3,27},{5,29},{7,31}} | collective-permute-start | bytes 1867784 | tf_op jit(solution)/shard_map/ppermute | solution.py:25
  52.0 10.9 %collective-permute-start.11 = (bf16[896,128]{1,0:T(8,128)(2,1)S(1)}, bf16[896,128]{1,0:T(8,128)(2,1)S(1)}, u32[]{:S(2)}, u32[]{:S(2)}) collective-permute-start(bf16[896,128]{1,0:T(8,128)(2,1)S(1)} %get-tuple-element.103), channel_id=1, source_target_pairs={{0,96},{8,104},{16,112},{24,120},{2,98},{10,106},{18,114},{26,122}... | collective-permute-start | bytes 688136 | tf_op jit(solution)/shard_map/ppermute | solution.py:25
  53.3 10.9 %collective-permute-start.12 = (bf16[896,128]{1,0:T(8,128)(2,1)S(1)}, bf16[896,128]{1,0:T(8,128)(2,1)S(1)}, u32[]{:S(2)}, u32[]{:S(2)}) collective-permute-start(bf16[896,128]{1,0:T(8,128)(2,1)S(1)} %get-tuple-element.104), channel_id=1, source_target_pairs={{0,64},{8,72},{16,80},{24,88},{2,66},{10,74},{18,82},{26,90},{4,68... | collective-permute-start | bytes 688136 | tf_op jit(solution)/shard_map/ppermute | solution.py:25
  57.5 11.4 %collective-permute-start.6 = (bf16[896,128]{1,0:T(8,128)(2,1)S(1)}, bf16[896,128]{1,0:T(8,128)(2,1)S(1)}, u32[]{:S(2)}, u32[]{:S(2)}) collective-permute-start(bf16[896,128]{1,0:T(8,128)(2,1)S(1)} %get-tuple-element.87), channel_id=1, source_target_pairs={{0,16},{32,48},{64,80},{96,112},{2,18},{34,50},{66,82},{98,114},{4... | collective-permute-start | bytes 688136 | tf_op jit(solution)/shard_map/ppermute | solution.py:25
  62.9 9.9 %collective-permute-start.4 = (bf16[896,128]{1,0:T(8,128)(2,1)S(1)}, bf16[896,128]{1,0:T(8,128)(2,1)S(1)}, u32[]{:S(2)}, u32[]{:S(2)}) collective-permute-start(bf16[896,128]{1,0:T(8,128)(2,1)S(1)} %get-tuple-element.77), channel_id=1, source_target_pairs={{0,8},{32,40},{64,72},{96,104},{2,10},{34,42},{66,74},{98,106},{4,... | collective-permute-start | bytes 688136 | tf_op jit(solution)/shard_map/ppermute | solution.py:25
  77.8 9.8 %collective-permute-start.15 = (bf16[2,384,128]{2,1,0:T(8,128)(2,1)S(1)}, bf16[2,384,128]{2,1,0:T(8,128)(2,1)S(1)}, u32[]{:S(2)}, u32[]{:S(2)}) collective-permute-start(bf16[2,384,128]{2,1,0:T(8,128)(2,1)S(1)} %pad_maximum_fusion.10), channel_id=1, source_target_pairs={{0,96},{32,64},{64,32},{96,0},{1,97},{33,65},{65,33},{97,1},{2,98}... | collective-permute-start | bytes 589832 | tf_op jit(solution)/shard_map/ppermute | solution.py:33
  120.2 43.6 %collective-permute-start = (bf16[2,512,1024]{2,1,0:T(8,128)(2,1)}, bf16[2,512,1024]{2,1,0:T(8,128)(2,1)}, u32[]{:S(2)}, u32[]{:S(2)}) collective-permute-start(bf16[2,512,1024]{2,1,0:T(8,128)(2,1)} %reshape.173.mine_ref), channel_id=1, source_target_pairs={{0,1},{1,0},{2,3},{3,2},{4,5},{5,4},{6,7},{7,6},{8,9},{9,8},{10,11... | collective-permute-start | bytes 6291464 | tf_op jit(solution)/shard_map/ppermute | solution.py:289
  126.1 16.3 %collective-permute-start.40 = (bf16[1,384,128]{2,1,0:T(8,128)(2,1)S(1)}, bf16[1,384,128]{2,1,0:T(8,128)(2,1)S(1)}, u32[]{:S(2)}, u32[]{:S(2)}) collective-permute-start(bf16[1,384,128]{2,1,0:T(8,128)(2,1)S(1)} %slice_bitcast_fusion), channel_id=1, source_target_pairs={{0,24},{8,16},{16,8},{24,0},{1,25},{9,17},{17,9},{25,1},{2,26},{10... | collective-permute-start | bytes 294920 | tf_op jit(solution)/shard_map/ppermute | solution.py:33
  128.8 11.9 %collective-permute-start.37 = (bf16[2,384,128]{2,1,0:T(8,128)(2,1)S(1)}, bf16[2,384,128]{2,1,0:T(8,128)(2,1)S(1)}, u32[]{:S(2)}, u32[]{:S(2)}) collective-permute-start(bf16[2,384,128]{2,1,0:T(8,128)(2,1)S(1)} %pad_maximum_fusion.14), channel_id=1, source_target_pairs={{0,24},{8,16},{16,8},{24,0},{1,25},{9,17},{17,9},{25,1},{2,26},{10... | collective-permute-start | bytes 589832 | tf_op jit(solution)/shard_map/ppermute | solution.py:33
  131.3 14.0 %collective-permute-start.32 = (bf16[2,384,128]{2,1,0:T(8,128)(2,1)S(1)}, bf16[2,384,128]{2,1,0:T(8,128)(2,1)S(1)}, u32[]{:S(2)}, u32[]{:S(2)}) collective-permute-start(bf16[2,384,128]{2,1,0:T(8,128)(2,1)S(1)} %pad_maximum_fusion.13), channel_id=1, source_target_pairs={{0,32},{32,0},{64,96},{96,64},{1,33},{33,1},{65,97},{97,65},{2,34}... | collective-permute-start | bytes 589832 | tf_op jit(solution)/shard_map/ppermute | solution.py:33
  140.7 11.1 %collective-permute-start.38 = (bf16[4,384,128]{2,1,0:T(8,128)(2,1)S(1)}, bf16[4,384,128]{2,1,0:T(8,128)(2,1)}, u32[]{:S(2)}, u32[]{:S(2)}) collective-permute-start(bf16[4,384,128]{2,1,0:T(8,128)(2,1)S(1)} %pad_maximum_fusion.8), channel_id=1, source_target_pairs={{0,32},{32,0},{64,96},{96,64},{1,33},{33,1},{65,97},{97,65},{2,34}... | collective-permute-start | bytes 1179656 | tf_op jit(solution)/shard_map/ppermute | solution.py:33
  143.3 13.8 %collective-permute-start.28 = (bf16[4,384,128]{2,1,0:T(8,128)(2,1)}, bf16[4,384,128]{2,1,0:T(8,128)(2,1)}, u32[]{:S(2)}, u32[]{:S(2)}) collective-permute-start(bf16[4,384,128]{2,1,0:T(8,128)(2,1)} %pad_maximum_fusion.6), channel_id=1, source_target_pairs={{0,8},{8,0},{16,24},{24,16},{1,9},{9,1},{17,25},{25,17},{2,10},{10... | collective-permute-start | bytes 1179656 | tf_op jit(solution)/shard_map/ppermute | solution.py:33
  145.4 14.4 %collective-permute-start.33 = (bf16[4,384,128]{2,1,0:T(8,128)(2,1)S(1)}, bf16[4,384,128]{2,1,0:T(8,128)(2,1)}, u32[]{:S(2)}, u32[]{:S(2)}) collective-permute-start(bf16[4,384,128]{2,1,0:T(8,128)(2,1)S(1)} %pad_maximum_fusion.7), channel_id=1, source_target_pairs={{0,24},{8,16},{16,8},{24,0},{1,25},{9,17},{17,9},{25,1},{2,26},{10... | collective-permute-start | bytes 1179656 | tf_op jit(solution)/shard_map/ppermute | solution.py:33
  150.4 12.9 %collective-permute-start.42 = (bf16[4,384,128]{2,1,0:T(8,128)(2,1)S(1)}, bf16[4,384,128]{2,1,0:T(8,128)(2,1)S(1)}, u32[]{:S(2)}, u32[]{:S(2)}) collective-permute-start(bf16[4,384,128]{2,1,0:T(8,128)(2,1)S(1)} %pad_maximum_fusion.9), channel_id=1, source_target_pairs={{0,96},{32,64},{64,32},{96,0},{1,97},{33,65},{65,33},{97,1},{2,98}... | collective-permute-start | bytes 1179656 | tf_op jit(solution)/shard_map/ppermute | solution.py:33
  152.8 23.6 %collective-permute-start.39 = (bf16[8,384,128]{2,1,0:T(8,128)(2,1)S(1)}, bf16[8,384,128]{2,1,0:T(8,128)(2,1)}, u32[]{:S(2)}, u32[]{:S(2)}) collective-permute-start(bf16[8,384,128]{2,1,0:T(8,128)(2,1)S(1)} %pad_maximum_fusion.2.rest_4_.rest_5_), channel_id=1, source_target_pairs={{0,96},{32,64},{64,32},{96,0},{1,97},{33,65},{65,33},{97,1},{2,98}... | collective-permute-start | bytes 2359304 | tf_op jit(solution)/shard_map/ppermute | solution.py:33
  158.2 19.2 %collective-permute-start.29 = (bf16[8,384,128]{2,1,0:T(8,128)(2,1)S(1)}, bf16[8,384,128]{2,1,0:T(8,128)(2,1)}, u32[]{:S(2)}, u32[]{:S(2)}) collective-permute-start(bf16[8,384,128]{2,1,0:T(8,128)(2,1)S(1)} %pad_maximum_fusion.rest_0_.rest_1_), channel_id=1, source_target_pairs={{0,24},{8,16},{16,8},{24,0},{1,25},{9,17},{17,9},{25,1},{2,26},{10... | collective-permute-start | bytes 2359304 | tf_op jit(solution)/shard_map/ppermute | solution.py:33
  160.8 17.7 %collective-permute-start.34 = (bf16[8,384,128]{2,1,0:T(8,128)(2,1)S(1)}, bf16[8,384,128]{2,1,0:T(8,128)(2,1)}, u32[]{:S(2)}, u32[]{:S(2)}) collective-permute-start(bf16[8,384,128]{2,1,0:T(8,128)(2,1)S(1)} %pad_maximum_fusion.1.rest_2_.rest_3_), channel_id=1, source_target_pairs={{0,8},{8,0},{16,24},{24,16},{1,9},{9,1},{17,25},{25,17},{2,10},{10... | collective-permute-start | bytes 2359304 | tf_op jit(solution)/shard_map/ppermute | solution.py:33
  163.4 15.3 %collective-permute-start.43 = (bf16[8,384,128]{2,1,0:T(8,128)(2,1)S(1)}, bf16[8,384,128]{2,1,0:T(8,128)(2,1)}, u32[]{:S(2)}, u32[]{:S(2)}) collective-permute-start(bf16[8,384,128]{2,1,0:T(8,128)(2,1)S(1)} %pad_maximum_fusion.3.rest_6_.rest_7_), channel_id=1, source_target_pairs={{0,32},{32,0},{64,96},{96,64},{1,33},{33,1},{65,97},{97,65},{2,34}... | collective-permute-start | bytes 2359304 | tf_op jit(solution)/shard_map/ppermute | solution.py:33
  (21 other events, 151.3 us)
Sparse Core Ops, SparseCore 0:
  88.4 51.0 all-gather.2

commit v12 on v10

--- a/solution.py
+++ b/solution.py
@@ -37,7 +37,7 @@
     parts = [p[None] for p in parts]
     for step in range(3):
         got = [swap(p, *order[step]) for p, order in zip(parts, ORDERS)]
-        if step == 0:
+        if step == 1:
             early, got[3] = lax.optimization_barrier((early, got[3]))
         parts = [jnp.concatenate([p, g], axis=0) for p, g in zip(parts, got)]
     got = [swap(p, *order[3]) for p, order in zip(parts, ORDERS)]

time: 199 us -> 201 us (1.010)
  other arithmetic: 7.46 us -> 10.2 us
    concatenate x12, other arithmetic: 1.55 us -> 4.29 us  [spread(): parts = [jnp.concatenate([p, g], axis=0) for p, g in zip(parts, got)]]
  transfers between devices with their start and end apart: 45 -> 45, of which waited for: 22 -> 23; matrix products, arithmetic and copies ran while one was open for 5% -> 6% of each run, Pallas kernels for 3% -> 3%
where the time goes in v12:
time: 201 us; the launch traced here: 200 us
  waiting for transfers between devices  78.4 us (39%)
  starting transfers between devices  61.6 us (31%)
  Pallas kernels  28.5 us (14%)
  between operations  14 us (7%)
  other arithmetic  10.2 us (5%)
  local copies, waits for them, and re-layouts  7.29 us (4%)
    ppermute x21, waiting for transfers between devices, permute(): return lax.ppermute(value, ROWS, [(flat(*a), flat(*b)) for a, b in moves])  40.3 us
    ppermute x21, starting transfers between devices, permute(): return lax.ppermute(value, ROWS, [(flat(*a), flat(*b)) for a, b in moves])  37.6 us
    ppermute x20, waiting for transfers between devices, swap(): return lax.ppermute(value, axis, [(i, i ^ flip) for i in range(4)])  36.4 us
    ppermute x20, starting transfers between devices, swap(): return lax.ppermute(value, axis, [(i, i ^ flip) for i in range(4)])  23.3 us
    pallas_call x1, Pallas kernels, update(): pl.pallas_call(update_kernel, grid_spec=pltpu.PrefetchScalarGridSpec(num_...  18.5 us
    pallas_call x4, Pallas kernels, step(): pl.pallas_call(kernel, grid_spec=pltpu.PrefetchScalarGridSpec(num_scalar_...  6.37 us
    reshape x1, local copies, waits for them, and re-layouts, local(): flat_factor = factor.reshape(2, 512, 1024)  4.44 us
    concatenate x12, other arithmetic, spread(): parts = [jnp.concatenate([p, g], axis=0) for p, g in zip(parts, got)]  4.29 us
  transfers between devices with their start and end apart: 45, of which 23 were waited for; matrix products, arithmetic and copies ran while one was open for 6% of the time, Pallas kernels for 3%

profile of v12, /device:TPU:6, one launch (start us, length us, event | category | flops | bytes accessed | tf_op | source)
XLA Modules:
  0.0 199.9 jit_solution(12878056427741124495)
XLA Ops:
  8.9 3.7 %shard_map.37 = (bf16[608,512]{1,0:T(8,128)(2,1)S(1)}, bf16[608,512]{1,0:T(8,128)(2,1)S(1)}, bf16[608,512]{1,0:T(8,128)(2,1)}, bf16[608,512]{1,0:T(8,128)(2,1)},...) custom-call(f32[2,512,2048]{2,1,0:T(8,128)} %rhs_ref.3, ...), custom_call_target="tpu_custom_call" | custom-call | tf_op jit(solution)/shard_map/pallas_call | solution.py:88
  12.6 4.3 %collective-permute-start.1 = (bf16[608,512]{1,0:T(8,128)(2,1)S(1)}, bf16[608,512]{1,0:T(8,128)(2,1)}, u32[]{:S(2)}, u32[]{:S(2)}) collective-permute-start(bf16[608,512]{1,0:T(8,128)(2,1)S(1)} %get-tuple-element.39), channel_id=1, source_target_pairs={{0,32},{2,34},{4,36},{6,38},{1,33},{3,35},{5,37},{7,39}} | collective-permute-start | bytes 1867784 | tf_op jit(solution)/shard_map/ppermute | solution.py:25
  16.9 3.1 %collective-permute-start.2 = (bf16[608,512]{1,0:T(8,128)(2,1)}, bf16[608,512]{1,0:T(8,128)(2,1)}, u32[]{:S(2)}, u32[]{:S(2)}) collective-permute-start(bf16[608,512]{1,0:T(8,128)(2,1)} %get-tuple-element.40), channel_id=1, source_target_pairs={{0,64},{2,66},{4,68},{6,70},{1,65},{3,67},{5,69},{7,71}} | collective-permute-start | bytes 1867784 | tf_op jit(solution)/shard_map/ppermute | solution.py:25
  26.4 4.1 %collective-permute-done.1 = bf16[608,512]{1,0:T(8,128)(2,1)} collective-permute-done((bf16[608,512]{1,0:T(8,128)(2,1)S(1)}, bf16[608,512]{1,0:T(8,128)(2,1)}, u32[]{:S(2)}, u32[]{:S(2)}) %collective-permute-start.1) | collective-permute-done | bytes 622624 | tf_op jit(solution)/shard_map/ppermute | solution.py:25
  34.0 8.7 %collective-permute-done.2 = bf16[608,512]{1,0:T(8,128)(2,1)} collective-permute-done((bf16[608,512]{1,0:T(8,128)(2,1)}, bf16[608,512]{1,0:T(8,128)(2,1)}, u32[]{:S(2)}, u32[]{:S(2)}) %collective-permute-start.2) | collective-permute-done | bytes 622624 | tf_op jit(solution)/shard_map/ppermute | solution.py:25
  44.3 5.9 %collective-permute-done.8 = bf16[608,512]{1,0:T(8,128)(2,1)} collective-permute-done((bf16[608,512]{1,0:T(8,128)(2,1)S(1)}, bf16[608,512]{1,0:T(8,128)(2,1)}, u32[]{:S(2)}, u32[]{:S(2)}) %collective-permute-start.8) | collective-permute-done | bytes 622624 | tf_op jit(solution)/shard_map/ppermute | solution.py:25
  57.5 5.4 %collective-permute-start.6 = (bf16[896,128]{1,0:T(8,128)(2,1)S(1)}, bf16[896,128]{1,0:T(8,128)(2,1)S(1)}, u32[]{:S(2)}, u32[]{:S(2)}) collective-permute-start(bf16[896,128]{1,0:T(8,128)(2,1)S(1)} %get-tuple-element.87), channel_id=1, source_target_pairs={{0,16},{32,48},{64,80},{96,112},{2,18},{34,50},{66,82},{98,114},{4... | collective-permute-start | bytes 688136 | tf_op jit(solution)/shard_map/ppermute | solution.py:25
  64.4 4.5 %collective-permute-done.6 = bf16[896,128]{1,0:T(8,128)(2,1)S(1)} collective-permute-done((bf16[896,128]{1,0:T(8,128)(2,1)S(1)}, bf16[896,128]{1,0:T(8,128)(2,1)S(1)}, u32[]{:S(2)}, u32[]{:S(2)}) %collective-permute-start.6) | collective-permute-done | bytes 229408 | tf_op jit(solution)/shard_map/ppermute | solution.py:25
  68.9 2.8 %collective-permute-done.4 = bf16[896,128]{1,0:T(8,128)(2,1)S(1)} collective-permute-done((bf16[896,128]{1,0:T(8,128)(2,1)S(1)}, bf16[896,128]{1,0:T(8,128)(2,1)S(1)}, u32[]{:S(2)}, u32[]{:S(2)}) %collective-permute-start.4) | collective-permute-done | bytes 229408 | tf_op jit(solution)/shard_map/ppermute | solution.py:25
  75.9 2.6 %collective-permute-start.14 = (bf16[384,128]{1,0:T(8,128)(2,1)S(1)}, bf16[384,128]{1,0:T(8,128)(2,1)S(1)}, u32[]{:S(2)}, u32[]{:S(2)}) collective-permute-start(bf16[384,128]{1,0:T(8,128)(2,1)S(1)} %slice.121), channel_id=1, source_target_pairs={{0,8},{8,0},{16,24},{24,16},{1,9},{9,1},{17,25},{25,17},{2,10},{10... | collective-permute-start | bytes 294920 | tf_op jit(solution)/shard_map/ppermute | solution.py:33
  83.7 6.7 %collective-permute-done.19 = bf16[2,384,128]{2,1,0:T(8,128)(2,1)S(1)} collective-permute-done((bf16[2,384,128]{2,1,0:T(8,128)(2,1)S(1)}, bf16[2,384,128]{2,1,0:T(8,128)(2,1)S(1)}, u32[]{:S(2)}, u32[]{:S(2)}) %collective-permute-start.19) | collective-permute-done | bytes 196640 | tf_op jit(solution)/shard_map/ppermute | solution.py:33
  96.5 7.0 %collective-permute-done.23.refs_9_ = bf16[512,128]{1,0:T(8,128)(2,1)S(1)} collective-permute-done((bf16[512,128]{1,0:T(8,128)(2,1)S(1)}, bf16[512,128]{1,0:T(8,128)(2,1)S(1)}, u32[]{:S(2)}, u32[]{:S(2)}) %collective-permute-start.23) | collective-permute-done | bytes 131104 | tf_op jit(solution)/shard_map/ppermute | solution.py:25
  106.5 5.6 %collective-permute-done.24.refs_8_ = bf16[512,128]{1,0:T(8,128)(2,1)S(1)} collective-permute-done((bf16[512,128]{1,0:T(8,128)(2,1)S(1)}, bf16[512,128]{1,0:T(8,128)(2,1)S(1)}, u32[]{:S(2)}, u32[]{:S(2)}) %collective-permute-start.24) | collective-permute-done | bytes 131104 | tf_op jit(solution)/shard_map/ppermute | solution.py:25
  117.9 4.4 %reshape.179.mine_ref = bf16[2,512,1024]{2,1,0:T(8,128)(2,1)} reshape(bf16[2,512,4,256]{3,2,1,0:T(4,128)(2,1)} %param.4) | data formatting | bytes 4194304 | tf_op jit(solution)/shard_map/reshape | solution.py:290
  124.8 2.7 %collective-permute-start.40 = (bf16[1,384,128]{2,1,0:T(8,128)(2,1)S(1)}, bf16[1,384,128]{2,1,0:T(8,128)(2,1)S(1)}, u32[]{:S(2)}, u32[]{:S(2)}) collective-permute-start(bf16[1,384,128]{2,1,0:T(8,128)(2,1)S(1)} %slice_bitcast_fusion), channel_id=1, source_target_pairs={{0,24},{8,16},{16,8},{24,0},{1,25},{9,17},{17,9},{25,1},{2,26},{10... | collective-permute-start | bytes 294920 | tf_op jit(solution)/shard_map/ppermute | solution.py:33
  128.4 2.3 %collective-permute-start.37 = (bf16[2,384,128]{2,1,0:T(8,128)(2,1)S(1)}, bf16[2,384,128]{2,1,0:T(8,128)(2,1)S(1)}, u32[]{:S(2)}, u32[]{:S(2)}) collective-permute-start(bf16[2,384,128]{2,1,0:T(8,128)(2,1)S(1)} %pad_maximum_fusion.14), channel_id=1, source_target_pairs={{0,24},{8,16},{16,8},{24,0},{1,25},{9,17},{17,9},{25,1},{2,26},{10... | collective-permute-start | bytes 589832 | tf_op jit(solution)/shard_map/ppermute | solution.py:33
  131.4 2.3 %collective-permute-start.27 = (bf16[2,384,128]{2,1,0:T(8,128)(2,1)S(1)}, bf16[2,384,128]{2,1,0:T(8,128)(2,1)S(1)}, u32[]{:S(2)}, u32[]{:S(2)}) collective-permute-start(bf16[2,384,128]{2,1,0:T(8,128)(2,1)S(1)} %pad_maximum_fusion.12), channel_id=1, source_target_pairs={{0,96},{32,64},{64,32},{96,0},{1,97},{33,65},{65,33},{97,1},{2,98}... | collective-permute-start | bytes 589832 | tf_op jit(solution)/shard_map/ppermute | solution.py:33
  133.7 2.9 %collective-permute-done.37 = bf16[2,384,128]{2,1,0:T(8,128)(2,1)S(1)} collective-permute-done((bf16[2,384,128]{2,1,0:T(8,128)(2,1)S(1)}, bf16[2,384,128]{2,1,0:T(8,128)(2,1)S(1)}, u32[]{:S(2)}, u32[]{:S(2)}) %collective-permute-start.37) | collective-permute-done | bytes 196640 | tf_op jit(solution)/shard_map/ppermute | solution.py:33
  142.8 2.7 %collective-permute-done.41 = bf16[2,384,128]{2,1,0:T(8,128)(2,1)S(1)} collective-permute-done((bf16[2,384,128]{2,1,0:T(8,128)(2,1)S(1)}, bf16[2,384,128]{2,1,0:T(8,128)(2,1)S(1)}, u32[]{:S(2)}, u32[]{:S(2)}) %collective-permute-start.41) | collective-permute-done | bytes 196640 | tf_op jit(solution)/shard_map/ppermute | solution.py:33
  145.5 2.8 %collective-permute-start.42 = (bf16[4,384,128]{2,1,0:T(8,128)(2,1)S(1)}, bf16[4,384,128]{2,1,0:T(8,128)(2,1)S(1)}, u32[]{:S(2)}, u32[]{:S(2)}) collective-permute-start(bf16[4,384,128]{2,1,0:T(8,128)(2,1)S(1)} %pad_maximum_fusion.9), channel_id=1, source_target_pairs={{0,96},{32,64},{64,32},{96,0},{1,97},{33,65},{65,33},{97,1},{2,98}... | collective-permute-start | bytes 1179656 | tf_op jit(solution)/shard_map/ppermute | solution.py:33
  153.0 2.6 %collective-permute-start.29 = (bf16[8,384,128]{2,1,0:T(8,128)(2,1)S(1)}, bf16[8,384,128]{2,1,0:T(8,128)(2,1)}, u32[]{:S(2)}, u32[]{:S(2)}) collective-permute-start(bf16[8,384,128]{2,1,0:T(8,128)(2,1)S(1)} %pad_maximum_fusion.rest_0_.rest_1_), channel_id=1, source_target_pairs={{0,24},{8,16},{16,8},{24,0},{1,25},{9,17},{17,9},{25,1},{2,26},{10... | collective-permute-start | bytes 2359304 | tf_op jit(solution)/shard_map/ppermute | solution.py:33
  159.3 12.2 %collective-permute-done.39.rest_12_.rest_13_ = bf16[8,384,128]{2,1,0:T(8,128)(2,1)} collective-permute-done((bf16[8,384,128]{2,1,0:T(8,128)(2,1)S(1)}, bf16[8,384,128]{2,1,0:T(8,128)(2,1)}, u32[]{:S(2)}, u32[]{:S(2)}) %collective-permute-start.39) | collective-permute-done | bytes 786464 | tf_op jit(solution)/shard_map/ppermute | solution.py:33
  171.9 2.5 %collective-permute-done.34.rest_10_.rest_11_ = bf16[8,384,128]{2,1,0:T(8,128)(2,1)} collective-permute-done((bf16[8,384,128]{2,1,0:T(8,128)(2,1)S(1)}, bf16[8,384,128]{2,1,0:T(8,128)(2,1)}, u32[]{:S(2)}, u32[]{:S(2)}) %collective-permute-start.34) | collective-permute-done | bytes 786464 | tf_op jit(solution)/shard_map/ppermute | solution.py:33
  174.6 18.5 %shard_map.42 = f32[2,512,2048]{2,1,0:T(8,128)} custom-call(s32[66]{0:T(128)S(1)} %pad_add_fusion.1.scalars, bf16[2,512,1024]{2,1,0:T(8,128)(2,1)} %reshape.179.mine_ref, bf16[2,512,1024]{2,1,0:T(8,128)(2,1)} %collective-permute-done.other_ref, f32[2,512,2048]{2,1,0:T(8,128)} %rhs_ref.3, bf16[16,512,128]{2,1,0:T(8,128)(2,1)} %bitcast.27, ...), custom_call_target="tpu_custom_call" | custom-call | tf_op jit(solution)/shard_map/pallas_call | solution.py:203
  (130 shorter events, 65.6 us)
Async XLA Ops:
  6.5 138.9 %all-gather.3.cloned.1.call-start = ((), (), s32[]{:S(2)}) async-start(), calls=%async_computation | async-start | bytes 2228224 | tf_op jit(solution)/shard_map/all_gather | solution.py:274
  12.6 17.9 %collective-permute-start.1 = (bf16[608,512]{1,0:T(8,128)(2,1)S(1)}, bf16[608,512]{1,0:T(8,128)(2,1)}, u32[]{:S(2)}, u32[]{:S(2)}) collective-permute-start(bf16[608,512]{1,0:T(8,128)(2,1)S(1)} %get-tuple-element.39), channel_id=1, source_target_pairs={{0,32},{2,34},{4,36},{6,38},{1,33},{3,35},{5,37},{7,39}} | collective-permute-start | bytes 1867784 | tf_op jit(solution)/shard_map/ppermute | solution.py:25
  16.9 25.9 %collective-permute-start.2 = (bf16[608,512]{1,0:T(8,128)(2,1)}, bf16[608,512]{1,0:T(8,128)(2,1)}, u32[]{:S(2)}, u32[]{:S(2)}) collective-permute-start(bf16[608,512]{1,0:T(8,128)(2,1)} %get-tuple-element.40), channel_id=1, source_target_pairs={{0,64},{2,66},{4,68},{6,70},{1,65},{3,67},{5,69},{7,71}} | collective-permute-start | bytes 1867784 | tf_op jit(solution)/shard_map/ppermute | solution.py:25
  20.0 22.7 %collective-permute-start.3 = (bf16[608,512]{1,0:T(8,128)(2,1)}, bf16[608,512]{1,0:T(8,128)(2,1)}, u32[]{:S(2)}, u32[]{:S(2)}) collective-permute-start(bf16[608,512]{1,0:T(8,128)(2,1)} %get-tuple-element.41), channel_id=1, source_target_pairs={{0,96},{2,98},{4,100},{6,102},{1,97},{3,99},{5,101},{7,103}} | collective-permute-start | bytes 1867784 | tf_op jit(solution)/shard_map/ppermute | solution.py:25
  22.1 22.2 %collective-permute-start.7 = (bf16[608,512]{1,0:T(8,128)(2,1)}, bf16[608,512]{1,0:T(8,128)(2,1)}, u32[]{:S(2)}, u32[]{:S(2)}) collective-permute-start(bf16[608,512]{1,0:T(8,128)(2,1)} %get-tuple-element.44), channel_id=1, source_target_pairs={{0,8},{2,10},{4,12},{6,14},{1,9},{3,11},{5,13},{7,15}} | collective-permute-start | bytes 1867784 | tf_op jit(solution)/shard_map/ppermute | solution.py:25
  24.3 26.0 %collective-permute-start.8 = (bf16[608,512]{1,0:T(8,128)(2,1)S(1)}, bf16[608,512]{1,0:T(8,128)(2,1)}, u32[]{:S(2)}, u32[]{:S(2)}) collective-permute-start(bf16[608,512]{1,0:T(8,128)(2,1)S(1)} %get-tuple-element.45), channel_id=1, source_target_pairs={{0,16},{2,18},{4,20},{6,22},{1,17},{3,19},{5,21},{7,23}} | collective-permute-start | bytes 1867784 | tf_op jit(solution)/shard_map/ppermute | solution.py:25
  30.4 19.8 %collective-permute-start.9 = (bf16[608,512]{1,0:T(8,128)(2,1)S(1)}, bf16[608,512]{1,0:T(8,128)(2,1)}, u32[]{:S(2)}, u32[]{:S(2)}) collective-permute-start(bf16[608,512]{1,0:T(8,128)(2,1)S(1)} %get-tuple-element.46), channel_id=1, source_target_pairs={{0,24},{2,26},{4,28},{6,30},{1,25},{3,27},{5,29},{7,31}} | collective-permute-start | bytes 1867784 | tf_op jit(solution)/shard_map/ppermute | solution.py:25
  52.0 10.9 %collective-permute-start.11 = (bf16[896,128]{1,0:T(8,128)(2,1)S(1)}, bf16[896,128]{1,0:T(8,128)(2,1)S(1)}, u32[]{:S(2)}, u32[]{:S(2)}) collective-permute-start(bf16[896,128]{1,0:T(8,128)(2,1)S(1)} %get-tuple-element.103), channel_id=1, source_target_pairs={{0,96},{8,104},{16,112},{24,120},{2,98},{10,106},{18,114},{26,122}... | collective-permute-start | bytes 688136 | tf_op jit(solution)/shard_map/ppermute | solution.py:25
  53.3 10.9 %collective-permute-start.12 = (bf16[896,128]{1,0:T(8,128)(2,1)S(1)}, bf16[896,128]{1,0:T(8,128)(2,1)S(1)}, u32[]{:S(2)}, u32[]{:S(2)}) collective-permute-start(bf16[896,128]{1,0:T(8,128)(2,1)S(1)} %get-tuple-element.104), channel_id=1, source_target_pairs={{0,64},{8,72},{16,80},{24,88},{2,66},{10,74},{18,82},{26,90},{4,68... | collective-permute-start | bytes 688136 | tf_op jit(solution)/shard_map/ppermute | solution.py:25
  54.6 9.6 %collective-permute-start.10 = (bf16[896,128]{1,0:T(8,128)(2,1)S(1)}, bf16[896,128]{1,0:T(8,128)(2,1)S(1)}, u32[]{:S(2)}, u32[]{:S(2)}) collective-permute-start(bf16[896,128]{1,0:T(8,128)(2,1)S(1)} %get-tuple-element.94), channel_id=1, source_target_pairs={{0,32},{8,40},{16,48},{24,56},{2,34},{10,42},{18,50},{26,58},{4,36... | collective-permute-start | bytes 688136 | tf_op jit(solution)/shard_map/ppermute | solution.py:25
  57.5 11.4 %collective-permute-start.6 = (bf16[896,128]{1,0:T(8,128)(2,1)S(1)}, bf16[896,128]{1,0:T(8,128)(2,1)S(1)}, u32[]{:S(2)}, u32[]{:S(2)}) collective-permute-start(bf16[896,128]{1,0:T(8,128)(2,1)S(1)} %get-tuple-element.87), channel_id=1, source_target_pairs={{0,16},{32,48},{64,80},{96,112},{2,18},{34,50},{66,82},{98,114},{4... | collective-permute-start | bytes 688136 | tf_op jit(solution)/shard_map/ppermute | solution.py:25
  73.8 9.0 %collective-permute-start.16 = (bf16[512,128]{1,0:T(8,128)(2,1)S(1)}, bf16[512,128]{1,0:T(8,128)(2,1)S(1)}, u32[]{:S(2)}, u32[]{:S(2)}) collective-permute-start(bf16[512,128]{1,0:T(8,128)(2,1)S(1)} %shard_map.38), channel_id=1, source_target_pairs={{0,6},{8,14},{16,22},{24,30},{32,38},{40,46},{48,54},{56,62},{64,7... | collective-permute-start | bytes 393224 | tf_op jit(solution)/shard_map/ppermute | solution.py:25
  94.5 8.9 %collective-permute-start.23 = (bf16[512,128]{1,0:T(8,128)(2,1)S(1)}, bf16[512,128]{1,0:T(8,128)(2,1)S(1)}, u32[]{:S(2)}, u32[]{:S(2)}) collective-permute-start(bf16[512,128]{1,0:T(8,128)(2,1)S(1)} %get-tuple-element.58), channel_id=1, source_target_pairs={{2,6},{10,14},{18,22},{26,30},{34,38},{42,46},{50,54},{58,62},{66,... | collective-permute-start | bytes 393224 | tf_op jit(solution)/shard_map/ppermute | solution.py:25
  122.3 37.0 %collective-permute-start = (bf16[2,512,1024]{2,1,0:T(8,128)(2,1)}, bf16[2,512,1024]{2,1,0:T(8,128)(2,1)}, u32[]{:S(2)}, u32[]{:S(2)}) collective-permute-start(bf16[2,512,1024]{2,1,0:T(8,128)(2,1)} %reshape.179.mine_ref), channel_id=1, source_target_pairs={{0,1},{1,0},{2,3},{3,2},{4,5},{5,4},{6,7},{7,6},{8,9},{9,8},{10,11... | collective-permute-start | bytes 6291464 | tf_op jit(solution)/shard_map/ppermute | solution.py:291
  124.8 12.8 %collective-permute-start.40 = (bf16[1,384,128]{2,1,0:T(8,128)(2,1)S(1)}, bf16[1,384,128]{2,1,0:T(8,128)(2,1)S(1)}, u32[]{:S(2)}, u32[]{:S(2)}) collective-permute-start(bf16[1,384,128]{2,1,0:T(8,128)(2,1)S(1)} %slice_bitcast_fusion), channel_id=1, source_target_pairs={{0,24},{8,16},{16,8},{24,0},{1,25},{9,17},{17,9},{25,1},{2,26},{10... | collective-permute-start | bytes 294920 | tf_op jit(solution)/shard_map/ppermute | solution.py:33
  130.8 10.0 %collective-permute-start.32 = (bf16[2,384,128]{2,1,0:T(8,128)(2,1)S(1)}, bf16[2,384,128]{2,1,0:T(8,128)(2,1)S(1)}, u32[]{:S(2)}, u32[]{:S(2)}) collective-permute-start(bf16[2,384,128]{2,1,0:T(8,128)(2,1)S(1)} %pad_maximum_fusion.13), channel_id=1, source_target_pairs={{0,32},{32,0},{64,96},{96,64},{1,33},{33,1},{65,97},{97,65},{2,34}... | collective-permute-start | bytes 589832 | tf_op jit(solution)/shard_map/ppermute | solution.py:33
  136.7 11.6 %collective-permute-start.38 = (bf16[4,384,128]{2,1,0:T(8,128)(2,1)S(1)}, bf16[4,384,128]{2,1,0:T(8,128)(2,1)}, u32[]{:S(2)}, u32[]{:S(2)}) collective-permute-start(bf16[4,384,128]{2,1,0:T(8,128)(2,1)S(1)} %pad_maximum_fusion.8), channel_id=1, source_target_pairs={{0,32},{32,0},{64,96},{96,64},{1,33},{33,1},{65,97},{97,65},{2,34}... | collective-permute-start | bytes 1179656 | tf_op jit(solution)/shard_map/ppermute | solution.py:33
  139.8 12.1 %collective-permute-start.28 = (bf16[4,384,128]{2,1,0:T(8,128)(2,1)}, bf16[4,384,128]{2,1,0:T(8,128)(2,1)}, u32[]{:S(2)}, u32[]{:S(2)}) collective-permute-start(bf16[4,384,128]{2,1,0:T(8,128)(2,1)} %pad_maximum_fusion.6), channel_id=1, source_target_pairs={{0,8},{8,0},{16,24},{24,16},{1,9},{9,1},{17,25},{25,17},{2,10},{10... | collective-permute-start | bytes 1179656 | tf_op jit(solution)/shard_map/ppermute | solution.py:33
  140.9 14.7 %collective-permute-start.33 = (bf16[4,384,128]{2,1,0:T(8,128)(2,1)S(1)}, bf16[4,384,128]{2,1,0:T(8,128)(2,1)}, u32[]{:S(2)}, u32[]{:S(2)}) collective-permute-start(bf16[4,384,128]{2,1,0:T(8,128)(2,1)S(1)} %pad_maximum_fusion.7), channel_id=1, source_target_pairs={{0,24},{8,16},{16,8},{24,0},{1,25},{9,17},{17,9},{25,1},{2,26},{10... | collective-permute-start | bytes 1179656 | tf_op jit(solution)/shard_map/ppermute | solution.py:33
  145.5 13.2 %collective-permute-start.42 = (bf16[4,384,128]{2,1,0:T(8,128)(2,1)S(1)}, bf16[4,384,128]{2,1,0:T(8,128)(2,1)S(1)}, u32[]{:S(2)}, u32[]{:S(2)}) collective-permute-start(bf16[4,384,128]{2,1,0:T(8,128)(2,1)S(1)} %pad_maximum_fusion.9), channel_id=1, source_target_pairs={{0,96},{32,64},{64,32},{96,0},{1,97},{33,65},{65,33},{97,1},{2,98}... | collective-permute-start | bytes 1179656 | tf_op jit(solution)/shard_map/ppermute | solution.py:33
  149.4 22.1 %collective-permute-start.39 = (bf16[8,384,128]{2,1,0:T(8,128)(2,1)S(1)}, bf16[8,384,128]{2,1,0:T(8,128)(2,1)}, u32[]{:S(2)}, u32[]{:S(2)}) collective-permute-start(bf16[8,384,128]{2,1,0:T(8,128)(2,1)S(1)} %pad_maximum_fusion.2.rest_4_.rest_5_), channel_id=1, source_target_pairs={{0,96},{32,64},{64,32},{96,0},{1,97},{33,65},{65,33},{97,1},{2,98}... | collective-permute-start | bytes 2359304 | tf_op jit(solution)/shard_map/ppermute | solution.py:33
  153.0 18.9 %collective-permute-start.29 = (bf16[8,384,128]{2,1,0:T(8,128)(2,1)S(1)}, bf16[8,384,128]{2,1,0:T(8,128)(2,1)}, u32[]{:S(2)}, u32[]{:S(2)}) collective-permute-start(bf16[8,384,128]{2,1,0:T(8,128)(2,1)S(1)} %pad_maximum_fusion.rest_0_.rest_1_), channel_id=1, source_target_pairs={{0,24},{8,16},{16,8},{24,0},{1,25},{9,17},{17,9},{25,1},{2,26},{10... | collective-permute-start | bytes 2359304 | tf_op jit(solution)/shard_map/ppermute | solution.py:33
  156.6 17.7 %collective-permute-start.34 = (bf16[8,384,128]{2,1,0:T(8,128)(2,1)S(1)}, bf16[8,384,128]{2,1,0:T(8,128)(2,1)}, u32[]{:S(2)}, u32[]{:S(2)}) collective-permute-start(bf16[8,384,128]{2,1,0:T(8,128)(2,1)S(1)} %pad_maximum_fusion.1.rest_2_.rest_3_), channel_id=1, source_target_pairs={{0,8},{8,0},{16,24},{24,16},{1,9},{9,1},{17,25},{25,17},{2,10},{10... | collective-permute-start | bytes 2359304 | tf_op jit(solution)/shard_map/ppermute | solution.py:33
  158.7 15.9 %collective-permute-start.43 = (bf16[8,384,128]{2,1,0:T(8,128)(2,1)S(1)}, bf16[8,384,128]{2,1,0:T(8,128)(2,1)}, u32[]{:S(2)}, u32[]{:S(2)}) collective-permute-start(bf16[8,384,128]{2,1,0:T(8,128)(2,1)S(1)} %pad_maximum_fusion.3.rest_6_.rest_7_), channel_id=1, source_target_pairs={{0,32},{32,0},{64,96},{96,64},{1,33},{33,1},{65,97},{97,65},{2,34}... | collective-permute-start | bytes 2359304 | tf_op jit(solution)/shard_map/ppermute | solution.py:33
  (21 other events, 138.7 us)
Sparse Core Ops, SparseCore 0:
  83.6 45.0 all-gather.2

commit v13 on v10

--- a/solution.py
+++ b/solution.py
@@ -239,7 +239,7 @@
         tail = [hold[512:, k * 128:(k + 1) * 128] for k in range(4)]
         message = lambda d: jnp.concatenate([hold[:512, d * 128:(d + 1) * 128]] + tail, axis=0)
         mine = jnp.where((z if axis == "y" else y) == 0, message(0), zero)
-        for d in (1, 3, 2):
+        for d in (2, 1, 3):
             if axis == "y":
                 moves = [((i, j, 0), (i, j, d)) for i in range(4) for j in range(4)]
             else:

time: 199 us -> 197 us (0.990)
    ppermute x21, waiting for transfers between devices: 40.3 us -> 35.1 us  [permute(): return lax.ppermute(value, ROWS, [(flat(*a), flat(*b)) for a, b in moves])]
    ppermute x20, waiting for transfers between devices: 37.1 us -> 42 us  [swap(): return lax.ppermute(value, axis, [(i, i ^ flip) for i in range(4)])]
  transfers between devices with their start and end apart: 45 -> 45, of which waited for: 22 -> 20; matrix products, arithmetic and copies ran while one was open for 5% -> 5% of each run, Pallas kernels for 3% -> 3%
where the time goes in v13:
time: 197 us
  waiting for transfers between devices  78.8 us (40%)
  starting transfers between devices  60.6 us (31%)
  Pallas kernels  28.5 us (14%)
  between operations  13.9 us (7%)
  other arithmetic  7.46 us (4%)
  local copies, waits for them, and re-layouts  7.3 us (4%)
    ppermute x20, waiting for transfers between devices, swap(): return lax.ppermute(value, axis, [(i, i ^ flip) for i in range(4)])  42 us
    ppermute x21, starting transfers between devices, permute(): return lax.ppermute(value, ROWS, [(flat(*a), flat(*b)) for a, b in moves])  38.2 us
    ppermute x21, waiting for transfers between devices, permute(): return lax.ppermute(value, ROWS, [(flat(*a), flat(*b)) for a, b in moves])  35.1 us
    ppermute x20, starting transfers between devices, swap(): return lax.ppermute(value, axis, [(i, i ^ flip) for i in range(4)])  22.2 us
    pallas_call x1, Pallas kernels, update(): pl.pallas_call(update_kernel, grid_spec=pltpu.PrefetchScalarGridSpec(num_...  18.5 us
    pallas_call x4, Pallas kernels, step(): pl.pallas_call(kernel, grid_spec=pltpu.PrefetchScalarGridSpec(num_scalar_...  6.36 us
    reshape x1, local copies, waits for them, and re-layouts, local(): flat_factor = factor.reshape(2, 512, 1024)  4.46 us
  transfers between devices with their start and end apart: 45, of which 20 were waited for; matrix products, arithmetic and copies ran while one was open for 5% of the time, Pallas kernels for 3%

profile of v13, /device:TPU:6, one launch (start us, length us, event | category | flops | bytes accessed | tf_op | source)
XLA Modules:
  0.0 196.6 jit_solution(10975847774286340304)
XLA Ops:
  8.9 3.7 %shard_map.37 = (bf16[608,512]{1,0:T(8,128)(2,1)S(1)}, bf16[608,512]{1,0:T(8,128)(2,1)S(1)}, bf16[608,512]{1,0:T(8,128)(2,1)}, bf16[608,512]{1,0:T(8,128)(2,1)},...) custom-call(f32[2,512,2048]{2,1,0:T(8,128)} %rhs_ref.3, ...), custom_call_target="tpu_custom_call" | custom-call | tf_op jit(solution)/shard_map/pallas_call | solution.py:88
  12.6 4.3 %collective-permute-start.1 = (bf16[608,512]{1,0:T(8,128)(2,1)S(1)}, bf16[608,512]{1,0:T(8,128)(2,1)}, u32[]{:S(2)}, u32[]{:S(2)}) collective-permute-start(bf16[608,512]{1,0:T(8,128)(2,1)S(1)} %get-tuple-element.39), channel_id=1, source_target_pairs={{0,32},{2,34},{4,36},{6,38},{1,33},{3,35},{5,37},{7,39}} | collective-permute-start | bytes 1867784 | tf_op jit(solution)/shard_map/ppermute | solution.py:25
  16.9 3.1 %collective-permute-start.2 = (bf16[608,512]{1,0:T(8,128)(2,1)}, bf16[608,512]{1,0:T(8,128)(2,1)}, u32[]{:S(2)}, u32[]{:S(2)}) collective-permute-start(bf16[608,512]{1,0:T(8,128)(2,1)} %get-tuple-element.40), channel_id=1, source_target_pairs={{0,64},{2,66},{4,68},{6,70},{1,65},{3,67},{5,69},{7,71}} | collective-permute-start | bytes 1867784 | tf_op jit(solution)/shard_map/ppermute | solution.py:25
  20.0 2.1 %collective-permute-start.3 = (bf16[608,512]{1,0:T(8,128)(2,1)}, bf16[608,512]{1,0:T(8,128)(2,1)}, u32[]{:S(2)}, u32[]{:S(2)}) collective-permute-start(bf16[608,512]{1,0:T(8,128)(2,1)} %get-tuple-element.41), channel_id=1, source_target_pairs={{0,96},{2,98},{4,100},{6,102},{1,97},{3,99},{5,101},{7,103}} | collective-permute-start | bytes 1867784 | tf_op jit(solution)/shard_map/ppermute | solution.py:25
  22.1 2.1 %collective-permute-start.7 = (bf16[608,512]{1,0:T(8,128)(2,1)}, bf16[608,512]{1,0:T(8,128)(2,1)}, u32[]{:S(2)}, u32[]{:S(2)}) collective-permute-start(bf16[608,512]{1,0:T(8,128)(2,1)} %get-tuple-element.44), channel_id=1, source_target_pairs={{0,8},{2,10},{4,12},{6,14},{1,9},{3,11},{5,13},{7,15}} | collective-permute-start | bytes 1867784 | tf_op jit(solution)/shard_map/ppermute | solution.py:25
  26.4 4.1 %collective-permute-done.1 = bf16[608,512]{1,0:T(8,128)(2,1)} collective-permute-done((bf16[608,512]{1,0:T(8,128)(2,1)S(1)}, bf16[608,512]{1,0:T(8,128)(2,1)}, u32[]{:S(2)}, u32[]{:S(2)}) %collective-permute-start.1) | collective-permute-done | bytes 622624 | tf_op jit(solution)/shard_map/ppermute | solution.py:25
  34.0 8.7 %collective-permute-done.2 = bf16[608,512]{1,0:T(8,128)(2,1)} collective-permute-done((bf16[608,512]{1,0:T(8,128)(2,1)}, bf16[608,512]{1,0:T(8,128)(2,1)}, u32[]{:S(2)}, u32[]{:S(2)}) %collective-permute-start.2) | collective-permute-done | bytes 622624 | tf_op jit(solution)/shard_map/ppermute | solution.py:25
  44.3 5.9 %collective-permute-done.8 = bf16[608,512]{1,0:T(8,128)(2,1)} collective-permute-done((bf16[608,512]{1,0:T(8,128)(2,1)S(1)}, bf16[608,512]{1,0:T(8,128)(2,1)}, u32[]{:S(2)}, u32[]{:S(2)}) %collective-permute-start.8) | collective-permute-done | bytes 622624 | tf_op jit(solution)/shard_map/ppermute | solution.py:25
  59.4 6.0 %collective-permute-start.4 = (bf16[896,128]{1,0:T(8,128)(2,1)S(1)}, bf16[896,128]{1,0:T(8,128)(2,1)S(1)}, u32[]{:S(2)}, u32[]{:S(2)}) collective-permute-start(bf16[896,128]{1,0:T(8,128)(2,1)S(1)} %get-tuple-element.77), channel_id=1, source_target_pairs={{0,16},{32,48},{64,80},{96,112},{2,18},{34,50},{66,82},{98,114},{4... | collective-permute-start | bytes 688136 | tf_op jit(solution)/shard_map/ppermute | solution.py:25
  65.6 3.3 %collective-permute-done.4 = bf16[896,128]{1,0:T(8,128)(2,1)S(1)} collective-permute-done((bf16[896,128]{1,0:T(8,128)(2,1)S(1)}, bf16[896,128]{1,0:T(8,128)(2,1)S(1)}, u32[]{:S(2)}, u32[]{:S(2)}) %collective-permute-start.4) | collective-permute-done | bytes 229408 | tf_op jit(solution)/shard_map/ppermute | solution.py:25
  72.9 2.6 %collective-permute-start.13 = (bf16[384,128]{1,0:T(8,128)(2,1)S(1)}, bf16[384,128]{1,0:T(8,128)(2,1)S(1)}, u32[]{:S(2)}, u32[]{:S(2)}) collective-permute-start(bf16[384,128]{1,0:T(8,128)(2,1)S(1)} %slice.120), channel_id=1, source_target_pairs={{0,32},{32,0},{64,96},{96,64},{1,33},{33,1},{65,97},{97,65},{2,34}... | collective-permute-start | bytes 294920 | tf_op jit(solution)/shard_map/ppermute | solution.py:33
  75.4 2.6 %collective-permute-done.13 = bf16[384,128]{1,0:T(8,128)(2,1)S(1)} collective-permute-done((bf16[384,128]{1,0:T(8,128)(2,1)S(1)}, bf16[384,128]{1,0:T(8,128)(2,1)S(1)}, u32[]{:S(2)}, u32[]{:S(2)}) %collective-permute-start.13) | collective-permute-done | bytes 98336 | tf_op jit(solution)/shard_map/ppermute | solution.py:33
  80.8 2.6 %collective-permute-start.19 = (bf16[2,384,128]{2,1,0:T(8,128)(2,1)S(1)}, bf16[2,384,128]{2,1,0:T(8,128)(2,1)S(1)}, u32[]{:S(2)}, u32[]{:S(2)}) collective-permute-start(bf16[2,384,128]{2,1,0:T(8,128)(2,1)S(1)} %pad_maximum_fusion.11), channel_id=1, source_target_pairs={{0,24},{8,16},{16,8},{24,0},{1,25},{9,17},{17,9},{25,1},{2,26},{10... | collective-permute-start | bytes 589832 | tf_op jit(solution)/shard_map/ppermute | solution.py:33
  83.5 4.2 %collective-permute-done.19 = bf16[2,384,128]{2,1,0:T(8,128)(2,1)S(1)} collective-permute-done((bf16[2,384,128]{2,1,0:T(8,128)(2,1)S(1)}, bf16[2,384,128]{2,1,0:T(8,128)(2,1)S(1)}, u32[]{:S(2)}, u32[]{:S(2)}) %collective-permute-start.19) | collective-permute-done | bytes 196640 | tf_op jit(solution)/shard_map/ppermute | solution.py:33
  87.9 2.5 %collective-permute-done.18 = bf16[2,384,128]{2,1,0:T(8,128)(2,1)S(1)} collective-permute-done((bf16[2,384,128]{2,1,0:T(8,128)(2,1)S(1)}, bf16[2,384,128]{2,1,0:T(8,128)(2,1)S(1)}, u32[]{:S(2)}, u32[]{:S(2)}) %collective-permute-start.18) | collective-permute-done | bytes 196640 | tf_op jit(solution)/shard_map/ppermute | solution.py:33
  95.9 7.0 %collective-permute-done.23.refs_9_ = bf16[512,128]{1,0:T(8,128)(2,1)S(1)} collective-permute-done((bf16[512,128]{1,0:T(8,128)(2,1)S(1)}, bf16[512,128]{1,0:T(8,128)(2,1)S(1)}, u32[]{:S(2)}, u32[]{:S(2)}) %collective-permute-start.23) | collective-permute-done | bytes 131104 | tf_op jit(solution)/shard_map/ppermute | solution.py:25
  105.8 5.6 %collective-permute-done.24.refs_8_ = bf16[512,128]{1,0:T(8,128)(2,1)S(1)} collective-permute-done((bf16[512,128]{1,0:T(8,128)(2,1)S(1)}, bf16[512,128]{1,0:T(8,128)(2,1)S(1)}, u32[]{:S(2)}, u32[]{:S(2)}) %collective-permute-start.24) | collective-permute-done | bytes 131104 | tf_op jit(solution)/shard_map/ppermute | solution.py:25
  117.2 4.5 %reshape.179.mine_ref = bf16[2,512,1024]{2,1,0:T(8,128)(2,1)} reshape(bf16[2,512,4,256]{3,2,1,0:T(4,128)(2,1)} %param.4) | data formatting | bytes 4194304 | tf_op jit(solution)/shard_map/reshape | solution.py:290
  125.6 2.3 %collective-permute-done.36 = bf16[1,384,128]{2,1,0:T(8,128)(2,1)S(1)} collective-permute-done((bf16[1,384,128]{2,1,0:T(8,128)(2,1)S(1)}, bf16[1,384,128]{2,1,0:T(8,128)(2,1)S(1)}, u32[]{:S(2)}, u32[]{:S(2)}) %collective-permute-start.36) | collective-permute-done | bytes 98336 | tf_op jit(solution)/shard_map/ppermute | solution.py:33
  132.4 3.7 %collective-permute-done.37 = bf16[2,384,128]{2,1,0:T(8,128)(2,1)S(1)} collective-permute-done((bf16[2,384,128]{2,1,0:T(8,128)(2,1)S(1)}, bf16[2,384,128]{2,1,0:T(8,128)(2,1)S(1)}, u32[]{:S(2)}, u32[]{:S(2)}) %collective-permute-start.37) | collective-permute-done | bytes 196640 | tf_op jit(solution)/shard_map/ppermute | solution.py:33
  141.2 4.4 %collective-permute-done.41 = bf16[2,384,128]{2,1,0:T(8,128)(2,1)S(1)} collective-permute-done((bf16[2,384,128]{2,1,0:T(8,128)(2,1)S(1)}, bf16[2,384,128]{2,1,0:T(8,128)(2,1)S(1)}, u32[]{:S(2)}, u32[]{:S(2)}) %collective-permute-start.41) | collective-permute-done | bytes 196640 | tf_op jit(solution)/shard_map/ppermute | solution.py:33
  153.2 5.8 %collective-permute-done.42 = bf16[4,384,128]{2,1,0:T(8,128)(2,1)S(1)} collective-permute-done((bf16[4,384,128]{2,1,0:T(8,128)(2,1)S(1)}, bf16[4,384,128]{2,1,0:T(8,128)(2,1)S(1)}, u32[]{:S(2)}, u32[]{:S(2)}) %collective-permute-start.42) | collective-permute-done | bytes 393248 | tf_op jit(solution)/shard_map/ppermute | solution.py:33
  159.4 11.9 %collective-permute-done.39.rest_12_.rest_13_ = bf16[8,384,128]{2,1,0:T(8,128)(2,1)} collective-permute-done((bf16[8,384,128]{2,1,0:T(8,128)(2,1)S(1)}, bf16[8,384,128]{2,1,0:T(8,128)(2,1)}, u32[]{:S(2)}, u32[]{:S(2)}) %collective-permute-start.39) | collective-permute-done | bytes 786464 | tf_op jit(solution)/shard_map/ppermute | solution.py:33
  171.3 18.5 %shard_map.42 = f32[2,512,2048]{2,1,0:T(8,128)} custom-call(s32[66]{0:T(128)S(1)} %pad_add_fusion.1.scalars, bf16[2,512,1024]{2,1,0:T(8,128)(2,1)} %reshape.179.mine_ref, bf16[2,512,1024]{2,1,0:T(8,128)(2,1)} %collective-permute-done.other_ref, f32[2,512,2048]{2,1,0:T(8,128)} %rhs_ref.3, bf16[16,512,128]{2,1,0:T(8,128)(2,1)} %bitcast.27, ...), custom_call_target="tpu_custom_call" | custom-call | tf_op jit(solution)/shard_map/pallas_call | solution.py:203
  (130 shorter events, 61.2 us)
Async XLA Ops:
  6.5 131.1 %all-gather.3.cloned.1.call-start = ((), (), s32[]{:S(2)}) async-start(), calls=%async_computation | async-start | bytes 2228224 | tf_op jit(solution)/shard_map/all_gather | solution.py:274
  12.6 17.9 %collective-permute-start.1 = (bf16[608,512]{1,0:T(8,128)(2,1)S(1)}, bf16[608,512]{1,0:T(8,128)(2,1)}, u32[]{:S(2)}, u32[]{:S(2)}) collective-permute-start(bf16[608,512]{1,0:T(8,128)(2,1)S(1)} %get-tuple-element.39), channel_id=1, source_target_pairs={{0,32},{2,34},{4,36},{6,38},{1,33},{3,35},{5,37},{7,39}} | collective-permute-start | bytes 1867784 | tf_op jit(solution)/shard_map/ppermute | solution.py:25
  16.9 25.9 %collective-permute-start.2 = (bf16[608,512]{1,0:T(8,128)(2,1)}, bf16[608,512]{1,0:T(8,128)(2,1)}, u32[]{:S(2)}, u32[]{:S(2)}) collective-permute-start(bf16[608,512]{1,0:T(8,128)(2,1)} %get-tuple-element.40), channel_id=1, source_target_pairs={{0,64},{2,66},{4,68},{6,70},{1,65},{3,67},{5,69},{7,71}} | collective-permute-start | bytes 1867784 | tf_op jit(solution)/shard_map/ppermute | solution.py:25
  20.0 22.7 %collective-permute-start.3 = (bf16[608,512]{1,0:T(8,128)(2,1)}, bf16[608,512]{1,0:T(8,128)(2,1)}, u32[]{:S(2)}, u32[]{:S(2)}) collective-permute-start(bf16[608,512]{1,0:T(8,128)(2,1)} %get-tuple-element.41), channel_id=1, source_target_pairs={{0,96},{2,98},{4,100},{6,102},{1,97},{3,99},{5,101},{7,103}} | collective-permute-start | bytes 1867784 | tf_op jit(solution)/shard_map/ppermute | solution.py:25
  22.1 22.2 %collective-permute-start.7 = (bf16[608,512]{1,0:T(8,128)(2,1)}, bf16[608,512]{1,0:T(8,128)(2,1)}, u32[]{:S(2)}, u32[]{:S(2)}) collective-permute-start(bf16[608,512]{1,0:T(8,128)(2,1)} %get-tuple-element.44), channel_id=1, source_target_pairs={{0,8},{2,10},{4,12},{6,14},{1,9},{3,11},{5,13},{7,15}} | collective-permute-start | bytes 1867784 | tf_op jit(solution)/shard_map/ppermute | solution.py:25
  24.3 26.0 %collective-permute-start.8 = (bf16[608,512]{1,0:T(8,128)(2,1)S(1)}, bf16[608,512]{1,0:T(8,128)(2,1)}, u32[]{:S(2)}, u32[]{:S(2)}) collective-permute-start(bf16[608,512]{1,0:T(8,128)(2,1)S(1)} %get-tuple-element.45), channel_id=1, source_target_pairs={{0,16},{2,18},{4,20},{6,22},{1,17},{3,19},{5,21},{7,23}} | collective-permute-start | bytes 1867784 | tf_op jit(solution)/shard_map/ppermute | solution.py:25
  30.4 19.8 %collective-permute-start.9 = (bf16[608,512]{1,0:T(8,128)(2,1)S(1)}, bf16[608,512]{1,0:T(8,128)(2,1)}, u32[]{:S(2)}, u32[]{:S(2)}) collective-permute-start(bf16[608,512]{1,0:T(8,128)(2,1)S(1)} %get-tuple-element.46), channel_id=1, source_target_pairs={{0,24},{2,26},{4,28},{6,30},{1,25},{3,27},{5,29},{7,31}} | collective-permute-start | bytes 1867784 | tf_op jit(solution)/shard_map/ppermute | solution.py:25
  53.3 12.0 %collective-permute-start.12 = (bf16[896,128]{1,0:T(8,128)(2,1)S(1)}, bf16[896,128]{1,0:T(8,128)(2,1)S(1)}, u32[]{:S(2)}, u32[]{:S(2)}) collective-permute-start(bf16[896,128]{1,0:T(8,128)(2,1)S(1)} %get-tuple-element.104), channel_id=1, source_target_pairs={{0,96},{8,104},{16,112},{24,120},{2,98},{10,106},{18,114},{26,122}... | collective-permute-start | bytes 688136 | tf_op jit(solution)/shard_map/ppermute | solution.py:25
  54.6 10.7 %collective-permute-start.10 = (bf16[896,128]{1,0:T(8,128)(2,1)S(1)}, bf16[896,128]{1,0:T(8,128)(2,1)S(1)}, u32[]{:S(2)}, u32[]{:S(2)}) collective-permute-start(bf16[896,128]{1,0:T(8,128)(2,1)S(1)} %get-tuple-element.94), channel_id=1, source_target_pairs={{0,64},{8,72},{16,80},{24,88},{2,66},{10,74},{18,82},{26,90},{4,68... | collective-permute-start | bytes 688136 | tf_op jit(solution)/shard_map/ppermute | solution.py:25
  56.2 9.3 %collective-permute-start.5 = (bf16[896,128]{1,0:T(8,128)(2,1)S(1)}, bf16[896,128]{1,0:T(8,128)(2,1)S(1)}, u32[]{:S(2)}, u32[]{:S(2)}) collective-permute-start(bf16[896,128]{1,0:T(8,128)(2,1)S(1)} %get-tuple-element.86), channel_id=1, source_target_pairs={{0,8},{32,40},{64,72},{96,104},{2,10},{34,42},{66,74},{98,106},{4,... | collective-permute-start | bytes 688136 | tf_op jit(solution)/shard_map/ppermute | solution.py:25
  59.4 9.5 %collective-permute-start.4 = (bf16[896,128]{1,0:T(8,128)(2,1)S(1)}, bf16[896,128]{1,0:T(8,128)(2,1)S(1)}, u32[]{:S(2)}, u32[]{:S(2)}) collective-permute-start(bf16[896,128]{1,0:T(8,128)(2,1)S(1)} %get-tuple-element.77), channel_id=1, source_target_pairs={{0,16},{32,48},{64,80},{96,112},{2,18},{34,50},{66,82},{98,114},{4... | collective-permute-start | bytes 688136 | tf_op jit(solution)/shard_map/ppermute | solution.py:25
  70.2 9.9 %collective-permute-start.17 = (bf16[512,128]{1,0:T(8,128)(2,1)S(1)}, bf16[512,128]{1,0:T(8,128)(2,1)S(1)}, u32[]{:S(2)}, u32[]{:S(2)}) collective-permute-start(bf16[512,128]{1,0:T(8,128)(2,1)S(1)} %shard_map.38), channel_id=1, source_target_pairs={{0,4},{8,12},{16,20},{24,28},{32,36},{40,44},{48,52},{56,60},{64,6... | collective-permute-start | bytes 393224 | tf_op jit(solution)/shard_map/ppermute | solution.py:25
  70.8 9.2 %collective-permute-start.16 = (bf16[512,128]{1,0:T(8,128)(2,1)S(1)}, bf16[512,128]{1,0:T(8,128)(2,1)S(1)}, u32[]{:S(2)}, u32[]{:S(2)}) collective-permute-start(bf16[512,128]{1,0:T(8,128)(2,1)S(1)} %shard_map.38), channel_id=1, source_target_pairs={{0,6},{8,14},{16,22},{24,30},{32,38},{40,46},{48,54},{56,62},{64,7... | collective-permute-start | bytes 393224 | tf_op jit(solution)/shard_map/ppermute | solution.py:25
  121.7 37.7 %collective-permute-start = (bf16[2,512,1024]{2,1,0:T(8,128)(2,1)}, bf16[2,512,1024]{2,1,0:T(8,128)(2,1)}, u32[]{:S(2)}, u32[]{:S(2)}) collective-permute-start(bf16[2,512,1024]{2,1,0:T(8,128)(2,1)} %reshape.179.mine_ref), channel_id=1, source_target_pairs={{0,1},{1,0},{2,3},{3,2},{4,5},{5,4},{6,7},{7,6},{8,9},{9,8},{10,11... | collective-permute-start | bytes 6291464 | tf_op jit(solution)/shard_map/ppermute | solution.py:291
  124.6 13.1 %collective-permute-start.40 = (bf16[1,384,128]{2,1,0:T(8,128)(2,1)S(1)}, bf16[1,384,128]{2,1,0:T(8,128)(2,1)S(1)}, u32[]{:S(2)}, u32[]{:S(2)}) collective-permute-start(bf16[1,384,128]{2,1,0:T(8,128)(2,1)S(1)} %slice_bitcast_fusion), channel_id=1, source_target_pairs={{0,24},{8,16},{16,8},{24,0},{1,25},{9,17},{17,9},{25,1},{2,26},{10... | collective-permute-start | bytes 294920 | tf_op jit(solution)/shard_map/ppermute | solution.py:33
  129.9 10.0 %collective-permute-start.32 = (bf16[2,384,128]{2,1,0:T(8,128)(2,1)S(1)}, bf16[2,384,128]{2,1,0:T(8,128)(2,1)S(1)}, u32[]{:S(2)}, u32[]{:S(2)}) collective-permute-start(bf16[2,384,128]{2,1,0:T(8,128)(2,1)S(1)} %pad_maximum_fusion.13), channel_id=1, source_target_pairs={{0,32},{32,0},{64,96},{96,64},{1,33},{33,1},{65,97},{97,65},{2,34}... | collective-permute-start | bytes 589832 | tf_op jit(solution)/shard_map/ppermute | solution.py:33
  136.2 10.7 %collective-permute-start.38 = (bf16[4,384,128]{2,1,0:T(8,128)(2,1)S(1)}, bf16[4,384,128]{2,1,0:T(8,128)(2,1)}, u32[]{:S(2)}, u32[]{:S(2)}) collective-permute-start(bf16[4,384,128]{2,1,0:T(8,128)(2,1)S(1)} %pad_maximum_fusion.8), channel_id=1, source_target_pairs={{0,32},{32,0},{64,96},{96,64},{1,33},{33,1},{65,97},{97,65},{2,34}... | collective-permute-start | bytes 1179656 | tf_op jit(solution)/shard_map/ppermute | solution.py:33
  138.1 14.0 %collective-permute-start.28 = (bf16[4,384,128]{2,1,0:T(8,128)(2,1)S(1)}, bf16[4,384,128]{2,1,0:T(8,128)(2,1)S(1)}, u32[]{:S(2)}, u32[]{:S(2)}) collective-permute-start(bf16[4,384,128]{2,1,0:T(8,128)(2,1)S(1)} %pad_maximum_fusion.6), channel_id=1, source_target_pairs={{0,8},{8,0},{16,24},{24,16},{1,9},{9,1},{17,25},{25,17},{2,10},{10... | collective-permute-start | bytes 1179656 | tf_op jit(solution)/shard_map/ppermute | solution.py:33
  140.0 12.7 %collective-permute-start.33 = (bf16[4,384,128]{2,1,0:T(8,128)(2,1)S(1)}, bf16[4,384,128]{2,1,0:T(8,128)(2,1)S(1)}, u32[]{:S(2)}, u32[]{:S(2)}) collective-permute-start(bf16[4,384,128]{2,1,0:T(8,128)(2,1)S(1)} %pad_maximum_fusion.7), channel_id=1, source_target_pairs={{0,24},{8,16},{16,8},{24,0},{1,25},{9,17},{17,9},{25,1},{2,26},{10... | collective-permute-start | bytes 1179656 | tf_op jit(solution)/shard_map/ppermute | solution.py:33
  145.7 13.3 %collective-permute-start.42 = (bf16[4,384,128]{2,1,0:T(8,128)(2,1)S(1)}, bf16[4,384,128]{2,1,0:T(8,128)(2,1)S(1)}, u32[]{:S(2)}, u32[]{:S(2)}) collective-permute-start(bf16[4,384,128]{2,1,0:T(8,128)(2,1)S(1)} %pad_maximum_fusion.9), channel_id=1, source_target_pairs={{0,96},{32,64},{64,32},{96,0},{1,97},{33,65},{65,33},{97,1},{2,98}... | collective-permute-start | bytes 1179656 | tf_op jit(solution)/shard_map/ppermute | solution.py:33
  148.0 23.3 %collective-permute-start.39 = (bf16[8,384,128]{2,1,0:T(8,128)(2,1)S(1)}, bf16[8,384,128]{2,1,0:T(8,128)(2,1)}, u32[]{:S(2)}, u32[]{:S(2)}) collective-permute-start(bf16[8,384,128]{2,1,0:T(8,128)(2,1)S(1)} %pad_maximum_fusion.2.rest_4_.rest_5_), channel_id=1, source_target_pairs={{0,96},{32,64},{64,32},{96,0},{1,97},{33,65},{65,33},{97,1},{2,98}... | collective-permute-start | bytes 2359304 | tf_op jit(solution)/shard_map/ppermute | solution.py:33
  152.2 19.1 %collective-permute-start.29 = (bf16[8,384,128]{2,1,0:T(8,128)(2,1)S(1)}, bf16[8,384,128]{2,1,0:T(8,128)(2,1)}, u32[]{:S(2)}, u32[]{:S(2)}) collective-permute-start(bf16[8,384,128]{2,1,0:T(8,128)(2,1)S(1)} %pad_maximum_fusion.rest_0_.rest_1_), channel_id=1, source_target_pairs={{0,24},{8,16},{16,8},{24,0},{1,25},{9,17},{17,9},{25,1},{2,26},{10... | collective-permute-start | bytes 2359304 | tf_op jit(solution)/shard_map/ppermute | solution.py:33
  152.8 18.5 %collective-permute-start.34 = (bf16[8,384,128]{2,1,0:T(8,128)(2,1)S(1)}, bf16[8,384,128]{2,1,0:T(8,128)(2,1)}, u32[]{:S(2)}, u32[]{:S(2)}) collective-permute-start(bf16[8,384,128]{2,1,0:T(8,128)(2,1)S(1)} %pad_maximum_fusion.1.rest_2_.rest_3_), channel_id=1, source_target_pairs={{0,8},{8,0},{16,24},{24,16},{1,9},{9,1},{17,25},{25,17},{2,10},{10... | collective-permute-start | bytes 2359304 | tf_op jit(solution)/shard_map/ppermute | solution.py:33
  159.1 12.2 %collective-permute-start.43 = (bf16[8,384,128]{2,1,0:T(8,128)(2,1)S(1)}, bf16[8,384,128]{2,1,0:T(8,128)(2,1)}, u32[]{:S(2)}, u32[]{:S(2)}) collective-permute-start(bf16[8,384,128]{2,1,0:T(8,128)(2,1)S(1)} %pad_maximum_fusion.3.rest_6_.rest_7_), channel_id=1, source_target_pairs={{0,32},{32,0},{64,96},{96,64},{1,33},{33,1},{65,97},{97,65},{2,34}... | collective-permute-start | bytes 2359304 | tf_op jit(solution)/shard_map/ppermute | solution.py:33
  (21 other events, 139.5 us)
Sparse Core Ops, SparseCore 0:
  80.9 47.7 all-gather.2

commit v14 on v13

--- a/solution.py
+++ b/solution.py
@@ -229,7 +229,7 @@
     slabs = loads(rhs, factor[0].reshape(1, 512, 1024))
     outward = {
         (p, d): permute(slabs[4 * p + d], [((i, 0, 0), (i, 0, d) if p else (i, d, 0)) for i in range(4)])
-        for p, d in ((0, 3), (0, 1), (1, 1), (0, 2), (1, 2), (1, 3))
+        for p, d in ((0, 3), (0, 2), (1, 2), (0, 1), (1, 1), (1, 3))
     }
     hold_a = jnp.where(owner, slabs[0], zero) + outward[0, 1] + outward[0, 2] + outward[0, 3]
     own_b, hold_a = lax.optimization_barrier((slabs[4], hold_a))

time: 197 us -> 197 us (level)
  no operation moved by 1% of the time
where the time goes in v14:
time: 197 us
  waiting for transfers between devices  78.8 us (40%)
  starting transfers between devices  60.6 us (31%)
  Pallas kernels  28.5 us (14%)
  between operations  13.9 us (7%)
  other arithmetic  7.46 us (4%)
  local copies, waits for them, and re-layouts  7.3 us (4%)
    ppermute x20, waiting for transfers between devices, swap(): return lax.ppermute(value, axis, [(i, i ^ flip) for i in range(4)])  42 us
    ppermute x21, starting transfers between devices, permute(): return lax.ppermute(value, ROWS, [(flat(*a), flat(*b)) for a, b in moves])  38.2 us
    ppermute x21, waiting for transfers between devices, permute(): return lax.ppermute(value, ROWS, [(flat(*a), flat(*b)) for a, b in moves])  35.1 us
    ppermute x20, starting transfers between devices, swap(): return lax.ppermute(value, axis, [(i, i ^ flip) for i in range(4)])  22.2 us
    pallas_call x1, Pallas kernels, update(): pl.pallas_call(update_kernel, grid_spec=pltpu.PrefetchScalarGridSpec(num_...  18.5 us
    pallas_call x4, Pallas kernels, step(): pl.pallas_call(kernel, grid_spec=pltpu.PrefetchScalarGridSpec(num_scalar_...  6.36 us
    reshape x1, local copies, waits for them, and re-layouts, local(): flat_factor = factor.reshape(2, 512, 1024)  4.46 us
  transfers between devices with their start and end apart: 45, of which 20 were waited for; matrix products, arithmetic and copies ran while one was open for 5% of the time, Pallas kernels for 3%

profile of v14, /device:TPU:6, one launch (start us, length us, event | category | flops | bytes accessed | tf_op | source)
XLA Modules:
  0.0 196.6 jit_solution(10975847774286340304)
XLA Ops:
  8.9 3.7 %shard_map.37 = (bf16[608,512]{1,0:T(8,128)(2,1)S(1)}, bf16[608,512]{1,0:T(8,128)(2,1)S(1)}, bf16[608,512]{1,0:T(8,128)(2,1)}, bf16[608,512]{1,0:T(8,128)(2,1)},...) custom-call(f32[2,512,2048]{2,1,0:T(8,128)} %rhs_ref.3, ...), custom_call_target="tpu_custom_call" | custom-call | tf_op jit(solution)/shard_map/pallas_call | solution.py:88
  12.6 4.3 %collective-permute-start.1 = (bf16[608,512]{1,0:T(8,128)(2,1)S(1)}, bf16[608,512]{1,0:T(8,128)(2,1)}, u32[]{:S(2)}, u32[]{:S(2)}) collective-permute-start(bf16[608,512]{1,0:T(8,128)(2,1)S(1)} %get-tuple-element.39), channel_id=1, source_target_pairs={{0,32},{2,34},{4,36},{6,38},{1,33},{3,35},{5,37},{7,39}} | collective-permute-start | bytes 1867784 | tf_op jit(solution)/shard_map/ppermute | solution.py:25
  16.9 3.1 %collective-permute-start.2 = (bf16[608,512]{1,0:T(8,128)(2,1)}, bf16[608,512]{1,0:T(8,128)(2,1)}, u32[]{:S(2)}, u32[]{:S(2)}) collective-permute-start(bf16[608,512]{1,0:T(8,128)(2,1)} %get-tuple-element.40), channel_id=1, source_target_pairs={{0,64},{2,66},{4,68},{6,70},{1,65},{3,67},{5,69},{7,71}} | collective-permute-start | bytes 1867784 | tf_op jit(solution)/shard_map/ppermute | solution.py:25
  20.0 2.1 %collective-permute-start.3 = (bf16[608,512]{1,0:T(8,128)(2,1)}, bf16[608,512]{1,0:T(8,128)(2,1)}, u32[]{:S(2)}, u32[]{:S(2)}) collective-permute-start(bf16[608,512]{1,0:T(8,128)(2,1)} %get-tuple-element.41), channel_id=1, source_target_pairs={{0,96},{2,98},{4,100},{6,102},{1,97},{3,99},{5,101},{7,103}} | collective-permute-start | bytes 1867784 | tf_op jit(solution)/shard_map/ppermute | solution.py:25
  22.1 2.1 %collective-permute-start.7 = (bf16[608,512]{1,0:T(8,128)(2,1)}, bf16[608,512]{1,0:T(8,128)(2,1)}, u32[]{:S(2)}, u32[]{:S(2)}) collective-permute-start(bf16[608,512]{1,0:T(8,128)(2,1)} %get-tuple-element.44), channel_id=1, source_target_pairs={{0,8},{2,10},{4,12},{6,14},{1,9},{3,11},{5,13},{7,15}} | collective-permute-start | bytes 1867784 | tf_op jit(solution)/shard_map/ppermute | solution.py:25
  26.4 4.1 %collective-permute-done.1 = bf16[608,512]{1,0:T(8,128)(2,1)} collective-permute-done((bf16[608,512]{1,0:T(8,128)(2,1)S(1)}, bf16[608,512]{1,0:T(8,128)(2,1)}, u32[]{:S(2)}, u32[]{:S(2)}) %collective-permute-start.1) | collective-permute-done | bytes 622624 | tf_op jit(solution)/shard_map/ppermute | solution.py:25
  34.0 8.7 %collective-permute-done.2 = bf16[608,512]{1,0:T(8,128)(2,1)} collective-permute-done((bf16[608,512]{1,0:T(8,128)(2,1)}, bf16[608,512]{1,0:T(8,128)(2,1)}, u32[]{:S(2)}, u32[]{:S(2)}) %collective-permute-start.2) | collective-permute-done | bytes 622624 | tf_op jit(solution)/shard_map/ppermute | solution.py:25
  44.3 5.9 %collective-permute-done.8 = bf16[608,512]{1,0:T(8,128)(2,1)} collective-permute-done((bf16[608,512]{1,0:T(8,128)(2,1)S(1)}, bf16[608,512]{1,0:T(8,128)(2,1)}, u32[]{:S(2)}, u32[]{:S(2)}) %collective-permute-start.8) | collective-permute-done | bytes 622624 | tf_op jit(solution)/shard_map/ppermute | solution.py:25
  59.4 6.0 %collective-permute-start.4 = (bf16[896,128]{1,0:T(8,128)(2,1)S(1)}, bf16[896,128]{1,0:T(8,128)(2,1)S(1)}, u32[]{:S(2)}, u32[]{:S(2)}) collective-permute-start(bf16[896,128]{1,0:T(8,128)(2,1)S(1)} %get-tuple-element.77), channel_id=1, source_target_pairs={{0,16},{32,48},{64,80},{96,112},{2,18},{34,50},{66,82},{98,114},{4... | collective-permute-start | bytes 688136 | tf_op jit(solution)/shard_map/ppermute | solution.py:25
  65.6 3.3 %collective-permute-done.4 = bf16[896,128]{1,0:T(8,128)(2,1)S(1)} collective-permute-done((bf16[896,128]{1,0:T(8,128)(2,1)S(1)}, bf16[896,128]{1,0:T(8,128)(2,1)S(1)}, u32[]{:S(2)}, u32[]{:S(2)}) %collective-permute-start.4) | collective-permute-done | bytes 229408 | tf_op jit(solution)/shard_map/ppermute | solution.py:25
  72.9 2.6 %collective-permute-start.13 = (bf16[384,128]{1,0:T(8,128)(2,1)S(1)}, bf16[384,128]{1,0:T(8,128)(2,1)S(1)}, u32[]{:S(2)}, u32[]{:S(2)}) collective-permute-start(bf16[384,128]{1,0:T(8,128)(2,1)S(1)} %slice.120), channel_id=1, source_target_pairs={{0,32},{32,0},{64,96},{96,64},{1,33},{33,1},{65,97},{97,65},{2,34}... | collective-permute-start | bytes 294920 | tf_op jit(solution)/shard_map/ppermute | solution.py:33
  75.4 2.6 %collective-permute-done.13 = bf16[384,128]{1,0:T(8,128)(2,1)S(1)} collective-permute-done((bf16[384,128]{1,0:T(8,128)(2,1)S(1)}, bf16[384,128]{1,0:T(8,128)(2,1)S(1)}, u32[]{:S(2)}, u32[]{:S(2)}) %collective-permute-start.13) | collective-permute-done | bytes 98336 | tf_op jit(solution)/shard_map/ppermute | solution.py:33
  80.8 2.6 %collective-permute-start.19 = (bf16[2,384,128]{2,1,0:T(8,128)(2,1)S(1)}, bf16[2,384,128]{2,1,0:T(8,128)(2,1)S(1)}, u32[]{:S(2)}, u32[]{:S(2)}) collective-permute-start(bf16[2,384,128]{2,1,0:T(8,128)(2,1)S(1)} %pad_maximum_fusion.11), channel_id=1, source_target_pairs={{0,24},{8,16},{16,8},{24,0},{1,25},{9,17},{17,9},{25,1},{2,26},{10... | collective-permute-start | bytes 589832 | tf_op jit(solution)/shard_map/ppermute | solution.py:33
  83.5 4.2 %collective-permute-done.19 = bf16[2,384,128]{2,1,0:T(8,128)(2,1)S(1)} collective-permute-done((bf16[2,384,128]{2,1,0:T(8,128)(2,1)S(1)}, bf16[2,384,128]{2,1,0:T(8,128)(2,1)S(1)}, u32[]{:S(2)}, u32[]{:S(2)}) %collective-permute-start.19) | collective-permute-done | bytes 196640 | tf_op jit(solution)/shard_map/ppermute | solution.py:33
  87.9 2.5 %collective-permute-done.18 = bf16[2,384,128]{2,1,0:T(8,128)(2,1)S(1)} collective-permute-done((bf16[2,384,128]{2,1,0:T(8,128)(2,1)S(1)}, bf16[2,384,128]{2,1,0:T(8,128)(2,1)S(1)}, u32[]{:S(2)}, u32[]{:S(2)}) %collective-permute-start.18) | collective-permute-done | bytes 196640 | tf_op jit(solution)/shard_map/ppermute | solution.py:33
  95.9 7.0 %collective-permute-done.23.refs_9_ = bf16[512,128]{1,0:T(8,128)(2,1)S(1)} collective-permute-done((bf16[512,128]{1,0:T(8,128)(2,1)S(1)}, bf16[512,128]{1,0:T(8,128)(2,1)S(1)}, u32[]{:S(2)}, u32[]{:S(2)}) %collective-permute-start.23) | collective-permute-done | bytes 131104 | tf_op jit(solution)/shard_map/ppermute | solution.py:25
  105.8 5.6 %collective-permute-done.24.refs_8_ = bf16[512,128]{1,0:T(8,128)(2,1)S(1)} collective-permute-done((bf16[512,128]{1,0:T(8,128)(2,1)S(1)}, bf16[512,128]{1,0:T(8,128)(2,1)S(1)}, u32[]{:S(2)}, u32[]{:S(2)}) %collective-permute-start.24) | collective-permute-done | bytes 131104 | tf_op jit(solution)/shard_map/ppermute | solution.py:25
  117.2 4.5 %reshape.179.mine_ref = bf16[2,512,1024]{2,1,0:T(8,128)(2,1)} reshape(bf16[2,512,4,256]{3,2,1,0:T(4,128)(2,1)} %param.4) | data formatting | bytes 4194304 | tf_op jit(solution)/shard_map/reshape | solution.py:290
  125.6 2.3 %collective-permute-done.36 = bf16[1,384,128]{2,1,0:T(8,128)(2,1)S(1)} collective-permute-done((bf16[1,384,128]{2,1,0:T(8,128)(2,1)S(1)}, bf16[1,384,128]{2,1,0:T(8,128)(2,1)S(1)}, u32[]{:S(2)}, u32[]{:S(2)}) %collective-permute-start.36) | collective-permute-done | bytes 98336 | tf_op jit(solution)/shard_map/ppermute | solution.py:33
  132.4 3.7 %collective-permute-done.37 = bf16[2,384,128]{2,1,0:T(8,128)(2,1)S(1)} collective-permute-done((bf16[2,384,128]{2,1,0:T(8,128)(2,1)S(1)}, bf16[2,384,128]{2,1,0:T(8,128)(2,1)S(1)}, u32[]{:S(2)}, u32[]{:S(2)}) %collective-permute-start.37) | collective-permute-done | bytes 196640 | tf_op jit(solution)/shard_map/ppermute | solution.py:33
  141.2 4.4 %collective-permute-done.41 = bf16[2,384,128]{2,1,0:T(8,128)(2,1)S(1)} collective-permute-done((bf16[2,384,128]{2,1,0:T(8,128)(2,1)S(1)}, bf16[2,384,128]{2,1,0:T(8,128)(2,1)S(1)}, u32[]{:S(2)}, u32[]{:S(2)}) %collective-permute-start.41) | collective-permute-done | bytes 196640 | tf_op jit(solution)/shard_map/ppermute | solution.py:33
  153.2 5.8 %collective-permute-done.42 = bf16[4,384,128]{2,1,0:T(8,128)(2,1)S(1)} collective-permute-done((bf16[4,384,128]{2,1,0:T(8,128)(2,1)S(1)}, bf16[4,384,128]{2,1,0:T(8,128)(2,1)S(1)}, u32[]{:S(2)}, u32[]{:S(2)}) %collective-permute-start.42) | collective-permute-done | bytes 393248 | tf_op jit(solution)/shard_map/ppermute | solution.py:33
  159.4 11.9 %collective-permute-done.39.rest_12_.rest_13_ = bf16[8,384,128]{2,1,0:T(8,128)(2,1)} collective-permute-done((bf16[8,384,128]{2,1,0:T(8,128)(2,1)S(1)}, bf16[8,384,128]{2,1,0:T(8,128)(2,1)}, u32[]{:S(2)}, u32[]{:S(2)}) %collective-permute-start.39) | collective-permute-done | bytes 786464 | tf_op jit(solution)/shard_map/ppermute | solution.py:33
  171.3 18.5 %shard_map.42 = f32[2,512,2048]{2,1,0:T(8,128)} custom-call(s32[66]{0:T(128)S(1)} %pad_add_fusion.1.scalars, bf16[2,512,1024]{2,1,0:T(8,128)(2,1)} %reshape.179.mine_ref, bf16[2,512,1024]{2,1,0:T(8,128)(2,1)} %collective-permute-done.other_ref, f32[2,512,2048]{2,1,0:T(8,128)} %rhs_ref.3, bf16[16,512,128]{2,1,0:T(8,128)(2,1)} %bitcast.27, ...), custom_call_target="tpu_custom_call" | custom-call | tf_op jit(solution)/shard_map/pallas_call | solution.py:203
  (130 shorter events, 61.2 us)
Async XLA Ops:
  6.5 131.1 %all-gather.3.cloned.1.call-start = ((), (), s32[]{:S(2)}) async-start(), calls=%async_computation | async-start | bytes 2228224 | tf_op jit(solution)/shard_map/all_gather | solution.py:274
  12.6 17.9 %collective-permute-start.1 = (bf16[608,512]{1,0:T(8,128)(2,1)S(1)}, bf16[608,512]{1,0:T(8,128)(2,1)}, u32[]{:S(2)}, u32[]{:S(2)}) collective-permute-start(bf16[608,512]{1,0:T(8,128)(2,1)S(1)} %get-tuple-element.39), channel_id=1, source_target_pairs={{0,32},{2,34},{4,36},{6,38},{1,33},{3,35},{5,37},{7,39}} | collective-permute-start | bytes 1867784 | tf_op jit(solution)/shard_map/ppermute | solution.py:25
  16.9 25.9 %collective-permute-start.2 = (bf16[608,512]{1,0:T(8,128)(2,1)}, bf16[608,512]{1,0:T(8,128)(2,1)}, u32[]{:S(2)}, u32[]{:S(2)}) collective-permute-start(bf16[608,512]{1,0:T(8,128)(2,1)} %get-tuple-element.40), channel_id=1, source_target_pairs={{0,64},{2,66},{4,68},{6,70},{1,65},{3,67},{5,69},{7,71}} | collective-permute-start | bytes 1867784 | tf_op jit(solution)/shard_map/ppermute | solution.py:25
  20.0 22.7 %collective-permute-start.3 = (bf16[608,512]{1,0:T(8,128)(2,1)}, bf16[608,512]{1,0:T(8,128)(2,1)}, u32[]{:S(2)}, u32[]{:S(2)}) collective-permute-start(bf16[608,512]{1,0:T(8,128)(2,1)} %get-tuple-element.41), channel_id=1, source_target_pairs={{0,96},{2,98},{4,100},{6,102},{1,97},{3,99},{5,101},{7,103}} | collective-permute-start | bytes 1867784 | tf_op jit(solution)/shard_map/ppermute | solution.py:25
  22.1 22.2 %collective-permute-start.7 = (bf16[608,512]{1,0:T(8,128)(2,1)}, bf16[608,512]{1,0:T(8,128)(2,1)}, u32[]{:S(2)}, u32[]{:S(2)}) collective-permute-start(bf16[608,512]{1,0:T(8,128)(2,1)} %get-tuple-element.44), channel_id=1, source_target_pairs={{0,8},{2,10},{4,12},{6,14},{1,9},{3,11},{5,13},{7,15}} | collective-permute-start | bytes 1867784 | tf_op jit(solution)/shard_map/ppermute | solution.py:25
  24.3 26.0 %collective-permute-start.8 = (bf16[608,512]{1,0:T(8,128)(2,1)S(1)}, bf16[608,512]{1,0:T(8,128)(2,1)}, u32[]{:S(2)}, u32[]{:S(2)}) collective-permute-start(bf16[608,512]{1,0:T(8,128)(2,1)S(1)} %get-tuple-element.45), channel_id=1, source_target_pairs={{0,16},{2,18},{4,20},{6,22},{1,17},{3,19},{5,21},{7,23}} | collective-permute-start | bytes 1867784 | tf_op jit(solution)/shard_map/ppermute | solution.py:25
  30.4 19.8 %collective-permute-start.9 = (bf16[608,512]{1,0:T(8,128)(2,1)S(1)}, bf16[608,512]{1,0:T(8,128)(2,1)}, u32[]{:S(2)}, u32[]{:S(2)}) collective-permute-start(bf16[608,512]{1,0:T(8,128)(2,1)S(1)} %get-tuple-element.46), channel_id=1, source_target_pairs={{0,24},{2,26},{4,28},{6,30},{1,25},{3,27},{5,29},{7,31}} | collective-permute-start | bytes 1867784 | tf_op jit(solution)/shard_map/ppermute | solution.py:25
  53.3 12.0 %collective-permute-start.12 = (bf16[896,128]{1,0:T(8,128)(2,1)S(1)}, bf16[896,128]{1,0:T(8,128)(2,1)S(1)}, u32[]{:S(2)}, u32[]{:S(2)}) collective-permute-start(bf16[896,128]{1,0:T(8,128)(2,1)S(1)} %get-tuple-element.104), channel_id=1, source_target_pairs={{0,96},{8,104},{16,112},{24,120},{2,98},{10,106},{18,114},{26,122}... | collective-permute-start | bytes 688136 | tf_op jit(solution)/shard_map/ppermute | solution.py:25
  54.6 10.7 %collective-permute-start.10 = (bf16[896,128]{1,0:T(8,128)(2,1)S(1)}, bf16[896,128]{1,0:T(8,128)(2,1)S(1)}, u32[]{:S(2)}, u32[]{:S(2)}) collective-permute-start(bf16[896,128]{1,0:T(8,128)(2,1)S(1)} %get-tuple-element.94), channel_id=1, source_target_pairs={{0,64},{8,72},{16,80},{24,88},{2,66},{10,74},{18,82},{26,90},{4,68... | collective-permute-start | bytes 688136 | tf_op jit(solution)/shard_map/ppermute | solution.py:25
  56.2 9.3 %collective-permute-start.5 = (bf16[896,128]{1,0:T(8,128)(2,1)S(1)}, bf16[896,128]{1,0:T(8,128)(2,1)S(1)}, u32[]{:S(2)}, u32[]{:S(2)}) collective-permute-start(bf16[896,128]{1,0:T(8,128)(2,1)S(1)} %get-tuple-element.86), channel_id=1, source_target_pairs={{0,8},{32,40},{64,72},{96,104},{2,10},{34,42},{66,74},{98,106},{4,... | collective-permute-start | bytes 688136 | tf_op jit(solution)/shard_map/ppermute | solution.py:25
  59.4 9.5 %collective-permute-start.4 = (bf16[896,128]{1,0:T(8,128)(2,1)S(1)}, bf16[896,128]{1,0:T(8,128)(2,1)S(1)}, u32[]{:S(2)}, u32[]{:S(2)}) collective-permute-start(bf16[896,128]{1,0:T(8,128)(2,1)S(1)} %get-tuple-element.77), channel_id=1, source_target_pairs={{0,16},{32,48},{64,80},{96,112},{2,18},{34,50},{66,82},{98,114},{4... | collective-permute-start | bytes 688136 | tf_op jit(solution)/shard_map/ppermute | solution.py:25
  70.2 9.9 %collective-permute-start.17 = (bf16[512,128]{1,0:T(8,128)(2,1)S(1)}, bf16[512,128]{1,0:T(8,128)(2,1)S(1)}, u32[]{:S(2)}, u32[]{:S(2)}) collective-permute-start(bf16[512,128]{1,0:T(8,128)(2,1)S(1)} %shard_map.38), channel_id=1, source_target_pairs={{0,4},{8,12},{16,20},{24,28},{32,36},{40,44},{48,52},{56,60},{64,6... | collective-permute-start | bytes 393224 | tf_op jit(solution)/shard_map/ppermute | solution.py:25
  70.8 9.2 %collective-permute-start.16 = (bf16[512,128]{1,0:T(8,128)(2,1)S(1)}, bf16[512,128]{1,0:T(8,128)(2,1)S(1)}, u32[]{:S(2)}, u32[]{:S(2)}) collective-permute-start(bf16[512,128]{1,0:T(8,128)(2,1)S(1)} %shard_map.38), channel_id=1, source_target_pairs={{0,6},{8,14},{16,22},{24,30},{32,38},{40,46},{48,54},{56,62},{64,7... | collective-permute-start | bytes 393224 | tf_op jit(solution)/shard_map/ppermute | solution.py:25
  121.7 37.7 %collective-permute-start = (bf16[2,512,1024]{2,1,0:T(8,128)(2,1)}, bf16[2,512,1024]{2,1,0:T(8,128)(2,1)}, u32[]{:S(2)}, u32[]{:S(2)}) collective-permute-start(bf16[2,512,1024]{2,1,0:T(8,128)(2,1)} %reshape.179.mine_ref), channel_id=1, source_target_pairs={{0,1},{1,0},{2,3},{3,2},{4,5},{5,4},{6,7},{7,6},{8,9},{9,8},{10,11... | collective-permute-start | bytes 6291464 | tf_op jit(solution)/shard_map/ppermute | solution.py:291
  124.6 13.1 %collective-permute-start.40 = (bf16[1,384,128]{2,1,0:T(8,128)(2,1)S(1)}, bf16[1,384,128]{2,1,0:T(8,128)(2,1)S(1)}, u32[]{:S(2)}, u32[]{:S(2)}) collective-permute-start(bf16[1,384,128]{2,1,0:T(8,128)(2,1)S(1)} %slice_bitcast_fusion), channel_id=1, source_target_pairs={{0,24},{8,16},{16,8},{24,0},{1,25},{9,17},{17,9},{25,1},{2,26},{10... | collective-permute-start | bytes 294920 | tf_op jit(solution)/shard_map/ppermute | solution.py:33
  129.9 10.0 %collective-permute-start.32 = (bf16[2,384,128]{2,1,0:T(8,128)(2,1)S(1)}, bf16[2,384,128]{2,1,0:T(8,128)(2,1)S(1)}, u32[]{:S(2)}, u32[]{:S(2)}) collective-permute-start(bf16[2,384,128]{2,1,0:T(8,128)(2,1)S(1)} %pad_maximum_fusion.13), channel_id=1, source_target_pairs={{0,32},{32,0},{64,96},{96,64},{1,33},{33,1},{65,97},{97,65},{2,34}... | collective-permute-start | bytes 589832 | tf_op jit(solution)/shard_map/ppermute | solution.py:33
  136.2 10.7 %collective-permute-start.38 = (bf16[4,384,128]{2,1,0:T(8,128)(2,1)S(1)}, bf16[4,384,128]{2,1,0:T(8,128)(2,1)}, u32[]{:S(2)}, u32[]{:S(2)}) collective-permute-start(bf16[4,384,128]{2,1,0:T(8,128)(2,1)S(1)} %pad_maximum_fusion.8), channel_id=1, source_target_pairs={{0,32},{32,0},{64,96},{96,64},{1,33},{33,1},{65,97},{97,65},{2,34}... | collective-permute-start | bytes 1179656 | tf_op jit(solution)/shard_map/ppermute | solution.py:33
  138.1 14.0 %collective-permute-start.28 = (bf16[4,384,128]{2,1,0:T(8,128)(2,1)S(1)}, bf16[4,384,128]{2,1,0:T(8,128)(2,1)S(1)}, u32[]{:S(2)}, u32[]{:S(2)}) collective-permute-start(bf16[4,384,128]{2,1,0:T(8,128)(2,1)S(1)} %pad_maximum_fusion.6), channel_id=1, source_target_pairs={{0,8},{8,0},{16,24},{24,16},{1,9},{9,1},{17,25},{25,17},{2,10},{10... | collective-permute-start | bytes 1179656 | tf_op jit(solution)/shard_map/ppermute | solution.py:33
  140.0 12.7 %collective-permute-start.33 = (bf16[4,384,128]{2,1,0:T(8,128)(2,1)S(1)}, bf16[4,384,128]{2,1,0:T(8,128)(2,1)S(1)}, u32[]{:S(2)}, u32[]{:S(2)}) collective-permute-start(bf16[4,384,128]{2,1,0:T(8,128)(2,1)S(1)} %pad_maximum_fusion.7), channel_id=1, source_target_pairs={{0,24},{8,16},{16,8},{24,0},{1,25},{9,17},{17,9},{25,1},{2,26},{10... | collective-permute-start | bytes 1179656 | tf_op jit(solution)/shard_map/ppermute | solution.py:33
  145.7 13.3 %collective-permute-start.42 = (bf16[4,384,128]{2,1,0:T(8,128)(2,1)S(1)}, bf16[4,384,128]{2,1,0:T(8,128)(2,1)S(1)}, u32[]{:S(2)}, u32[]{:S(2)}) collective-permute-start(bf16[4,384,128]{2,1,0:T(8,128)(2,1)S(1)} %pad_maximum_fusion.9), channel_id=1, source_target_pairs={{0,96},{32,64},{64,32},{96,0},{1,97},{33,65},{65,33},{97,1},{2,98}... | collective-permute-start | bytes 1179656 | tf_op jit(solution)/shard_map/ppermute | solution.py:33
  148.0 23.3 %collective-permute-start.39 = (bf16[8,384,128]{2,1,0:T(8,128)(2,1)S(1)}, bf16[8,384,128]{2,1,0:T(8,128)(2,1)}, u32[]{:S(2)}, u32[]{:S(2)}) collective-permute-start(bf16[8,384,128]{2,1,0:T(8,128)(2,1)S(1)} %pad_maximum_fusion.2.rest_4_.rest_5_), channel_id=1, source_target_pairs={{0,96},{32,64},{64,32},{96,0},{1,97},{33,65},{65,33},{97,1},{2,98}... | collective-permute-start | bytes 2359304 | tf_op jit(solution)/shard_map/ppermute | solution.py:33
  152.2 19.1 %collective-permute-start.29 = (bf16[8,384,128]{2,1,0:T(8,128)(2,1)S(1)}, bf16[8,384,128]{2,1,0:T(8,128)(2,1)}, u32[]{:S(2)}, u32[]{:S(2)}) collective-permute-start(bf16[8,384,128]{2,1,0:T(8,128)(2,1)S(1)} %pad_maximum_fusion.rest_0_.rest_1_), channel_id=1, source_target_pairs={{0,24},{8,16},{16,8},{24,0},{1,25},{9,17},{17,9},{25,1},{2,26},{10... | collective-permute-start | bytes 2359304 | tf_op jit(solution)/shard_map/ppermute | solution.py:33
  152.8 18.5 %collective-permute-start.34 = (bf16[8,384,128]{2,1,0:T(8,128)(2,1)S(1)}, bf16[8,384,128]{2,1,0:T(8,128)(2,1)}, u32[]{:S(2)}, u32[]{:S(2)}) collective-permute-start(bf16[8,384,128]{2,1,0:T(8,128)(2,1)S(1)} %pad_maximum_fusion.1.rest_2_.rest_3_), channel_id=1, source_target_pairs={{0,8},{8,0},{16,24},{24,16},{1,9},{9,1},{17,25},{25,17},{2,10},{10... | collective-permute-start | bytes 2359304 | tf_op jit(solution)/shard_map/ppermute | solution.py:33
  159.1 12.2 %collective-permute-start.43 = (bf16[8,384,128]{2,1,0:T(8,128)(2,1)S(1)}, bf16[8,384,128]{2,1,0:T(8,128)(2,1)}, u32[]{:S(2)}, u32[]{:S(2)}) collective-permute-start(bf16[8,384,128]{2,1,0:T(8,128)(2,1)S(1)} %pad_maximum_fusion.3.rest_6_.rest_7_), channel_id=1, source_target_pairs={{0,32},{32,0},{64,96},{96,64},{1,33},{33,1},{65,97},{97,65},{2,34}... | collective-permute-start | bytes 2359304 | tf_op jit(solution)/shard_map/ppermute | solution.py:33
  (21 other events, 139.5 us)
Sparse Core Ops, SparseCore 0:
  80.9 47.7 all-gather.2

commit v15 on v14

--- a/solution.py
+++ b/solution.py
@@ -279,8 +279,8 @@
     state, sent = step(where, state, inverse, block, 2, (got,))
     sent_2 = jnp.where(x == 2, sent_2, sent_1)
     sent = jnp.where(x == 3, sent, sent_2)
+    far = hop(sent, (2, 0), (3, 1))
     back = hop(sent, (1, 0), (2, 1), (3, 2))
-    far = hop(sent, (2, 0), (3, 1))
     wrap = hop(sent, (3, 0))
     panel_1 = jnp.where(x == 1, sent, jnp.where(x == 0, back, gots_1[0] + gots_1[1]))
     panel_2 = jnp.where(x == 2, sent, jnp.where(x == 3, got, jnp.where(x == 1, back, far)))

time: 197 us -> 197 us (level)
  no operation moved by 1% of the time
where the time goes in v15:
time: 197 us
  waiting for transfers between devices  78.8 us (40%)
  starting transfers between devices  60.6 us (31%)
  Pallas kernels  28.5 us (14%)
  between operations  13.9 us (7%)
  other arithmetic  7.46 us (4%)
  local copies, waits for them, and re-layouts  7.3 us (4%)
    ppermute x20, waiting for transfers between devices, swap(): return lax.ppermute(value, axis, [(i, i ^ flip) for i in range(4)])  42 us
    ppermute x21, starting transfers between devices, permute(): return lax.ppermute(value, ROWS, [(flat(*a), flat(*b)) for a, b in moves])  38.2 us
    ppermute x21, waiting for transfers between devices, permute(): return lax.ppermute(value, ROWS, [(flat(*a), flat(*b)) for a, b in moves])  35.1 us
    ppermute x20, starting transfers between devices, swap(): return lax.ppermute(value, axis, [(i, i ^ flip) for i in range(4)])  22.2 us
    pallas_call x1, Pallas kernels, update(): pl.pallas_call(update_kernel, grid_spec=pltpu.PrefetchScalarGridSpec(num_...  18.5 us
    pallas_call x4, Pallas kernels, step(): pl.pallas_call(kernel, grid_spec=pltpu.PrefetchScalarGridSpec(num_scalar_...  6.36 us
    reshape x1, local copies, waits for them, and re-layouts, local(): flat_factor = factor.reshape(2, 512, 1024)  4.46 us
  transfers between devices with their start and end apart: 45, of which 20 were waited for; matrix products, arithmetic and copies ran while one was open for 5% of the time, Pallas kernels for 3%

profile of v15, /device:TPU:6, one launch (start us, length us, event | category | flops | bytes accessed | tf_op | source)
XLA Modules:
  0.0 196.6 jit_solution(10975847774286340304)
XLA Ops:
  8.9 3.7 %shard_map.37 = (bf16[608,512]{1,0:T(8,128)(2,1)S(1)}, bf16[608,512]{1,0:T(8,128)(2,1)S(1)}, bf16[608,512]{1,0:T(8,128)(2,1)}, bf16[608,512]{1,0:T(8,128)(2,1)},...) custom-call(f32[2,512,2048]{2,1,0:T(8,128)} %rhs_ref.3, ...), custom_call_target="tpu_custom_call" | custom-call | tf_op jit(solution)/shard_map/pallas_call | solution.py:88
  12.6 4.3 %collective-permute-start.1 = (bf16[608,512]{1,0:T(8,128)(2,1)S(1)}, bf16[608,512]{1,0:T(8,128)(2,1)}, u32[]{:S(2)}, u32[]{:S(2)}) collective-permute-start(bf16[608,512]{1,0:T(8,128)(2,1)S(1)} %get-tuple-element.39), channel_id=1, source_target_pairs={{0,32},{2,34},{4,36},{6,38},{1,33},{3,35},{5,37},{7,39}} | collective-permute-start | bytes 1867784 | tf_op jit(solution)/shard_map/ppermute | solution.py:25
  16.9 3.1 %collective-permute-start.2 = (bf16[608,512]{1,0:T(8,128)(2,1)}, bf16[608,512]{1,0:T(8,128)(2,1)}, u32[]{:S(2)}, u32[]{:S(2)}) collective-permute-start(bf16[608,512]{1,0:T(8,128)(2,1)} %get-tuple-element.40), channel_id=1, source_target_pairs={{0,64},{2,66},{4,68},{6,70},{1,65},{3,67},{5,69},{7,71}} | collective-permute-start | bytes 1867784 | tf_op jit(solution)/shard_map/ppermute | solution.py:25
  20.0 2.1 %collective-permute-start.3 = (bf16[608,512]{1,0:T(8,128)(2,1)}, bf16[608,512]{1,0:T(8,128)(2,1)}, u32[]{:S(2)}, u32[]{:S(2)}) collective-permute-start(bf16[608,512]{1,0:T(8,128)(2,1)} %get-tuple-element.41), channel_id=1, source_target_pairs={{0,96},{2,98},{4,100},{6,102},{1,97},{3,99},{5,101},{7,103}} | collective-permute-start | bytes 1867784 | tf_op jit(solution)/shard_map/ppermute | solution.py:25
  22.1 2.1 %collective-permute-start.7 = (bf16[608,512]{1,0:T(8,128)(2,1)}, bf16[608,512]{1,0:T(8,128)(2,1)}, u32[]{:S(2)}, u32[]{:S(2)}) collective-permute-start(bf16[608,512]{1,0:T(8,128)(2,1)} %get-tuple-element.44), channel_id=1, source_target_pairs={{0,8},{2,10},{4,12},{6,14},{1,9},{3,11},{5,13},{7,15}} | collective-permute-start | bytes 1867784 | tf_op jit(solution)/shard_map/ppermute | solution.py:25
  26.4 4.1 %collective-permute-done.1 = bf16[608,512]{1,0:T(8,128)(2,1)} collective-permute-done((bf16[608,512]{1,0:T(8,128)(2,1)S(1)}, bf16[608,512]{1,0:T(8,128)(2,1)}, u32[]{:S(2)}, u32[]{:S(2)}) %collective-permute-start.1) | collective-permute-done | bytes 622624 | tf_op jit(solution)/shard_map/ppermute | solution.py:25
  34.0 8.7 %collective-permute-done.2 = bf16[608,512]{1,0:T(8,128)(2,1)} collective-permute-done((bf16[608,512]{1,0:T(8,128)(2,1)}, bf16[608,512]{1,0:T(8,128)(2,1)}, u32[]{:S(2)}, u32[]{:S(2)}) %collective-permute-start.2) | collective-permute-done | bytes 622624 | tf_op jit(solution)/shard_map/ppermute | solution.py:25
  44.3 5.9 %collective-permute-done.8 = bf16[608,512]{1,0:T(8,128)(2,1)} collective-permute-done((bf16[608,512]{1,0:T(8,128)(2,1)S(1)}, bf16[608,512]{1,0:T(8,128)(2,1)}, u32[]{:S(2)}, u32[]{:S(2)}) %collective-permute-start.8) | collective-permute-done | bytes 622624 | tf_op jit(solution)/shard_map/ppermute | solution.py:25
  59.4 6.0 %collective-permute-start.4 = (bf16[896,128]{1,0:T(8,128)(2,1)S(1)}, bf16[896,128]{1,0:T(8,128)(2,1)S(1)}, u32[]{:S(2)}, u32[]{:S(2)}) collective-permute-start(bf16[896,128]{1,0:T(8,128)(2,1)S(1)} %get-tuple-element.77), channel_id=1, source_target_pairs={{0,16},{32,48},{64,80},{96,112},{2,18},{34,50},{66,82},{98,114},{4... | collective-permute-start | bytes 688136 | tf_op jit(solution)/shard_map/ppermute | solution.py:25
  65.6 3.3 %collective-permute-done.4 = bf16[896,128]{1,0:T(8,128)(2,1)S(1)} collective-permute-done((bf16[896,128]{1,0:T(8,128)(2,1)S(1)}, bf16[896,128]{1,0:T(8,128)(2,1)S(1)}, u32[]{:S(2)}, u32[]{:S(2)}) %collective-permute-start.4) | collective-permute-done | bytes 229408 | tf_op jit(solution)/shard_map/ppermute | solution.py:25
  72.9 2.6 %collective-permute-start.13 = (bf16[384,128]{1,0:T(8,128)(2,1)S(1)}, bf16[384,128]{1,0:T(8,128)(2,1)S(1)}, u32[]{:S(2)}, u32[]{:S(2)}) collective-permute-start(bf16[384,128]{1,0:T(8,128)(2,1)S(1)} %slice.120), channel_id=1, source_target_pairs={{0,32},{32,0},{64,96},{96,64},{1,33},{33,1},{65,97},{97,65},{2,34}... | collective-permute-start | bytes 294920 | tf_op jit(solution)/shard_map/ppermute | solution.py:33
  75.4 2.6 %collective-permute-done.13 = bf16[384,128]{1,0:T(8,128)(2,1)S(1)} collective-permute-done((bf16[384,128]{1,0:T(8,128)(2,1)S(1)}, bf16[384,128]{1,0:T(8,128)(2,1)S(1)}, u32[]{:S(2)}, u32[]{:S(2)}) %collective-permute-start.13) | collective-permute-done | bytes 98336 | tf_op jit(solution)/shard_map/ppermute | solution.py:33
  80.8 2.6 %collective-permute-start.19 = (bf16[2,384,128]{2,1,0:T(8,128)(2,1)S(1)}, bf16[2,384,128]{2,1,0:T(8,128)(2,1)S(1)}, u32[]{:S(2)}, u32[]{:S(2)}) collective-permute-start(bf16[2,384,128]{2,1,0:T(8,128)(2,1)S(1)} %pad_maximum_fusion.11), channel_id=1, source_target_pairs={{0,24},{8,16},{16,8},{24,0},{1,25},{9,17},{17,9},{25,1},{2,26},{10... | collective-permute-start | bytes 589832 | tf_op jit(solution)/shard_map/ppermute | solution.py:33
  83.5 4.2 %collective-permute-done.19 = bf16[2,384,128]{2,1,0:T(8,128)(2,1)S(1)} collective-permute-done((bf16[2,384,128]{2,1,0:T(8,128)(2,1)S(1)}, bf16[2,384,128]{2,1,0:T(8,128)(2,1)S(1)}, u32[]{:S(2)}, u32[]{:S(2)}) %collective-permute-start.19) | collective-permute-done | bytes 196640 | tf_op jit(solution)/shard_map/ppermute | solution.py:33
  87.9 2.5 %collective-permute-done.18 = bf16[2,384,128]{2,1,0:T(8,128)(2,1)S(1)} collective-permute-done((bf16[2,384,128]{2,1,0:T(8,128)(2,1)S(1)}, bf16[2,384,128]{2,1,0:T(8,128)(2,1)S(1)}, u32[]{:S(2)}, u32[]{:S(2)}) %collective-permute-start.18) | collective-permute-done | bytes 196640 | tf_op jit(solution)/shard_map/ppermute | solution.py:33
  95.9 7.0 %collective-permute-done.23.refs_9_ = bf16[512,128]{1,0:T(8,128)(2,1)S(1)} collective-permute-done((bf16[512,128]{1,0:T(8,128)(2,1)S(1)}, bf16[512,128]{1,0:T(8,128)(2,1)S(1)}, u32[]{:S(2)}, u32[]{:S(2)}) %collective-permute-start.23) | collective-permute-done | bytes 131104 | tf_op jit(solution)/shard_map/ppermute | solution.py:25
  105.8 5.6 %collective-permute-done.24.refs_8_ = bf16[512,128]{1,0:T(8,128)(2,1)S(1)} collective-permute-done((bf16[512,128]{1,0:T(8,128)(2,1)S(1)}, bf16[512,128]{1,0:T(8,128)(2,1)S(1)}, u32[]{:S(2)}, u32[]{:S(2)}) %collective-permute-start.24) | collective-permute-done | bytes 131104 | tf_op jit(solution)/shard_map/ppermute | solution.py:25
  117.2 4.5 %reshape.179.mine_ref = bf16[2,512,1024]{2,1,0:T(8,128)(2,1)} reshape(bf16[2,512,4,256]{3,2,1,0:T(4,128)(2,1)} %param.4) | data formatting | bytes 4194304 | tf_op jit(solution)/shard_map/reshape | solution.py:290
  125.6 2.3 %collective-permute-done.36 = bf16[1,384,128]{2,1,0:T(8,128)(2,1)S(1)} collective-permute-done((bf16[1,384,128]{2,1,0:T(8,128)(2,1)S(1)}, bf16[1,384,128]{2,1,0:T(8,128)(2,1)S(1)}, u32[]{:S(2)}, u32[]{:S(2)}) %collective-permute-start.36) | collective-permute-done | bytes 98336 | tf_op jit(solution)/shard_map/ppermute | solution.py:33
  132.4 3.7 %collective-permute-done.37 = bf16[2,384,128]{2,1,0:T(8,128)(2,1)S(1)} collective-permute-done((bf16[2,384,128]{2,1,0:T(8,128)(2,1)S(1)}, bf16[2,384,128]{2,1,0:T(8,128)(2,1)S(1)}, u32[]{:S(2)}, u32[]{:S(2)}) %collective-permute-start.37) | collective-permute-done | bytes 196640 | tf_op jit(solution)/shard_map/ppermute | solution.py:33
  141.2 4.4 %collective-permute-done.41 = bf16[2,384,128]{2,1,0:T(8,128)(2,1)S(1)} collective-permute-done((bf16[2,384,128]{2,1,0:T(8,128)(2,1)S(1)}, bf16[2,384,128]{2,1,0:T(8,128)(2,1)S(1)}, u32[]{:S(2)}, u32[]{:S(2)}) %collective-permute-start.41) | collective-permute-done | bytes 196640 | tf_op jit(solution)/shard_map/ppermute | solution.py:33
  153.2 5.8 %collective-permute-done.42 = bf16[4,384,128]{2,1,0:T(8,128)(2,1)S(1)} collective-permute-done((bf16[4,384,128]{2,1,0:T(8,128)(2,1)S(1)}, bf16[4,384,128]{2,1,0:T(8,128)(2,1)S(1)}, u32[]{:S(2)}, u32[]{:S(2)}) %collective-permute-start.42) | collective-permute-done | bytes 393248 | tf_op jit(solution)/shard_map/ppermute | solution.py:33
  159.4 11.9 %collective-permute-done.39.rest_12_.rest_13_ = bf16[8,384,128]{2,1,0:T(8,128)(2,1)} collective-permute-done((bf16[8,384,128]{2,1,0:T(8,128)(2,1)S(1)}, bf16[8,384,128]{2,1,0:T(8,128)(2,1)}, u32[]{:S(2)}, u32[]{:S(2)}) %collective-permute-start.39) | collective-permute-done | bytes 786464 | tf_op jit(solution)/shard_map/ppermute | solution.py:33
  171.3 18.5 %shard_map.42 = f32[2,512,2048]{2,1,0:T(8,128)} custom-call(s32[66]{0:T(128)S(1)} %pad_add_fusion.1.scalars, bf16[2,512,1024]{2,1,0:T(8,128)(2,1)} %reshape.179.mine_ref, bf16[2,512,1024]{2,1,0:T(8,128)(2,1)} %collective-permute-done.other_ref, f32[2,512,2048]{2,1,0:T(8,128)} %rhs_ref.3, bf16[16,512,128]{2,1,0:T(8,128)(2,1)} %bitcast.27, ...), custom_call_target="tpu_custom_call" | custom-call | tf_op jit(solution)/shard_map/pallas_call | solution.py:203
  (130 shorter events, 61.2 us)
Async XLA Ops:
  6.5 131.1 %all-gather.3.cloned.1.call-start = ((), (), s32[]{:S(2)}) async-start(), calls=%async_computation | async-start | bytes 2228224 | tf_op jit(solution)/shard_map/all_gather | solution.py:274
  12.6 17.9 %collective-permute-start.1 = (bf16[608,512]{1,0:T(8,128)(2,1)S(1)}, bf16[608,512]{1,0:T(8,128)(2,1)}, u32[]{:S(2)}, u32[]{:S(2)}) collective-permute-start(bf16[608,512]{1,0:T(8,128)(2,1)S(1)} %get-tuple-element.39), channel_id=1, source_target_pairs={{0,32},{2,34},{4,36},{6,38},{1,33},{3,35},{5,37},{7,39}} | collective-permute-start | bytes 1867784 | tf_op jit(solution)/shard_map/ppermute | solution.py:25
  16.9 25.9 %collective-permute-start.2 = (bf16[608,512]{1,0:T(8,128)(2,1)}, bf16[608,512]{1,0:T(8,128)(2,1)}, u32[]{:S(2)}, u32[]{:S(2)}) collective-permute-start(bf16[608,512]{1,0:T(8,128)(2,1)} %get-tuple-element.40), channel_id=1, source_target_pairs={{0,64},{2,66},{4,68},{6,70},{1,65},{3,67},{5,69},{7,71}} | collective-permute-start | bytes 1867784 | tf_op jit(solution)/shard_map/ppermute | solution.py:25
  20.0 22.7 %collective-permute-start.3 = (bf16[608,512]{1,0:T(8,128)(2,1)}, bf16[608,512]{1,0:T(8,128)(2,1)}, u32[]{:S(2)}, u32[]{:S(2)}) collective-permute-start(bf16[608,512]{1,0:T(8,128)(2,1)} %get-tuple-element.41), channel_id=1, source_target_pairs={{0,96},{2,98},{4,100},{6,102},{1,97},{3,99},{5,101},{7,103}} | collective-permute-start | bytes 1867784 | tf_op jit(solution)/shard_map/ppermute | solution.py:25
  22.1 22.2 %collective-permute-start.7 = (bf16[608,512]{1,0:T(8,128)(2,1)}, bf16[608,512]{1,0:T(8,128)(2,1)}, u32[]{:S(2)}, u32[]{:S(2)}) collective-permute-start(bf16[608,512]{1,0:T(8,128)(2,1)} %get-tuple-element.44), channel_id=1, source_target_pairs={{0,8},{2,10},{4,12},{6,14},{1,9},{3,11},{5,13},{7,15}} | collective-permute-start | bytes 1867784 | tf_op jit(solution)/shard_map/ppermute | solution.py:25
  24.3 26.0 %collective-permute-start.8 = (bf16[608,512]{1,0:T(8,128)(2,1)S(1)}, bf16[608,512]{1,0:T(8,128)(2,1)}, u32[]{:S(2)}, u32[]{:S(2)}) collective-permute-start(bf16[608,512]{1,0:T(8,128)(2,1)S(1)} %get-tuple-element.45), channel_id=1, source_target_pairs={{0,16},{2,18},{4,20},{6,22},{1,17},{3,19},{5,21},{7,23}} | collective-permute-start | bytes 1867784 | tf_op jit(solution)/shard_map/ppermute | solution.py:25
  30.4 19.8 %collective-permute-start.9 = (bf16[608,512]{1,0:T(8,128)(2,1)S(1)}, bf16[608,512]{1,0:T(8,128)(2,1)}, u32[]{:S(2)}, u32[]{:S(2)}) collective-permute-start(bf16[608,512]{1,0:T(8,128)(2,1)S(1)} %get-tuple-element.46), channel_id=1, source_target_pairs={{0,24},{2,26},{4,28},{6,30},{1,25},{3,27},{5,29},{7,31}} | collective-permute-start | bytes 1867784 | tf_op jit(solution)/shard_map/ppermute | solution.py:25
  53.3 12.0 %collective-permute-start.12 = (bf16[896,128]{1,0:T(8,128)(2,1)S(1)}, bf16[896,128]{1,0:T(8,128)(2,1)S(1)}, u32[]{:S(2)}, u32[]{:S(2)}) collective-permute-start(bf16[896,128]{1,0:T(8,128)(2,1)S(1)} %get-tuple-element.104), channel_id=1, source_target_pairs={{0,96},{8,104},{16,112},{24,120},{2,98},{10,106},{18,114},{26,122}... | collective-permute-start | bytes 688136 | tf_op jit(solution)/shard_map/ppermute | solution.py:25
  54.6 10.7 %collective-permute-start.10 = (bf16[896,128]{1,0:T(8,128)(2,1)S(1)}, bf16[896,128]{1,0:T(8,128)(2,1)S(1)}, u32[]{:S(2)}, u32[]{:S(2)}) collective-permute-start(bf16[896,128]{1,0:T(8,128)(2,1)S(1)} %get-tuple-element.94), channel_id=1, source_target_pairs={{0,64},{8,72},{16,80},{24,88},{2,66},{10,74},{18,82},{26,90},{4,68... | collective-permute-start | bytes 688136 | tf_op jit(solution)/shard_map/ppermute | solution.py:25
  56.2 9.3 %collective-permute-start.5 = (bf16[896,128]{1,0:T(8,128)(2,1)S(1)}, bf16[896,128]{1,0:T(8,128)(2,1)S(1)}, u32[]{:S(2)}, u32[]{:S(2)}) collective-permute-start(bf16[896,128]{1,0:T(8,128)(2,1)S(1)} %get-tuple-element.86), channel_id=1, source_target_pairs={{0,8},{32,40},{64,72},{96,104},{2,10},{34,42},{66,74},{98,106},{4,... | collective-permute-start | bytes 688136 | tf_op jit(solution)/shard_map/ppermute | solution.py:25
  59.4 9.5 %collective-permute-start.4 = (bf16[896,128]{1,0:T(8,128)(2,1)S(1)}, bf16[896,128]{1,0:T(8,128)(2,1)S(1)}, u32[]{:S(2)}, u32[]{:S(2)}) collective-permute-start(bf16[896,128]{1,0:T(8,128)(2,1)S(1)} %get-tuple-element.77), channel_id=1, source_target_pairs={{0,16},{32,48},{64,80},{96,112},{2,18},{34,50},{66,82},{98,114},{4... | collective-permute-start | bytes 688136 | tf_op jit(solution)/shard_map/ppermute | solution.py:25
  70.2 9.9 %collective-permute-start.17 = (bf16[512,128]{1,0:T(8,128)(2,1)S(1)}, bf16[512,128]{1,0:T(8,128)(2,1)S(1)}, u32[]{:S(2)}, u32[]{:S(2)}) collective-permute-start(bf16[512,128]{1,0:T(8,128)(2,1)S(1)} %shard_map.38), channel_id=1, source_target_pairs={{0,4},{8,12},{16,20},{24,28},{32,36},{40,44},{48,52},{56,60},{64,6... | collective-permute-start | bytes 393224 | tf_op jit(solution)/shard_map/ppermute | solution.py:25
  70.8 9.2 %collective-permute-start.16 = (bf16[512,128]{1,0:T(8,128)(2,1)S(1)}, bf16[512,128]{1,0:T(8,128)(2,1)S(1)}, u32[]{:S(2)}, u32[]{:S(2)}) collective-permute-start(bf16[512,128]{1,0:T(8,128)(2,1)S(1)} %shard_map.38), channel_id=1, source_target_pairs={{0,6},{8,14},{16,22},{24,30},{32,38},{40,46},{48,54},{56,62},{64,7... | collective-permute-start | bytes 393224 | tf_op jit(solution)/shard_map/ppermute | solution.py:25
  121.7 37.7 %collective-permute-start = (bf16[2,512,1024]{2,1,0:T(8,128)(2,1)}, bf16[2,512,1024]{2,1,0:T(8,128)(2,1)}, u32[]{:S(2)}, u32[]{:S(2)}) collective-permute-start(bf16[2,512,1024]{2,1,0:T(8,128)(2,1)} %reshape.179.mine_ref), channel_id=1, source_target_pairs={{0,1},{1,0},{2,3},{3,2},{4,5},{5,4},{6,7},{7,6},{8,9},{9,8},{10,11... | collective-permute-start | bytes 6291464 | tf_op jit(solution)/shard_map/ppermute | solution.py:291
  124.6 13.1 %collective-permute-start.40 = (bf16[1,384,128]{2,1,0:T(8,128)(2,1)S(1)}, bf16[1,384,128]{2,1,0:T(8,128)(2,1)S(1)}, u32[]{:S(2)}, u32[]{:S(2)}) collective-permute-start(bf16[1,384,128]{2,1,0:T(8,128)(2,1)S(1)} %slice_bitcast_fusion), channel_id=1, source_target_pairs={{0,24},{8,16},{16,8},{24,0},{1,25},{9,17},{17,9},{25,1},{2,26},{10... | collective-permute-start | bytes 294920 | tf_op jit(solution)/shard_map/ppermute | solution.py:33
  129.9 10.0 %collective-permute-start.32 = (bf16[2,384,128]{2,1,0:T(8,128)(2,1)S(1)}, bf16[2,384,128]{2,1,0:T(8,128)(2,1)S(1)}, u32[]{:S(2)}, u32[]{:S(2)}) collective-permute-start(bf16[2,384,128]{2,1,0:T(8,128)(2,1)S(1)} %pad_maximum_fusion.13), channel_id=1, source_target_pairs={{0,32},{32,0},{64,96},{96,64},{1,33},{33,1},{65,97},{97,65},{2,34}... | collective-permute-start | bytes 589832 | tf_op jit(solution)/shard_map/ppermute | solution.py:33
  136.2 10.7 %collective-permute-start.38 = (bf16[4,384,128]{2,1,0:T(8,128)(2,1)S(1)}, bf16[4,384,128]{2,1,0:T(8,128)(2,1)}, u32[]{:S(2)}, u32[]{:S(2)}) collective-permute-start(bf16[4,384,128]{2,1,0:T(8,128)(2,1)S(1)} %pad_maximum_fusion.8), channel_id=1, source_target_pairs={{0,32},{32,0},{64,96},{96,64},{1,33},{33,1},{65,97},{97,65},{2,34}... | collective-permute-start | bytes 1179656 | tf_op jit(solution)/shard_map/ppermute | solution.py:33
  138.1 14.0 %collective-permute-start.28 = (bf16[4,384,128]{2,1,0:T(8,128)(2,1)S(1)}, bf16[4,384,128]{2,1,0:T(8,128)(2,1)S(1)}, u32[]{:S(2)}, u32[]{:S(2)}) collective-permute-start(bf16[4,384,128]{2,1,0:T(8,128)(2,1)S(1)} %pad_maximum_fusion.6), channel_id=1, source_target_pairs={{0,8},{8,0},{16,24},{24,16},{1,9},{9,1},{17,25},{25,17},{2,10},{10... | collective-permute-start | bytes 1179656 | tf_op jit(solution)/shard_map/ppermute | solution.py:33
  140.0 12.7 %collective-permute-start.33 = (bf16[4,384,128]{2,1,0:T(8,128)(2,1)S(1)}, bf16[4,384,128]{2,1,0:T(8,128)(2,1)S(1)}, u32[]{:S(2)}, u32[]{:S(2)}) collective-permute-start(bf16[4,384,128]{2,1,0:T(8,128)(2,1)S(1)} %pad_maximum_fusion.7), channel_id=1, source_target_pairs={{0,24},{8,16},{16,8},{24,0},{1,25},{9,17},{17,9},{25,1},{2,26},{10... | collective-permute-start | bytes 1179656 | tf_op jit(solution)/shard_map/ppermute | solution.py:33
  145.7 13.3 %collective-permute-start.42 = (bf16[4,384,128]{2,1,0:T(8,128)(2,1)S(1)}, bf16[4,384,128]{2,1,0:T(8,128)(2,1)S(1)}, u32[]{:S(2)}, u32[]{:S(2)}) collective-permute-start(bf16[4,384,128]{2,1,0:T(8,128)(2,1)S(1)} %pad_maximum_fusion.9), channel_id=1, source_target_pairs={{0,96},{32,64},{64,32},{96,0},{1,97},{33,65},{65,33},{97,1},{2,98}... | collective-permute-start | bytes 1179656 | tf_op jit(solution)/shard_map/ppermute | solution.py:33
  148.0 23.3 %collective-permute-start.39 = (bf16[8,384,128]{2,1,0:T(8,128)(2,1)S(1)}, bf16[8,384,128]{2,1,0:T(8,128)(2,1)}, u32[]{:S(2)}, u32[]{:S(2)}) collective-permute-start(bf16[8,384,128]{2,1,0:T(8,128)(2,1)S(1)} %pad_maximum_fusion.2.rest_4_.rest_5_), channel_id=1, source_target_pairs={{0,96},{32,64},{64,32},{96,0},{1,97},{33,65},{65,33},{97,1},{2,98}... | collective-permute-start | bytes 2359304 | tf_op jit(solution)/shard_map/ppermute | solution.py:33
  152.2 19.1 %collective-permute-start.29 = (bf16[8,384,128]{2,1,0:T(8,128)(2,1)S(1)}, bf16[8,384,128]{2,1,0:T(8,128)(2,1)}, u32[]{:S(2)}, u32[]{:S(2)}) collective-permute-start(bf16[8,384,128]{2,1,0:T(8,128)(2,1)S(1)} %pad_maximum_fusion.rest_0_.rest_1_), channel_id=1, source_target_pairs={{0,24},{8,16},{16,8},{24,0},{1,25},{9,17},{17,9},{25,1},{2,26},{10... | collective-permute-start | bytes 2359304 | tf_op jit(solution)/shard_map/ppermute | solution.py:33
  152.8 18.5 %collective-permute-start.34 = (bf16[8,384,128]{2,1,0:T(8,128)(2,1)S(1)}, bf16[8,384,128]{2,1,0:T(8,128)(2,1)}, u32[]{:S(2)}, u32[]{:S(2)}) collective-permute-start(bf16[8,384,128]{2,1,0:T(8,128)(2,1)S(1)} %pad_maximum_fusion.1.rest_2_.rest_3_), channel_id=1, source_target_pairs={{0,8},{8,0},{16,24},{24,16},{1,9},{9,1},{17,25},{25,17},{2,10},{10... | collective-permute-start | bytes 2359304 | tf_op jit(solution)/shard_map/ppermute | solution.py:33
  159.1 12.2 %collective-permute-start.43 = (bf16[8,384,128]{2,1,0:T(8,128)(2,1)S(1)}, bf16[8,384,128]{2,1,0:T(8,128)(2,1)}, u32[]{:S(2)}, u32[]{:S(2)}) collective-permute-start(bf16[8,384,128]{2,1,0:T(8,128)(2,1)S(1)} %pad_maximum_fusion.3.rest_6_.rest_7_), channel_id=1, source_target_pairs={{0,32},{32,0},{64,96},{96,64},{1,33},{33,1},{65,97},{97,65},{2,34}... | collective-permute-start | bytes 2359304 | tf_op jit(solution)/shard_map/ppermute | solution.py:33
  (21 other events, 139.5 us)
Sparse Core Ops, SparseCore 0:
  80.9 47.7 all-gather.2
